TPU v7x, 32 devices: a whole 2x2x4 slice. The times are simulated.
32 devices in a mesh: space: 4 (over z), tm: 4 (over x, core), cores: 2 (over y).
Axes of the slice: x: 2, y: 2, z: 4, core: 2. Of those that a mesh axis runs over, the one named last changes fastest.
Arguments:
- initial_state: float32 [128, 64, 512], P('space', 'cores'), may hold values from -6 to 6
- heat_source: float32 [128, 64, 512], P('space', 'cores'), may hold values from -3 to 3
- source_amplitude: float32 [32], P('tm'), may hold values from 0.5 to 1.5
- diffusivity: float32 [4], P('space'), may hold values from 0.5 to 2
- robin_param: float32 [4], P('space'), may hold values from 0.5 to 4
- spectrum_x: float32 [32], replicated, may hold values from 0.002 to 0.38
- spectrum_y: float32 [64], P('cores'), may hold values from 0.002 to 0.38
- spectrum_z: float32 [512], replicated, may hold values from 0.002 to 0.38
- robin_in: float32 [4, 2, 32, 64, 512], P('space', None, 'tm', 'cores'), may hold values from -8 to 8
- open_flag: int32 [4, 64], P(None, 'cores'), may hold values from 0 to 1, as said below
- owner_side: int32 [4, 64], P(None, 'cores'), may hold values from 0 to 1, as said below
Outputs:
- robin_out: float32 [4, 2, 32, 64, 512], P('space', None, 'tm', 'cores')
- window_end: float32 [4, 128, 64, 512], P('tm', 'space', 'cores')
Inputs may be any that keep to these rules, and one draw needn't show every extreme that they name: In each aligned group of 4 modes b of an interface exactly one has open_flag 0. In each aligned pair of modes b of an interface exactly one has owner_side 1.
All inputs are finite; a program needn't handle non-finite values.
Results may differ from a plain program's by a relative error of at most 0.00015.
Values sent between devices are 32-bit elements; how exact they have to be, the bound alone decides.
No kernel may reach another device: no remote copies, remote signals or barrier semaphores. Data moves between devices by JAX's collectives and lax.ppermute only.
A program may use at most 128 MiB of HBM per device.

v0:
```python
import functools
import jax
import numpy as np
import jax.numpy as jnp
from jax import lax
from jax.experimental import pallas as pl
from jax.experimental.pallas import tpu as pltpu
from jax.sharding import PartitionSpec as P


F32 = jnp.float32
BF16 = jnp.bfloat16
SUB = 8


VM = pl.BlockSpec(memory_space=pltpu.VMEM)
SM = pl.BlockSpec(memory_space=pltpu.SMEM)


def cosine(order, mode, node):
    mode = mode.astype(F32)
    node = node.astype(F32)
    scaling = jnp.where(mode == 0, jnp.sqrt(1.0 / order), jnp.sqrt(2.0 / order))
    return scaling * jnp.cos(jnp.pi * mode * (node + 0.5) / order)


def halves(w):
    hi = lax.reduce_precision(w, exponent_bits=8, mantissa_bits=7)
    return hi.astype(BF16), (w - hi).astype(BF16)


def iotas(rows, cols):
    shape = (rows, cols)
    return lax.broadcasted_iota(jnp.int32, shape, 0), lax.broadcasted_iota(jnp.int32, shape, 1)


def cut(x):
    hi = x.astype(BF16)
    return hi, (x - hi.astype(F32)).astype(BF16)


def mm(a, b):
    return jnp.dot(a, b, preferred_element_type=F32)


def mmt(a, b):
    return lax.dot_general(a, b, (((1,), (1,)), ((), ())), preferred_element_type=F32)


def const_times(wh, wl, x):
    xh, xl = cut(x)
    return mm(wh, xh) + mm(wh, xl) + mm(wl, xh)


def np_cosine(order, mode, node):
    mode = np.asarray(mode, np.float32)
    node = np.asarray(node, np.float32)
    scaling = np.where(mode == 0, np.sqrt(np.float32(1.0 / order)), np.sqrt(np.float32(2.0 / order)))
    angle = np.float32(np.pi) * mode * (node + np.float32(0.5)) / np.float32(order)
    return (scaling * np.cos(angle.astype(np.float64))).astype(np.float32)


def np_halves(w):
    hi = w.astype(BF16)
    return hi, (w - hi.astype(np.float32)).astype(BF16)


def np_modes(n):
    return np.concatenate([np.arange(0, n, 2), np.arange(1, n, 2)])


def np_bar(n, back):
    a = np_modes(n)
    base = np_cosine(n, a[:, None], np.arange(n)[None])
    edge = np_cosine(n, a, np.zeros(n))[:, None]
    w = (base * edge).T if back else base / edge
    return np_halves(np.kron(w, np.eye(SUB, dtype=np.float32)))


def tree(parts):
    while len(parts) > 1:
        parts = [a + b for a, b in zip(parts[::2], parts[1::2])] + (
            [parts[-1]] if len(parts) % 2 else []
        )
    return parts[0]


def split_kernel(nt, q_ref, amp_ref, *refs):
    ins, outs = refs[:nt], refs[nt:]
    steps = amp_ref.shape[0]
    rows = outs[0].shape[0] - steps
    cq = outs[0].shape[1]
    for d in range(nt):
        outs[d][0:rows, :] = ins[d][...].reshape(rows, cq)
        for k in range(steps):
            outs[d][rows + k : rows + k + 1, :] = jnp.full((1, cq), amp_ref[k], F32)


def forward_kernel(q_ref, x_ref, c_ref, kxh_ref, kxl_ref, out_ref):
    nx, _, nz = x_ref.shape
    cq = out_ref.shape[-1]
    xh, xl = cut(x_ref[...].reshape(nx * SUB, nz))
    both = mmt(xh, c_ref[...].reshape(2 * cq, nz))
    z = both[:, :cq] + both[:, cq:] + mmt(xl, c_ref[0])
    zh, zl = cut(z)
    both = mm(kxh_ref[...], jnp.concatenate([zh, zl], axis=1))
    res = both[:, :cq] + both[:, cq:] + mm(kxl_ref[...], zh)
    out_ref[...] = res.reshape(nx, SUB, cq)


def factor_into(f_ref, sx_ref, diff_ref, sy, sz):
    for a in range(f_ref.shape[0]):
        rate = (sx_ref[a] + sy) + sz
        f_ref[a] = 1.0 / (1.0 + diff_ref[0] * rate)


def gather_windows(nt, q, ins, u_s, amp_s):
    steps = amp_s.shape[1]
    rows = ins[0].shape[0] - steps
    for d in range(nt):
        w = jnp.bitwise_xor(q, d)
        u_s[w] = ins[d][0:rows, :].reshape(u_s.shape[1:])
        amp_s[w] = ins[d][rows:, :]


def own_kernel(dims, q_ref, sx_ref, diff_ref, par_ref, *refs):
    nt, steps, nx, hy, cq = dims
    n0, s0, n1, s1 = refs[:4]
    pieces = refs[4 : 4 + nt]
    (tab_ref, sz_ref, kyh_ref, kyl_ref, wv_ref, wd_ref) = refs[4 + nt : 10 + nt]
    ql_ref, qr_ref, clos_ref, mo_ref, so_ref = refs[10 + nt : 15 + nt]
    m_s, s_s, f_s, vd, u_s, amp_s = refs[15 + nt :]
    tiles = hy // SUB
    pack = kyh_ref.shape[0] // (2 * hy)
    half = pack * hy

    gather_windows(nt, q_ref[0], pieces, u_s, amp_s)
    factor_into(f_s, sx_ref, diff_ref, tab_ref[0:hy, :], sz_ref[...])

    def ytrans(ag, _):
        at = pl.ds(ag * pack, pack)
        cols = [
            jnp.concatenate([here[at].reshape(half, cq), there[at].reshape(half, cq)], axis=0)
            for here, there in ((n0, n1), (s0, s1))
        ]
        res = const_times(kyh_ref[...], kyl_ref[...], jnp.concatenate(cols, axis=1))
        for f, own, oth in ((0, m_s, mo_ref), (1, s_s, so_ref)):
            part = res[:, f * cq : (f + 1) * cq]
            own[at] = part[:half].reshape(pack, hy, cq)
            oth[at] = part[half:].reshape(pack, hy, cq)
        return 0

    lax.fori_loop(0, nx // pack, ytrans, 0)
    ha = nx // 2
    chunk = min(SUB, ha)
    for j in range(tiles):
        rows = slice(j * SUB, (j + 1) * SUB)
        for par in range(2):
            for first in range(0, ha, chunk):
                modes = [par * ha + first + i for i in range(chunk)]
                s = [s_s[a, rows, :] for a in modes]
                f = [f_s[a, rows, :] for a in modes]
                wv = [wv_ref[a] for a in modes]
                wd = [wd_ref[a] for a in modes]

                def window(w, cur, j=j, par=par, first=first, rows=rows, modes=modes, s=s, f=f, wv=wv, wd=wd):
                    cur = list(cur)
                    for k in range(steps):
                        r0 = u_s[w, 0, k, pl.ds(j, SUB, stride=tiles), :]
                        r1 = u_s[w, 1, k, pl.ds(j, SUB, stride=tiles), :]
                        u = r0 + r1 if par == 0 else r0 - r1
                        amp = amp_s[w, k : k + 1, :]
                        cur = [(x + (amp * y + u)) * z for x, y, z in zip(cur, s, f)]
                        m = w * steps + k
                        v = tree([x * y for x, y in zip(cur, wv)])
                        d = tree([x * y for x, y in zip(cur, wd)])
                        if first:
                            v = v + vd[par, 0, m, j]
                            d = d + vd[par, 1, m, j]
                        vd[par, 0, m, j] = v
                        vd[par, 1, m, j] = d
                    for a, x in zip(modes, cur):
                        clos_ref[w, a, rows, :] = x
                    return tuple(cur)

                lax.fori_loop(0, nt, window, tuple(m_s[a, rows, :] for a in modes))

    owner, closed = tab_ref.at[hy : 3 * hy], tab_ref.at[3 * hy :]

    def combine(m, _):
        left, right = [], []
        for j in range(tiles):
            ve, vo = vd[0, 0, m, j], vd[1, 0, m, j]
            de, do = vd[0, 1, m, j], vd[1, 1, m, j]
            p = [
                jnp.where(owner[i * hy + j * SUB : i * hy + (j + 1) * SUB, :] < 0.5, par_ref[i], par_ref[i + 1])
                for i in range(2)
            ]
            left.append((de + do) + p[0] * (ve + vo))
            right.append(p[1] * (ve - vo) + (de - do))
        for i in range(tiles - 1):
            rows = slice(i * SUB, (i + 1) * SUB)
            le = [closed[(n * (tiles - 1) + i) * SUB : (n * (tiles - 1) + i + 1) * SUB, :] > 0.5 for n in range(2)]
            ql_ref[m, rows, :] = jnp.where(le[0], left[i + 1], left[i])
            qr_ref[m, rows, :] = jnp.where(le[1], right[i + 1], right[i])
        return 0

    lax.fori_loop(0, nt * steps, combine, 0)


def other_kernel(dims, q_ref, sx_ref, diff_ref, m_ref, s_ref, *refs):
    nt, steps, nx, hy, cq = dims
    pieces = refs[:nt]
    sy_ref, sz_ref, clos_ref, kih_ref, kil_ref, kxh_ref, kxl_ref = refs[nt : nt + 7]
    outs = refs[nt + 7 : 2 * nt + 7]
    f_s, cl, t_s, u_s, amp_s = refs[2 * nt + 7 :]
    tiles = hy // SUB
    gather_windows(nt, q_ref[0], pieces, u_s, amp_s)
    factor_into(f_s, sx_ref, diff_ref, sy_ref[...], sz_ref[...])
    ha = nx // 2
    for j in range(tiles):
        rows = slice(j * SUB, (j + 1) * SUB)
        for par in range(2):
            modes = [par * ha + i for i in range(ha)]
            s = [s_ref[a, rows, :] for a in modes]
            f = [f_s[a, rows, :] for a in modes]

            def window(w, cur, j=j, par=par, rows=rows, modes=modes, s=s, f=f):
                cur = list(cur)
                for k in range(steps):
                    r0 = u_s[w, 0, k, pl.ds(j, SUB, stride=tiles), :]
                    r1 = u_s[w, 1, k, pl.ds(j, SUB, stride=tiles), :]
                    u = r0 + r1 if par == 0 else r0 - r1
                    amp = amp_s[w, k : k + 1, :]
                    cur = [(x + (amp * y + u)) * z for x, y, z in zip(cur, s, f)]
                for a, x in zip(modes, cur):
                    cl[w, a, rows, :] = x
                return tuple(cur)

            lax.fori_loop(0, nt, window, tuple(m_ref[a, rows, :] for a in modes))
    pack = kih_ref.shape[0] // hy
    half = pack * hy
    for e in range(0, nt, 2):
        ws = [jnp.bitwise_xor(q_ref[0], e + i) for i in range(2)]

        def yback(ag, _, ws=ws):
            at = pl.ds(ag * pack, pack)
            cols = [
                jnp.concatenate([clos_ref[w, at].reshape(half, cq), cl[w, at].reshape(half, cq)], axis=0)
                for w in ws
            ]
            res = const_times(kih_ref[...], kil_ref[...], jnp.concatenate(cols, axis=1))
            t_s[at] = res.reshape(pack, hy, 2 * cq)
            return 0

        lax.fori_loop(0, nx // pack, yback, 0)
        for yb in range(tiles):
            x = t_s[:, yb * SUB : (yb + 1) * SUB, :].reshape(nx * SUB, 2 * cq)
            res = const_times(kxh_ref[...], kxl_ref[...], x).reshape(nx, SUB, 2 * cq)
            for i in range(2):
                outs[e + i][:, yb * SUB : (yb + 1) * SUB, :] = res[:, :, i * cq : (i + 1) * cq]


def final_kernel(nt, q_ref, *refs):
    ws, ins, out_ref, wh, wl = refs[:nt], refs[nt : 2 * nt], refs[2 * nt], refs[2 * nt + 1], refs[2 * nt + 2]
    xb, hy, nz = out_ref.shape[1:]
    cq = nz // nt

    @pl.when(pl.program_id(0) == 0)
    def _():
        for d in range(nt):
            wh[d * cq : (d + 1) * cq, :] = ws[d][0]
            wl[d * cq : (d + 1) * cq, :] = ws[d][1]

    xh, xl = cut(jnp.concatenate([x[...].reshape(xb * hy, cq) for x in ins], axis=1))
    res = mm(xh, wh[...]) + mm(xh, wl[...]) + mm(xl, wh[...])
    out_ref[0] = res.reshape(xb, hy, nz)


def deal_kernel(nt, steps, q_ref, f0_ref, f1_ref, *outs):
    for d in range(nt):
        w = jnp.bitwise_xor(q_ref[0], d)
        outs[d][0] = f0_ref[pl.ds(w * steps, steps)]
        outs[d][1] = f1_ref[pl.ds(w * steps, steps)]


def spread_kernel(nt, steps, q_ref, tab_ref, *refs):
    ins, out_ref, slots, line = refs[:nt], refs[nt], refs[nt + 1], refs[nt + 2]
    hy = out_ref.shape[3]
    cq = out_ref.shape[4] // nt
    tiles = hy // SUB
    for d in range(nt):
        slots[jnp.bitwise_xor(q_ref[0], d)] = ins[d][...]
    for face in range(2):
        base = 3 * hy + face * (tiles - 1) * SUB
        le = [tab_ref[base + i * SUB : base + (i + 1) * SUB, :] > 0.5 for i in range(tiles - 1)]
        zero = jnp.zeros((SUB, cq), F32)
        for c in range(nt):

            def step(k, _, face=face, c=c):
                r = [slots[c, face, k, i * SUB : (i + 1) * SUB, :] for i in range(tiles - 1)]
                for j in range(tiles):
                    if j == 0:
                        v = jnp.where(le[0], zero, r[0])
                    elif j < tiles - 1:
                        v = jnp.where(le[j], jnp.where(le[j - 1], r[j - 1], zero), r[j])
                    else:
                        v = jnp.where(le[j - 1], r[j - 1], zero)
                    line[face, k, pl.ds(j, SUB, stride=tiles), :] = v
                out_ref[0, face, k, :, c * cq : (c + 1) * cq] = line[face, k]
                return 0

            lax.fori_loop(0, steps, step, 0)


def sds(*shape):
    return jax.ShapeDtypeStruct(shape, F32)


def cost(flops, nbytes):
    return pl.CostEstimate(flops=int(flops), bytes_accessed=int(nbytes), transcendentals=0)


def grant(mib):
    return pltpu.CompilerParams(vmem_limit_bytes=mib << 20)


def local(
    initial_state,
    heat_source,
    source_amplitude,
    diffusivity,
    robin_param,
    spectrum_x,
    spectrum_y,
    spectrum_z,
    robin_in,
    open_flag,
    owner_side,
):
    nx, hy, nz = initial_state.shape
    nt = lax.axis_size("tm")
    ncores = lax.axis_size("cores")
    assert ncores == 2 and nt & (nt - 1) == 0 and nt >= 2
    ny = hy * ncores
    cq = nz // nt
    steps = source_amplitude.shape[0]
    tiles = hy // SUB
    assert tiles == 4 and nx % 4 == 0
    q = lax.axis_index("tm")
    yc = lax.axis_index("cores")
    space = lax.axis_size("space")
    me = lax.axis_index("space")
    left_index = (me + space - 1) % space
    qv = jnp.reshape(q, (1,)).astype(jnp.int32)
    dims = (nt, steps, nx, hy, cq)
    ha = nx // 2
    tied = lax.optimization_barrier

    def xor_permute(x, d):
        return lax.ppermute(x, "tm", [(i, i ^ d) for i in range(nt)])

    def swap(x):
        return lax.ppermute(x, "cores", [(0, 1), (1, 0)])

    def along(x, by):
        return lax.ppermute(x, "space", [(i, (i + by) % space) for i in range(space)])

    rows = 2 * steps * hy
    block = (None, 2, steps, hy, cq)
    cuts = pl.pallas_call(
        functools.partial(split_kernel, nt),
        out_shape=[sds(rows + steps, cq)] * nt,
        grid_spec=pltpu.PrefetchScalarGridSpec(
            num_scalar_prefetch=1,
            grid=(1,),
            in_specs=[SM]
            + [
                pl.BlockSpec(block, lambda i, q, d=d: (0, 0, 0, 0, jnp.bitwise_xor(q[0], d)))
                for d in range(nt)
            ],
            out_specs=[pl.BlockSpec((rows + steps, cq), lambda i, q: (0, 0))] * nt,
        ),
        compiler_params=grant(8),
        cost_estimate=cost(0, 8 * nt * rows * cq),
        name="split",
    )(qv, source_amplitude, *([robin_in] * nt))
    there = [swap(cuts[0])]
    dealt = [cuts[0]] + [xor_permute(cuts[d], d) for d in range(1, nt)]

    base = np.stack(np_halves(np_cosine(nz, np.arange(nz)[:, None], np.arange(nz)[None])))
    base = jnp.asarray(base.reshape(2, nt, cq, nz).swapaxes(0, 1))
    kxh, kxl = (jnp.asarray(w) for w in np_bar(nx, False))
    kxih, kxil = (jnp.asarray(w) for w in np_bar(nx, True))
    whole = lambda shape: pl.BlockSpec(shape, lambda i, q: (0,) * len(shape))

    def forward(values):
        return pl.pallas_call(
            forward_kernel,
            out_shape=sds(nx, hy, cq),
            grid_spec=pltpu.PrefetchScalarGridSpec(
                num_scalar_prefetch=1,
                grid=(tiles,),
                in_specs=[
                    pl.BlockSpec((nx, SUB, nz), lambda i, q: (0, i, 0)),
                    pl.BlockSpec((None, 2, cq, nz), lambda i, q: (q[0], 0, 0, 0)),
                    whole((nx * SUB, nx * SUB)),
                    whole((nx * SUB, nx * SUB)),
                ],
                out_specs=pl.BlockSpec((nx, SUB, cq), lambda i, q: (0, i, 0)),
            ),
            compiler_params=grant(8),
            cost_estimate=cost(1e9, 3e6),
        )(qv, values, base, kxh, kxl)

    n0 = forward(initial_state)
    n1 = swap(n0)
    s0 = forward(tied((heat_source, n0))[0])
    s1 = swap(s0)
    there += [swap(dealt[d]) for d in range(1, nt)]

    robin_param, spectrum_y, spectrum_x, spectrum_z, open_flag, owner_side, yc, _ = tied(
        (robin_param, spectrum_y, spectrum_x, spectrum_z, open_flag, owner_side, yc, s0)
    )
    right_param = along(robin_param, -1)
    left_param = along(robin_param, 1)
    params = jnp.concatenate([left_param, robin_param, right_param])
    sy_there = swap(spectrum_y)

    pack = 256 // (2 * hy)
    half = pack * hy

    def mode_of(i):
        side = jnp.where(i // half == 0, yc, 1 - yc)
        line = i % hy
        return side * hy + tiles * (line % (hy // tiles)) + line // (hy // tiles)

    def node_of(i):
        return jnp.where(i // half == 0, yc, 1 - yc) * hy + i % hy

    r, c = iotas(2 * half, 2 * half)
    same = (r // hy) % pack == (c // hy) % pack
    kyh, kyl = halves(jnp.where(same, cosine(ny, mode_of(r), node_of(c)), 0.0))
    r, c = iotas(half, 2 * half)
    same = (r // hy) % pack == (c // hy) % pack
    kih, kil = halves(jnp.where(same, cosine(ny, mode_of(c), node_of(r)), 0.0))

    def lanes(v):
        return jnp.broadcast_to(v[:, None], v.shape + (cq,)).astype(F32)

    def modes_by_tile(v):
        return jnp.swapaxes(v.reshape(-1, hy // tiles, tiles), -1, -2).reshape(-1)

    sx = jnp.swapaxes(spectrum_x.reshape(ha, 2), 0, 1).reshape(nx)
    sz = lax.dynamic_slice_in_dim(spectrum_z, q * cq, cq, 0)[None]
    pick = lambda v: jnp.concatenate(
        [lax.dynamic_slice_in_dim(v, left_index, 1, 0), lax.dynamic_slice_in_dim(v, me, 1, 0)]
    )
    opened = pick(open_flag).reshape(2, hy // tiles, tiles)
    closed = jnp.stack(
        [jnp.any(opened[:, :, : i + 1] == 0, axis=2) for i in range(tiles - 1)], axis=1
    )
    flat = jnp.concatenate(
        [
            modes_by_tile(spectrum_y),
            modes_by_tile(pick(owner_side).astype(F32)),
            closed.astype(F32).reshape(-1),
        ]
    )
    tab = lanes(flat)
    sy_there = lanes(modes_by_tile(sy_there))
    a = np_modes(nx)
    first = np_cosine(nx, a, np.zeros(nx))
    second = np_cosine(nx, a, np.ones(nx))
    fill = lambda v: jnp.asarray(np.broadcast_to(v[:, None, None], (nx, SUB, cq)).astype(np.float32))
    wv, wd = fill(first * first), fill(first * (second - first))

    scratch = [pltpu.VMEM((nt, 2, steps, hy, cq), F32), pltpu.VMEM((nt, steps, cq), F32)]
    ql, qr, clos, m_there, s_there = pl.pallas_call(
        functools.partial(own_kernel, dims),
        out_shape=[sds(nt * steps, (tiles - 1) * SUB, cq)] * 2
        + [sds(nt, nx, hy, cq), sds(nx, hy, cq), sds(nx, hy, cq)],
        in_specs=[SM] * 4 + [VM] * (10 + nt),
        out_specs=[VM] * 5,
        scratch_shapes=[pltpu.VMEM((nx, hy, cq), F32)] * 3
        + [pltpu.VMEM((2, 2, nt * steps, tiles, SUB, cq), F32)]
        + scratch,
        compiler_params=grant(20),
        cost_estimate=cost(4e9, 8e6),
        name="own",
    )(qv, sx, diffusivity, params, n0, s0, n1, s1, *dealt, tab, sz, kyh, kyl, wv, wd)
    to_left = along(ql, -1)
    to_right = along(qr, 1)

    other = pl.pallas_call(
        functools.partial(other_kernel, dims),
        out_shape=[sds(nx, hy, cq)] * nt,
        in_specs=[SM] * 3 + [VM] * (9 + nt),
        out_specs=[VM] * nt,
        scratch_shapes=[
            pltpu.VMEM((nx, hy, cq), F32),
            pltpu.VMEM((nt, nx, hy, cq), F32),
            pltpu.VMEM((nx, hy, 2 * cq), F32),
        ]
        + scratch,
        compiler_params=grant(20),
        cost_estimate=cost(6e9, 8e6),
        name="other",
    )
    outs = other(qv, sx, diffusivity, m_there, s_there, *there, sy_there, sz, clos, kih, kil, kxih, kxil)
    ends = [outs[0]] + [xor_permute(outs[d], d) for d in range(1, nt)]

    short = sds(2, steps, (tiles - 1) * SUB, cq)
    hands = pl.pallas_call(
        functools.partial(deal_kernel, nt, steps),
        out_shape=[short] * nt,
        in_specs=[SM, VM, VM],
        out_specs=[VM] * nt,
        compiler_params=grant(8),
        cost_estimate=cost(0, 2e6),
        name="deal",
    )(qv, to_right, to_left)
    hands = [hands[0]] + [xor_permute(hands[d], d) for d in range(1, nt)]

    xb = SUB
    window_end = pl.pallas_call(
        functools.partial(final_kernel, nt),
        out_shape=sds(1, nx, hy, nz),
        grid_spec=pltpu.PrefetchScalarGridSpec(
            num_scalar_prefetch=1,
            grid=(nx // xb,),
            in_specs=[
                pl.BlockSpec((None, 2, cq, nz), lambda i, q, d=d: (jnp.bitwise_xor(q[0], d), 0, 0, 0))
                for d in range(nt)
            ]
            + [pl.BlockSpec((xb, hy, cq), lambda i, q: (i, 0, 0))] * nt,
            out_specs=pl.BlockSpec((1, xb, hy, nz), lambda i, q: (0, i, 0, 0)),
            scratch_shapes=[pltpu.VMEM((nz, nz), BF16)] * 2,
        ),
        compiler_params=grant(16),
        cost_estimate=cost(2e9, 6e6),
        name="final",
    )(qv, *([base] * nt), *ends)

    robin_out = pl.pallas_call(
        functools.partial(spread_kernel, nt, steps),
        out_shape=sds(1, 2, steps, hy, nz),
        in_specs=[SM] + [VM] * (nt + 1),
        out_specs=VM,
        scratch_shapes=[
            pltpu.VMEM((nt,) + short.shape, F32),
            pltpu.VMEM((2, steps, hy, cq), F32),
        ],
        compiler_params=grant(8),
        cost_estimate=cost(0, 2e6),
        name="spread",
    )(qv, tab, *hands)
    return robin_out, window_end


def solution(mesh):
    placed = (
        P("space", "cores", None),
        P("space", "cores", None),
        P("tm"),
        P("space"),
        P("space"),
        P(),
        P("cores"),
        P(),
        P("space", None, "tm", "cores", None),
        P(None, "cores"),
        P(None, "cores"),
    )

    return jax.shard_map(
        local,
        mesh=mesh,
        in_specs=placed,
        out_specs=(P("space", None, "tm", "cores", None), P("tm", "space", "cores", None)),
        check_vma=False,
    )
```

profile of v0, /device:TPU:0, one launch (start us, length us, event | category | flops | bytes accessed | tf_op | source)
XLA Modules:
  0.0 114.7 jit_solution(6210519528391780719)
XLA Ops:
  0.7 1.2 %copy-done.1 = bf16[4,2,128,512]{3,2,1,0:T(8,128)(2,1)S(1)} copy-done((bf16[4,2,128,512]{3,2,1,0:T(8,128)(2,1)S(1)}, bf16[4,2,128,512]{3,2,1,0:T(8,128)(2,1)}, u32[]{:S(2)}) %copy-start.1) | copy-done | bytes 1048600
  1.9 1.6 %copy-done.4 = f32[32,32,512]{2,1,0:T(8,128)S(1)} copy-done((f32[32,32,512]{2,1,0:T(8,128)S(1)}, f32[32,32,512]{2,1,0:T(8,128)}, u32[]{:S(2)}) %copy-start.4) | copy-done | bytes 2097176
  3.5 0.9 copy-done.6
  4.4 0.9 copy-done.7
  5.3 2.5 %shard_map.185.refs_0_ = f32[32,32,128]{2,1,0:T(8,128)S(1)} custom-call(s32[1]{0:T(128)} %bitcast.q_ref, f32[32,32,512]{2,1,0:T(8,128)S(1)} %copy-done.4, bf16[4,2,128,512]{3,2,1,0:T(8,128)(2,1)S(1)} %copy-done.1, bf16[256,256]{1,0:T(8,128)(2,1)S(1)} %copy-done.6, bf16[256,256]{1,0:T(8,128)(2,1)S(1)} %copy-done.7), custom_call_target="tpu_custom_call" | custom-call | flops 1000000000 | bytes 3000000 | tf_op jit(solution)/shard_map/pallas_call | solution.py:398
  7.8 2.5 %shard_map.186.refs_1_ = f32[32,32,128]{2,1,0:T(8,128)S(1)} custom-call(s32[1]{0:T(128)} %bitcast.q_ref, f32[32,32,512]{2,1,0:T(8,128)S(1)} %copy-done.5, bf16[4,2,128,512]{3,2,1,0:T(8,128)(2,1)S(1)} %copy-done.2, bf16[256,256]{1,0:T(8,128)(2,1)S(1)} %copy-done.6, bf16[256,256]{1,0:T(8,128)(2,1)S(1)} %copy-done.7), custom_call_target="tpu_custom_call" | custom-call | flops 1000000000 | bytes 3000000 | tf_op jit(solution)/shard_map/pallas_call | solution.py:398
  10.3 3.1 %collective-permute-start = (f32[1]{0:T(128)}, f32[1]{0:T(128)}, u32[]{:S(2)}, u32[]{:S(2)}) collective-permute-start(f32[1]{0:T(128)} %param.22), channel_id=1, source_target_pairs={{0,8},{8,16},{16,24},{24,0},{1,9},{9,17},{17,25},{25,1},{2,10},{10... | collective-permute-start | bytes 20 | tf_op jit(solution)/shard_map/ppermute | solution.py:367
  13.4 2.1 %collective-permute-start.1 = (f32[1]{0:T(128)}, f32[1]{0:T(128)}, u32[]{:S(2)}, u32[]{:S(2)}) collective-permute-start(f32[1]{0:T(128)} %param.22), channel_id=1, source_target_pairs={{0,24},{8,0},{16,8},{24,16},{1,25},{9,1},{17,9},{25,17},{2,26},{10... | collective-permute-start | bytes 20 | tf_op jit(solution)/shard_map/ppermute | solution.py:367
  15.5 1.7 %collective-permute-start.3 = (f32[32,32,128]{2,1,0:T(8,128)S(1)}, f32[32,32,128]{2,1,0:T(8,128)}, u32[]{:S(2)}, u32[]{:S(2)}) collective-permute-start(f32[32,32,128]{2,1,0:T(8,128)S(1)} %shard_map.186.refs_1_), channel_id=1, source_target_pairs={{0,1},{1,0},{2,3},{3,2},{4,5},{5,4},{6,7},{7,6},{8,9},{9,8},{10,11... | collective-permute-start | bytes 1572872 | tf_op jit(solution)/shard_map/ppermute | solution.py:364
  17.6 1.3 %split.1 = (f32[520,128]{1,0:T(8,128)S(1)}, f32[520,128]{1,0:T(8,128)}, f32[520,128]{1,0:T(8,128)S(1)}, f32[520,128]{1,0:T(8,128)S(1)}) custom-call(s32[1]{0:T(128)} %bitcast.q_ref, f32[8]{0:T(128)S(1)} %copy-done.8, f32[1,2,8,32,512]{4,3,2,1,0:T(8,128)S(1)} %copy-done.3, f32[1,2,8,32,512]{4,3,2,1,0:T(8,128)S(1)} %copy-done.3, ...), custom_call_target="tpu_custom_call" | custom-call | bytes 2097152 | tf_op jit(solution)/shard_map/split/pallas_call | solution.py:371
  21.9 2.3 %fusion = (bf16[256,256]{1,0:T(8,128)(2,1)S(1)}, bf16[256,256]{1,0:T(8,128)(2,1)S(1)}) fusion(s32[256]{0:T(256)S(1)} %get-tuple-element.65, s32[256]{0:T(256)S(1)} %get-tuple-element.67, pred[256]{0:T(512)(128)(4,1)S(1)} %get-tuple-element.62, s32[256]{0:T(256)S(1)} %get-tuple-element.66, s32[256]{0:T(256)S(1)} %get-tuple-element.68, ...), kind=kLoop, calls=%fused_computation.24 | loop fusion | flops 4718592 | bytes 269064 | tf_op jit(solution)/shard_map/convert_element_type | solution.py:29
  25.8 1.7 %collective-permute-start.16 = (f32[32]{0:T(128)}, f32[32]{0:T(128)S(1)}, u32[]{:S(2)}, u32[]{:S(2)}) collective-permute-start(f32[32]{0:T(128)} %param.24), channel_id=1, source_target_pairs={{0,1},{1,0},{2,3},{3,2},{4,5},{5,4},{6,7},{7,6},{8,9},{9,8},{10,11... | collective-permute-start | bytes 392 | tf_op jit(solution)/shard_map/ppermute | solution.py:364
  27.5 1.5 %collective-permute-start.5 = (f32[520,128]{1,0:T(8,128)}, f32[520,128]{1,0:T(8,128)}, u32[]{:S(2)}, u32[]{:S(2)}) collective-permute-start(f32[520,128]{1,0:T(8,128)} %copy-done.10), channel_id=1, source_target_pairs={{0,4},{2,6},{4,0},{6,2},{1,5},{3,7},{5,1},{7,3},{8,12},{10,14},{12... | collective-permute-start | bytes 798728 | tf_op jit(solution)/shard_map/ppermute | solution.py:361
  29.0 11.2 %collective-permute-done.16 = f32[32]{0:T(128)S(1)} collective-permute-done((f32[32]{0:T(128)}, f32[32]{0:T(128)S(1)}, u32[]{:S(2)}, u32[]{:S(2)}) %collective-permute-start.16) | collective-permute-done | bytes 160 | tf_op jit(solution)/shard_map/ppermute | solution.py:364
  43.8 1.3 %pad_maximum_fusion.1.par_ref = f32[3]{0:T(128)S(1)} fusion(f32[1]{0:T(128)} %collective-permute-done.1, f32[1]{0:T(128)S(6)} %copy.31, f32[1]{0:T(128)} %collective-permute-done), kind=kLoop, calls=%fused_computation.106 | loop fusion | flops 6 | bytes 24 | tf_op jit(solution)/shard_map/concatenate | solution.py:427
  45.4 1.5 %collective-permute-start.12 = (f32[520,128]{1,0:T(8,128)S(1)}, f32[520,128]{1,0:T(8,128)S(1)}, u32[]{:S(2)}, u32[]{:S(2)}) collective-permute-start(f32[520,128]{1,0:T(8,128)S(1)} %get-tuple-element.33.refs_4_), channel_id=1, source_target_pairs={{0,1},{1,0},{2,3},{3,2},{4,5},{5,4},{6,7},{7,6},{8,9},{9,8},{10,11... | collective-permute-start | bytes 798728 | tf_op jit(solution)/shard_map/ppermute | solution.py:364
  47.4 1.8 %collective-permute-done.6.refs_7_ = f32[520,128]{1,0:T(8,128)} collective-permute-done((f32[520,128]{1,0:T(8,128)}, f32[520,128]{1,0:T(8,128)}, u32[]{:S(2)}, u32[]{:S(2)}) %collective-permute-start.6) | collective-permute-done | bytes 266272 | tf_op jit(solution)/shard_map/ppermute | solution.py:361
  49.2 1.5 %collective-permute-start.14 = (f32[520,128]{1,0:T(8,128)}, f32[520,128]{1,0:T(8,128)S(1)}, u32[]{:S(2)}, u32[]{:S(2)}) collective-permute-start(f32[520,128]{1,0:T(8,128)} %collective-permute-done.5.refs_6_), channel_id=1, source_target_pairs={{0,1},{1,0},{2,3},{3,2},{4,5},{5,4},{6,7},{7,6},{8,9},{9,8},{10,11... | collective-permute-start | bytes 798728 | tf_op jit(solution)/shard_map/ppermute | solution.py:364
  52.2 9.2 %own.1 = (f32[32,24,128]{2,1,0:T(8,128)S(1)}, f32[32,24,128]{2,1,0:T(8,128)S(1)}, f32[4,32,32,128]{3,2,1,0:T(8,128)S(1)}, f32[32,32,128]{2,1,0:T(8,128)S(1)}, f32[32,32,128]{2,1,0:T(8,128)S(1)}) custom-call(s32[1]{0:T(128)} %bitcast.q_ref, f32[32]{0:T(128)S(1)} %reshape.45.sx_ref, f32[1]{0:T(128)S(6)} %copy.30.diff_ref, f32[3]{0:T(128)S(1)} %pad_maximum_fusion.1.par_ref, ...), custom_call_target="tpu_custom_call" | custom-call | flops 4000000000 | bytes 8000000 | tf_op jit(solution)/shard_map/own/pallas_call | solution.py:479
  61.5 3.9 %collective-permute-done.14.refs_2_ = f32[520,128]{1,0:T(8,128)S(1)} collective-permute-done((f32[520,128]{1,0:T(8,128)}, f32[520,128]{1,0:T(8,128)S(1)}, u32[]{:S(2)}, u32[]{:S(2)}) %collective-permute-start.14) | collective-permute-done | bytes 266272 | tf_op jit(solution)/shard_map/ppermute | solution.py:364
  65.4 5.7 %collective-permute-done.15.refs_3_ = f32[520,128]{1,0:T(8,128)S(1)} collective-permute-done((f32[520,128]{1,0:T(8,128)}, f32[520,128]{1,0:T(8,128)S(1)}, u32[]{:S(2)}, u32[]{:S(2)}) %collective-permute-start.15) | collective-permute-done | bytes 266272 | tf_op jit(solution)/shard_map/ppermute | solution.py:364
  71.2 8.5 %other.1 = (f32[32,32,128]{2,1,0:T(8,128)S(1)}, f32[32,32,128]{2,1,0:T(8,128)S(1)}, f32[32,32,128]{2,1,0:T(8,128)S(1)}, f32[32,32,128]{2,1,0:T(8,128)S(1)}) custom-call(s32[1]{0:T(128)} %bitcast.q_ref, f32[32]{0:T(128)S(1)} %reshape.45.sx_ref, f32[1]{0:T(128)S(6)} %copy.30.diff_ref, f32[32,32,128]{2,1,0:T(8,128)S(1)} %get-tuple-element.45.m_ref, ...), custom_call_target="tpu_custom_call" | custom-call | flops 6000000000 | bytes 8000000 | tf_op jit(solution)/shard_map/other/pallas_call | solution.py:510
  80.2 1.4 %collective-permute-start.18 = (f32[32,32,128]{2,1,0:T(8,128)S(1)}, f32[32,32,128]{2,1,0:T(8,128)S(1)}, u32[]{:S(2)}, u32[]{:S(2)}) collective-permute-start(f32[32,32,128]{2,1,0:T(8,128)S(1)} %get-tuple-element.50), channel_id=1, source_target_pairs={{0,4},{2,6},{4,0},{6,2},{1,5},{3,7},{5,1},{7,3},{8,12},{10,14},{12... | collective-permute-start | bytes 1572872 | tf_op jit(solution)/shard_map/ppermute | solution.py:361
  81.7 3.8 %collective-permute-start.8 = (f32[32,24,128]{2,1,0:T(8,128)S(1)}, f32[32,24,128]{2,1,0:T(8,128)S(1)}, u32[]{:S(2)}, u32[]{:S(2)}) collective-permute-start(f32[32,24,128]{2,1,0:T(8,128)S(1)} %get-tuple-element.40), channel_id=1, source_target_pairs={{0,24},{8,0},{16,8},{24,16},{1,25},{9,1},{17,9},{25,17},{2,26},{10... | collective-permute-start | bytes 1179656 | tf_op jit(solution)/shard_map/ppermute | solution.py:367
  85.5 10.0 %collective-permute-done.7.f0_ref = f32[32,24,128]{2,1,0:T(8,128)S(1)} collective-permute-done((f32[32,24,128]{2,1,0:T(8,128)S(1)}, f32[32,24,128]{2,1,0:T(8,128)S(1)}, u32[]{:S(2)}, u32[]{:S(2)}) %collective-permute-start.7) | collective-permute-done | bytes 393248 | tf_op jit(solution)/shard_map/ppermute | solution.py:367
  95.5 6.3 %collective-permute-done.8.f1_ref = f32[32,24,128]{2,1,0:T(8,128)S(1)} collective-permute-done((f32[32,24,128]{2,1,0:T(8,128)S(1)}, f32[32,24,128]{2,1,0:T(8,128)S(1)}, u32[]{:S(2)}, u32[]{:S(2)}) %collective-permute-start.8) | collective-permute-done | bytes 393248 | tf_op jit(solution)/shard_map/ppermute | solution.py:367
  101.9 1.5 %collective-permute-start.10 = (f32[2,8,24,128]{3,2,1,0:T(8,128)S(1)}, f32[2,8,24,128]{3,2,1,0:T(8,128)S(1)}, u32[]{:S(2)}, u32[]{:S(2)}) collective-permute-start(f32[2,8,24,128]{3,2,1,0:T(8,128)S(1)} %get-tuple-element.43), channel_id=1, source_target_pairs={{0,4},{2,6},{4,0},{6,2},{1,5},{3,7},{5,1},{7,3},{8,12},{10,14},{12... | collective-permute-start | bytes 589832 | tf_op jit(solution)/shard_map/ppermute | solution.py:361
  104.1 1.1 collective-permute-done.19.refs_7_
  105.2 3.4 %final.1 = f32[1,32,32,512]{3,2,1,0:T(8,128)} custom-call(s32[1]{0:T(128)} %bitcast.q_ref, bf16[4,2,128,512]{3,2,1,0:T(8,128)(2,1)S(1)} %copy-done.2, bf16[4,2,128,512]{3,2,1,0:T(8,128)(2,1)S(1)} %copy-done.2, bf16[4,2,128,512]{3,2,1,0:T(8,128)(2,1)S(1)} %copy-done.2, bf16[4,2,128,512]{3,2,1,0:T(8,128)(2,1)S(1)} %copy-done.2, ...), custom_call_target="tpu_custom_call" | custom-call | flops 2000000000 | bytes 6000000 | tf_op jit(solution)/shard_map/final/pallas_call | solution.py:526
  108.6 1.8 %collective-permute-done.10.refs_2_ = f32[2,8,24,128]{3,2,1,0:T(8,128)S(1)} collective-permute-done((f32[2,8,24,128]{3,2,1,0:T(8,128)S(1)}, f32[2,8,24,128]{3,2,1,0:T(8,128)S(1)}, u32[]{:S(2)}, u32[]{:S(2)}) %collective-permute-start.10) | collective-permute-done | bytes 196640 | tf_op jit(solution)/shard_map/ppermute | solution.py:361
  110.5 2.6 %collective-permute-done.11.refs_3_ = f32[2,8,24,128]{3,2,1,0:T(8,128)S(1)} collective-permute-done((f32[2,8,24,128]{3,2,1,0:T(8,128)S(1)}, f32[2,8,24,128]{3,2,1,0:T(8,128)S(1)}, u32[]{:S(2)}, u32[]{:S(2)}) %collective-permute-start.11) | collective-permute-done | bytes 196640 | tf_op jit(solution)/shard_map/ppermute | solution.py:361
  113.1 1.6 %spread.1 = f32[1,2,8,32,512]{4,3,2,1,0:T(8,128)} custom-call(s32[1]{0:T(128)} %bitcast.q_ref, f32[144,128]{1,0:T(8,128)S(1)} %broadcast_in_dim.56.refs_8_.tab_ref, f32[2,8,24,128]{3,2,1,0:T(8,128)S(1)} %get-tuple-element.41.refs_0_, f32[2,8,24,128]{3,2,1,0:T(8,128)S(1)} %collective-permute-done.9.refs_1_, ...), custom_call_target="tpu_custom_call" | custom-call | bytes 2000000 | tf_op jit(solution)/shard_map/spread/pallas_call | solution.py:545
  (89 shorter events, 10.8 us)
Async XLA Ops:
  0.6 39.6 %copy-start = (f32[512]{0:T(512)S(1)}, f32[512]{0:T(512)}, u32[]{:S(2)}) copy-start(f32[512]{0:T(512)} %param.25) | copy-start | bytes 6148
  0.7 1.2 %copy-start.1 = (bf16[4,2,128,512]{3,2,1,0:T(8,128)(2,1)S(1)}, bf16[4,2,128,512]{3,2,1,0:T(8,128)(2,1)}, u32[]{:S(2)}) copy-start(bf16[4,2,128,512]{3,2,1,0:T(8,128)(2,1)} %constant.247.clone.c_ref.refs_0_.refs_1_.refs_2_.refs_3_) | copy-start | bytes 3145732
  1.9 1.6 %copy-start.4 = (f32[32,32,512]{2,1,0:T(8,128)S(1)}, f32[32,32,512]{2,1,0:T(8,128)}, u32[]{:S(2)}) copy-start(f32[32,32,512]{2,1,0:T(8,128)} %x_ref.1) | copy-start | bytes 6291460
  5.3 2.5 %copy-start.2 = (bf16[4,2,128,512]{3,2,1,0:T(8,128)(2,1)S(1)}, bf16[4,2,128,512]{3,2,1,0:T(8,128)(2,1)}, u32[]{:S(2)}) copy-start(bf16[4,2,128,512]{3,2,1,0:T(8,128)(2,1)} %constant.247.clone.c_ref.refs_0_.refs_1_.refs_2_.refs_3_) | copy-start | bytes 3145732
  5.3 2.5 %copy-start.5 = (f32[32,32,512]{2,1,0:T(8,128)S(1)}, f32[32,32,512]{2,1,0:T(8,128)}, u32[]{:S(2)}) copy-start(f32[32,32,512]{2,1,0:T(8,128)} %x_ref.2) | copy-start | bytes 6291460
  7.8 9.8 %copy-start.3 = (f32[1,2,8,32,512]{4,3,2,1,0:T(8,128)S(1)}, f32[1,2,8,32,512]{4,3,2,1,0:T(8,128)}, u32[]{:S(2)}) copy-start(f32[1,2,8,32,512]{4,3,2,1,0:T(8,128)} %refs_3_.2) | copy-start | bytes 3145732
  7.8 9.8 %copy-start.8 = (f32[8]{0:T(128)S(1)}, f32[8]{0:T(128)}, u32[]{:S(2)}) copy-start(f32[8]{0:T(128)} %amp_ref.1) | copy-start | bytes 100
  10.3 10.0 %copy-start.15 = (s32[4,32]{1,0:T(4,128)S(1)}, s32[4,32]{1,0:T(4,128)}, u32[]{:S(2)}) copy-start(s32[4,32]{1,0:T(4,128)} %param.27) | copy-start | bytes 1540
  10.3 41.0 %copy-start.13 = (f32[32,8,128]{2,1,0:T(8,128)S(1)}, f32[32,8,128]{2,1,0:T(8,128)}, u32[]{:S(2)}) copy-start(f32[32,8,128]{2,1,0:T(8,128)} %constant.252.clone.refs_12_) | copy-start | bytes 393220
  10.3 15.5 %collective-permute-start = (f32[1]{0:T(128)}, f32[1]{0:T(128)}, u32[]{:S(2)}, u32[]{:S(2)}) collective-permute-start(f32[1]{0:T(128)} %param.22), channel_id=1, source_target_pairs={{0,8},{8,16},{16,24},{24,0},{1,9},{9,17},{17,25},{25,1},{2,10},{10... | collective-permute-start | bytes 20 | tf_op jit(solution)/shard_map/ppermute | solution.py:367
  13.4 14.1 %collective-permute-start.1 = (f32[1]{0:T(128)}, f32[1]{0:T(128)}, u32[]{:S(2)}, u32[]{:S(2)}) collective-permute-start(f32[1]{0:T(128)} %param.22), channel_id=1, source_target_pairs={{0,24},{8,0},{16,8},{24,16},{1,25},{9,1},{17,9},{25,17},{2,26},{10... | collective-permute-start | bytes 20 | tf_op jit(solution)/shard_map/ppermute | solution.py:367
  15.5 35.2 %collective-permute-start.3 = (f32[32,32,128]{2,1,0:T(8,128)S(1)}, f32[32,32,128]{2,1,0:T(8,128)}, u32[]{:S(2)}, u32[]{:S(2)}) collective-permute-start(f32[32,32,128]{2,1,0:T(8,128)S(1)} %shard_map.186.refs_1_), channel_id=1, source_target_pairs={{0,1},{1,0},{2,3},{3,2},{4,5},{5,4},{6,7},{7,6},{8,9},{9,8},{10,11... | collective-permute-start | bytes 1572872 | tf_op jit(solution)/shard_map/ppermute | solution.py:364
  17.2 34.1 %collective-permute-start.2 = (f32[32,32,128]{2,1,0:T(8,128)S(1)}, f32[32,32,128]{2,1,0:T(8,128)}, u32[]{:S(2)}, u32[]{:S(2)}) collective-permute-start(f32[32,32,128]{2,1,0:T(8,128)S(1)} %shard_map.185.refs_0_), channel_id=1, source_target_pairs={{0,1},{1,0},{2,3},{3,2},{4,5},{5,4},{6,7},{7,6},{8,9},{9,8},{10,11... | collective-permute-start | bytes 1572872 | tf_op jit(solution)/shard_map/ppermute | solution.py:364
  20.3 25.1 %collective-permute-start.4 = (f32[520,128]{1,0:T(8,128)}, f32[520,128]{1,0:T(8,128)}, u32[]{:S(2)}, u32[]{:S(2)}) collective-permute-start(f32[520,128]{1,0:T(8,128)} %get-tuple-element.34), channel_id=1, source_target_pairs={{0,2},{2,0},{4,6},{6,4},{1,3},{3,1},{5,7},{7,5},{8,10},{10,8},{12,... | collective-permute-start | bytes 798728 | tf_op jit(solution)/shard_map/ppermute | solution.py:361
  25.8 14.4 %collective-permute-start.16 = (f32[32]{0:T(128)}, f32[32]{0:T(128)S(1)}, u32[]{:S(2)}, u32[]{:S(2)}) collective-permute-start(f32[32]{0:T(128)} %param.24), channel_id=1, source_target_pairs={{0,1},{1,0},{2,3},{3,2},{4,5},{5,4},{6,7},{7,6},{8,9},{9,8},{10,11... | collective-permute-start | bytes 392 | tf_op jit(solution)/shard_map/ppermute | solution.py:364
  27.5 19.4 %collective-permute-start.5 = (f32[520,128]{1,0:T(8,128)}, f32[520,128]{1,0:T(8,128)}, u32[]{:S(2)}, u32[]{:S(2)}) collective-permute-start(f32[520,128]{1,0:T(8,128)} %copy-done.10), channel_id=1, source_target_pairs={{0,4},{2,6},{4,0},{6,2},{1,5},{3,7},{5,1},{7,3},{8,12},{10,14},{12... | collective-permute-start | bytes 798728 | tf_op jit(solution)/shard_map/ppermute | solution.py:361
  40.3 9.0 %collective-permute-start.6 = (f32[520,128]{1,0:T(8,128)}, f32[520,128]{1,0:T(8,128)}, u32[]{:S(2)}, u32[]{:S(2)}) collective-permute-start(f32[520,128]{1,0:T(8,128)} %copy-done.9), channel_id=1, source_target_pairs={{0,6},{2,4},{4,2},{6,0},{1,7},{3,5},{5,3},{7,1},{8,14},{10,12},{12... | collective-permute-start | bytes 798728 | tf_op jit(solution)/shard_map/ppermute | solution.py:361
  45.4 16.1 %collective-permute-start.12 = (f32[520,128]{1,0:T(8,128)S(1)}, f32[520,128]{1,0:T(8,128)S(1)}, u32[]{:S(2)}, u32[]{:S(2)}) collective-permute-start(f32[520,128]{1,0:T(8,128)S(1)} %get-tuple-element.33.refs_4_), channel_id=1, source_target_pairs={{0,1},{1,0},{2,3},{3,2},{4,5},{5,4},{6,7},{7,6},{8,9},{9,8},{10,11... | collective-permute-start | bytes 798728 | tf_op jit(solution)/shard_map/ppermute | solution.py:364
  46.9 14.6 %collective-permute-start.13 = (f32[520,128]{1,0:T(8,128)}, f32[520,128]{1,0:T(8,128)S(1)}, u32[]{:S(2)}, u32[]{:S(2)}) collective-permute-start(f32[520,128]{1,0:T(8,128)} %collective-permute-done.4.refs_5_), channel_id=1, source_target_pairs={{0,1},{1,0},{2,3},{3,2},{4,5},{5,4},{6,7},{7,6},{8,9},{9,8},{10,11... | collective-permute-start | bytes 798728 | tf_op jit(solution)/shard_map/ppermute | solution.py:364
  49.2 16.2 %collective-permute-start.14 = (f32[520,128]{1,0:T(8,128)}, f32[520,128]{1,0:T(8,128)S(1)}, u32[]{:S(2)}, u32[]{:S(2)}) collective-permute-start(f32[520,128]{1,0:T(8,128)} %collective-permute-done.5.refs_6_), channel_id=1, source_target_pairs={{0,1},{1,0},{2,3},{3,2},{4,5},{5,4},{6,7},{7,6},{8,9},{9,8},{10,11... | collective-permute-start | bytes 798728 | tf_op jit(solution)/shard_map/ppermute | solution.py:364
  50.7 20.4 %collective-permute-start.15 = (f32[520,128]{1,0:T(8,128)}, f32[520,128]{1,0:T(8,128)S(1)}, u32[]{:S(2)}, u32[]{:S(2)}) collective-permute-start(f32[520,128]{1,0:T(8,128)} %collective-permute-done.6.refs_7_), channel_id=1, source_target_pairs={{0,1},{1,0},{2,3},{3,2},{4,5},{5,4},{6,7},{7,6},{8,9},{9,8},{10,11... | collective-permute-start | bytes 798728 | tf_op jit(solution)/shard_map/ppermute | solution.py:364
  51.3 0.9 copy-start.14
  52.2 19.0 %copy-start.11 = (bf16[256,256]{1,0:T(8,128)(2,1)S(1)}, bf16[256,256]{1,0:T(8,128)(2,1)}, u32[]{:S(2)}) copy-start(bf16[256,256]{1,0:T(8,128)(2,1)} %constant.250.clone.refs_9_) | copy-start | bytes 393220
  52.2 19.0 %copy-start.12 = (bf16[256,256]{1,0:T(8,128)(2,1)S(1)}, bf16[256,256]{1,0:T(8,128)(2,1)}, u32[]{:S(2)}) copy-start(bf16[256,256]{1,0:T(8,128)(2,1)} %constant.251.clone.refs_10_) | copy-start | bytes 393220
  79.7 23.7 %collective-permute-start.17 = (f32[32,32,128]{2,1,0:T(8,128)S(1)}, f32[32,32,128]{2,1,0:T(8,128)S(1)}, u32[]{:S(2)}, u32[]{:S(2)}) collective-permute-start(f32[32,32,128]{2,1,0:T(8,128)S(1)} %get-tuple-element.49), channel_id=1, source_target_pairs={{0,2},{2,0},{4,6},{6,4},{1,3},{3,1},{5,7},{7,5},{8,10},{10,8},{12,... | collective-permute-start | bytes 1572872 | tf_op jit(solution)/shard_map/ppermute | solution.py:361
  80.2 23.9 %collective-permute-start.18 = (f32[32,32,128]{2,1,0:T(8,128)S(1)}, f32[32,32,128]{2,1,0:T(8,128)S(1)}, u32[]{:S(2)}, u32[]{:S(2)}) collective-permute-start(f32[32,32,128]{2,1,0:T(8,128)S(1)} %get-tuple-element.50), channel_id=1, source_target_pairs={{0,4},{2,6},{4,0},{6,2},{1,5},{3,7},{5,1},{7,3},{8,12},{10,14},{12... | collective-permute-start | bytes 1572872 | tf_op jit(solution)/shard_map/ppermute | solution.py:361
  81.7 23.6 %collective-permute-start.19 = (f32[32,32,128]{2,1,0:T(8,128)S(1)}, f32[32,32,128]{2,1,0:T(8,128)S(1)}, u32[]{:S(2)}, u32[]{:S(2)}) collective-permute-start(f32[32,32,128]{2,1,0:T(8,128)S(1)} %get-tuple-element.51), channel_id=1, source_target_pairs={{0,6},{2,4},{4,2},{6,0},{1,7},{3,5},{5,3},{7,1},{8,14},{10,12},{12... | collective-permute-start | bytes 1572872 | tf_op jit(solution)/shard_map/ppermute | solution.py:361
  81.7 13.8 %collective-permute-start.7 = (f32[32,24,128]{2,1,0:T(8,128)S(1)}, f32[32,24,128]{2,1,0:T(8,128)S(1)}, u32[]{:S(2)}, u32[]{:S(2)}) collective-permute-start(f32[32,24,128]{2,1,0:T(8,128)S(1)} %get-tuple-element.39), channel_id=1, source_target_pairs={{0,8},{8,16},{16,24},{24,0},{1,9},{9,17},{17,25},{25,1},{2,10},{10... | collective-permute-start | bytes 1179656 | tf_op jit(solution)/shard_map/ppermute | solution.py:367
  81.7 20.1 %collective-permute-start.8 = (f32[32,24,128]{2,1,0:T(8,128)S(1)}, f32[32,24,128]{2,1,0:T(8,128)S(1)}, u32[]{:S(2)}, u32[]{:S(2)}) collective-permute-start(f32[32,24,128]{2,1,0:T(8,128)S(1)} %get-tuple-element.40), channel_id=1, source_target_pairs={{0,24},{8,0},{16,8},{24,16},{1,25},{9,1},{17,9},{25,17},{2,26},{10... | collective-permute-start | bytes 1179656 | tf_op jit(solution)/shard_map/ppermute | solution.py:367
  101.9 8.6 %collective-permute-start.10 = (f32[2,8,24,128]{3,2,1,0:T(8,128)S(1)}, f32[2,8,24,128]{3,2,1,0:T(8,128)S(1)}, u32[]{:S(2)}, u32[]{:S(2)}) collective-permute-start(f32[2,8,24,128]{3,2,1,0:T(8,128)S(1)} %get-tuple-element.43), channel_id=1, source_target_pairs={{0,4},{2,6},{4,0},{6,2},{1,5},{3,7},{5,1},{7,3},{8,12},{10,14},{12... | collective-permute-start | bytes 589832 | tf_op jit(solution)/shard_map/ppermute | solution.py:361
  103.4 9.7 %collective-permute-start.11 = (f32[2,8,24,128]{3,2,1,0:T(8,128)S(1)}, f32[2,8,24,128]{3,2,1,0:T(8,128)S(1)}, u32[]{:S(2)}, u32[]{:S(2)}) collective-permute-start(f32[2,8,24,128]{3,2,1,0:T(8,128)S(1)} %get-tuple-element.44), channel_id=1, source_target_pairs={{0,6},{2,4},{4,2},{6,0},{1,7},{3,5},{5,3},{7,1},{8,14},{10,12},{12... | collective-permute-start | bytes 589832 | tf_op jit(solution)/shard_map/ppermute | solution.py:361
  103.4 9.7 %collective-permute-start.9 = (f32[2,8,24,128]{3,2,1,0:T(8,128)S(1)}, f32[2,8,24,128]{3,2,1,0:T(8,128)S(1)}, u32[]{:S(2)}, u32[]{:S(2)}) collective-permute-start(f32[2,8,24,128]{3,2,1,0:T(8,128)S(1)} %get-tuple-element.42), channel_id=1, source_target_pairs={{0,2},{2,0},{4,6},{6,4},{1,3},{3,1},{5,7},{7,5},{8,10},{10,8},{12,... | collective-permute-start | bytes 589832 | tf_op jit(solution)/shard_map/ppermute | solution.py:361
  (4 other events, 3.2 us)
where the time goes:
time: 115 us
  waiting for transfers between devices  44.6 us (39%)
  Pallas kernels  29 us (25%)
  starting transfers between devices  22.5 us (20%)
  local copies, waits for them, and re-layouts  10.5 us (9%)
  other arithmetic  5.81 us (5%)
  between operations  2.24 us (2%)
    ppermute x7, waiting for transfers between devices, swap(): return lax.ppermute(x, 'cores', [(0, 1), (1, 0)])  20.9 us
    ppermute x4, waiting for transfers between devices, along(): lax.ppermute(x, 'space', [(i, (i + by) % space) for i in range(space)])  16.3 us
    pallas_call x1, Pallas kernels, local(): pl.pallas_call(functools.partial(own_kernel, dims), out_shape=[sds(nt * s...  9.22 us
    ppermute x4, starting transfers between devices, along(): lax.ppermute(x, 'space', [(i, (i + by) % space) for i in range(space)])  9.02 us
    pallas_call x1, Pallas kernels, local(): other(qv, sx, diffusivity, m_there, s_there, *there, sy_there, sz, clos,...  8.49 us
    ppermute x7, starting transfers between devices, swap(): return lax.ppermute(x, 'cores', [(0, 1), (1, 0)])  7.82 us
    ppermute x9, waiting for transfers between devices, xor_permute(): return lax.ppermute(x, 'tm', [(i, i ^ d) for i in range(nt)])  7.37 us
    unnamed x32, local copies, waits for them, and re-layouts  6.98 us
  transfers between devices with their start and end apart: 20, of which 9 were waited for; matrix products, arithmetic and copies ran while one was open for 8% of the time, Pallas kernels for 12%

commit v1 on v0

--- a/solution.py
+++ b/solution.py
@@ -114,27 +114,27 @@
         f_ref[a] = 1.0 / (1.0 + diff_ref[0] * rate)
 
 
-def gather_windows(nt, q, ins, u_s, amp_s):
-    steps = amp_s.shape[1]
+def order_kernel(nt, q_ref, *refs):
+    ins, u_ref, amp_ref, outs = refs[:nt], refs[nt], refs[nt + 1], refs[nt + 2 :]
+    steps = amp_ref.shape[1]
     rows = ins[0].shape[0] - steps
     for d in range(nt):
-        w = jnp.bitwise_xor(q, d)
-        u_s[w] = ins[d][0:rows, :].reshape(u_s.shape[1:])
-        amp_s[w] = ins[d][rows:, :]
+        w = jnp.bitwise_xor(q_ref[0], d)
+        u_ref[w] = ins[d][0:rows, :].reshape(u_ref.shape[1:])
+        amp_ref[w] = ins[d][rows:, :]
+    for w in range(nt):
+        outs[w][...] = u_ref[w]
 
 
 def own_kernel(dims, q_ref, sx_ref, diff_ref, par_ref, *refs):
     nt, steps, nx, hy, cq = dims
-    n0, s0, n1, s1 = refs[:4]
-    pieces = refs[4 : 4 + nt]
-    (tab_ref, sz_ref, kyh_ref, kyl_ref, wv_ref, wd_ref) = refs[4 + nt : 10 + nt]
-    ql_ref, qr_ref, clos_ref, mo_ref, so_ref = refs[10 + nt : 15 + nt]
-    m_s, s_s, f_s, vd, u_s, amp_s = refs[15 + nt :]
+    n0, s0, n1, s1, u_s, amp_s, tab_ref, sz_ref, kyh_ref, kyl_ref, wv_ref, wd_ref = refs[:12]
+    hands, (clos_ref, mo_ref, so_ref) = refs[12 : 12 + nt], refs[12 + nt : 15 + nt]
+    m_s, s_s, f_s, vd = refs[15 + nt :]
     tiles = hy // SUB
     pack = kyh_ref.shape[0] // (2 * hy)
     half = pack * hy
 
-    gather_windows(nt, q_ref[0], pieces, u_s, amp_s)
     factor_into(f_s, sx_ref, diff_ref, tab_ref[0:hy, :], sz_ref[...])
 
     def ytrans(ag, _):
@@ -187,35 +187,42 @@
 
     owner, closed = tab_ref.at[hy : 3 * hy], tab_ref.at[3 * hy :]
 
-    def combine(m, _):
-        left, right = [], []
-        for j in range(tiles):
-            ve, vo = vd[0, 0, m, j], vd[1, 0, m, j]
-            de, do = vd[0, 1, m, j], vd[1, 1, m, j]
-            p = [
-                jnp.where(owner[i * hy + j * SUB : i * hy + (j + 1) * SUB, :] < 0.5, par_ref[i], par_ref[i + 1])
-                for i in range(2)
-            ]
-            left.append((de + do) + p[0] * (ve + vo))
-            right.append(p[1] * (ve - vo) + (de - do))
-        for i in range(tiles - 1):
-            rows = slice(i * SUB, (i + 1) * SUB)
-            le = [closed[(n * (tiles - 1) + i) * SUB : (n * (tiles - 1) + i + 1) * SUB, :] > 0.5 for n in range(2)]
-            ql_ref[m, rows, :] = jnp.where(le[0], left[i + 1], left[i])
-            qr_ref[m, rows, :] = jnp.where(le[1], right[i + 1], right[i])
-        return 0
-
-    lax.fori_loop(0, nt * steps, combine, 0)
-
-
-def other_kernel(dims, q_ref, sx_ref, diff_ref, m_ref, s_ref, *refs):
+    for slot in range(nt):
+        w = jnp.bitwise_xor(q_ref[0], slot)
+
+        def combine(k, _, slot=slot, w=w):
+            m = w * steps + k
+            left, right = [], []
+            for j in range(tiles):
+                ve, vo = vd[0, 0, m, j], vd[1, 0, m, j]
+                de, do = vd[0, 1, m, j], vd[1, 1, m, j]
+                p = [
+                    jnp.where(owner[i * hy + j * SUB : i * hy + (j + 1) * SUB, :] < 0.5, par_ref[i], par_ref[i + 1])
+                    for i in range(2)
+                ]
+                left.append((de + do) + p[0] * (ve + vo))
+                right.append(p[1] * (ve - vo) + (de - do))
+            for face, line in enumerate((left, right)):
+                for i in range(tiles - 1):
+                    at = (face * (tiles - 1) + i) * SUB
+                    le = closed[at : at + SUB, :] > 0.5
+                    hands[slot][face, k, i * SUB : (i + 1) * SUB, :] = jnp.where(le, line[i + 1], line[i])
+            return 0
+
+        lax.fori_loop(0, steps, combine, 0)
+
+
+def other_kernel(dims, first, last, q_ref, sx_ref, diff_ref, m_ref, s_ref, *refs):
     nt, steps, nx, hy, cq = dims
-    pieces = refs[:nt]
-    sy_ref, sz_ref, clos_ref, kih_ref, kil_ref, kxh_ref, kxl_ref = refs[nt : nt + 7]
-    outs = refs[nt + 7 : 2 * nt + 7]
-    f_s, cl, t_s, u_s, amp_s = refs[2 * nt + 7 :]
+    count = last - first
+    us = refs[:count]
+    amp_ref, sy_ref, sz_ref, clos_ref, kih_ref, kil_ref, kxh_ref, kxl_ref = refs[count : count + 8]
+    nout = nt if count > 1 else 1
+    outs = refs[count + 8 : count + 8 + nout]
+    st_ref, f_s, cl, t_s, u_s = refs[count + 8 + nout :]
     tiles = hy // SUB
-    gather_windows(nt, q_ref[0], pieces, u_s, amp_s)
+    for i in range(count):
+        u_s[i] = us[i][...]
     factor_into(f_s, sx_ref, diff_ref, sy_ref[...], sz_ref[...])
     ha = nx // 2
     for j in range(tiles):
@@ -231,38 +238,47 @@
                     r0 = u_s[w, 0, k, pl.ds(j, SUB, stride=tiles), :]
                     r1 = u_s[w, 1, k, pl.ds(j, SUB, stride=tiles), :]
                     u = r0 + r1 if par == 0 else r0 - r1
-                    amp = amp_s[w, k : k + 1, :]
+                    amp = amp_ref[w + first, k : k + 1, :]
                     cur = [(x + (amp * y + u)) * z for x, y, z in zip(cur, s, f)]
                 for a, x in zip(modes, cur):
                     cl[w, a, rows, :] = x
                 return tuple(cur)
 
-            lax.fori_loop(0, nt, window, tuple(m_ref[a, rows, :] for a in modes))
+            end = lax.fori_loop(0, count, window, tuple(m_ref[a, rows, :] for a in modes))
+            for a, x in zip(modes, end):
+                st_ref[a, rows, :] = x
     pack = kih_ref.shape[0] // hy
     half = pack * hy
-    for e in range(0, nt, 2):
-        ws = [jnp.bitwise_xor(q_ref[0], e + i) for i in range(2)]
-
-        def yback(ag, _, ws=ws):
+    for e in range(0, nout, 2):
+        if count > 1:
+            ws = [jnp.minimum(jnp.bitwise_xor(q_ref[0], e + i), last - 1) for i in range(2)]
+        else:
+            ws = [first]
+        width = len(ws) * cq
+
+        def yback(ag, _, ws=ws, width=width):
             at = pl.ds(ag * pack, pack)
             cols = [
-                jnp.concatenate([clos_ref[w, at].reshape(half, cq), cl[w, at].reshape(half, cq)], axis=0)
+                jnp.concatenate(
+                    [clos_ref[w, at].reshape(half, cq), cl[w - first, at].reshape(half, cq)], axis=0
+                )
                 for w in ws
             ]
             res = const_times(kih_ref[...], kil_ref[...], jnp.concatenate(cols, axis=1))
-            t_s[at] = res.reshape(pack, hy, 2 * cq)
+            t_s[at] = res.reshape(pack, hy, width)
             return 0
 
         lax.fori_loop(0, nx // pack, yback, 0)
         for yb in range(tiles):
-            x = t_s[:, yb * SUB : (yb + 1) * SUB, :].reshape(nx * SUB, 2 * cq)
-            res = const_times(kxh_ref[...], kxl_ref[...], x).reshape(nx, SUB, 2 * cq)
-            for i in range(2):
+            x = t_s[:, yb * SUB : (yb + 1) * SUB, :].reshape(nx * SUB, width)
+            res = const_times(kxh_ref[...], kxl_ref[...], x).reshape(nx, SUB, width)
+            for i in range(len(ws)):
                 outs[e + i][:, yb * SUB : (yb + 1) * SUB, :] = res[:, :, i * cq : (i + 1) * cq]
 
 
 def final_kernel(nt, q_ref, *refs):
-    ws, ins, out_ref, wh, wl = refs[:nt], refs[nt : 2 * nt], refs[2 * nt], refs[2 * nt + 1], refs[2 * nt + 2]
+    ws, most, late = refs[:nt], refs[nt : 2 * nt], refs[2 * nt : 3 * nt]
+    out_ref, wh, wl = refs[3 * nt :]
     xb, hy, nz = out_ref.shape[1:]
     cq = nz // nt
 
@@ -272,33 +288,32 @@
             wh[d * cq : (d + 1) * cq, :] = ws[d][0]
             wl[d * cq : (d + 1) * cq, :] = ws[d][1]
 
-    xh, xl = cut(jnp.concatenate([x[...].reshape(xb * hy, cq) for x in ins], axis=1))
+    is_last = q_ref[0] == nt - 1
+    ins = [jnp.where(is_last, b[...], a[...]) for a, b in zip(most, late)]
+    xh, xl = cut(jnp.concatenate([x.reshape(xb * hy, cq) for x in ins], axis=1))
     res = mm(xh, wh[...]) + mm(xh, wl[...]) + mm(xl, wh[...])
     out_ref[0] = res.reshape(xb, hy, nz)
 
 
-def deal_kernel(nt, steps, q_ref, f0_ref, f1_ref, *outs):
+def merge_kernel(nt, q_ref, *refs):
+    ins, outs = refs[:nt], refs[nt:]
     for d in range(nt):
-        w = jnp.bitwise_xor(q_ref[0], d)
-        outs[d][0] = f0_ref[pl.ds(w * steps, steps)]
-        outs[d][1] = f1_ref[pl.ds(w * steps, steps)]
-
-
-def spread_kernel(nt, steps, q_ref, tab_ref, *refs):
-    ins, out_ref, slots, line = refs[:nt], refs[nt], refs[nt + 1], refs[nt + 2]
+        for face in range(2):
+            outs[face][jnp.bitwise_xor(q_ref[0], d)] = ins[d][face]
+
+
+def spread_kernel(nt, steps, tab_ref, left_ref, right_ref, out_ref, line):
     hy = out_ref.shape[3]
     cq = out_ref.shape[4] // nt
     tiles = hy // SUB
-    for d in range(nt):
-        slots[jnp.bitwise_xor(q_ref[0], d)] = ins[d][...]
-    for face in range(2):
+    zero = jnp.zeros((SUB, cq), F32)
+    for face, ref in enumerate((left_ref, right_ref)):
         base = 3 * hy + face * (tiles - 1) * SUB
         le = [tab_ref[base + i * SUB : base + (i + 1) * SUB, :] > 0.5 for i in range(tiles - 1)]
-        zero = jnp.zeros((SUB, cq), F32)
         for c in range(nt):
 
-            def step(k, _, face=face, c=c):
-                r = [slots[c, face, k, i * SUB : (i + 1) * SUB, :] for i in range(tiles - 1)]
+            def step(k, _, face=face, c=c, ref=ref, le=le):
+                r = [ref[c, k, i * SUB : (i + 1) * SUB, :] for i in range(tiles - 1)]
                 for j in range(tiles):
                     if j == 0:
                         v = jnp.where(le[0], zero, r[0])
@@ -385,7 +400,6 @@
         cost_estimate=cost(0, 8 * nt * rows * cq),
         name="split",
     )(qv, source_amplitude, *([robin_in] * nt))
-    there = [swap(cuts[0])]
     dealt = [cuts[0]] + [xor_permute(cuts[d], d) for d in range(1, nt)]
 
     base = np.stack(np_halves(np_cosine(nz, np.arange(nz)[:, None], np.arange(nz)[None])))
@@ -409,7 +423,7 @@
                 ],
                 out_specs=pl.BlockSpec((nx, SUB, cq), lambda i, q: (0, i, 0)),
             ),
-            compiler_params=grant(8),
+            compiler_params=grant(56),
             cost_estimate=cost(1e9, 3e6),
         )(qv, values, base, kxh, kxl)
 
@@ -417,7 +431,16 @@
     n1 = swap(n0)
     s0 = forward(tied((heat_source, n0))[0])
     s1 = swap(s0)
-    there += [swap(dealt[d]) for d in range(1, nt)]
+    u_own, amps, *windows = pl.pallas_call(
+        functools.partial(order_kernel, nt),
+        out_shape=[sds(nt, 2, steps, hy, cq), sds(nt, steps, cq)] + [sds(2, steps, hy, cq)] * nt,
+        in_specs=[SM] + [VM] * nt,
+        out_specs=[VM] * (nt + 2),
+        compiler_params=grant(10),
+        cost_estimate=cost(0, 3e6),
+        name="order",
+    )(qv, *dealt)
+    there = [swap(u) for u in windows]
 
     robin_param, spectrum_y, spectrum_x, spectrum_z, open_flag, owner_side, yc, _ = tied(
         (robin_param, spectrum_y, spectrum_x, spectrum_z, open_flag, owner_side, yc, s0)
@@ -475,52 +498,62 @@
     fill = lambda v: jnp.asarray(np.broadcast_to(v[:, None, None], (nx, SUB, cq)).astype(np.float32))
     wv, wd = fill(first * first), fill(first * (second - first))
 
-    scratch = [pltpu.VMEM((nt, 2, steps, hy, cq), F32), pltpu.VMEM((nt, steps, cq), F32)]
-    ql, qr, clos, m_there, s_there = pl.pallas_call(
+    short = sds(2, steps, (tiles - 1) * SUB, cq)
+    *hands, clos, m_there, s_there = pl.pallas_call(
         functools.partial(own_kernel, dims),
-        out_shape=[sds(nt * steps, (tiles - 1) * SUB, cq)] * 2
-        + [sds(nt, nx, hy, cq), sds(nx, hy, cq), sds(nx, hy, cq)],
-        in_specs=[SM] * 4 + [VM] * (10 + nt),
-        out_specs=[VM] * 5,
+        out_shape=[short] * nt + [sds(nt, nx, hy, cq), sds(nx, hy, cq), sds(nx, hy, cq)],
+        in_specs=[SM] * 4 + [VM] * 12,
+        out_specs=[VM] * (nt + 3),
         scratch_shapes=[pltpu.VMEM((nx, hy, cq), F32)] * 3
-        + [pltpu.VMEM((2, 2, nt * steps, tiles, SUB, cq), F32)]
-        + scratch,
-        compiler_params=grant(20),
+        + [pltpu.VMEM((2, 2, nt * steps, tiles, SUB, cq), F32)],
+        compiler_params=grant(18),
         cost_estimate=cost(4e9, 8e6),
         name="own",
-    )(qv, sx, diffusivity, params, n0, s0, n1, s1, *dealt, tab, sz, kyh, kyl, wv, wd)
-    to_left = along(ql, -1)
-    to_right = along(qr, 1)
-
-    other = pl.pallas_call(
-        functools.partial(other_kernel, dims),
-        out_shape=[sds(nx, hy, cq)] * nt,
-        in_specs=[SM] * 3 + [VM] * (9 + nt),
-        out_specs=[VM] * nt,
-        scratch_shapes=[
-            pltpu.VMEM((nx, hy, cq), F32),
-            pltpu.VMEM((nt, nx, hy, cq), F32),
-            pltpu.VMEM((nx, hy, 2 * cq), F32),
-        ]
-        + scratch,
-        compiler_params=grant(20),
-        cost_estimate=cost(6e9, 8e6),
-        name="other",
-    )
-    outs = other(qv, sx, diffusivity, m_there, s_there, *there, sy_there, sz, clos, kih, kil, kxih, kxil)
-    ends = [outs[0]] + [xor_permute(outs[d], d) for d in range(1, nt)]
-
-    short = sds(2, steps, (tiles - 1) * SUB, cq)
-    hands = pl.pallas_call(
-        functools.partial(deal_kernel, nt, steps),
-        out_shape=[short] * nt,
-        in_specs=[SM, VM, VM],
-        out_specs=[VM] * nt,
+    )(qv, sx, diffusivity, params, n0, s0, n1, s1, u_own, amps, tab, sz, kyh, kyl, wv, wd)
+    for d in range(1, nt):
+        hands[d] = xor_permute(hands[d], d)
+
+    def finish(first, last, state):
+        count = last - first
+        nout = nt if count > 1 else 1
+        call = pl.pallas_call(
+            functools.partial(other_kernel, dims, first, last),
+            out_shape=[sds(nx, hy, cq)] * (nout + 1),
+            in_specs=[SM] * 3 + [VM] * (10 + count),
+            out_specs=[VM] * (nout + 1),
+            scratch_shapes=[
+                pltpu.VMEM((nx, hy, cq), F32),
+                pltpu.VMEM((count, nx, hy, cq), F32),
+                pltpu.VMEM((nx, hy, min(count, 2) * cq), F32),
+                pltpu.VMEM((count, 2, steps, hy, cq), F32),
+            ],
+            compiler_params=grant(18),
+            cost_estimate=cost(1.5e9 * count, 2e6 * count),
+        )
+        return call(
+            qv, sx, diffusivity, state, s_there, *there[first:last], amps, sy_there, sz,
+            clos, kih, kil, kxih, kxil,
+        )
+
+    final = nt - 1
+    *most, state = finish(0, final, m_there)
+    for d in range(1, nt):
+        most[d] = lax.ppermute(most[d], "tm", [(i, i ^ d) for i in range(nt) if i ^ d != final])
+    left, right = pl.pallas_call(
+        functools.partial(merge_kernel, nt),
+        out_shape=[sds(nt, steps, (tiles - 1) * SUB, cq)] * 2,
+        in_specs=[SM] + [VM] * nt,
+        out_specs=[VM] * 2,
         compiler_params=grant(8),
         cost_estimate=cost(0, 2e6),
-        name="deal",
-    )(qv, to_right, to_left)
-    hands = [hands[0]] + [xor_permute(hands[d], d) for d in range(1, nt)]
+        name="merge",
+    )(qv, *hands)
+    from_right = along(left, -1)
+    from_left = along(right, 1)
+    late, _ = finish(final, nt, state)
+    late = [late]
+    for d in range(1, nt):
+        late.append(lax.ppermute(late[0], "tm", [(final ^ d, final)]))
 
     xb = SUB
     window_end = pl.pallas_call(
@@ -533,28 +566,25 @@
                 pl.BlockSpec((None, 2, cq, nz), lambda i, q, d=d: (jnp.bitwise_xor(q[0], d), 0, 0, 0))
                 for d in range(nt)
             ]
-            + [pl.BlockSpec((xb, hy, cq), lambda i, q: (i, 0, 0))] * nt,
+            + [pl.BlockSpec((xb, hy, cq), lambda i, q: (i, 0, 0))] * (2 * nt),
             out_specs=pl.BlockSpec((1, xb, hy, nz), lambda i, q: (0, i, 0, 0)),
             scratch_shapes=[pltpu.VMEM((nz, nz), BF16)] * 2,
         ),
         compiler_params=grant(16),
         cost_estimate=cost(2e9, 6e6),
         name="final",
-    )(qv, *([base] * nt), *ends)
+    )(qv, *([base] * nt), *most, *late)
 
     robin_out = pl.pallas_call(
         functools.partial(spread_kernel, nt, steps),
         out_shape=sds(1, 2, steps, hy, nz),
-        in_specs=[SM] + [VM] * (nt + 1),
+        in_specs=[VM] * 3,
         out_specs=VM,
-        scratch_shapes=[
-            pltpu.VMEM((nt,) + short.shape, F32),
-            pltpu.VMEM((2, steps, hy, cq), F32),
-        ],
+        scratch_shapes=[pltpu.VMEM((2, steps, hy, cq), F32)],
         compiler_params=grant(8),
         cost_estimate=cost(0, 2e6),
         name="spread",
-    )(qv, tab, *hands)
+    )(tab, from_left, from_right)
     return robin_out, window_end
 
 

time: 115 us -> 137 us (1.19)
  waiting for transfers between devices: 44.6 us -> 58.1 us
  starting transfers between devices: 22.5 us -> 31.2 us
  local copies, waits for them, and re-layouts: 10.5 us -> 3.14 us
  Pallas kernels: 29 us -> 35.8 us
    ppermute x0 -> x6, waiting for transfers between devices: none -> 17.8 us  [the longest x3 17.8 us: local(): lax.ppermute(most[d], 'tm', [(i, i ^ d) for i in range(nt) if i ^ d != fi...]
    ppermute x4, waiting for transfers between devices: 16.3 us -> 0.01 us  [along(): lax.ppermute(x, 'space', [(i, (i + by) % space) for i in range(space)])]
    ppermute x9 -> x6, waiting for transfers between devices: 7.37 us -> 20.8 us  [xor_permute(): return lax.ppermute(x, 'tm', [(i, i ^ d) for i in range(nt)])]
    ppermute x0 -> x6, starting transfers between devices: none -> 11.8 us  [the longest x3 6.55 us: local(): lax.ppermute(most[d], 'tm', [(i, i ^ d) for i in range(nt) if i ^ d != fi...]
    unnamed x32 -> x30, local copies, waits for them, and re-layouts: 6.98 us -> 1.67 us
    pallas_call x2, Pallas kernels: 4.95 us -> 9.51 us  [forward(): pl.pallas_call(forward_kernel, out_shape=sds(nx, hy, cq), grid_spec=pltpu...]
    ppermute x9 -> x6, starting transfers between devices: 5.69 us -> 2.49 us  [xor_permute(): return lax.ppermute(x, 'tm', [(i, i ^ d) for i in range(nt)])]
    pallas_call x3 -> x5, Pallas kernels: 17.8 us -> 20.1 us  [the longest x2 11.1 us: finish(): call(qv, sx, diffusivity, state, s_there, *there[first:last], amps, sy_th...]
  transfers between devices with their start and end apart: 20 -> 23, of which waited for: 9 -> 8; matrix products, arithmetic and copies ran while one was open for 8% -> 5% of each run, Pallas kernels for 12% -> 16%
where the time goes in v1:
time: 137 us; the launch traced here: 136 us
  waiting for transfers between devices  58.1 us (42%)
  Pallas kernels  35.8 us (26%)
  starting transfers between devices  31.2 us (23%)
  other arithmetic  5.78 us (4%)
  local copies, waits for them, and re-layouts  3.14 us (2%)
  between operations  2.34 us (2%)
    ppermute x6, waiting for transfers between devices, xor_permute(): return lax.ppermute(x, 'tm', [(i, i ^ d) for i in range(nt)])  20.8 us
    ppermute x7, waiting for transfers between devices, swap(): return lax.ppermute(x, 'cores', [(0, 1), (1, 0)])  19.4 us
    ppermute x3, waiting for transfers between devices, local(): lax.ppermute(most[d], 'tm', [(i, i ^ d) for i in range(nt) if i ^ d != fi...  17.8 us
    pallas_call x2, Pallas kernels, finish(): call(qv, sx, diffusivity, state, s_there, *there[first:last], amps, sy_th...  11.1 us
    pallas_call x2, Pallas kernels, forward(): pl.pallas_call(forward_kernel, out_shape=sds(nx, hy, cq), grid_spec=pltpu...  9.51 us
    ppermute x4, starting transfers between devices, along(): lax.ppermute(x, 'space', [(i, (i + by) % space) for i in range(space)])  9.06 us
    pallas_call x1, Pallas kernels, local(): pl.pallas_call(functools.partial(own_kernel, dims), out_shape=[short] * n...  8.76 us
    ppermute x7, starting transfers between devices, swap(): return lax.ppermute(x, 'cores', [(0, 1), (1, 0)])  7.88 us
  transfers between devices with their start and end apart: 23, of which 8 were waited for; matrix products, arithmetic and copies ran while one was open for 5% of the time, Pallas kernels for 16%

profile of v1, /device:TPU:0, one launch (start us, length us, event | category | flops | bytes accessed | tf_op | source)
XLA Modules:
  0.0 136.4 jit_solution(11275524784257838654)
XLA Ops:
  0.7 4.7 %shard_map.185.refs_0_ = f32[32,32,128]{2,1,0:T(8,128)} custom-call(s32[1]{0:T(128)} %bitcast.q_ref, f32[32,32,512]{2,1,0:T(8,128)} %x_ref.1, bf16[4,2,128,512]{3,2,1,0:T(8,128)(2,1)} %constant.247.clone.c_ref.refs_0_.refs_1_.refs_2_.refs_3_, bf16[256,256]{1,0:T(8,128)(2,1)} %constant.248.clone.kxh_ref, bf16[256,256]{1,0:T(8,128)(2,1)} %constant.249.clone.kxl_ref), custom_call_target="tpu_custom_call" | custom-call | flops 1000000000 | bytes 3000000 | tf_op jit(solution)/shard_map/pallas_call | solution.py:412
  5.4 4.8 %shard_map.186.refs_1_ = f32[32,32,128]{2,1,0:T(8,128)} custom-call(s32[1]{0:T(128)} %bitcast.q_ref, f32[32,32,512]{2,1,0:T(8,128)} %x_ref.2, bf16[4,2,128,512]{3,2,1,0:T(8,128)(2,1)} %constant.247.clone.c_ref.refs_0_.refs_1_.refs_2_.refs_3_, bf16[256,256]{1,0:T(8,128)(2,1)} %constant.248.clone.kxh_ref, bf16[256,256]{1,0:T(8,128)(2,1)} %constant.249.clone.kxl_ref), custom_call_target="tpu_custom_call" | custom-call | flops 1000000000 | bytes 3000000 | tf_op jit(solution)/shard_map/pallas_call | solution.py:412
  10.2 3.1 %collective-permute-start = (f32[1]{0:T(128)}, f32[1]{0:T(128)}, u32[]{:S(2)}, u32[]{:S(2)}) collective-permute-start(f32[1]{0:T(128)} %param.22), channel_id=1, source_target_pairs={{0,8},{8,16},{16,24},{24,0},{1,9},{9,17},{17,25},{25,1},{2,10},{10... | collective-permute-start | bytes 20 | tf_op jit(solution)/shard_map/ppermute | solution.py:382
  13.3 2.1 %collective-permute-start.1 = (f32[1]{0:T(128)}, f32[1]{0:T(128)}, u32[]{:S(2)}, u32[]{:S(2)}) collective-permute-start(f32[1]{0:T(128)} %param.22), channel_id=1, source_target_pairs={{0,24},{8,0},{16,8},{24,16},{1,25},{9,1},{17,9},{25,17},{2,26},{10... | collective-permute-start | bytes 20 | tf_op jit(solution)/shard_map/ppermute | solution.py:382
  15.4 1.7 %collective-permute-start.3 = (f32[32,32,128]{2,1,0:T(8,128)}, f32[32,32,128]{2,1,0:T(8,128)S(1)}, u32[]{:S(2)}, u32[]{:S(2)}) collective-permute-start(f32[32,32,128]{2,1,0:T(8,128)} %shard_map.186.refs_1_), channel_id=1, source_target_pairs={{0,1},{1,0},{2,3},{3,2},{4,5},{5,4},{6,7},{7,6},{8,9},{9,8},{10,11... | collective-permute-start | bytes 1572872 | tf_op jit(solution)/shard_map/ppermute | solution.py:379
  17.4 1.3 split.1
  20.4 2.3 %fusion = (bf16[256,256]{1,0:T(8,128)(2,1)S(1)}, bf16[256,256]{1,0:T(8,128)(2,1)S(1)}) fusion(s32[256]{0:T(256)S(1)} %get-tuple-element.81, s32[256]{0:T(256)S(1)} %get-tuple-element.83, pred[256]{0:T(512)(128)(4,1)S(1)} %get-tuple-element.78, s32[256]{0:T(256)S(1)} %get-tuple-element.82, s32[256]{0:T(256)S(1)} %get-tuple-element.84, ...), kind=kLoop, calls=%fused_computation.24 | loop fusion | flops 4718592 | bytes 269064 | tf_op jit(solution)/shard_map/convert_element_type | solution.py:29
  23.5 0.8 reduce-precision_convert_fusion.1.refs_7_.refs_5_
  24.3 1.7 %collective-permute-start.15 = (f32[32]{0:T(128)S(1)}, f32[32]{0:T(128)S(1)}, u32[]{:S(2)}, u32[]{:S(2)}) collective-permute-start(f32[32]{0:T(128)S(1)} %copy-done.13), channel_id=1, source_target_pairs={{0,1},{1,0},{2,3},{3,2},{4,5},{5,4},{6,7},{7,6},{8,9},{9,8},{10,11... | collective-permute-start | bytes 392 | tf_op jit(solution)/shard_map/ppermute | solution.py:379
  26.0 1.5 %collective-permute-start.5 = (f32[520,128]{1,0:T(8,128)}, f32[520,128]{1,0:T(8,128)S(1)}, u32[]{:S(2)}, u32[]{:S(2)}) collective-permute-start(f32[520,128]{1,0:T(8,128)} %copy-done.6), channel_id=1, source_target_pairs={{0,4},{2,6},{4,0},{6,2},{1,5},{3,7},{5,1},{7,3},{8,12},{10,14},{12... | collective-permute-start | bytes 798728 | tf_op jit(solution)/shard_map/ppermute | solution.py:376
  27.5 12.9 %collective-permute-done.15 = f32[32]{0:T(128)S(1)} collective-permute-done((f32[32]{0:T(128)S(1)}, f32[32]{0:T(128)S(1)}, u32[]{:S(2)}, u32[]{:S(2)}) %collective-permute-start.15) | collective-permute-done | bytes 160 | tf_op jit(solution)/shard_map/ppermute | solution.py:379
  42.6 1.3 pad_maximum_fusion.1.par_ref
  44.2 4.8 %collective-permute-done.6.refs_3_ = f32[520,128]{1,0:T(8,128)S(1)} collective-permute-done((f32[520,128]{1,0:T(8,128)S(1)}, f32[520,128]{1,0:T(8,128)S(1)}, u32[]{:S(2)}, u32[]{:S(2)}) %collective-permute-start.6) | collective-permute-done | bytes 266272 | tf_op jit(solution)/shard_map/ppermute | solution.py:376
  49.1 1.6 %collective-permute-start.12 = (f32[2,8,32,128]{3,2,1,0:T(8,128)S(1)}, f32[2,8,32,128]{3,2,1,0:T(8,128)S(1)}, u32[]{:S(2)}, u32[]{:S(2)}) collective-permute-start(f32[2,8,32,128]{3,2,1,0:T(8,128)S(1)} %get-tuple-element.57), channel_id=1, source_target_pairs={{0,1},{1,0},{2,3},{3,2},{4,5},{5,4},{6,7},{7,6},{8,9},{9,8},{10,11... | collective-permute-start | bytes 786440 | tf_op jit(solution)/shard_map/ppermute | solution.py:379
  51.2 1.5 %collective-permute-start.14 = (f32[2,8,32,128]{3,2,1,0:T(8,128)S(1)}, f32[2,8,32,128]{3,2,1,0:T(8,128)S(1)}, u32[]{:S(2)}, u32[]{:S(2)}) collective-permute-start(f32[2,8,32,128]{3,2,1,0:T(8,128)S(1)} %get-tuple-element.59), channel_id=1, source_target_pairs={{0,1},{1,0},{2,3},{3,2},{4,5},{5,4},{6,7},{7,6},{8,9},{9,8},{10,11... | collective-permute-start | bytes 786440 | tf_op jit(solution)/shard_map/ppermute | solution.py:379
  53.4 0.9 copy-done.10
  54.3 8.8 %own.1 = (f32[2,8,24,128]{3,2,1,0:T(8,128)S(1)}, f32[2,8,24,128]{3,2,1,0:T(8,128)S(1)}, f32[2,8,24,128]{3,2,1,0:T(8,128)S(1)}, f32[2,8,24,128]{3,2,1,0:T(8,128)S...) custom-call(s32[1]{0:T(128)} %bitcast.q_ref, f32[32]{0:T(128)S(1)} %reshape.45.sx_ref, ...), custom_call_target="tpu_custom_call" | custom-call | flops 4000000000 | bytes 8000000 | tf_op jit(solution)/shard_map/own/pallas_call | solution.py:502
  63.1 0.9 collective-permute-done.13.refs_1_
  64.0 5.6 %collective-permute-done.14.refs_2_ = f32[2,8,32,128]{3,2,1,0:T(8,128)S(1)} collective-permute-done((f32[2,8,32,128]{3,2,1,0:T(8,128)S(1)}, f32[2,8,32,128]{3,2,1,0:T(8,128)S(1)}, u32[]{:S(2)}, u32[]{:S(2)}) %collective-permute-start.14) | collective-permute-done | bytes 262176 | tf_op jit(solution)/shard_map/ppermute | solution.py:379
  69.7 7.5 %shard_map.187 = (f32[32,32,128]{2,1,0:T(8,128)S(1)}, f32[32,32,128]{2,1,0:T(8,128)S(1)}, f32[32,32,128]{2,1,0:T(8,128)S(1)}, f32[32,32,128]{2,1,0:T(8,128)S(1)}, f32[32,32,128]{2,1,0:T(8,128)S(1)}) custom-call(s32[1]{0:T(128)} %bitcast.q_ref, f32[32]{0:T(128)S(1)} %reshape.45.sx_ref, f32[1]{0:T(128)S(6)} %copy.30.diff_ref, ...), custom_call_target="tpu_custom_call" | custom-call | flops 4499999744 | bytes 6000000 | tf_op jit(solution)/shard_map/pallas_call | solution.py:533
  77.3 3.6 %shard_map.188 = (f32[32,32,128]{2,1,0:T(8,128)S(1)}, f32[32,32,128]{2,1,0:T(8,128)}) custom-call(s32[1]{0:T(128)} %bitcast.q_ref, f32[32]{0:T(128)S(1)} %reshape.45.sx_ref, f32[1]{0:T(128)S(6)} %copy.30.diff_ref, f32[32,32,128]{2,1,0:T(8,128)S(1)} %get-tuple-element.65.m_ref, f32[32,32,128]{2,1,0:T(8,128)S(1)} %get-tuple-element.56.s_ref, ...), custom_call_target="tpu_custom_call" | custom-call | flops 1500000000 | bytes 2000000 | tf_op jit(solution)/shard_map/pallas_call | solution.py:533
  82.3 3.9 %collective-permute-start.22 = (f32[32,32,128]{2,1,0:T(8,128)S(1)}, f32[32,32,128]{2,1,0:T(8,128)S(1)}, u32[]{:S(2)}, u32[]{:S(2)}) collective-permute-start(f32[32,32,128]{2,1,0:T(8,128)S(1)} %get-tuple-element.67.refs_8_), channel_id=1, source_target_pairs={{0,6},{1,7},{8,14},{9,15},{16,22},{17,23},{24,30},{25,31}} | collective-permute-start | bytes 1572872 | tf_op jit(solution)/shard_map/ppermute | solution.py:556
  86.3 0.8 collective-permute-start.9
  87.1 15.5 %collective-permute-done.8.refs_2_ = f32[2,8,24,128]{3,2,1,0:T(8,128)S(1)} collective-permute-done((f32[2,8,24,128]{3,2,1,0:T(8,128)S(1)}, f32[2,8,24,128]{3,2,1,0:T(8,128)S(1)}, u32[]{:S(2)}, u32[]{:S(2)}) %collective-permute-start.8) | collective-permute-done | bytes 196640 | tf_op jit(solution)/shard_map/ppermute | solution.py:376
  102.7 1.9 %collective-permute-start.16 = (f32[32,32,128]{2,1,0:T(8,128)S(1)}, f32[32,32,128]{2,1,0:T(8,128)S(1)}, u32[]{:S(2)}, u32[]{:S(2)}) collective-permute-start(f32[32,32,128]{2,1,0:T(8,128)S(1)} %get-tuple-element.62), channel_id=1, source_target_pairs={{0,2},{2,0},{6,4},{1,3},{3,1},{7,5},{8,10},{10,8},{14,12},{9,11},{... | collective-permute-start | bytes 1572872 | tf_op jit(solution)/shard_map/ppermute | solution.py:541
  105.0 3.3 %collective-permute-start.17 = (f32[32,32,128]{2,1,0:T(8,128)S(1)}, f32[32,32,128]{2,1,0:T(8,128)S(1)}, u32[]{:S(2)}, u32[]{:S(2)}) collective-permute-start(f32[32,32,128]{2,1,0:T(8,128)S(1)} %get-tuple-element.63), channel_id=1, source_target_pairs={{0,4},{4,0},{6,2},{1,5},{5,1},{7,3},{8,12},{12,8},{14,10},{9,13},{... | collective-permute-start | bytes 1572872 | tf_op jit(solution)/shard_map/ppermute | solution.py:541
  108.4 1.3 collective-permute-start.18
  109.8 3.8 %collective-permute-start.11 = (f32[4,8,24,128]{3,2,1,0:T(8,128)S(1)}, f32[4,8,24,128]{3,2,1,0:T(8,128)S(1)}, u32[]{:S(2)}, u32[]{:S(2)}) collective-permute-start(f32[4,8,24,128]{3,2,1,0:T(8,128)S(1)} %get-tuple-element.54), channel_id=1, source_target_pairs={{0,24},{8,0},{16,8},{24,16},{1,25},{9,1},{17,9},{25,17},{2,26},{10... | collective-permute-start | bytes 1179656 | tf_op jit(solution)/shard_map/ppermute | solution.py:382
  113.6 8.1 %collective-permute-done.17.refs_6_ = f32[32,32,128]{2,1,0:T(8,128)S(1)} collective-permute-done((f32[32,32,128]{2,1,0:T(8,128)S(1)}, f32[32,32,128]{2,1,0:T(8,128)S(1)}, u32[]{:S(2)}, u32[]{:S(2)}) %collective-permute-start.17) | collective-permute-done | bytes 524320 | tf_op jit(solution)/shard_map/ppermute | solution.py:541
  121.7 9.8 %collective-permute-done.18.refs_7_ = f32[32,32,128]{2,1,0:T(8,128)S(1)} collective-permute-done((f32[32,32,128]{2,1,0:T(8,128)S(1)}, f32[32,32,128]{2,1,0:T(8,128)S(1)}, u32[]{:S(2)}, u32[]{:S(2)}) %collective-permute-start.18) | collective-permute-done | bytes 524320 | tf_op jit(solution)/shard_map/ppermute | solution.py:541
  131.5 3.4 %final.1 = f32[1,32,32,512]{3,2,1,0:T(8,128)} custom-call(s32[1]{0:T(128)} %bitcast.q_ref, bf16[4,2,128,512]{3,2,1,0:T(8,128)(2,1)S(1)} %copy-done.1, bf16[4,2,128,512]{3,2,1,0:T(8,128)(2,1)S(1)} %copy-done.1, bf16[4,2,128,512]{3,2,1,0:T(8,128)(2,1)S(1)} %copy-done.1, bf16[4,2,128,512]{3,2,1,0:T(8,128)(2,1)S(1)} %copy-done.1, ...), custom_call_target="tpu_custom_call" | custom-call | flops 2000000000 | bytes 6000000 | tf_op jit(solution)/shard_map/final/pallas_call | solution.py:559
  134.9 1.5 %spread.1 = f32[1,2,8,32,512]{4,3,2,1,0:T(8,128)} custom-call(f32[144,128]{1,0:T(8,128)S(1)} %broadcast_in_dim.56.refs_6_.tab_ref, f32[4,8,24,128]{3,2,1,0:T(8,128)S(1)} %collective-permute-done.10.left_ref, f32[4,8,24,128]{3,2,1,0:T(8,128)S(1)} %collective-permute-done.11.right_ref), custom_call_target="tpu_custom_call" | custom-call | bytes 2000000 | tf_op jit(solution)/shard_map/spread/pallas_call | solution.py:578
  (95 shorter events, 7.2 us)
Async XLA Ops:
  0.6 39.7 %copy-start = (f32[512]{0:T(512)S(1)}, f32[512]{0:T(512)}, u32[]{:S(2)}) copy-start(f32[512]{0:T(512)} %param.25) | copy-start | bytes 6148
  5.4 12.1 %copy-start.5 = (f32[8]{0:T(128)S(1)}, f32[8]{0:T(128)}, u32[]{:S(2)}) copy-start(f32[8]{0:T(128)} %amp_ref.1) | copy-start | bytes 100
  10.2 14.1 %copy-start.13 = (f32[32]{0:T(128)S(1)}, f32[32]{0:T(128)}, u32[]{:S(2)}) copy-start(f32[32]{0:T(128)} %param.24) | copy-start | bytes 388
  10.2 31.4 %copy-start.14 = (f32[32]{0:T(128)S(1)}, f32[32]{0:T(128)}, u32[]{:S(2)}) copy-start(f32[32]{0:T(128)} %param.23) | copy-start | bytes 388
  10.2 43.2 %copy-start.4 = (f32[32,32,128]{2,1,0:T(8,128)S(1)}, f32[32,32,128]{2,1,0:T(8,128)}, u32[]{:S(2)}) copy-start(f32[32,32,128]{2,1,0:T(8,128)} %shard_map.186.refs_1_) | copy-start | bytes 1572868
  10.2 43.2 %copy-start.9 = (f32[32,8,128]{2,1,0:T(8,128)S(1)}, f32[32,8,128]{2,1,0:T(8,128)}, u32[]{:S(2)}) copy-start(f32[32,8,128]{2,1,0:T(8,128)} %constant.252.clone.refs_10_) | copy-start | bytes 393220
  10.2 14.0 %collective-permute-start = (f32[1]{0:T(128)}, f32[1]{0:T(128)}, u32[]{:S(2)}, u32[]{:S(2)}) collective-permute-start(f32[1]{0:T(128)} %param.22), channel_id=1, source_target_pairs={{0,8},{8,16},{16,24},{24,0},{1,9},{9,17},{17,25},{25,1},{2,10},{10... | collective-permute-start | bytes 20 | tf_op jit(solution)/shard_map/ppermute | solution.py:382
  13.3 12.7 %collective-permute-start.1 = (f32[1]{0:T(128)}, f32[1]{0:T(128)}, u32[]{:S(2)}, u32[]{:S(2)}) collective-permute-start(f32[1]{0:T(128)} %param.22), channel_id=1, source_target_pairs={{0,24},{8,0},{16,8},{24,16},{1,25},{9,1},{17,9},{25,17},{2,26},{10... | collective-permute-start | bytes 20 | tf_op jit(solution)/shard_map/ppermute | solution.py:382
  15.4 37.3 %collective-permute-start.3 = (f32[32,32,128]{2,1,0:T(8,128)}, f32[32,32,128]{2,1,0:T(8,128)S(1)}, u32[]{:S(2)}, u32[]{:S(2)}) collective-permute-start(f32[32,32,128]{2,1,0:T(8,128)} %shard_map.186.refs_1_), channel_id=1, source_target_pairs={{0,1},{1,0},{2,3},{3,2},{4,5},{5,4},{6,7},{7,6},{8,9},{9,8},{10,11... | collective-permute-start | bytes 1572872 | tf_op jit(solution)/shard_map/ppermute | solution.py:379
  17.1 36.2 %collective-permute-start.2 = (f32[32,32,128]{2,1,0:T(8,128)S(1)}, f32[32,32,128]{2,1,0:T(8,128)}, u32[]{:S(2)}, u32[]{:S(2)}) collective-permute-start(f32[32,32,128]{2,1,0:T(8,128)S(1)} %copy-done.3), channel_id=1, source_target_pairs={{0,1},{1,0},{2,3},{3,2},{4,5},{5,4},{6,7},{7,6},{8,9},{9,8},{10,11... | collective-permute-start | bytes 1572872 | tf_op jit(solution)/shard_map/ppermute | solution.py:379
  19.5 24.7 %collective-permute-start.4 = (f32[520,128]{1,0:T(8,128)}, f32[520,128]{1,0:T(8,128)S(1)}, u32[]{:S(2)}, u32[]{:S(2)}) collective-permute-start(f32[520,128]{1,0:T(8,128)} %get-tuple-element.42), channel_id=1, source_target_pairs={{0,2},{2,0},{4,6},{6,4},{1,3},{3,1},{5,7},{7,5},{8,10},{10,8},{12,... | collective-permute-start | bytes 798728 | tf_op jit(solution)/shard_map/ppermute | solution.py:376
  24.3 16.1 %collective-permute-start.15 = (f32[32]{0:T(128)S(1)}, f32[32]{0:T(128)S(1)}, u32[]{:S(2)}, u32[]{:S(2)}) collective-permute-start(f32[32]{0:T(128)S(1)} %copy-done.13), channel_id=1, source_target_pairs={{0,1},{1,0},{2,3},{3,2},{4,5},{5,4},{6,7},{7,6},{8,9},{9,8},{10,11... | collective-permute-start | bytes 392 | tf_op jit(solution)/shard_map/ppermute | solution.py:379
  26.0 18.2 %collective-permute-start.5 = (f32[520,128]{1,0:T(8,128)}, f32[520,128]{1,0:T(8,128)S(1)}, u32[]{:S(2)}, u32[]{:S(2)}) collective-permute-start(f32[520,128]{1,0:T(8,128)} %copy-done.6), channel_id=1, source_target_pairs={{0,4},{2,6},{4,0},{6,2},{1,5},{3,7},{5,1},{7,3},{8,12},{10,14},{12... | collective-permute-start | bytes 798728 | tf_op jit(solution)/shard_map/ppermute | solution.py:376
  40.4 8.7 %collective-permute-start.6 = (f32[520,128]{1,0:T(8,128)S(1)}, f32[520,128]{1,0:T(8,128)S(1)}, u32[]{:S(2)}, u32[]{:S(2)}) collective-permute-start(f32[520,128]{1,0:T(8,128)S(1)} %get-tuple-element.44), channel_id=1, source_target_pairs={{0,6},{2,4},{4,2},{6,0},{1,7},{3,5},{5,3},{7,1},{8,14},{10,12},{12... | collective-permute-start | bytes 798728 | tf_op jit(solution)/shard_map/ppermute | solution.py:376
  49.1 13.9 %collective-permute-start.12 = (f32[2,8,32,128]{3,2,1,0:T(8,128)S(1)}, f32[2,8,32,128]{3,2,1,0:T(8,128)S(1)}, u32[]{:S(2)}, u32[]{:S(2)}) collective-permute-start(f32[2,8,32,128]{3,2,1,0:T(8,128)S(1)} %get-tuple-element.57), channel_id=1, source_target_pairs={{0,1},{1,0},{2,3},{3,2},{4,5},{5,4},{6,7},{7,6},{8,9},{9,8},{10,11... | collective-permute-start | bytes 786440 | tf_op jit(solution)/shard_map/ppermute | solution.py:379
  50.7 13.3 %collective-permute-start.13 = (f32[2,8,32,128]{3,2,1,0:T(8,128)S(1)}, f32[2,8,32,128]{3,2,1,0:T(8,128)S(1)}, u32[]{:S(2)}, u32[]{:S(2)}) collective-permute-start(f32[2,8,32,128]{3,2,1,0:T(8,128)S(1)} %get-tuple-element.58), channel_id=1, source_target_pairs={{0,1},{1,0},{2,3},{3,2},{4,5},{5,4},{6,7},{7,6},{8,9},{9,8},{10,11... | collective-permute-start | bytes 786440 | tf_op jit(solution)/shard_map/ppermute | solution.py:379
  51.2 18.4 %collective-permute-start.14 = (f32[2,8,32,128]{3,2,1,0:T(8,128)S(1)}, f32[2,8,32,128]{3,2,1,0:T(8,128)S(1)}, u32[]{:S(2)}, u32[]{:S(2)}) collective-permute-start(f32[2,8,32,128]{3,2,1,0:T(8,128)S(1)} %get-tuple-element.59), channel_id=1, source_target_pairs={{0,1},{1,0},{2,3},{3,2},{4,5},{5,4},{6,7},{7,6},{8,9},{9,8},{10,11... | collective-permute-start | bytes 786440 | tf_op jit(solution)/shard_map/ppermute | solution.py:379
  52.8 24.5 %collective-permute-start.19 = (f32[2,8,32,128]{3,2,1,0:T(8,128)S(1)}, f32[2,8,32,128]{3,2,1,0:T(8,128)S(1)}, u32[]{:S(2)}, u32[]{:S(2)}) collective-permute-start(f32[2,8,32,128]{3,2,1,0:T(8,128)S(1)} %get-tuple-element.66), channel_id=1, source_target_pairs={{0,1},{1,0},{2,3},{3,2},{4,5},{5,4},{6,7},{7,6},{8,9},{9,8},{10,11... | collective-permute-start | bytes 786440 | tf_op jit(solution)/shard_map/ppermute | solution.py:379
  54.3 15.4 %copy-start.7 = (bf16[256,256]{1,0:T(8,128)(2,1)S(1)}, bf16[256,256]{1,0:T(8,128)(2,1)}, u32[]{:S(2)}) copy-start(bf16[256,256]{1,0:T(8,128)(2,1)} %constant.250.clone.refs_9_.refs_7_) | copy-start | bytes 393220
  54.3 15.4 %copy-start.8 = (bf16[256,256]{1,0:T(8,128)(2,1)S(1)}, bf16[256,256]{1,0:T(8,128)(2,1)}, u32[]{:S(2)}) copy-start(bf16[256,256]{1,0:T(8,128)(2,1)} %constant.251.clone.refs_10_.refs_8_) | copy-start | bytes 393220
  77.2 54.2 %copy-start.1 = (bf16[4,2,128,512]{3,2,1,0:T(8,128)(2,1)S(1)}, bf16[4,2,128,512]{3,2,1,0:T(8,128)(2,1)}, u32[]{:S(2)}) copy-start(bf16[4,2,128,512]{3,2,1,0:T(8,128)(2,1)} %constant.247.clone.c_ref.refs_0_.refs_1_.refs_2_.refs_3_) | copy-start | bytes 3145732
  80.8 27.5 %collective-permute-start.20 = (f32[32,32,128]{2,1,0:T(8,128)S(1)}, f32[32,32,128]{2,1,0:T(8,128)S(1)}, u32[]{:S(2)}, u32[]{:S(2)}) collective-permute-start(f32[32,32,128]{2,1,0:T(8,128)S(1)} %get-tuple-element.67.refs_8_), channel_id=1, source_target_pairs={{4,6},{5,7},{12,14},{13,15},{20,22},{21,23},{28,30},{29,31}} | collective-permute-start | bytes 1572872 | tf_op jit(solution)/shard_map/ppermute | solution.py:556
  81.5 4.7 %collective-permute-start.7 = (f32[2,8,24,128]{3,2,1,0:T(8,128)S(1)}, f32[2,8,24,128]{3,2,1,0:T(8,128)S(1)}, u32[]{:S(2)}, u32[]{:S(2)}) collective-permute-start(f32[2,8,24,128]{3,2,1,0:T(8,128)S(1)} %get-tuple-element.50), channel_id=1, source_target_pairs={{0,2},{2,0},{4,6},{6,4},{1,3},{3,1},{5,7},{7,5},{8,10},{10,8},{12,... | collective-permute-start | bytes 589832 | tf_op jit(solution)/shard_map/ppermute | solution.py:376
  81.6 28.1 %collective-permute-start.21 = (f32[32,32,128]{2,1,0:T(8,128)S(1)}, f32[32,32,128]{2,1,0:T(8,128)S(1)}, u32[]{:S(2)}, u32[]{:S(2)}) collective-permute-start(f32[32,32,128]{2,1,0:T(8,128)S(1)} %get-tuple-element.67.refs_8_), channel_id=1, source_target_pairs={{2,6},{3,7},{10,14},{11,15},{18,22},{19,23},{26,30},{27,31}} | collective-permute-start | bytes 1572872 | tf_op jit(solution)/shard_map/ppermute | solution.py:556
  82.3 27.5 %collective-permute-start.22 = (f32[32,32,128]{2,1,0:T(8,128)S(1)}, f32[32,32,128]{2,1,0:T(8,128)S(1)}, u32[]{:S(2)}, u32[]{:S(2)}) collective-permute-start(f32[32,32,128]{2,1,0:T(8,128)S(1)} %get-tuple-element.67.refs_8_), channel_id=1, source_target_pairs={{0,6},{1,7},{8,14},{9,15},{16,22},{17,23},{24,30},{25,31}} | collective-permute-start | bytes 1572872 | tf_op jit(solution)/shard_map/ppermute | solution.py:556
  86.2 16.5 %collective-permute-start.8 = (f32[2,8,24,128]{3,2,1,0:T(8,128)S(1)}, f32[2,8,24,128]{3,2,1,0:T(8,128)S(1)}, u32[]{:S(2)}, u32[]{:S(2)}) collective-permute-start(f32[2,8,24,128]{3,2,1,0:T(8,128)S(1)} %get-tuple-element.51), channel_id=1, source_target_pairs={{0,4},{2,6},{4,0},{6,2},{1,5},{3,7},{5,1},{7,3},{8,12},{10,14},{12... | collective-permute-start | bytes 589832 | tf_op jit(solution)/shard_map/ppermute | solution.py:376
  86.3 18.7 %collective-permute-start.9 = (f32[2,8,24,128]{3,2,1,0:T(8,128)S(1)}, f32[2,8,24,128]{3,2,1,0:T(8,128)S(1)}, u32[]{:S(2)}, u32[]{:S(2)}) collective-permute-start(f32[2,8,24,128]{3,2,1,0:T(8,128)S(1)} %get-tuple-element.52), channel_id=1, source_target_pairs={{0,6},{2,4},{4,2},{6,0},{1,7},{3,5},{5,3},{7,1},{8,14},{10,12},{12... | collective-permute-start | bytes 589832 | tf_op jit(solution)/shard_map/ppermute | solution.py:376
  102.7 11.0 %collective-permute-start.16 = (f32[32,32,128]{2,1,0:T(8,128)S(1)}, f32[32,32,128]{2,1,0:T(8,128)S(1)}, u32[]{:S(2)}, u32[]{:S(2)}) collective-permute-start(f32[32,32,128]{2,1,0:T(8,128)S(1)} %get-tuple-element.62), channel_id=1, source_target_pairs={{0,2},{2,0},{6,4},{1,3},{3,1},{7,5},{8,10},{10,8},{14,12},{9,11},{... | collective-permute-start | bytes 1572872 | tf_op jit(solution)/shard_map/ppermute | solution.py:541
  105.0 16.7 %collective-permute-start.17 = (f32[32,32,128]{2,1,0:T(8,128)S(1)}, f32[32,32,128]{2,1,0:T(8,128)S(1)}, u32[]{:S(2)}, u32[]{:S(2)}) collective-permute-start(f32[32,32,128]{2,1,0:T(8,128)S(1)} %get-tuple-element.63), channel_id=1, source_target_pairs={{0,4},{4,0},{6,2},{1,5},{5,1},{7,3},{8,12},{12,8},{14,10},{9,13},{... | collective-permute-start | bytes 1572872 | tf_op jit(solution)/shard_map/ppermute | solution.py:541
  108.4 23.1 %collective-permute-start.18 = (f32[32,32,128]{2,1,0:T(8,128)S(1)}, f32[32,32,128]{2,1,0:T(8,128)S(1)}, u32[]{:S(2)}, u32[]{:S(2)}) collective-permute-start(f32[32,32,128]{2,1,0:T(8,128)S(1)} %get-tuple-element.64), channel_id=1, source_target_pairs={{2,4},{4,2},{6,0},{3,5},{5,3},{7,1},{10,12},{12,10},{14,8},{11,13}... | collective-permute-start | bytes 1572872 | tf_op jit(solution)/shard_map/ppermute | solution.py:541
  109.8 25.2 %collective-permute-start.10 = (f32[4,8,24,128]{3,2,1,0:T(8,128)S(1)}, f32[4,8,24,128]{3,2,1,0:T(8,128)S(1)}, u32[]{:S(2)}, u32[]{:S(2)}) collective-permute-start(f32[4,8,24,128]{3,2,1,0:T(8,128)S(1)} %get-tuple-element.53), channel_id=1, source_target_pairs={{0,8},{8,16},{16,24},{24,0},{1,9},{9,17},{17,25},{25,1},{2,10},{10... | collective-permute-start | bytes 1179656 | tf_op jit(solution)/shard_map/ppermute | solution.py:382
  109.8 25.1 %collective-permute-start.11 = (f32[4,8,24,128]{3,2,1,0:T(8,128)S(1)}, f32[4,8,24,128]{3,2,1,0:T(8,128)S(1)}, u32[]{:S(2)}, u32[]{:S(2)}) collective-permute-start(f32[4,8,24,128]{3,2,1,0:T(8,128)S(1)} %get-tuple-element.54), channel_id=1, source_target_pairs={{0,24},{8,0},{16,8},{24,16},{1,25},{9,1},{17,9},{25,17},{2,26},{10... | collective-permute-start | bytes 1179656 | tf_op jit(solution)/shard_map/ppermute | solution.py:382
  (6 other events, 44.1 us)

commit v2 on v1

v2 whole, which is shorter than its diff:
```python
import functools
import jax
import numpy as np
import jax.numpy as jnp
from jax import lax
from jax.experimental import pallas as pl
from jax.experimental.pallas import tpu as pltpu
from jax.sharding import PartitionSpec as P


F32 = jnp.float32
BF16 = jnp.bfloat16
SUB = 8


VM = pl.BlockSpec(memory_space=pltpu.VMEM)
SM = pl.BlockSpec(memory_space=pltpu.SMEM)


def cut(x):
    hi = x.astype(BF16)
    return hi, (x - hi.astype(F32)).astype(BF16)


def mm(a, b):
    return jnp.dot(a, b, preferred_element_type=F32)


def mmt(a, b):
    return lax.dot_general(a, b, (((1,), (1,)), ((), ())), preferred_element_type=F32)


def const_times(wh, wl, x):
    n = x.shape[1]
    xh, xl = cut(x)
    if n > 128:
        return mm(wh, xh) + mm(wh, xl) + mm(wl, xh)
    both = mm(wh, jnp.concatenate([xh, xl], axis=1))
    return both[:, :n] + both[:, n:] + mm(wl, xh)


def np_cosine(order, mode, node):
    mode = np.asarray(mode, np.float32)
    node = np.asarray(node, np.float32)
    scaling = np.where(mode == 0, np.sqrt(np.float32(1.0 / order)), np.sqrt(np.float32(2.0 / order)))
    angle = np.float32(np.pi) * mode * (node + np.float32(0.5)) / np.float32(order)
    return (scaling * np.cos(angle.astype(np.float64))).astype(np.float32)


def np_halves(w):
    hi = w.astype(BF16)
    return hi, (w - hi.astype(np.float32)).astype(BF16)


def np_modes(n):
    return np.concatenate([np.arange(0, n, 2), np.arange(1, n, 2)])


def np_bar(n, back):
    a = np_modes(n)
    base = np_cosine(n, a[:, None], np.arange(n)[None])
    edge = np_cosine(n, a, np.zeros(n))[:, None]
    w = (base * edge).T if back else base / edge
    return np_halves(np.kron(w, np.eye(SUB, dtype=np.float32)))


def np_second(hy):
    ny = 2 * hy
    pack = 256 // ny
    tiles = hy // SUB
    line = np.arange(hy)
    modes = tiles * (line % SUB) + line // SUB
    eye = np.eye(pack, dtype=np.float32)
    there, back = [], []
    for yc in range(2):
        sides = (yc, 1 - yc)
        blocks = [[np_cosine(ny, (m * hy + modes)[:, None], (n * hy + line)[None]) for n in sides] for m in sides]
        there.append(np.block([[np.kron(eye, b) for b in row] for row in blocks]))
        back.append(np.concatenate([np.kron(eye, row[0].T) for row in blocks], axis=1))
    return [np.stack([np_halves(w) for w in ws]) for ws in map(np.stack, (there, back))]


def tree(parts):
    while len(parts) > 1:
        parts = [a + b for a, b in zip(parts[::2], parts[1::2])] + (
            [parts[-1]] if len(parts) % 2 else []
        )
    return parts[0]


def split_kernel(nt, q_ref, amp_ref, *refs):
    ins, outs = refs[:nt], refs[nt:]
    steps = amp_ref.shape[0]
    rows = outs[0].shape[0] - steps
    cq = outs[0].shape[1]
    for d in range(nt):
        outs[d][0:rows, :] = ins[d][...].reshape(rows, cq)
        for k in range(steps):
            outs[d][rows + k : rows + k + 1, :] = jnp.full((1, cq), amp_ref[k], F32)


def forward_block(x, c_ref, kxh_ref, kxl_ref):
    nx, _, nz = x.shape
    cq = c_ref.shape[1]
    xh, xl = cut(x.reshape(nx * SUB, nz))
    both = mmt(xh, c_ref[...].reshape(2 * cq, nz))
    z = both[:, :cq] + both[:, cq:] + mmt(xl, c_ref[0])
    return const_times(kxh_ref[...], kxl_ref[...], z).reshape(nx, SUB, cq)


def forward_first_kernel(q_ref, sy_ref, x_hbm, c_hbm, kxh_hbm, kxl_hbm, out_ref, x_s, c_s, kxh_s, kxl_s, sem):
    tiles, nx, _, _ = x_s.shape
    hy = tiles * SUB
    cq = out_ref.shape[2]
    copies = [
        pltpu.make_async_copy(c_hbm.at[q_ref[0]], c_s, sem.at[0]),
        pltpu.make_async_copy(x_hbm.at[:, 0:SUB, :], x_s.at[0], sem.at[3]),
        pltpu.make_async_copy(kxh_hbm, kxh_s, sem.at[1]),
        pltpu.make_async_copy(kxl_hbm, kxl_s, sem.at[2]),
    ]
    copies += [
        pltpu.make_async_copy(x_hbm.at[:, t * SUB : (t + 1) * SUB, :], x_s.at[t], sem.at[3 + t])
        for t in range(1, tiles)
    ]
    for copy in copies:
        copy.start()
    for r in range(hy):
        b = tiles * (r % SUB) + r // SUB
        out_ref[nx, r : r + 1, :] = jnp.full((1, cq), sy_ref[b], F32)
    for copy in copies[:4]:
        copy.wait()
    for t in range(tiles):
        if t > 0:
            copies[3 + t].wait()
        out_ref[0:nx, t * SUB : (t + 1) * SUB, :] = forward_block(x_s[t], c_s, kxh_s, kxl_s)


def forward_kernel(q_ref, x_ref, c_ref, kxh_ref, kxl_ref, out_ref):
    tiles = x_ref.shape[1] // SUB
    for t in range(tiles):
        at = slice(t * SUB, (t + 1) * SUB)
        out_ref[:, at, :] = forward_block(x_ref[:, at, :], c_ref.at[q_ref[0]], kxh_ref, kxl_ref)


def factor_into(f_ref, sx_ref, diff_ref, sy, sz):
    for i, a in enumerate(np_modes(f_ref.shape[0])):
        rate = (sx_ref[int(a)] + sy) + sz
        f_ref[i] = 1.0 / (1.0 + diff_ref[0] * rate)


def order_kernel(nt, q_ref, faces_ref, sx_ref, sy_ref, diff_ref, open_ref, owner_ref, sz_ref, n1_ref, *refs):
    ins, (u_ref, amp_ref, tab_ref, fo_ref, ft_ref), outs = refs[:nt], refs[nt : nt + 5], refs[nt + 5 :]
    steps = amp_ref.shape[1]
    rows = ins[0].shape[0] - steps
    nx, hy, cq = fo_ref.shape
    tiles = hy // SUB
    for d in range(nt):
        w = jnp.bitwise_xor(q_ref[0], d)
        u_ref[w] = ins[d][0:rows, :].reshape(u_ref.shape[1:])
        amp_ref[w] = ins[d][rows:, :]
    w = 0
    for out in outs:
        out[...] = u_ref[w : w + out.shape[0]]
        w += out.shape[0]
    for face in range(2):
        i = faces_ref[face]
        for g in range(hy // tiles):
            closed = False
            for j in range(tiles):
                b = tiles * g + j
                r = face * hy + j * SUB + g
                tab_ref[r : r + 1, :] = jnp.full((1, cq), owner_ref[i, b], jnp.int32)
                closed = jnp.logical_or(closed, open_ref[i, b] == 0)
                if j < tiles - 1:
                    r = 2 * hy + (face * (tiles - 1) + j) * SUB + g
                    tab_ref[r : r + 1, :] = jnp.full((1, cq), closed.astype(jnp.int32), jnp.int32)
    sz = sz_ref[pl.ds(q_ref[0], 1), :]
    for r in range(hy):
        b = tiles * (r % SUB) + r // SUB
        fo_ref[0, r : r + 1, :] = jnp.full((1, cq), sy_ref[b], F32)
    factor_into(fo_ref, sx_ref, diff_ref, fo_ref[0], sz)
    factor_into(ft_ref, sx_ref, diff_ref, n1_ref[nx], sz)


def closed_rows(tab_ref, face, tiles, hy):
    base = 2 * hy + face * (tiles - 1) * SUB
    return [tab_ref[base + i * SUB : base + (i + 1) * SUB, :] > 0 for i in range(tiles - 1)]


def own_kernel(dims, q_ref, yc_ref, p0_ref, p1_ref, p2_ref, *refs):
    nt, steps, nx, hy, cq = dims
    n0, s0, n1, s1, u_s, amp_s, tab_ref, f_s, ky_ref = refs[:9]
    hands, (clos_ref, mo_ref, so_ref) = refs[9 : 9 + nt], refs[9 + nt : 12 + nt]
    m_s, s_s, vd = refs[12 + nt :]
    tiles = hy // SUB
    pack = ky_ref.shape[2] // (2 * hy)
    half = pack * hy
    yc = yc_ref[0]

    def ytrans(ag, _):
        at = pl.ds(ag * pack, pack)
        cols = [
            jnp.concatenate([here[at].reshape(half, cq), there[at].reshape(half, cq)], axis=0)
            for here, there in ((n0, n1), (s0, s1))
        ]
        res = const_times(ky_ref[yc, 0], ky_ref[yc, 1], jnp.concatenate(cols, axis=1))
        for f, own, oth in ((0, m_s, mo_ref), (1, s_s, so_ref)):
            part = res[:, f * cq : (f + 1) * cq]
            own[at] = part[:half].reshape(pack, hy, cq)
            oth[at] = part[half:].reshape(pack, hy, cq)
        return 0

    lax.fori_loop(0, nx // pack, ytrans, 0)
    ha = nx // 2
    chunk = min(SUB, ha)
    order = np_modes(nx)
    edge = np_cosine(nx, order, np.zeros(nx)).astype(np.float64)
    slope = np_cosine(nx, order, np.ones(nx)).astype(np.float64) - edge
    for j in range(tiles):
        rows = slice(j * SUB, (j + 1) * SUB)
        for par in range(2):
            for first in range(0, ha, chunk):
                modes = [par * ha + first + i for i in range(chunk)]
                s = [s_s[a, rows, :] for a in modes]
                f = [f_s[a, rows, :] for a in modes]
                wv = [float(np.float32(edge[a] * edge[a])) for a in modes]
                wd = [float(np.float32(edge[a] * slope[a])) for a in modes]

                def window(w, cur, j=j, par=par, first=first, rows=rows, modes=modes, s=s, f=f, wv=wv, wd=wd):
                    cur = list(cur)
                    for k in range(steps):
                        r0 = u_s[w, 0, k, pl.ds(j, SUB, stride=tiles), :]
                        r1 = u_s[w, 1, k, pl.ds(j, SUB, stride=tiles), :]
                        u = r0 + r1 if par == 0 else r0 - r1
                        amp = amp_s[w, k : k + 1, :]
                        cur = [(x + (amp * y + u)) * z for x, y, z in zip(cur, s, f)]
                        m = w * steps + k
                        v = tree([x * y for x, y in zip(cur, wv)])
                        d = tree([x * y for x, y in zip(cur, wd)])
                        if first:
                            v = v + vd[par, 0, m, j]
                            d = d + vd[par, 1, m, j]
                        vd[par, 0, m, j] = v
                        vd[par, 1, m, j] = d
                    for a, x in zip(modes, cur):
                        clos_ref[w, a, rows, :] = x
                    return tuple(cur)

                lax.fori_loop(0, nt, window, tuple(m_s[a, rows, :] for a in modes))

    params = (p0_ref[0], p1_ref[0], p2_ref[0])
    for slot in range(nt):
        w = jnp.bitwise_xor(q_ref[0], slot)

        def combine(k, _, slot=slot, w=w):
            m = w * steps + k
            left, right = [], []
            for j in range(tiles):
                ve, vo = vd[0, 0, m, j], vd[1, 0, m, j]
                de, do = vd[0, 1, m, j], vd[1, 1, m, j]
                p = [
                    jnp.where(
                        tab_ref[i * hy + j * SUB : i * hy + (j + 1) * SUB, :] == 0, params[i], params[i + 1]
                    )
                    for i in range(2)
                ]
                left.append((de + do) + p[0] * (ve + vo))
                right.append(p[1] * (ve - vo) + (de - do))
            for face, line in enumerate((left, right)):
                for i, le in enumerate(closed_rows(tab_ref, face, tiles, hy)):
                    hands[slot][face, k, i * SUB : (i + 1) * SUB, :] = jnp.where(le, line[i + 1], line[i])
            return 0

        lax.fori_loop(0, steps, combine, 0)


def other_kernel(dims, first, count, prior, q_ref, yc_ref, m_ref, s_ref, f_ref, u_s, amp_ref, clos_ref, ki_ref, kxh_ref, kxl_ref, *refs):
    nt, steps, nx, hy, cq = dims
    refs = refs[prior:]
    last = first + count == nt
    outs = refs[: 1 if last else nt]
    st_ref, cl, t_s, x_s = refs[len(outs) :]
    tiles = hy // SUB
    ha = nx // 2
    for j in range(tiles):
        rows = slice(j * SUB, (j + 1) * SUB)
        for par in range(2):
            modes = [par * ha + i for i in range(ha)]
            s = [s_ref[a, rows, :] for a in modes]
            f = [f_ref[a, rows, :] for a in modes]

            def window(w, cur, j=j, par=par, rows=rows, modes=modes, s=s, f=f):
                cur = list(cur)
                for k in range(steps):
                    r0 = u_s[w, 0, k, pl.ds(j, SUB, stride=tiles), :]
                    r1 = u_s[w, 1, k, pl.ds(j, SUB, stride=tiles), :]
                    u = r0 + r1 if par == 0 else r0 - r1
                    amp = amp_ref[w + first, k : k + 1, :]
                    cur = [(x + (amp * y + u)) * z for x, y, z in zip(cur, s, f)]
                for a, x in zip(modes, cur):
                    cl[w, a, rows, :] = x
                return tuple(cur)

            end = lax.fori_loop(0, count, window, tuple(m_ref[a, rows, :] for a in modes))
            for a, x in zip(modes, end):
                st_ref[a, rows, :] = x
    pack = ki_ref.shape[2] // hy
    half = pack * hy
    width = count * cq
    yc = yc_ref[0]

    def yback(ag, _):
        at = pl.ds(ag * pack, pack)
        cols = [
            jnp.concatenate([clos_ref[first + w, at].reshape(half, cq), cl[w, at].reshape(half, cq)], axis=0)
            for w in range(count)
        ]
        res = const_times(ki_ref[yc, 0], ki_ref[yc, 1], jnp.concatenate(cols, axis=1))
        t_s[at] = res.reshape(pack, hy, width)
        return 0

    lax.fori_loop(0, nx // pack, yback, 0)
    for yb in range(tiles):
        at = slice(yb * SUB, (yb + 1) * SUB)
        res = const_times(kxh_ref[...], kxl_ref[...], t_s[:, at, :].reshape(nx * SUB, width))
        res = res.reshape(nx, SUB, width)
        for w in range(count):
            (outs[0] if last else x_s.at[w])[:, at, :] = res[:, :, w * cq : (w + 1) * cq]
    if not last:
        for w in range(count):
            for d in range(nt):

                @pl.when(jnp.bitwise_xor(q_ref[0], d) == first + w)
                def _(w=w, d=d):
                    outs[d][...] = x_s[w]


def final_kernel(nt, q_ref, *refs):
    ws, most, late = refs[:nt], refs[nt : 2 * nt], refs[2 * nt : 3 * nt]
    out_ref, wh, wl = refs[3 * nt :]
    xb, hy, nz = out_ref.shape[1:]
    cq = nz // nt

    @pl.when(pl.program_id(0) == 0)
    def _():
        for d in range(nt):
            wh[d * cq : (d + 1) * cq, :] = ws[d][0]
            wl[d * cq : (d + 1) * cq, :] = ws[d][1]

    is_last = q_ref[0] == nt - 1
    ins = [jnp.where(is_last, b[...], a[...]) for a, b in zip(most, late)]
    xh, xl = cut(jnp.concatenate([x.reshape(xb * hy, cq) for x in ins], axis=1))
    res = mm(xh, wh[...]) + mm(xh, wl[...]) + mm(xl, wh[...])
    out_ref[0] = res.reshape(xb, hy, nz)


def merge_kernel(nt, q_ref, *refs):
    ins, outs = refs[:nt], refs[nt:]
    for d in range(nt):
        for face in range(2):
            outs[face][jnp.bitwise_xor(q_ref[0], d)] = ins[d][face]


def spread_kernel(nt, steps, tab_ref, left_ref, right_ref, out_ref, line):
    hy = out_ref.shape[3]
    cq = out_ref.shape[4] // nt
    tiles = hy // SUB
    zero = jnp.zeros((SUB, cq), F32)
    for face, ref in enumerate((left_ref, right_ref)):
        le = closed_rows(tab_ref, face, tiles, hy)
        for c in range(nt):

            def step(k, _, face=face, c=c, ref=ref, le=le):
                r = [ref[c, k, i * SUB : (i + 1) * SUB, :] for i in range(tiles - 1)]
                for j in range(tiles):
                    if j == 0:
                        v = jnp.where(le[0], zero, r[0])
                    elif j < tiles - 1:
                        v = jnp.where(le[j], jnp.where(le[j - 1], r[j - 1], zero), r[j])
                    else:
                        v = jnp.where(le[j - 1], r[j - 1], zero)
                    line[face, k, pl.ds(j, SUB, stride=tiles), :] = v
                out_ref[0, face, k, :, c * cq : (c + 1) * cq] = line[face, k]
                return 0

            lax.fori_loop(0, steps, step, 0)


def sds(*shape):
    return jax.ShapeDtypeStruct(shape, F32)


def cost(flops, nbytes):
    return pl.CostEstimate(flops=int(flops), bytes_accessed=int(nbytes), transcendentals=0)


def grant(mib):
    return pltpu.CompilerParams(vmem_limit_bytes=mib << 20)


def local(
    initial_state,
    heat_source,
    source_amplitude,
    diffusivity,
    robin_param,
    spectrum_x,
    spectrum_y,
    spectrum_z,
    robin_in,
    open_flag,
    owner_side,
):
    nx, hy, nz = initial_state.shape
    nt = lax.axis_size("tm")
    ncores = lax.axis_size("cores")
    assert ncores == 2 and nt & (nt - 1) == 0 and nt >= 2
    cq = nz // nt
    steps = source_amplitude.shape[0]
    tiles = hy // SUB
    assert tiles == 4 and nx % 4 == 0
    q = lax.axis_index("tm")
    yc = lax.axis_index("cores")
    space = lax.axis_size("space")
    me = lax.axis_index("space")
    left_index = (me + space - 1) % space
    qv = jnp.reshape(q, (1,)).astype(jnp.int32)
    dims = (nt, steps, nx, hy, cq)

    def xor_permute(x, d):
        return lax.ppermute(x, "tm", [(i, i ^ d) for i in range(nt)])

    def swap(x):
        return lax.ppermute(x, "cores", [(0, 1), (1, 0)])

    def along(x, by):
        return lax.ppermute(x, "space", [(i, (i + by) % space) for i in range(space)])

    base = np.stack(np_halves(np_cosine(nz, np.arange(nz)[:, None], np.arange(nz)[None])))
    base = jnp.asarray(base.reshape(2, nt, cq, nz).swapaxes(0, 1))
    kxh, kxl = (jnp.asarray(w) for w in np_bar(nx, False))
    kxih, kxil = (jnp.asarray(w) for w in np_bar(nx, True))
    ky, ki = (jnp.asarray(w) for w in np_second(hy))
    HB = pl.BlockSpec(memory_space=pltpu.HBM)
    n0 = pl.pallas_call(
        forward_first_kernel,
        out_shape=sds(nx + 1, hy, cq),
        in_specs=[SM, SM] + [HB] * 4,
        out_specs=VM,
        scratch_shapes=[
            pltpu.VMEM((tiles, nx, SUB, nz), F32),
            pltpu.VMEM((2, cq, nz), BF16),
            pltpu.VMEM((nx * SUB, nx * SUB), BF16),
            pltpu.VMEM((nx * SUB, nx * SUB), BF16),
            pltpu.SemaphoreType.DMA((3 + tiles,)),
        ],
        compiler_params=grant(8),
        cost_estimate=cost(1e9, 3e6),
        name="forward0",
    )(qv, spectrum_y, initial_state, base, kxh, kxl)
    n1 = swap(n0)

    rows = 2 * steps * hy
    block = (None, 2, steps, hy, cq)
    cutting = pl.pallas_call(
        functools.partial(split_kernel, nt),
        out_shape=[sds(rows + steps, cq)] * nt,
        grid_spec=pltpu.PrefetchScalarGridSpec(
            num_scalar_prefetch=1,
            grid=(1,),
            in_specs=[SM]
            + [
                pl.BlockSpec(block, lambda i, q, d=d: (0, 0, 0, 0, jnp.bitwise_xor(q[0], d)))
                for d in range(nt)
            ],
            out_specs=[pl.BlockSpec((rows + steps, cq), lambda i, q: (0, 0))] * nt,
        ),
        compiler_params=grant(8),
        cost_estimate=cost(0, 8 * nt * rows * cq),
        name="split",
    )
    dealt = list(cutting(qv, source_amplitude, *([robin_in] * nt)))
    for d in range(1, nt):
        dealt[d] = xor_permute(dealt[d], d)

    s0 = pl.pallas_call(
        forward_kernel,
        out_shape=sds(nx, hy, cq),
        in_specs=[SM] + [VM] * 4,
        out_specs=VM,
        compiler_params=grant(10),
        cost_estimate=cost(1e9, 3e6),
        name="forward1",
    )(qv, heat_source, base, kxh, kxl)
    s1 = swap(s0)
    right_param = along(robin_param, -1)
    left_param = along(robin_param, 1)

    faces = jnp.stack([left_index, me]).astype(jnp.int32)
    ycv = jnp.reshape(yc, (1,)).astype(jnp.int32)
    counts = [nt - 2] + [1, 1]
    counts = [c for c in counts if c > 0]
    table = jax.ShapeDtypeStruct((2 * hy + 2 * (tiles - 1) * SUB, cq), jnp.int32)
    u_own, amps, tab, f_own, f_there, *windows = pl.pallas_call(
        functools.partial(order_kernel, nt),
        out_shape=[sds(nt, 2, steps, hy, cq), sds(nt, steps, cq), table]
        + [sds(nx, hy, cq)] * 2
        + [sds(c, 2, steps, hy, cq) for c in counts],
        in_specs=[SM] * 7 + [VM] * (2 + nt),
        out_specs=[VM] * (5 + len(counts)),
        compiler_params=grant(12),
        cost_estimate=cost(0, 3e6),
        name="order",
    )(
        qv, faces, spectrum_x, spectrum_y, diffusivity, open_flag, owner_side,
        spectrum_z.reshape(nt, cq), n1, *dealt,
    )
    there = []
    for u in windows:
        there.append(swap(u))

    short = sds(2, steps, (tiles - 1) * SUB, cq)
    *hands, clos, m_there, s_there = pl.pallas_call(
        functools.partial(own_kernel, dims),
        out_shape=[short] * nt + [sds(nt, nx, hy, cq), sds(nx, hy, cq), sds(nx, hy, cq)],
        in_specs=[SM] * 5 + [VM] * 9,
        out_specs=[VM] * (nt + 3),
        scratch_shapes=[pltpu.VMEM((nx, hy, cq), F32)] * 2
        + [pltpu.VMEM((2, 2, nt * steps, tiles, SUB, cq), F32)],
        compiler_params=grant(18),
        cost_estimate=cost(4e9, 8e6),
        name="own",
    )(qv, ycv, left_param, robin_param, right_param, n0, s0, n1, s1, u_own, amps, tab, f_own, ky)
    for d in range(1, nt):
        hands[d] = xor_permute(hands[d], d)

    state, most, first = m_there, [], 0
    final = nt - 1
    for i, count in enumerate(counts):
        last = first + count == nt
        nout = 1 if last else nt
        operands = (
            qv, ycv, state, s_there, f_there, there[i], amps, clos, ki, kxih, kxil, *([] if last else most),
        )
        prior = 0 if last else len(most)
        *outs, state = pl.pallas_call(
            functools.partial(other_kernel, dims, first, count, prior),
            out_shape=[sds(nx, hy, cq)] * (nout + 1),
            in_specs=[SM] * 2 + [VM] * (9 + prior),
            out_specs=[VM] * (nout + 1),
            scratch_shapes=[
                pltpu.VMEM((count, nx, hy, cq), F32),
                pltpu.VMEM((nx, hy, count * cq), F32),
                pltpu.VMEM((count, nx, hy, cq), F32),
            ],
            input_output_aliases={11 + d: d for d in range(prior)},
            compiler_params=grant(18),
            cost_estimate=cost(1.5e9 * count, 2e6 * count),
        )(*operands)
        first += count
        if not last:
            most = list(outs)
            continue
        late = list(outs)
    for d in range(1, nt):
        most[d] = lax.ppermute(most[d], "tm", [(i, i ^ d) for i in range(nt) if i ^ d != final])
    left, right = pl.pallas_call(
        functools.partial(merge_kernel, nt),
        out_shape=[sds(nt, steps, (tiles - 1) * SUB, cq)] * 2,
        in_specs=[SM] + [VM] * nt,
        out_specs=[VM] * 2,
        compiler_params=grant(8),
        cost_estimate=cost(0, 2e6),
        name="merge",
    )(qv, *hands)
    from_right = along(left, -1)
    from_left = along(right, 1)
    for d in range(1, nt):
        late.append(lax.ppermute(late[0], "tm", [(final ^ d, final)]))

    xb = SUB
    window_end = pl.pallas_call(
        functools.partial(final_kernel, nt),
        out_shape=sds(1, nx, hy, nz),
        grid_spec=pltpu.PrefetchScalarGridSpec(
            num_scalar_prefetch=1,
            grid=(nx // xb,),
            in_specs=[
                pl.BlockSpec((None, 2, cq, nz), lambda i, q, d=d: (jnp.bitwise_xor(q[0], d), 0, 0, 0))
                for d in range(nt)
            ]
            + [pl.BlockSpec((xb, hy, cq), lambda i, q: (i, 0, 0))] * (2 * nt),
            out_specs=pl.BlockSpec((1, xb, hy, nz), lambda i, q: (0, i, 0, 0)),
            scratch_shapes=[pltpu.VMEM((nz, nz), BF16)] * 2,
        ),
        compiler_params=grant(16),
        cost_estimate=cost(2e9, 6e6),
        name="final",
    )(qv, *([base] * nt), *most, *late)

    robin_out = pl.pallas_call(
        functools.partial(spread_kernel, nt, steps),
        out_shape=sds(1, 2, steps, hy, nz),
        in_specs=[VM] * 3,
        out_specs=VM,
        scratch_shapes=[pltpu.VMEM((2, steps, hy, cq), F32)],
        compiler_params=grant(8),
        cost_estimate=cost(0, 2e6),
        name="spread",
    )(tab, from_left, from_right)
    return robin_out, window_end


def solution(mesh):
    placed = (
        P("space", "cores", None),
        P("space", "cores", None),
        P("tm"),
        P("space"),
        P("space"),
        P(),
        P("cores"),
        P(),
        P("space", None, "tm", "cores", None),
        P(None, "cores"),
        P(None, "cores"),
    )

    return jax.shard_map(
        local,
        mesh=mesh,
        in_specs=placed,
        out_specs=(P("space", None, "tm", "cores", None), P("tm", "space", "cores", None)),
        check_vma=False,
    )
```

time: 137 us -> 122 us (0.89)
  the two profiles are of different devices: /device:TPU:0 before, /device:TPU:25 now
where the time goes in v2:
time: 122 us; the launch traced here: 121 us
  waiting for transfers between devices  37.5 us (31%)
  starting transfers between devices  34.5 us (28%)
  Pallas kernels  33.4 us (27%)
  local copies, waits for them, and re-layouts  13.5 us (11%)
  between operations  2.27 us (2%)
    ppermute x3, waiting for transfers between devices, local(): lax.ppermute(most[d], 'tm', [(i, i ^ d) for i in range(nt) if i ^ d != fi...  19.8 us
    ppermute x3, starting transfers between devices, local(): lax.ppermute(most[d], 'tm', [(i, i ^ d) for i in range(nt) if i ^ d != fi...  16.2 us
    unnamed x54, local copies, waits for them, and re-layouts  13.5 us
    ppermute x6, waiting for transfers between devices, xor_permute(): return lax.ppermute(x, 'tm', [(i, i ^ d) for i in range(nt)])  11.4 us
    pallas_call x3, Pallas kernels, local(): pl.pallas_call(functools.partial(other_kernel, dims, first, count, prior)...  10.4 us
    pallas_call x1, Pallas kernels, local(): pl.pallas_call(functools.partial(own_kernel, dims), out_shape=[short] * n...  9.6 us
    ppermute x6, starting transfers between devices, xor_permute(): return lax.ppermute(x, 'tm', [(i, i ^ d) for i in range(nt)])  6.38 us
    ppermute x4, waiting for transfers between devices, along(): lax.ppermute(x, 'space', [(i, (i + by) % space) for i in range(space)])  6.33 us
  transfers between devices with their start and end apart: 21, of which 7 were waited for; matrix products, arithmetic and copies ran while one was open for 0% of the time, Pallas kernels for 22%

profile of v2, /device:TPU:25, one launch (start us, length us, event | category | flops | bytes accessed | tf_op | source)
XLA Modules:
  0.0 121.3 jit_solution(7614272687528926958)
XLA Ops:
  0.6 1.2 %copy-done = bf16[4,2,128,512]{3,2,1,0:T(8,128)(2,1)S(1)} copy-done((bf16[4,2,128,512]{3,2,1,0:T(8,128)(2,1)S(1)}, bf16[4,2,128,512]{3,2,1,0:T(8,128)(2,1)}, u32[]{:S(2)}) %copy-start) | copy-done | bytes 1048600
  1.9 1.6 %copy-done.3 = f32[32,32,512]{2,1,0:T(8,128)S(1)} copy-done((f32[32,32,512]{2,1,0:T(8,128)S(1)}, f32[32,32,512]{2,1,0:T(8,128)}, u32[]{:S(2)}) %copy-start.3) | copy-done | bytes 2097176
  5.9 3.3 %forward0.1.refs_0_ = f32[33,32,128]{2,1,0:T(8,128)S(1)} custom-call(s32[1]{0:T(128)} %bitcast.q_ref, f32[32]{0:T(128)S(1)} %copy-done.16, f32[32,32,512]{2,1,0:T(8,128)S(1)} %copy-done.3, bf16[4,2,128,512]{3,2,1,0:T(8,128)(2,1)S(1)} %copy-done, bf16[256,256]{1,0:T(8,128)(2,1)S(1)} %copy-done.5, bf16[256,256]{1,0:T(8,128)(2,1)S(1)} %copy-done.7), custom_call_target="tpu_custom_call" | custom-call | flops 1000000000 | bytes 3000000 | tf_op jit(solution)/shard_map/forward0/pallas_call | solution.py:445
  9.2 1.3 %collective-permute-start = (f32[33,32,128]{2,1,0:T(8,128)S(1)}, f32[33,32,128]{2,1,0:T(8,128)S(1)}, u32[]{:S(2)}, u32[]{:S(2)}) collective-permute-start(f32[33,32,128]{2,1,0:T(8,128)S(1)} %forward0.1.refs_0_), channel_id=1, source_target_pairs={{0,1},{1,0},{2,3},{3,2},{4,5},{5,4},{6,7},{7,6},{8,9},{9,8},{10,11... | collective-permute-start | bytes 1622024 | tf_op jit(solution)/shard_map/ppermute | solution.py:434
  10.5 1.6 %forward1.1.refs_1_ = f32[32,32,128]{2,1,0:T(8,128)S(1)} custom-call(s32[1]{0:T(128)} %bitcast.q_ref, f32[32,32,512]{2,1,0:T(8,128)S(1)} %copy-done.4, bf16[4,2,128,512]{3,2,1,0:T(8,128)(2,1)S(1)} %copy-done.1, bf16[256,256]{1,0:T(8,128)(2,1)S(1)} %copy-done.6, bf16[256,256]{1,0:T(8,128)(2,1)S(1)} %copy-done.7), custom_call_target="tpu_custom_call" | custom-call | flops 1000000000 | bytes 3000000 | tf_op jit(solution)/shard_map/forward1/pallas_call | solution.py:486
  12.5 1.5 %split.1 = (f32[520,128]{1,0:T(8,128)S(1)}, f32[520,128]{1,0:T(8,128)}, f32[520,128]{1,0:T(8,128)}, f32[520,128]{1,0:T(8,128)}) custom-call(s32[1]{0:T(128)} %bitcast.q_ref, f32[8]{0:T(128)S(1)} %copy-done.18, f32[1,2,8,32,512]{4,3,2,1,0:T(8,128)S(1)} %copy-done.2, f32[1,2,8,32,512]{4,3,2,1,0:T(8,128)S(1)} %copy-done.2, f32[1,2,8,32,512]{4,3,2,1,0:T(8,128)S(1)} %copy-done.2, ...), custom_call_target="tpu_custom_call" | custom-call | bytes 2097152 | tf_op jit(solution)/shard_map/split/pallas_call | solution.py:482
  14.0 1.2 %collective-permute-start.1 = (f32[520,128]{1,0:T(8,128)}, f32[520,128]{1,0:T(8,128)S(1)}, u32[]{:S(2)}, u32[]{:S(2)}) collective-permute-start(f32[520,128]{1,0:T(8,128)} %get-tuple-element.35), channel_id=1, source_target_pairs={{0,2},{2,0},{4,6},{6,4},{1,3},{3,1},{5,7},{7,5},{8,10},{10,8},{12,... | collective-permute-start | bytes 798728 | tf_op jit(solution)/shard_map/ppermute | solution.py:431
  15.2 1.2 collective-permute-start.2
  18.3 5.2 %collective-permute-done.2.refs_2_ = f32[520,128]{1,0:T(8,128)} collective-permute-done((f32[520,128]{1,0:T(8,128)}, f32[520,128]{1,0:T(8,128)}, u32[]{:S(2)}, u32[]{:S(2)}) %collective-permute-start.2) | collective-permute-done | bytes 266272 | tf_op jit(solution)/shard_map/ppermute | solution.py:431
  23.5 6.2 %collective-permute-done.3.refs_3_ = f32[520,128]{1,0:T(8,128)} collective-permute-done((f32[520,128]{1,0:T(8,128)}, f32[520,128]{1,0:T(8,128)}, u32[]{:S(2)}, u32[]{:S(2)}) %collective-permute-start.3) | collective-permute-done | bytes 266272 | tf_op jit(solution)/shard_map/ppermute | solution.py:431
  30.7 2.1 %order.1 = (f32[4,2,8,32,128]{4,3,2,1,0:T(8,128)S(1)}, f32[4,8,128]{2,1,0:T(8,128)S(1)}, s32[112,128]{1,0:T(8,128)S(1)}, f32[32,32,128]{2,1,0:T(8,128)S(1)}, f32...) custom-call(s32[1]{0:T(128)} %bitcast.q_ref, ...), custom_call_target="tpu_custom_call" | custom-call | bytes 3000000 | tf_op jit(solution)/shard_map/order/pallas_call | solution.py:504
  32.8 1.0 copy-done.20
  36.0 1.2 %collective-permute-start.12 = (f32[2,2,8,32,128]{4,3,2,1,0:T(8,128)}, f32[2,2,8,32,128]{4,3,2,1,0:T(8,128)}, u32[]{:S(2)}, u32[]{:S(2)}) collective-permute-start(f32[2,2,8,32,128]{4,3,2,1,0:T(8,128)} %get-tuple-element.51), channel_id=1, source_target_pairs={{0,1},{1,0},{2,3},{3,2},{4,5},{5,4},{6,7},{7,6},{8,9},{9,8},{10,11... | collective-permute-start | bytes 1572872 | tf_op jit(solution)/shard_map/ppermute | solution.py:434
  37.2 1.5 %collective-permute-start.5 = (f32[1]{0:T(128)}, f32[1]{0:T(128)}, u32[]{:S(2)}, u32[]{:S(2)}) collective-permute-start(f32[1]{0:T(128)} %param.22), channel_id=1, source_target_pairs={{0,24},{8,0},{16,8},{24,16},{1,25},{9,1},{17,9},{25,17},{2,26},{10... | collective-permute-start | bytes 20 | tf_op jit(solution)/shard_map/ppermute | solution.py:437
  41.5 1.2 %copy-done.21 = f32[4,2,8,32,128]{4,3,2,1,0:T(8,128)S(1)} copy-done((f32[4,2,8,32,128]{4,3,2,1,0:T(8,128)S(1)}, f32[4,2,8,32,128]{4,3,2,1,0:T(8,128)}, u32[]{:S(2)}) %copy-start.21) | copy-done | bytes 1048600
  42.8 1.0 copy-done.23
  43.8 1.0 copy-done.26
  44.8 9.6 %own.1 = (f32[2,8,24,128]{3,2,1,0:T(8,128)S(1)}, f32[2,8,24,128]{3,2,1,0:T(8,128)S(1)}, f32[2,8,24,128]{3,2,1,0:T(8,128)S(1)}, f32[2,8,24,128]{3,2,1,0:T(8,128)S...) custom-call(s32[1]{0:T(128)} %bitcast.q_ref, s32[1]{0:T(128)} %bitcast.4.yc_ref, ...), custom_call_target="tpu_custom_call" | custom-call | flops 4000000000 | bytes 8000000 | tf_op jit(solution)/shard_map/own/pallas_call | solution.py:523
  54.4 1.8 %collective-permute-start.7 = (f32[2,8,24,128]{3,2,1,0:T(8,128)S(1)}, f32[2,8,24,128]{3,2,1,0:T(8,128)S(1)}, u32[]{:S(2)}, u32[]{:S(2)}) collective-permute-start(f32[2,8,24,128]{3,2,1,0:T(8,128)S(1)} %get-tuple-element.43), channel_id=1, source_target_pairs={{0,2},{2,0},{4,6},{6,4},{1,3},{3,1},{5,7},{7,5},{8,10},{10,8},{12,... | collective-permute-start | bytes 589832 | tf_op jit(solution)/shard_map/ppermute | solution.py:431
  56.2 1.2 %collective-permute-start.8 = (f32[2,8,24,128]{3,2,1,0:T(8,128)S(1)}, f32[2,8,24,128]{3,2,1,0:T(8,128)S(1)}, u32[]{:S(2)}, u32[]{:S(2)}) collective-permute-start(f32[2,8,24,128]{3,2,1,0:T(8,128)S(1)} %get-tuple-element.44), channel_id=1, source_target_pairs={{0,4},{2,6},{4,0},{6,2},{1,5},{3,7},{5,1},{7,3},{8,12},{10,14},{12... | collective-permute-start | bytes 589832 | tf_op jit(solution)/shard_map/ppermute | solution.py:431
  58.0 5.0 %shard_map.185 = (f32[32,32,128]{2,1,0:T(8,128)S(1)}, f32[32,32,128]{2,1,0:T(8,128)S(1)}, f32[32,32,128]{2,1,0:T(8,128)S(1)}, f32[32,32,128]{2,1,0:T(8,128)S(1)}, f32[32,32,128]{2,1,0:T(8,128)S(1)}) custom-call(s32[1]{0:T(128)} %bitcast.q_ref, s32[1]{0:T(128)} %bitcast.4.yc_ref, f32[32,32,128]{2,1,0:T(8,128)S(1)} %get-tuple-element.48.m_ref, ...), custom_call_target="tpu_custom_call" | custom-call | flops 3000000000 | bytes 4000000 | tf_op jit(solution)/shard_map/pallas_call | solution.py:546
  62.9 2.6 %shard_map.186 = (f32[32,32,128]{2,1,0:T(8,128)S(1)}, f32[32,32,128]{2,1,0:T(8,128)S(1)}, f32[32,32,128]{2,1,0:T(8,128)S(1)}, f32[32,32,128]{2,1,0:T(8,128)S(1)}, f32[32,32,128]{2,1,0:T(8,128)S(1)}) custom-call(s32[1]{0:T(128)} %bitcast.q_ref, s32[1]{0:T(128)} %bitcast.4.yc_ref, ...), custom_call_target="tpu_custom_call", output_to_operand_aliasing={{0}: (11, {}), {1}: (12, {}), {2}: (13, {}), {3}: (14, {})} | custom-call | flops 1500000000 | bytes 2000000 | tf_op jit(solution)/shard_map/pallas_call | solution.py:546
  65.6 2.8 %shard_map.187 = (f32[32,32,128]{2,1,0:T(8,128)S(1)}, f32[32,32,128]{2,1,0:T(8,128)}) custom-call(s32[1]{0:T(128)} %bitcast.q_ref, s32[1]{0:T(128)} %bitcast.4.yc_ref, f32[32,32,128]{2,1,0:T(8,128)S(1)} %get-tuple-element.63.m_ref, f32[32,32,128]{2,1,0:T(8,128)S(1)} %get-tuple-element.49.s_ref, f32[32,32,128]{2,1,0:T(8,128)S(1)} %get-tuple-element.50.f_ref, ...), custom_call_target="tpu_custom_call" | custom-call | flops 1500000000 | bytes 2000000 | tf_op jit(solution)/shard_map/pallas_call | solution.py:546
  70.7 3.7 %collective-permute-start.19 = (f32[32,32,128]{2,1,0:T(8,128)S(1)}, f32[32,32,128]{2,1,0:T(8,128)S(1)}, u32[]{:S(2)}, u32[]{:S(2)}) collective-permute-start(f32[32,32,128]{2,1,0:T(8,128)S(1)} %get-tuple-element.65.refs_8_), channel_id=1, source_target_pairs={{2,6},{3,7},{10,14},{11,15},{18,22},{19,23},{26,30},{27,31}} | collective-permute-start | bytes 1572872 | tf_op jit(solution)/shard_map/ppermute | solution.py:579
  75.1 5.2 %collective-permute-done.10.left_ref = f32[4,8,24,128]{3,2,1,0:T(8,128)S(1)} collective-permute-done((f32[4,8,24,128]{3,2,1,0:T(8,128)S(1)}, f32[4,8,24,128]{3,2,1,0:T(8,128)S(1)}, u32[]{:S(2)}, u32[]{:S(2)}) %collective-permute-start.10) | collective-permute-done | bytes 393248 | tf_op jit(solution)/shard_map/ppermute | solution.py:437
  80.3 10.7 %collective-permute-start.14 = (f32[32,32,128]{2,1,0:T(8,128)S(1)}, f32[32,32,128]{2,1,0:T(8,128)S(1)}, u32[]{:S(2)}, u32[]{:S(2)}) collective-permute-start(f32[32,32,128]{2,1,0:T(8,128)S(1)} %get-tuple-element.60), channel_id=1, source_target_pairs={{0,2},{2,0},{6,4},{1,3},{3,1},{7,5},{8,10},{10,8},{14,12},{9,11},{... | collective-permute-start | bytes 1572872 | tf_op jit(solution)/shard_map/ppermute | solution.py:566
  91.1 1.3 %collective-permute-start.15 = (f32[32,32,128]{2,1,0:T(8,128)S(1)}, f32[32,32,128]{2,1,0:T(8,128)S(1)}, u32[]{:S(2)}, u32[]{:S(2)}) collective-permute-start(f32[32,32,128]{2,1,0:T(8,128)S(1)} %get-tuple-element.61), channel_id=1, source_target_pairs={{0,4},{4,0},{6,2},{1,5},{5,1},{7,3},{8,12},{12,8},{14,10},{9,13},{... | collective-permute-start | bytes 1572872 | tf_op jit(solution)/shard_map/ppermute | solution.py:566
  92.4 4.2 %collective-permute-start.16 = (f32[32,32,128]{2,1,0:T(8,128)S(1)}, f32[32,32,128]{2,1,0:T(8,128)S(1)}, u32[]{:S(2)}, u32[]{:S(2)}) collective-permute-start(f32[32,32,128]{2,1,0:T(8,128)S(1)} %get-tuple-element.62), channel_id=1, source_target_pairs={{2,4},{4,2},{6,0},{3,5},{5,3},{7,1},{10,12},{12,10},{14,8},{11,13}... | collective-permute-start | bytes 1572872 | tf_op jit(solution)/shard_map/ppermute | solution.py:566
  96.6 1.5 %spread.1 = f32[1,2,8,32,512]{4,3,2,1,0:T(8,128)} custom-call(s32[112,128]{1,0:T(8,128)S(1)} %get-tuple-element.38.refs_6_.tab_ref, f32[4,8,24,128]{3,2,1,0:T(8,128)S(1)} %collective-permute-done.10.left_ref, f32[4,8,24,128]{3,2,1,0:T(8,128)S(1)} %collective-permute-done.11.right_ref), custom_call_target="tpu_custom_call" | custom-call | bytes 2000000 | tf_op jit(solution)/shard_map/spread/pallas_call | solution.py:601
  98.1 8.3 %collective-permute-done.15.refs_6_ = f32[32,32,128]{2,1,0:T(8,128)S(1)} collective-permute-done((f32[32,32,128]{2,1,0:T(8,128)S(1)}, f32[32,32,128]{2,1,0:T(8,128)S(1)}, u32[]{:S(2)}, u32[]{:S(2)}) %collective-permute-start.15) | collective-permute-done | bytes 524320 | tf_op jit(solution)/shard_map/ppermute | solution.py:566
  106.4 11.4 %collective-permute-done.16.refs_7_ = f32[32,32,128]{2,1,0:T(8,128)S(1)} collective-permute-done((f32[32,32,128]{2,1,0:T(8,128)S(1)}, f32[32,32,128]{2,1,0:T(8,128)S(1)}, u32[]{:S(2)}, u32[]{:S(2)}) %collective-permute-start.16) | collective-permute-done | bytes 524320 | tf_op jit(solution)/shard_map/ppermute | solution.py:566
  117.9 3.4 %final.1 = f32[1,32,32,512]{3,2,1,0:T(8,128)} custom-call(s32[1]{0:T(128)} %bitcast.q_ref, bf16[4,2,128,512]{3,2,1,0:T(8,128)(2,1)S(1)} %copy-done.1, bf16[4,2,128,512]{3,2,1,0:T(8,128)(2,1)S(1)} %copy-done.1, bf16[4,2,128,512]{3,2,1,0:T(8,128)(2,1)S(1)} %copy-done.1, bf16[4,2,128,512]{3,2,1,0:T(8,128)(2,1)S(1)} %copy-done.1, ...), custom_call_target="tpu_custom_call" | custom-call | flops 2000000000 | bytes 6000000 | tf_op jit(solution)/shard_map/final/pallas_call | solution.py:582
  (76 shorter events, 12.8 us)
Async XLA Ops:
  5.9 4.6 %copy-start.1 = (bf16[4,2,128,512]{3,2,1,0:T(8,128)(2,1)S(1)}, bf16[4,2,128,512]{3,2,1,0:T(8,128)(2,1)}, u32[]{:S(2)}) copy-start(bf16[4,2,128,512]{3,2,1,0:T(8,128)(2,1)} %constant.41.clone.c_hbm.c_ref.refs_0_.refs_1_.refs_2_.refs_3_) | copy-start | bytes 3145732
  5.9 4.6 %copy-start.4 = (f32[32,32,512]{2,1,0:T(8,128)S(1)}, f32[32,32,512]{2,1,0:T(8,128)}, u32[]{:S(2)}) copy-start(f32[32,32,512]{2,1,0:T(8,128)} %x_ref.1) | copy-start | bytes 6291460
  5.9 4.6 %copy-start.6 = (bf16[256,256]{1,0:T(8,128)(2,1)S(1)}, bf16[256,256]{1,0:T(8,128)(2,1)}, u32[]{:S(2)}) copy-start(bf16[256,256]{1,0:T(8,128)(2,1)} %constant.42.clone.kxh_hbm.kxh_ref) | copy-start | bytes 393220
  9.2 20.4 %collective-permute-start = (f32[33,32,128]{2,1,0:T(8,128)S(1)}, f32[33,32,128]{2,1,0:T(8,128)S(1)}, u32[]{:S(2)}, u32[]{:S(2)}) collective-permute-start(f32[33,32,128]{2,1,0:T(8,128)S(1)} %forward0.1.refs_0_), channel_id=1, source_target_pairs={{0,1},{1,0},{2,3},{3,2},{4,5},{5,4},{6,7},{7,6},{8,9},{9,8},{10,11... | collective-permute-start | bytes 1622024 | tf_op jit(solution)/shard_map/ppermute | solution.py:434
  12.1 17.5 %copy-start.13 = (s32[4,32]{1,0:T(4,128)S(1)}, s32[4,32]{1,0:T(4,128)}, u32[]{:S(2)}) copy-start(s32[4,32]{1,0:T(4,128)} %open_ref.1) | copy-start | bytes 1540
  12.1 17.5 %copy-start.14 = (s32[4,32]{1,0:T(4,128)S(1)}, s32[4,32]{1,0:T(4,128)}, u32[]{:S(2)}) copy-start(s32[4,32]{1,0:T(4,128)} %owner_ref.1) | copy-start | bytes 1540
  12.2 17.5 %copy-start.15 = (f32[512]{0:T(512)S(1)}, f32[512]{0:T(512)}, u32[]{:S(2)}) copy-start(f32[512]{0:T(512)} %param.25) | copy-start | bytes 6148
  12.2 17.5 %copy-start.17 = (f32[32]{0:T(128)S(1)}, f32[32]{0:T(128)}, u32[]{:S(2)}) copy-start(f32[32]{0:T(128)} %sy_ref.3) | copy-start | bytes 388
  12.2 17.5 %copy-start.19 = (f32[32]{0:T(128)S(1)}, f32[32]{0:T(128)}, u32[]{:S(2)}) copy-start(f32[32]{0:T(128)} %sx_ref.1) | copy-start | bytes 388
  12.2 29.3 %collective-permute-start.6 = (f32[32,32,128]{2,1,0:T(8,128)S(1)}, f32[32,32,128]{2,1,0:T(8,128)}, u32[]{:S(2)}, u32[]{:S(2)}) collective-permute-start(f32[32,32,128]{2,1,0:T(8,128)S(1)} %forward1.1.refs_1_), channel_id=1, source_target_pairs={{0,1},{1,0},{2,3},{3,2},{4,5},{5,4},{6,7},{7,6},{8,9},{9,8},{10,11... | collective-permute-start | bytes 1572872 | tf_op jit(solution)/shard_map/ppermute | solution.py:434
  14.0 3.6 %collective-permute-start.1 = (f32[520,128]{1,0:T(8,128)}, f32[520,128]{1,0:T(8,128)S(1)}, u32[]{:S(2)}, u32[]{:S(2)}) collective-permute-start(f32[520,128]{1,0:T(8,128)} %get-tuple-element.35), channel_id=1, source_target_pairs={{0,2},{2,0},{4,6},{6,4},{1,3},{3,1},{5,7},{7,5},{8,10},{10,8},{12,... | collective-permute-start | bytes 798728 | tf_op jit(solution)/shard_map/ppermute | solution.py:431
  15.2 8.3 %collective-permute-start.2 = (f32[520,128]{1,0:T(8,128)}, f32[520,128]{1,0:T(8,128)}, u32[]{:S(2)}, u32[]{:S(2)}) collective-permute-start(f32[520,128]{1,0:T(8,128)} %get-tuple-element.36), channel_id=1, source_target_pairs={{0,4},{2,6},{4,0},{6,2},{1,5},{3,7},{5,1},{7,3},{8,12},{10,14},{12... | collective-permute-start | bytes 798728 | tf_op jit(solution)/shard_map/ppermute | solution.py:431
  16.4 13.2 %collective-permute-start.3 = (f32[520,128]{1,0:T(8,128)}, f32[520,128]{1,0:T(8,128)}, u32[]{:S(2)}, u32[]{:S(2)}) collective-permute-start(f32[520,128]{1,0:T(8,128)} %get-tuple-element.37), channel_id=1, source_target_pairs={{0,6},{2,4},{4,2},{6,0},{1,7},{3,5},{5,3},{7,1},{8,14},{10,12},{12... | collective-permute-start | bytes 798728 | tf_op jit(solution)/shard_map/ppermute | solution.py:431
  36.0 21.5 %collective-permute-start.12 = (f32[2,2,8,32,128]{4,3,2,1,0:T(8,128)}, f32[2,2,8,32,128]{4,3,2,1,0:T(8,128)}, u32[]{:S(2)}, u32[]{:S(2)}) collective-permute-start(f32[2,2,8,32,128]{4,3,2,1,0:T(8,128)} %get-tuple-element.51), channel_id=1, source_target_pairs={{0,1},{1,0},{2,3},{3,2},{4,5},{5,4},{6,7},{7,6},{8,9},{9,8},{10,11... | collective-permute-start | bytes 1572872 | tf_op jit(solution)/shard_map/ppermute | solution.py:434
  37.2 3.0 %collective-permute-start.4 = (f32[1]{0:T(128)}, f32[1]{0:T(128)}, u32[]{:S(2)}, u32[]{:S(2)}) collective-permute-start(f32[1]{0:T(128)} %param.22), channel_id=1, source_target_pairs={{0,8},{8,16},{16,24},{24,0},{1,9},{9,17},{17,25},{25,1},{2,10},{10... | collective-permute-start | bytes 20 | tf_op jit(solution)/shard_map/ppermute | solution.py:437
  37.2 4.3 %collective-permute-start.5 = (f32[1]{0:T(128)}, f32[1]{0:T(128)}, u32[]{:S(2)}, u32[]{:S(2)}) collective-permute-start(f32[1]{0:T(128)} %param.22), channel_id=1, source_target_pairs={{0,24},{8,0},{16,8},{24,16},{1,25},{9,1},{17,9},{25,17},{2,26},{10... | collective-permute-start | bytes 20 | tf_op jit(solution)/shard_map/ppermute | solution.py:437
  39.4 23.6 %collective-permute-start.13 = (f32[1,2,8,32,128]{4,3,2,1,0:T(8,128)}, f32[1,2,8,32,128]{4,3,2,1,0:T(8,128)S(1)}, u32[]{:S(2)}, u32[]{:S(2)}) collective-permute-start(f32[1,2,8,32,128]{4,3,2,1,0:T(8,128)} %copy-done.25), channel_id=1, source_target_pairs={{0,1},{1,0},{2,3},{3,2},{4,5},{5,4},{6,7},{7,6},{8,9},{9,8},{10,11... | collective-permute-start | bytes 786440 | tf_op jit(solution)/shard_map/ppermute | solution.py:434
  40.2 25.4 %collective-permute-start.17 = (f32[1,2,8,32,128]{4,3,2,1,0:T(8,128)}, f32[1,2,8,32,128]{4,3,2,1,0:T(8,128)S(1)}, u32[]{:S(2)}, u32[]{:S(2)}) collective-permute-start(f32[1,2,8,32,128]{4,3,2,1,0:T(8,128)} %copy-done.24), channel_id=1, source_target_pairs={{0,1},{1,0},{2,3},{3,2},{4,5},{5,4},{6,7},{7,6},{8,9},{9,8},{10,11... | collective-permute-start | bytes 786440 | tf_op jit(solution)/shard_map/ppermute | solution.py:434
  44.8 13.1 %copy-start.10 = (bf16[2,2,128,256]{3,2,1,0:T(8,128)(2,1)S(1)}, bf16[2,2,128,256]{3,2,1,0:T(8,128)(2,1)}, u32[]{:S(2)}) copy-start(bf16[2,2,128,256]{3,2,1,0:T(8,128)(2,1)} %constant.47.clone.ki_ref) | copy-start | bytes 786436
  44.8 13.1 %copy-start.11 = (bf16[256,256]{1,0:T(8,128)(2,1)S(1)}, bf16[256,256]{1,0:T(8,128)(2,1)}, u32[]{:S(2)}) copy-start(bf16[256,256]{1,0:T(8,128)(2,1)} %constant.44.clone.kxh_ref) | copy-start | bytes 393220
  44.8 13.1 %copy-start.12 = (bf16[256,256]{1,0:T(8,128)(2,1)S(1)}, bf16[256,256]{1,0:T(8,128)(2,1)}, u32[]{:S(2)}) copy-start(bf16[256,256]{1,0:T(8,128)(2,1)} %constant.45.clone.kxl_ref) | copy-start | bytes 393220
  54.4 14.6 %collective-permute-start.7 = (f32[2,8,24,128]{3,2,1,0:T(8,128)S(1)}, f32[2,8,24,128]{3,2,1,0:T(8,128)S(1)}, u32[]{:S(2)}, u32[]{:S(2)}) collective-permute-start(f32[2,8,24,128]{3,2,1,0:T(8,128)S(1)} %get-tuple-element.43), channel_id=1, source_target_pairs={{0,2},{2,0},{4,6},{6,4},{1,3},{3,1},{5,7},{7,5},{8,10},{10,8},{12,... | collective-permute-start | bytes 589832 | tf_op jit(solution)/shard_map/ppermute | solution.py:431
  56.2 12.8 %collective-permute-start.8 = (f32[2,8,24,128]{3,2,1,0:T(8,128)S(1)}, f32[2,8,24,128]{3,2,1,0:T(8,128)S(1)}, u32[]{:S(2)}, u32[]{:S(2)}) collective-permute-start(f32[2,8,24,128]{3,2,1,0:T(8,128)S(1)} %get-tuple-element.44), channel_id=1, source_target_pairs={{0,4},{2,6},{4,0},{6,2},{1,5},{3,7},{5,1},{7,3},{8,12},{10,14},{12... | collective-permute-start | bytes 589832 | tf_op jit(solution)/shard_map/ppermute | solution.py:431
  57.5 11.6 %collective-permute-start.9 = (f32[2,8,24,128]{3,2,1,0:T(8,128)S(1)}, f32[2,8,24,128]{3,2,1,0:T(8,128)S(1)}, u32[]{:S(2)}, u32[]{:S(2)}) collective-permute-start(f32[2,8,24,128]{3,2,1,0:T(8,128)S(1)} %get-tuple-element.45), channel_id=1, source_target_pairs={{0,6},{2,4},{4,2},{6,0},{1,7},{3,5},{5,3},{7,1},{8,14},{10,12},{12... | collective-permute-start | bytes 589832 | tf_op jit(solution)/shard_map/ppermute | solution.py:431
  68.4 24.0 %collective-permute-start.18 = (f32[32,32,128]{2,1,0:T(8,128)S(1)}, f32[32,32,128]{2,1,0:T(8,128)S(1)}, u32[]{:S(2)}, u32[]{:S(2)}) collective-permute-start(f32[32,32,128]{2,1,0:T(8,128)S(1)} %get-tuple-element.65.refs_8_), channel_id=1, source_target_pairs={{4,6},{5,7},{12,14},{13,15},{20,22},{21,23},{28,30},{29,31}} | collective-permute-start | bytes 1572872 | tf_op jit(solution)/shard_map/ppermute | solution.py:579
  69.2 11.2 %collective-permute-start.10 = (f32[4,8,24,128]{3,2,1,0:T(8,128)S(1)}, f32[4,8,24,128]{3,2,1,0:T(8,128)S(1)}, u32[]{:S(2)}, u32[]{:S(2)}) collective-permute-start(f32[4,8,24,128]{3,2,1,0:T(8,128)S(1)} %get-tuple-element.46), channel_id=1, source_target_pairs={{0,8},{8,16},{16,24},{24,0},{1,9},{9,17},{17,25},{25,1},{2,10},{10... | collective-permute-start | bytes 1179656 | tf_op jit(solution)/shard_map/ppermute | solution.py:437
  69.9 21.1 %collective-permute-start.11 = (f32[4,8,24,128]{3,2,1,0:T(8,128)S(1)}, f32[4,8,24,128]{3,2,1,0:T(8,128)S(1)}, u32[]{:S(2)}, u32[]{:S(2)}) collective-permute-start(f32[4,8,24,128]{3,2,1,0:T(8,128)S(1)} %get-tuple-element.47), channel_id=1, source_target_pairs={{0,24},{8,0},{16,8},{24,16},{1,25},{9,1},{17,9},{25,17},{2,26},{10... | collective-permute-start | bytes 1179656 | tf_op jit(solution)/shard_map/ppermute | solution.py:437
  70.7 27.4 %collective-permute-start.19 = (f32[32,32,128]{2,1,0:T(8,128)S(1)}, f32[32,32,128]{2,1,0:T(8,128)S(1)}, u32[]{:S(2)}, u32[]{:S(2)}) collective-permute-start(f32[32,32,128]{2,1,0:T(8,128)S(1)} %get-tuple-element.65.refs_8_), channel_id=1, source_target_pairs={{2,6},{3,7},{10,14},{11,15},{18,22},{19,23},{26,30},{27,31}} | collective-permute-start | bytes 1572872 | tf_op jit(solution)/shard_map/ppermute | solution.py:579
  74.4 23.7 %collective-permute-start.20 = (f32[32,32,128]{2,1,0:T(8,128)S(1)}, f32[32,32,128]{2,1,0:T(8,128)S(1)}, u32[]{:S(2)}, u32[]{:S(2)}) collective-permute-start(f32[32,32,128]{2,1,0:T(8,128)S(1)} %get-tuple-element.65.refs_8_), channel_id=1, source_target_pairs={{0,6},{1,7},{8,14},{9,15},{16,22},{17,23},{24,30},{25,31}} | collective-permute-start | bytes 1572872 | tf_op jit(solution)/shard_map/ppermute | solution.py:579
  80.3 17.8 %collective-permute-start.14 = (f32[32,32,128]{2,1,0:T(8,128)S(1)}, f32[32,32,128]{2,1,0:T(8,128)S(1)}, u32[]{:S(2)}, u32[]{:S(2)}) collective-permute-start(f32[32,32,128]{2,1,0:T(8,128)S(1)} %get-tuple-element.60), channel_id=1, source_target_pairs={{0,2},{2,0},{6,4},{1,3},{3,1},{7,5},{8,10},{10,8},{14,12},{9,11},{... | collective-permute-start | bytes 1572872 | tf_op jit(solution)/shard_map/ppermute | solution.py:566
  91.1 15.4 %collective-permute-start.15 = (f32[32,32,128]{2,1,0:T(8,128)S(1)}, f32[32,32,128]{2,1,0:T(8,128)S(1)}, u32[]{:S(2)}, u32[]{:S(2)}) collective-permute-start(f32[32,32,128]{2,1,0:T(8,128)S(1)} %get-tuple-element.61), channel_id=1, source_target_pairs={{0,4},{4,0},{6,2},{1,5},{5,1},{7,3},{8,12},{12,8},{14,10},{9,13},{... | collective-permute-start | bytes 1572872 | tf_op jit(solution)/shard_map/ppermute | solution.py:566
  92.4 25.5 %collective-permute-start.16 = (f32[32,32,128]{2,1,0:T(8,128)S(1)}, f32[32,32,128]{2,1,0:T(8,128)S(1)}, u32[]{:S(2)}, u32[]{:S(2)}) collective-permute-start(f32[32,32,128]{2,1,0:T(8,128)S(1)} %get-tuple-element.62), channel_id=1, source_target_pairs={{2,4},{4,2},{6,0},{3,5},{5,3},{7,1},{10,12},{12,10},{14,8},{11,13}... | collective-permute-start | bytes 1572872 | tf_op jit(solution)/shard_map/ppermute | solution.py:566
  (16 other events, 20.0 us)

commit v3 on v2

--- a/solution.py
+++ b/solution.py
@@ -108,7 +108,10 @@
     return const_times(kxh_ref[...], kxl_ref[...], z).reshape(nx, SUB, cq)
 
 
-def forward_first_kernel(q_ref, sy_ref, x_hbm, c_hbm, kxh_hbm, kxl_hbm, out_ref, x_s, c_s, kxh_s, kxl_s, sem):
+def forward_first_kernel(
+    q_ref, yc_ref, me_ref, sy_ref, diff_ref, par_ref, x_hbm, c_hbm, kxh_hbm, kxl_hbm,
+    out_ref, diff_out, par_out, x_s, c_s, kxh_s, kxl_s, sem,
+):
     tiles, nx, _, _ = x_s.shape
     hy = tiles * SUB
     cq = out_ref.shape[2]
@@ -127,6 +130,8 @@
     for r in range(hy):
         b = tiles * (r % SUB) + r // SUB
         out_ref[nx, r : r + 1, :] = jnp.full((1, cq), sy_ref[b], F32)
+    diff_out[...] = jnp.full(diff_out.shape, diff_ref[0], F32)
+    par_out[...] = jnp.full(par_out.shape, par_ref[0], F32)
     for copy in copies[:4]:
         copy.wait()
     for t in range(tiles):
@@ -145,10 +150,10 @@
 def factor_into(f_ref, sx_ref, diff_ref, sy, sz):
     for i, a in enumerate(np_modes(f_ref.shape[0])):
         rate = (sx_ref[int(a)] + sy) + sz
-        f_ref[i] = 1.0 / (1.0 + diff_ref[0] * rate)
-
-
-def order_kernel(nt, q_ref, faces_ref, sx_ref, sy_ref, diff_ref, open_ref, owner_ref, sz_ref, n1_ref, *refs):
+        f_ref[i] = 1.0 / (1.0 + diff_ref[0:1, :] * rate)
+
+
+def order_kernel(nt, space, q_ref, me_ref, sx_ref, sy_ref, open_ref, owner_ref, diff_ref, sz_ref, n1_ref, *refs):
     ins, (u_ref, amp_ref, tab_ref, fo_ref, ft_ref), outs = refs[:nt], refs[nt : nt + 5], refs[nt + 5 :]
     steps = amp_ref.shape[1]
     rows = ins[0].shape[0] - steps
@@ -163,7 +168,7 @@
         out[...] = u_ref[w : w + out.shape[0]]
         w += out.shape[0]
     for face in range(2):
-        i = faces_ref[face]
+        i = lax.rem(me_ref[0] + space - 1, space) if face == 0 else me_ref[0]
         for g in range(hy // tiles):
             closed = False
             for j in range(tiles):
@@ -187,11 +192,11 @@
     return [tab_ref[base + i * SUB : base + (i + 1) * SUB, :] > 0 for i in range(tiles - 1)]
 
 
-def own_kernel(dims, q_ref, yc_ref, p0_ref, p1_ref, p2_ref, *refs):
+def own_kernel(dims, q_ref, yc_ref, *refs):
     nt, steps, nx, hy, cq = dims
-    n0, s0, n1, s1, u_s, amp_s, tab_ref, f_s, ky_ref = refs[:9]
-    hands, (clos_ref, mo_ref, so_ref) = refs[9 : 9 + nt], refs[9 + nt : 12 + nt]
-    m_s, s_s, vd = refs[12 + nt :]
+    params, (n0, s0, n1, s1, u_s, amp_s, tab_ref, f_s, ky_ref) = refs[:3], refs[3:12]
+    hands, (clos_ref, mo_ref, so_ref) = refs[12 : 12 + nt], refs[12 + nt : 15 + nt]
+    m_s, s_s, vd = refs[15 + nt :]
     tiles = hy // SUB
     pack = ky_ref.shape[2] // (2 * hy)
     half = pack * hy
@@ -248,7 +253,7 @@
 
                 lax.fori_loop(0, nt, window, tuple(m_s[a, rows, :] for a in modes))
 
-    params = (p0_ref[0], p1_ref[0], p2_ref[0])
+    params = [ref[...] for ref in params]
     for slot in range(nt):
         w = jnp.bitwise_xor(q_ref[0], slot)
 
@@ -277,9 +282,8 @@
 def other_kernel(dims, first, count, prior, q_ref, yc_ref, m_ref, s_ref, f_ref, u_s, amp_ref, clos_ref, ki_ref, kxh_ref, kxl_ref, *refs):
     nt, steps, nx, hy, cq = dims
     refs = refs[prior:]
-    last = first + count == nt
-    outs = refs[: 1 if last else nt]
-    st_ref, cl, t_s, x_s = refs[len(outs) :]
+    outs = refs[:nt]
+    st_ref, cl, t_s, x_s = refs[nt:]
     tiles = hy // SUB
     ha = nx // 2
     for j in range(tiles):
@@ -325,19 +329,17 @@
         res = const_times(kxh_ref[...], kxl_ref[...], t_s[:, at, :].reshape(nx * SUB, width))
         res = res.reshape(nx, SUB, width)
         for w in range(count):
-            (outs[0] if last else x_s.at[w])[:, at, :] = res[:, :, w * cq : (w + 1) * cq]
-    if not last:
-        for w in range(count):
-            for d in range(nt):
-
-                @pl.when(jnp.bitwise_xor(q_ref[0], d) == first + w)
-                def _(w=w, d=d):
-                    outs[d][...] = x_s[w]
+            x_s[w, :, at, :] = res[:, :, w * cq : (w + 1) * cq]
+    for w in range(count):
+        for d in range(nt):
+
+            @pl.when(jnp.bitwise_xor(q_ref[0], d) == first + w)
+            def _(w=w, d=d):
+                outs[d][...] = x_s[w]
 
 
 def final_kernel(nt, q_ref, *refs):
-    ws, most, late = refs[:nt], refs[nt : 2 * nt], refs[2 * nt : 3 * nt]
-    out_ref, wh, wl = refs[3 * nt :]
+    ws, ins, (out_ref, wh, wl) = refs[:nt], refs[nt : 2 * nt], refs[2 * nt :]
     xb, hy, nz = out_ref.shape[1:]
     cq = nz // nt
 
@@ -347,9 +349,7 @@
             wh[d * cq : (d + 1) * cq, :] = ws[d][0]
             wl[d * cq : (d + 1) * cq, :] = ws[d][1]
 
-    is_last = q_ref[0] == nt - 1
-    ins = [jnp.where(is_last, b[...], a[...]) for a, b in zip(most, late)]
-    xh, xl = cut(jnp.concatenate([x.reshape(xb * hy, cq) for x in ins], axis=1))
+    xh, xl = cut(jnp.concatenate([x[...].reshape(xb * hy, cq) for x in ins], axis=1))
     res = mm(xh, wh[...]) + mm(xh, wl[...]) + mm(xl, wh[...])
     out_ref[0] = res.reshape(xb, hy, nz)
 
@@ -423,8 +423,7 @@
     yc = lax.axis_index("cores")
     space = lax.axis_size("space")
     me = lax.axis_index("space")
-    left_index = (me + space - 1) % space
-    qv = jnp.reshape(q, (1,)).astype(jnp.int32)
+    qv, ycv, mev = (jnp.reshape(i, (1,)).astype(jnp.int32) for i in (q, yc, me))
     dims = (nt, steps, nx, hy, cq)
 
     def xor_permute(x, d):
@@ -442,11 +441,11 @@
     kxih, kxil = (jnp.asarray(w) for w in np_bar(nx, True))
     ky, ki = (jnp.asarray(w) for w in np_second(hy))
     HB = pl.BlockSpec(memory_space=pltpu.HBM)
-    n0 = pl.pallas_call(
+    n0, diff_rows, robin_param = pl.pallas_call(
         forward_first_kernel,
-        out_shape=sds(nx + 1, hy, cq),
-        in_specs=[SM, SM] + [HB] * 4,
-        out_specs=VM,
+        out_shape=[sds(nx + 1, hy, cq), sds(SUB, cq), sds(SUB, cq)],
+        in_specs=[SM] * 6 + [HB] * 4,
+        out_specs=[VM] * 3,
         scratch_shapes=[
             pltpu.VMEM((tiles, nx, SUB, nz), F32),
             pltpu.VMEM((2, cq, nz), BF16),
@@ -454,10 +453,10 @@
             pltpu.VMEM((nx * SUB, nx * SUB), BF16),
             pltpu.SemaphoreType.DMA((3 + tiles,)),
         ],
-        compiler_params=grant(8),
+        compiler_params=grant(60),
         cost_estimate=cost(1e9, 3e6),
         name="forward0",
-    )(qv, spectrum_y, initial_state, base, kxh, kxl)
+    )(qv, ycv, mev, spectrum_y, diffusivity, robin_param, initial_state, base, kxh, kxl)
     n1 = swap(n0)
 
     rows = 2 * steps * hy
@@ -475,7 +474,7 @@
             ],
             out_specs=[pl.BlockSpec((rows + steps, cq), lambda i, q: (0, 0))] * nt,
         ),
-        compiler_params=grant(8),
+        compiler_params=grant(18),
         cost_estimate=cost(0, 8 * nt * rows * cq),
         name="split",
     )
@@ -488,7 +487,7 @@
         out_shape=sds(nx, hy, cq),
         in_specs=[SM] + [VM] * 4,
         out_specs=VM,
-        compiler_params=grant(10),
+        compiler_params=grant(18),
         cost_estimate=cost(1e9, 3e6),
         name="forward1",
     )(qv, heat_source, base, kxh, kxl)
@@ -496,23 +495,21 @@
     right_param = along(robin_param, -1)
     left_param = along(robin_param, 1)
 
-    faces = jnp.stack([left_index, me]).astype(jnp.int32)
-    ycv = jnp.reshape(yc, (1,)).astype(jnp.int32)
     counts = [nt - 2] + [1, 1]
     counts = [c for c in counts if c > 0]
     table = jax.ShapeDtypeStruct((2 * hy + 2 * (tiles - 1) * SUB, cq), jnp.int32)
     u_own, amps, tab, f_own, f_there, *windows = pl.pallas_call(
-        functools.partial(order_kernel, nt),
+        functools.partial(order_kernel, nt, space),
         out_shape=[sds(nt, 2, steps, hy, cq), sds(nt, steps, cq), table]
         + [sds(nx, hy, cq)] * 2
         + [sds(c, 2, steps, hy, cq) for c in counts],
-        in_specs=[SM] * 7 + [VM] * (2 + nt),
+        in_specs=[SM] * 6 + [VM] * (3 + nt),
         out_specs=[VM] * (5 + len(counts)),
-        compiler_params=grant(12),
+        compiler_params=grant(18),
         cost_estimate=cost(0, 3e6),
         name="order",
     )(
-        qv, faces, spectrum_x, spectrum_y, diffusivity, open_flag, owner_side,
+        qv, mev, spectrum_x, spectrum_y, open_flag, owner_side, diff_rows,
         spectrum_z.reshape(nt, cq), n1, *dealt,
     )
     there = []
@@ -523,7 +520,7 @@
     *hands, clos, m_there, s_there = pl.pallas_call(
         functools.partial(own_kernel, dims),
         out_shape=[short] * nt + [sds(nt, nx, hy, cq), sds(nx, hy, cq), sds(nx, hy, cq)],
-        in_specs=[SM] * 5 + [VM] * 9,
+        in_specs=[SM] * 2 + [VM] * 12,
         out_specs=[VM] * (nt + 3),
         scratch_shapes=[pltpu.VMEM((nx, hy, cq), F32)] * 2
         + [pltpu.VMEM((2, 2, nt * steps, tiles, SUB, cq), F32)],
@@ -534,50 +531,36 @@
     for d in range(1, nt):
         hands[d] = xor_permute(hands[d], d)
 
-    state, most, first = m_there, [], 0
-    final = nt - 1
+    state, ends, first = m_there, [], 0
     for i, count in enumerate(counts):
-        last = first + count == nt
-        nout = 1 if last else nt
-        operands = (
-            qv, ycv, state, s_there, f_there, there[i], amps, clos, ki, kxih, kxil, *([] if last else most),
-        )
-        prior = 0 if last else len(most)
-        *outs, state = pl.pallas_call(
-            functools.partial(other_kernel, dims, first, count, prior),
-            out_shape=[sds(nx, hy, cq)] * (nout + 1),
-            in_specs=[SM] * 2 + [VM] * (9 + prior),
-            out_specs=[VM] * (nout + 1),
+        *ends, state = pl.pallas_call(
+            functools.partial(other_kernel, dims, first, count, len(ends)),
+            out_shape=[sds(nx, hy, cq)] * (nt + 1),
+            in_specs=[SM] * 2 + [VM] * (9 + len(ends)),
+            out_specs=[VM] * (nt + 1),
             scratch_shapes=[
                 pltpu.VMEM((count, nx, hy, cq), F32),
                 pltpu.VMEM((nx, hy, count * cq), F32),
                 pltpu.VMEM((count, nx, hy, cq), F32),
             ],
-            input_output_aliases={11 + d: d for d in range(prior)},
+            input_output_aliases={11 + d: d for d in range(len(ends))},
             compiler_params=grant(18),
             cost_estimate=cost(1.5e9 * count, 2e6 * count),
-        )(*operands)
+        )(qv, ycv, state, s_there, f_there, there[i], amps, clos, ki, kxih, kxil, *ends)
         first += count
-        if not last:
-            most = list(outs)
-            continue
-        late = list(outs)
     for d in range(1, nt):
-        most[d] = lax.ppermute(most[d], "tm", [(i, i ^ d) for i in range(nt) if i ^ d != final])
+        ends[d] = xor_permute(ends[d], d)
     left, right = pl.pallas_call(
         functools.partial(merge_kernel, nt),
         out_shape=[sds(nt, steps, (tiles - 1) * SUB, cq)] * 2,
         in_specs=[SM] + [VM] * nt,
         out_specs=[VM] * 2,
-        compiler_params=grant(8),
+        compiler_params=grant(18),
         cost_estimate=cost(0, 2e6),
         name="merge",
     )(qv, *hands)
     from_right = along(left, -1)
     from_left = along(right, 1)
-    for d in range(1, nt):
-        late.append(lax.ppermute(late[0], "tm", [(final ^ d, final)]))
-
     xb = SUB
     window_end = pl.pallas_call(
         functools.partial(final_kernel, nt),
@@ -589,14 +572,14 @@
                 pl.BlockSpec((None, 2, cq, nz), lambda i, q, d=d: (jnp.bitwise_xor(q[0], d), 0, 0, 0))
                 for d in range(nt)
             ]
-            + [pl.BlockSpec((xb, hy, cq), lambda i, q: (i, 0, 0))] * (2 * nt),
+            + [pl.BlockSpec((xb, hy, cq), lambda i, q: (i, 0, 0))] * nt,
             out_specs=pl.BlockSpec((1, xb, hy, nz), lambda i, q: (0, i, 0, 0)),
             scratch_shapes=[pltpu.VMEM((nz, nz), BF16)] * 2,
         ),
-        compiler_params=grant(16),
+        compiler_params=grant(18),
         cost_estimate=cost(2e9, 6e6),
         name="final",
-    )(qv, *([base] * nt), *most, *late)
+    )(qv, *([base] * nt), *ends)
 
     robin_out = pl.pallas_call(
         functools.partial(spread_kernel, nt, steps),
@@ -604,7 +587,7 @@
         in_specs=[VM] * 3,
         out_specs=VM,
         scratch_shapes=[pltpu.VMEM((2, steps, hy, cq), F32)],
-        compiler_params=grant(8),
+        compiler_params=grant(18),
         cost_estimate=cost(0, 2e6),
         name="spread",
     )(tab, from_left, from_right)

time: 122 us -> 88.6 us (0.73)
  the two profiles are of different devices: /device:TPU:25 before, /device:TPU:0 now
where the time goes in v3:
time: 88.6 us; the launch traced here: 88.4 us
  waiting for transfers between devices  36.3 us (41%)
  Pallas kernels  30.3 us (34%)
  starting transfers between devices  19.2 us (22%)
  between operations  2.58 us (3%)
    ppermute x4, waiting for transfers between devices, along(): lax.ppermute(x, 'space', [(i, (i + by) % space) for i in range(space)])  18.5 us
    ppermute x9, waiting for transfers between devices, xor_permute(): return lax.ppermute(x, 'tm', [(i, i ^ d) for i in range(nt)])  12.7 us
    pallas_call x3, Pallas kernels, local(): pl.pallas_call(functools.partial(other_kernel, dims, first, count, len(en...  9.94 us
    ppermute x4, starting transfers between devices, along(): lax.ppermute(x, 'space', [(i, (i + by) % space) for i in range(space)])  7.76 us
    pallas_call x1, Pallas kernels, local(): pl.pallas_call(functools.partial(own_kernel, dims), out_shape=[short] * n...  7.31 us
    ppermute x5, starting transfers between devices, swap(): return lax.ppermute(x, 'cores', [(0, 1), (1, 0)])  5.73 us
    ppermute x9, starting transfers between devices, xor_permute(): return lax.ppermute(x, 'tm', [(i, i ^ d) for i in range(nt)])  5.66 us
    ppermute x5, waiting for transfers between devices, swap(): return lax.ppermute(x, 'cores', [(0, 1), (1, 0)])  5.09 us
  transfers between devices with their start and end apart: 18, of which 9 were waited for; matrix products, arithmetic and copies ran while one was open for 0% of the time, Pallas kernels for 25%

profile of v3, /device:TPU:0, one launch (start us, length us, event | category | flops | bytes accessed | tf_op | source)
XLA Modules:
  0.0 88.4 jit_solution(5457049009041954717)
XLA Ops:
  2.3 4.9 %forward0.1 = (f32[33,32,128]{2,1,0:T(8,128)}, f32[8,128]{1,0:T(8,128)}, f32[8,128]{1,0:T(8,128)}) custom-call(s32[1]{0:T(128)} %bitcast.q_ref, s32[1]{0:T(128)} %bitcast.2.yc_ref, s32[1]{0:T(128)} %bitcast.1.me_ref, f32[32]{0:T(128)} %sy_ref.3, f32[1]{0:T(128)S(6)} %copy.36.diff_ref, f32[1]{0:T(128)S(6)} %copy.37.par_ref, f32[32,32,512]{2,1,0:T(8,128)} %x_hbm.1, ...), custom_call_target="tpu_custom_call" | custom-call | flops 1000000000 | bytes 3000000 | tf_op jit(solution)/shard_map/forward0/pallas_call | solution.py:444
  7.2 3.1 %collective-permute-start = (f32[33,32,128]{2,1,0:T(8,128)}, f32[33,32,128]{2,1,0:T(8,128)S(1)}, u32[]{:S(2)}, u32[]{:S(2)}) collective-permute-start(f32[33,32,128]{2,1,0:T(8,128)} %get-tuple-element.41.refs_3_), channel_id=1, source_target_pairs={{0,1},{1,0},{2,3},{3,2},{4,5},{5,4},{6,7},{7,6},{8,9},{9,8},{10,11... | collective-permute-start | bytes 1622024 | tf_op jit(solution)/shard_map/ppermute | solution.py:433
  10.3 1.6 %forward1.1.refs_4_ = f32[32,32,128]{2,1,0:T(8,128)S(1)} custom-call(s32[1]{0:T(128)} %bitcast.q_ref, f32[32,32,512]{2,1,0:T(8,128)S(1)} %copy-done.2, bf16[4,2,128,512]{3,2,1,0:T(8,128)(2,1)S(1)} %copy-done, bf16[256,256]{1,0:T(8,128)(2,1)S(1)} %copy-done.6, bf16[256,256]{1,0:T(8,128)(2,1)S(1)} %copy-done.7), custom_call_target="tpu_custom_call" | custom-call | flops 1000000000 | bytes 3000000 | tf_op jit(solution)/shard_map/forward1/pallas_call | solution.py:485
  12.0 0.1 collective-permute-start.6
  12.1 0.6 split.1
  12.8 2.0 %collective-permute-start.2 = (f32[520,128]{1,0:T(8,128)S(1)}, f32[520,128]{1,0:T(8,128)S(1)}, u32[]{:S(2)}, u32[]{:S(2)}) collective-permute-start(f32[520,128]{1,0:T(8,128)S(1)} %get-tuple-element.44), channel_id=1, source_target_pairs={{0,4},{2,6},{4,0},{6,2},{1,5},{3,7},{5,1},{7,3},{8,12},{10,14},{12... | collective-permute-start | bytes 798728 | tf_op jit(solution)/shard_map/ppermute | solution.py:430
  14.9 7.3 %collective-permute-done.2.refs_2_ = f32[520,128]{1,0:T(8,128)S(1)} collective-permute-done((f32[520,128]{1,0:T(8,128)S(1)}, f32[520,128]{1,0:T(8,128)S(1)}, u32[]{:S(2)}, u32[]{:S(2)}) %collective-permute-start.2) | collective-permute-done | bytes 266272 | tf_op jit(solution)/shard_map/ppermute | solution.py:430
  22.1 5.1 %collective-permute-done.3.refs_3_ = f32[520,128]{1,0:T(8,128)S(1)} collective-permute-done((f32[520,128]{1,0:T(8,128)S(1)}, f32[520,128]{1,0:T(8,128)S(1)}, u32[]{:S(2)}, u32[]{:S(2)}) %collective-permute-start.3) | collective-permute-done | bytes 266272 | tf_op jit(solution)/shard_map/ppermute | solution.py:430
  27.3 1.0 %order.1 = (f32[4,2,8,32,128]{4,3,2,1,0:T(8,128)S(1)}, f32[4,8,128]{2,1,0:T(8,128)S(1)}, s32[112,128]{1,0:T(8,128)S(1)}, f32[32,32,128]{2,1,0:T(8,128)S(1)}, f32...) custom-call(s32[1]{0:T(128)} %bitcast.q_ref, ...), custom_call_target="tpu_custom_call" | custom-call | bytes 3000000 | tf_op jit(solution)/shard_map/order/pallas_call | solution.py:501
  28.3 1.6 %collective-permute-start.12 = (f32[2,2,8,32,128]{4,3,2,1,0:T(8,128)S(1)}, f32[2,2,8,32,128]{4,3,2,1,0:T(8,128)S(1)}, u32[]{:S(2)}, u32[]{:S(2)}) collective-permute-start(f32[2,2,8,32,128]{4,3,2,1,0:T(8,128)S(1)} %get-tuple-element.60), channel_id=1, source_target_pairs={{0,1},{1,0},{2,3},{3,2},{4,5},{5,4},{6,7},{7,6},{8,9},{9,8},{10,11... | collective-permute-start | bytes 1572872 | tf_op jit(solution)/shard_map/ppermute | solution.py:433
  29.9 1.6 %collective-permute-start.4 = (f32[8,128]{1,0:T(8,128)S(1)}, f32[8,128]{1,0:T(8,128)S(1)}, u32[]{:S(2)}, u32[]{:S(2)}) collective-permute-start(f32[8,128]{1,0:T(8,128)S(1)} %copy-done.16), channel_id=1, source_target_pairs={{0,8},{8,16},{16,24},{24,0},{1,9},{9,17},{17,25},{25,1},{2,10},{10... | collective-permute-start | bytes 12296 | tf_op jit(solution)/shard_map/ppermute | solution.py:436
  31.5 2.2 %collective-permute-start.5 = (f32[8,128]{1,0:T(8,128)S(1)}, f32[8,128]{1,0:T(8,128)S(1)}, u32[]{:S(2)}, u32[]{:S(2)}) collective-permute-start(f32[8,128]{1,0:T(8,128)S(1)} %copy-done.16), channel_id=1, source_target_pairs={{0,24},{8,0},{16,8},{24,16},{1,25},{9,1},{17,9},{25,17},{2,26},{10... | collective-permute-start | bytes 12296 | tf_op jit(solution)/shard_map/ppermute | solution.py:436
  33.7 0.5 collective-permute-start.13
  34.2 1.1 %collective-permute-done.4.refs_0_ = f32[8,128]{1,0:T(8,128)S(1)} collective-permute-done((f32[8,128]{1,0:T(8,128)S(1)}, f32[8,128]{1,0:T(8,128)S(1)}, u32[]{:S(2)}, u32[]{:S(2)}) %collective-permute-start.4) | collective-permute-done | bytes 4128 | tf_op jit(solution)/shard_map/ppermute | solution.py:436
  35.3 0.5 collective-permute-start.14
  35.8 7.3 %own.1 = (f32[2,8,24,128]{3,2,1,0:T(8,128)S(1)}, f32[2,8,24,128]{3,2,1,0:T(8,128)S(1)}, f32[2,8,24,128]{3,2,1,0:T(8,128)S(1)}, f32[2,8,24,128]{3,2,1,0:T(8,128)S...) custom-call(s32[1]{0:T(128)} %bitcast.q_ref, s32[1]{0:T(128)} %bitcast.2.yc_ref, ...), custom_call_target="tpu_custom_call" | custom-call | flops 4000000000 | bytes 8000000 | tf_op jit(solution)/shard_map/own/pallas_call | solution.py:520
  43.2 1.6 %collective-permute-start.8 = (f32[2,8,24,128]{3,2,1,0:T(8,128)S(1)}, f32[2,8,24,128]{3,2,1,0:T(8,128)S(1)}, u32[]{:S(2)}, u32[]{:S(2)}) collective-permute-start(f32[2,8,24,128]{3,2,1,0:T(8,128)S(1)} %get-tuple-element.53), channel_id=1, source_target_pairs={{0,4},{2,6},{4,0},{6,2},{1,5},{3,7},{5,1},{7,3},{8,12},{10,14},{12... | collective-permute-start | bytes 589832 | tf_op jit(solution)/shard_map/ppermute | solution.py:430
  44.8 1.3 %collective-permute-done.12.u_s = f32[2,2,8,32,128]{4,3,2,1,0:T(8,128)S(1)} collective-permute-done((f32[2,2,8,32,128]{4,3,2,1,0:T(8,128)S(1)}, f32[2,2,8,32,128]{4,3,2,1,0:T(8,128)S(1)}, u32[]{:S(2)}, u32[]{:S(2)}) %collective-permute-start.12) | collective-permute-done | bytes 524320 | tf_op jit(solution)/shard_map/ppermute | solution.py:433
  46.1 3.9 %shard_map.185 = (f32[32,32,128]{2,1,0:T(8,128)S(1)}, f32[32,32,128]{2,1,0:T(8,128)S(1)}, f32[32,32,128]{2,1,0:T(8,128)S(1)}, f32[32,32,128]{2,1,0:T(8,128)S(1)}, f32[32,32,128]{2,1,0:T(8,128)S(1)}) custom-call(s32[1]{0:T(128)} %bitcast.q_ref, s32[1]{0:T(128)} %bitcast.2.yc_ref, f32[32,32,128]{2,1,0:T(8,128)S(1)} %get-tuple-element.57.m_ref, ...), custom_call_target="tpu_custom_call" | custom-call | flops 3000000000 | bytes 4000000 | tf_op jit(solution)/shard_map/pallas_call | solution.py:536
  50.0 1.7 %collective-permute-done.13.u_s = f32[1,2,8,32,128]{4,3,2,1,0:T(8,128)S(1)} collective-permute-done((f32[1,2,8,32,128]{4,3,2,1,0:T(8,128)S(1)}, f32[1,2,8,32,128]{4,3,2,1,0:T(8,128)S(1)}, u32[]{:S(2)}, u32[]{:S(2)}) %collective-permute-start.13) | collective-permute-done | bytes 262176 | tf_op jit(solution)/shard_map/ppermute | solution.py:433
  51.7 2.6 %shard_map.186 = (f32[32,32,128]{2,1,0:T(8,128)S(1)}, f32[32,32,128]{2,1,0:T(8,128)S(1)}, f32[32,32,128]{2,1,0:T(8,128)S(1)}, f32[32,32,128]{2,1,0:T(8,128)S(1)}, f32[32,32,128]{2,1,0:T(8,128)S(1)}) custom-call(s32[1]{0:T(128)} %bitcast.q_ref, s32[1]{0:T(128)} %bitcast.2.yc_ref, ...), custom_call_target="tpu_custom_call", output_to_operand_aliasing={{0}: (11, {}), {1}: (12, {}), {2}: (13, {}), {3}: (14, {})} | custom-call | flops 1500000000 | bytes 2000000 | tf_op jit(solution)/shard_map/pallas_call | solution.py:536
  54.3 2.1 %collective-permute-done.14.u_s = f32[1,2,8,32,128]{4,3,2,1,0:T(8,128)S(1)} collective-permute-done((f32[1,2,8,32,128]{4,3,2,1,0:T(8,128)S(1)}, f32[1,2,8,32,128]{4,3,2,1,0:T(8,128)S(1)}, u32[]{:S(2)}, u32[]{:S(2)}) %collective-permute-start.14) | collective-permute-done | bytes 262176 | tf_op jit(solution)/shard_map/ppermute | solution.py:433
  56.5 3.4 %shard_map.187 = (f32[32,32,128]{2,1,0:T(8,128)S(1)}, f32[32,32,128]{2,1,0:T(8,128)S(1)}, f32[32,32,128]{2,1,0:T(8,128)S(1)}, f32[32,32,128]{2,1,0:T(8,128)S(1)}, f32[32,32,128]{2,1,0:T(8,128)}) custom-call(s32[1]{0:T(128)} %bitcast.q_ref, s32[1]{0:T(128)} %bitcast.2.yc_ref, ...), custom_call_target="tpu_custom_call", output_to_operand_aliasing={{0}: (11, {}), {1}: (12, {}), {2}: (13, {}), {3}: (14, {})} | custom-call | flops 1500000000 | bytes 2000000 | tf_op jit(solution)/shard_map/pallas_call | solution.py:536
  59.9 1.7 %collective-permute-start.16 = (f32[32,32,128]{2,1,0:T(8,128)S(1)}, f32[32,32,128]{2,1,0:T(8,128)S(1)}, u32[]{:S(2)}, u32[]{:S(2)}) collective-permute-start(f32[32,32,128]{2,1,0:T(8,128)S(1)} %get-tuple-element.76), channel_id=1, source_target_pairs={{0,4},{2,6},{4,0},{6,2},{1,5},{3,7},{5,1},{7,3},{8,12},{10,14},{12... | collective-permute-start | bytes 1572872 | tf_op jit(solution)/shard_map/ppermute | solution.py:430
  61.6 0.2 collective-permute-start.17
  61.8 1.8 %collective-permute-start.10 = (f32[4,8,24,128]{3,2,1,0:T(8,128)S(1)}, f32[4,8,24,128]{3,2,1,0:T(8,128)S(1)}, u32[]{:S(2)}, u32[]{:S(2)}) collective-permute-start(f32[4,8,24,128]{3,2,1,0:T(8,128)S(1)} %get-tuple-element.55), channel_id=1, source_target_pairs={{0,8},{8,16},{16,24},{24,0},{1,9},{9,17},{17,25},{25,1},{2,10},{10... | collective-permute-start | bytes 1179656 | tf_op jit(solution)/shard_map/ppermute | solution.py:436
  63.7 2.1 %collective-permute-start.11 = (f32[4,8,24,128]{3,2,1,0:T(8,128)S(1)}, f32[4,8,24,128]{3,2,1,0:T(8,128)S(1)}, u32[]{:S(2)}, u32[]{:S(2)}) collective-permute-start(f32[4,8,24,128]{3,2,1,0:T(8,128)S(1)} %get-tuple-element.56), channel_id=1, source_target_pairs={{0,24},{8,0},{16,8},{24,16},{1,25},{9,1},{17,9},{25,17},{2,26},{10... | collective-permute-start | bytes 1179656 | tf_op jit(solution)/shard_map/ppermute | solution.py:436
  65.7 9.9 %collective-permute-done.10.left_ref = f32[4,8,24,128]{3,2,1,0:T(8,128)S(1)} collective-permute-done((f32[4,8,24,128]{3,2,1,0:T(8,128)S(1)}, f32[4,8,24,128]{3,2,1,0:T(8,128)S(1)}, u32[]{:S(2)}, u32[]{:S(2)}) %collective-permute-start.10) | collective-permute-done | bytes 393248 | tf_op jit(solution)/shard_map/ppermute | solution.py:436
  75.7 7.4 %collective-permute-done.11.right_ref = f32[4,8,24,128]{3,2,1,0:T(8,128)S(1)} collective-permute-done((f32[4,8,24,128]{3,2,1,0:T(8,128)S(1)}, f32[4,8,24,128]{3,2,1,0:T(8,128)S(1)}, u32[]{:S(2)}, u32[]{:S(2)}) %collective-permute-start.11) | collective-permute-done | bytes 393248 | tf_op jit(solution)/shard_map/ppermute | solution.py:436
  83.1 1.5 %spread.1 = f32[1,2,8,32,512]{4,3,2,1,0:T(8,128)} custom-call(s32[112,128]{1,0:T(8,128)S(1)} %get-tuple-element.46.refs_9_.tab_ref, f32[4,8,24,128]{3,2,1,0:T(8,128)S(1)} %collective-permute-done.10.left_ref, f32[4,8,24,128]{3,2,1,0:T(8,128)S(1)} %collective-permute-done.11.right_ref), custom_call_target="tpu_custom_call" | custom-call | bytes 2000000 | tf_op jit(solution)/shard_map/spread/pallas_call | solution.py:584
  84.6 0.4 collective-permute-done.17.refs_7_
  85.0 3.4 %final.1 = f32[1,32,32,512]{3,2,1,0:T(8,128)} custom-call(s32[1]{0:T(128)} %bitcast.q_ref, bf16[4,2,128,512]{3,2,1,0:T(8,128)(2,1)S(1)} %copy-done, bf16[4,2,128,512]{3,2,1,0:T(8,128)(2,1)S(1)} %copy-done, bf16[4,2,128,512]{3,2,1,0:T(8,128)(2,1)S(1)} %copy-done, bf16[4,2,128,512]{3,2,1,0:T(8,128)(2,1)S(1)} %copy-done, ...), custom_call_target="tpu_custom_call" | custom-call | flops 2000000000 | bytes 6000000 | tf_op jit(solution)/shard_map/final/pallas_call | solution.py:565
  (51 shorter events, 0.4 us)
Async XLA Ops:
  0.6 9.7 %copy-start = (bf16[4,2,128,512]{3,2,1,0:T(8,128)(2,1)S(1)}, bf16[4,2,128,512]{3,2,1,0:T(8,128)(2,1)}, u32[]{:S(2)}) copy-start(bf16[4,2,128,512]{3,2,1,0:T(8,128)(2,1)} %constant.25.clone.c_hbm.c_ref.refs_0_.refs_1_.refs_2_.refs_3_) | copy-start | bytes 3145732
  0.6 9.6 %copy-start.6 = (bf16[256,256]{1,0:T(8,128)(2,1)S(1)}, bf16[256,256]{1,0:T(8,128)(2,1)}, u32[]{:S(2)}) copy-start(bf16[256,256]{1,0:T(8,128)(2,1)} %constant.26.clone.kxh_hbm.kxh_ref) | copy-start | bytes 393220
  7.2 20.0 %collective-permute-start = (f32[33,32,128]{2,1,0:T(8,128)}, f32[33,32,128]{2,1,0:T(8,128)S(1)}, u32[]{:S(2)}, u32[]{:S(2)}) collective-permute-start(f32[33,32,128]{2,1,0:T(8,128)} %get-tuple-element.41.refs_3_), channel_id=1, source_target_pairs={{0,1},{1,0},{2,3},{3,2},{4,5},{5,4},{6,7},{7,6},{8,9},{9,8},{10,11... | collective-permute-start | bytes 1622024 | tf_op jit(solution)/shard_map/ppermute | solution.py:433
  11.9 15.3 %copy-start.8 = (f32[8,128]{1,0:T(8,128)S(1)}, f32[8,128]{1,0:T(8,128)}, u32[]{:S(2)}) copy-start(f32[8,128]{1,0:T(8,128)} %get-tuple-element.40.diff_ref) | copy-start | bytes 12292
  11.9 15.3 %copy-start.9 = (s32[4,32]{1,0:T(4,128)S(1)}, s32[4,32]{1,0:T(4,128)}, u32[]{:S(2)}) copy-start(s32[4,32]{1,0:T(4,128)} %open_ref.1) | copy-start | bytes 1540
  11.9 15.3 %copy-start.10 = (s32[4,32]{1,0:T(4,128)S(1)}, s32[4,32]{1,0:T(4,128)}, u32[]{:S(2)}) copy-start(s32[4,32]{1,0:T(4,128)} %owner_ref.1) | copy-start | bytes 1540
  11.9 15.3 %copy-start.11 = (f32[512]{0:T(512)S(1)}, f32[512]{0:T(512)}, u32[]{:S(2)}) copy-start(f32[512]{0:T(512)} %param.25) | copy-start | bytes 6148
  11.9 15.3 %copy-start.12 = (f32[32]{0:T(128)S(1)}, f32[32]{0:T(128)}, u32[]{:S(2)}) copy-start(f32[32]{0:T(128)} %sx_ref.1) | copy-start | bytes 388
  11.9 15.3 %copy-start.13 = (f32[32]{0:T(128)S(1)}, f32[32]{0:T(128)}, u32[]{:S(2)}) copy-start(f32[32]{0:T(128)} %sy_ref.3) | copy-start | bytes 388
  12.0 17.9 %copy-start.16 = (f32[8,128]{1,0:T(8,128)S(1)}, f32[8,128]{1,0:T(8,128)}, u32[]{:S(2)}) copy-start(f32[8,128]{1,0:T(8,128)} %get-tuple-element.47.refs_1_) | copy-start | bytes 12292
  12.0 23.8 %copy-start.15 = (f32[33,32,128]{2,1,0:T(8,128)S(1)}, f32[33,32,128]{2,1,0:T(8,128)}, u32[]{:S(2)}) copy-start(f32[33,32,128]{2,1,0:T(8,128)} %get-tuple-element.41.refs_3_) | copy-start | bytes 1622020
  12.0 23.8 %copy-start.17 = (bf16[2,2,256,256]{3,2,1,0:T(8,128)(2,1)S(1)}, bf16[2,2,256,256]{3,2,1,0:T(8,128)(2,1)}, u32[]{:S(2)}) copy-start(bf16[2,2,256,256]{3,2,1,0:T(8,128)(2,1)} %constant.30.clone.refs_11_) | copy-start | bytes 1572868
  12.0 23.8 %collective-permute-start.6 = (f32[32,32,128]{2,1,0:T(8,128)S(1)}, f32[32,32,128]{2,1,0:T(8,128)S(1)}, u32[]{:S(2)}, u32[]{:S(2)}) collective-permute-start(f32[32,32,128]{2,1,0:T(8,128)S(1)} %forward1.1.refs_4_), channel_id=1, source_target_pairs={{0,1},{1,0},{2,3},{3,2},{4,5},{5,4},{6,7},{7,6},{8,9},{9,8},{10,11... | collective-permute-start | bytes 1572872 | tf_op jit(solution)/shard_map/ppermute | solution.py:433
  12.7 2.1 %collective-permute-start.1 = (f32[520,128]{1,0:T(8,128)S(1)}, f32[520,128]{1,0:T(8,128)S(1)}, u32[]{:S(2)}, u32[]{:S(2)}) collective-permute-start(f32[520,128]{1,0:T(8,128)S(1)} %get-tuple-element.43), channel_id=1, source_target_pairs={{0,2},{2,0},{4,6},{6,4},{1,3},{3,1},{5,7},{7,5},{8,10},{10,8},{12,... | collective-permute-start | bytes 798728 | tf_op jit(solution)/shard_map/ppermute | solution.py:430
  12.8 9.3 %collective-permute-start.2 = (f32[520,128]{1,0:T(8,128)S(1)}, f32[520,128]{1,0:T(8,128)S(1)}, u32[]{:S(2)}, u32[]{:S(2)}) collective-permute-start(f32[520,128]{1,0:T(8,128)S(1)} %get-tuple-element.44), channel_id=1, source_target_pairs={{0,4},{2,6},{4,0},{6,2},{1,5},{3,7},{5,1},{7,3},{8,12},{10,14},{12... | collective-permute-start | bytes 798728 | tf_op jit(solution)/shard_map/ppermute | solution.py:430
  14.8 12.4 %collective-permute-start.3 = (f32[520,128]{1,0:T(8,128)S(1)}, f32[520,128]{1,0:T(8,128)S(1)}, u32[]{:S(2)}, u32[]{:S(2)}) collective-permute-start(f32[520,128]{1,0:T(8,128)S(1)} %get-tuple-element.45), channel_id=1, source_target_pairs={{0,6},{2,4},{4,2},{6,0},{1,7},{3,5},{5,3},{7,1},{8,14},{10,12},{12... | collective-permute-start | bytes 798728 | tf_op jit(solution)/shard_map/ppermute | solution.py:430
  28.3 17.8 %collective-permute-start.12 = (f32[2,2,8,32,128]{4,3,2,1,0:T(8,128)S(1)}, f32[2,2,8,32,128]{4,3,2,1,0:T(8,128)S(1)}, u32[]{:S(2)}, u32[]{:S(2)}) collective-permute-start(f32[2,2,8,32,128]{4,3,2,1,0:T(8,128)S(1)} %get-tuple-element.60), channel_id=1, source_target_pairs={{0,1},{1,0},{2,3},{3,2},{4,5},{5,4},{6,7},{7,6},{8,9},{9,8},{10,11... | collective-permute-start | bytes 1572872 | tf_op jit(solution)/shard_map/ppermute | solution.py:433
  29.9 5.4 %collective-permute-start.4 = (f32[8,128]{1,0:T(8,128)S(1)}, f32[8,128]{1,0:T(8,128)S(1)}, u32[]{:S(2)}, u32[]{:S(2)}) collective-permute-start(f32[8,128]{1,0:T(8,128)S(1)} %copy-done.16), channel_id=1, source_target_pairs={{0,8},{8,16},{16,24},{24,0},{1,9},{9,17},{17,25},{25,1},{2,10},{10... | collective-permute-start | bytes 12296 | tf_op jit(solution)/shard_map/ppermute | solution.py:436
  31.5 4.3 %collective-permute-start.5 = (f32[8,128]{1,0:T(8,128)S(1)}, f32[8,128]{1,0:T(8,128)S(1)}, u32[]{:S(2)}, u32[]{:S(2)}) collective-permute-start(f32[8,128]{1,0:T(8,128)S(1)} %copy-done.16), channel_id=1, source_target_pairs={{0,24},{8,0},{16,8},{24,16},{1,25},{9,1},{17,9},{25,17},{2,26},{10... | collective-permute-start | bytes 12296 | tf_op jit(solution)/shard_map/ppermute | solution.py:436
  33.7 18.0 %collective-permute-start.13 = (f32[1,2,8,32,128]{4,3,2,1,0:T(8,128)S(1)}, f32[1,2,8,32,128]{4,3,2,1,0:T(8,128)S(1)}, u32[]{:S(2)}, u32[]{:S(2)}) collective-permute-start(f32[1,2,8,32,128]{4,3,2,1,0:T(8,128)S(1)} %get-tuple-element.63), channel_id=1, source_target_pairs={{0,1},{1,0},{2,3},{3,2},{4,5},{5,4},{6,7},{7,6},{8,9},{9,8},{10,11... | collective-permute-start | bytes 786440 | tf_op jit(solution)/shard_map/ppermute | solution.py:433
  35.3 21.2 %collective-permute-start.14 = (f32[1,2,8,32,128]{4,3,2,1,0:T(8,128)S(1)}, f32[1,2,8,32,128]{4,3,2,1,0:T(8,128)S(1)}, u32[]{:S(2)}, u32[]{:S(2)}) collective-permute-start(f32[1,2,8,32,128]{4,3,2,1,0:T(8,128)S(1)} %get-tuple-element.69), channel_id=1, source_target_pairs={{0,1},{1,0},{2,3},{3,2},{4,5},{5,4},{6,7},{7,6},{8,9},{9,8},{10,11... | collective-permute-start | bytes 786440 | tf_op jit(solution)/shard_map/ppermute | solution.py:433
  35.8 10.3 %copy-start.3 = (bf16[2,2,128,256]{3,2,1,0:T(8,128)(2,1)S(1)}, bf16[2,2,128,256]{3,2,1,0:T(8,128)(2,1)}, u32[]{:S(2)}) copy-start(bf16[2,2,128,256]{3,2,1,0:T(8,128)(2,1)} %constant.31.clone.ki_ref) | copy-start | bytes 786436
  35.8 10.3 %copy-start.4 = (bf16[256,256]{1,0:T(8,128)(2,1)S(1)}, bf16[256,256]{1,0:T(8,128)(2,1)}, u32[]{:S(2)}) copy-start(bf16[256,256]{1,0:T(8,128)(2,1)} %constant.28.clone.kxh_ref) | copy-start | bytes 393220
  35.8 10.3 %copy-start.5 = (bf16[256,256]{1,0:T(8,128)(2,1)S(1)}, bf16[256,256]{1,0:T(8,128)(2,1)}, u32[]{:S(2)}) copy-start(bf16[256,256]{1,0:T(8,128)(2,1)} %constant.29.clone.kxl_ref) | copy-start | bytes 393220
  43.1 18.4 %collective-permute-start.7 = (f32[2,8,24,128]{3,2,1,0:T(8,128)S(1)}, f32[2,8,24,128]{3,2,1,0:T(8,128)S(1)}, u32[]{:S(2)}, u32[]{:S(2)}) collective-permute-start(f32[2,8,24,128]{3,2,1,0:T(8,128)S(1)} %get-tuple-element.52), channel_id=1, source_target_pairs={{0,2},{2,0},{4,6},{6,4},{1,3},{3,1},{5,7},{7,5},{8,10},{10,8},{12,... | collective-permute-start | bytes 589832 | tf_op jit(solution)/shard_map/ppermute | solution.py:430
  43.2 18.5 %collective-permute-start.8 = (f32[2,8,24,128]{3,2,1,0:T(8,128)S(1)}, f32[2,8,24,128]{3,2,1,0:T(8,128)S(1)}, u32[]{:S(2)}, u32[]{:S(2)}) collective-permute-start(f32[2,8,24,128]{3,2,1,0:T(8,128)S(1)} %get-tuple-element.53), channel_id=1, source_target_pairs={{0,4},{2,6},{4,0},{6,2},{1,5},{3,7},{5,1},{7,3},{8,12},{10,14},{12... | collective-permute-start | bytes 589832 | tf_op jit(solution)/shard_map/ppermute | solution.py:430
  46.1 15.7 %collective-permute-start.9 = (f32[2,8,24,128]{3,2,1,0:T(8,128)S(1)}, f32[2,8,24,128]{3,2,1,0:T(8,128)S(1)}, u32[]{:S(2)}, u32[]{:S(2)}) collective-permute-start(f32[2,8,24,128]{3,2,1,0:T(8,128)S(1)} %get-tuple-element.54), channel_id=1, source_target_pairs={{0,6},{2,4},{4,2},{6,0},{1,7},{3,5},{5,3},{7,1},{8,14},{10,12},{12... | collective-permute-start | bytes 589832 | tf_op jit(solution)/shard_map/ppermute | solution.py:430
  59.9 24.7 %collective-permute-start.15 = (f32[32,32,128]{2,1,0:T(8,128)S(1)}, f32[32,32,128]{2,1,0:T(8,128)S(1)}, u32[]{:S(2)}, u32[]{:S(2)}) collective-permute-start(f32[32,32,128]{2,1,0:T(8,128)S(1)} %get-tuple-element.75), channel_id=1, source_target_pairs={{0,2},{2,0},{4,6},{6,4},{1,3},{3,1},{5,7},{7,5},{8,10},{10,8},{12,... | collective-permute-start | bytes 1572872 | tf_op jit(solution)/shard_map/ppermute | solution.py:430
  59.9 24.7 %collective-permute-start.16 = (f32[32,32,128]{2,1,0:T(8,128)S(1)}, f32[32,32,128]{2,1,0:T(8,128)S(1)}, u32[]{:S(2)}, u32[]{:S(2)}) collective-permute-start(f32[32,32,128]{2,1,0:T(8,128)S(1)} %get-tuple-element.76), channel_id=1, source_target_pairs={{0,4},{2,6},{4,0},{6,2},{1,5},{3,7},{5,1},{7,3},{8,12},{10,14},{12... | collective-permute-start | bytes 1572872 | tf_op jit(solution)/shard_map/ppermute | solution.py:430
  61.6 23.4 %collective-permute-start.17 = (f32[32,32,128]{2,1,0:T(8,128)S(1)}, f32[32,32,128]{2,1,0:T(8,128)S(1)}, u32[]{:S(2)}, u32[]{:S(2)}) collective-permute-start(f32[32,32,128]{2,1,0:T(8,128)S(1)} %get-tuple-element.77), channel_id=1, source_target_pairs={{0,6},{2,4},{4,2},{6,0},{1,7},{3,5},{5,3},{7,1},{8,14},{10,12},{12... | collective-permute-start | bytes 1572872 | tf_op jit(solution)/shard_map/ppermute | solution.py:430
  61.8 13.9 %collective-permute-start.10 = (f32[4,8,24,128]{3,2,1,0:T(8,128)S(1)}, f32[4,8,24,128]{3,2,1,0:T(8,128)S(1)}, u32[]{:S(2)}, u32[]{:S(2)}) collective-permute-start(f32[4,8,24,128]{3,2,1,0:T(8,128)S(1)} %get-tuple-element.55), channel_id=1, source_target_pairs={{0,8},{8,16},{16,24},{24,0},{1,9},{9,17},{17,25},{25,1},{2,10},{10... | collective-permute-start | bytes 1179656 | tf_op jit(solution)/shard_map/ppermute | solution.py:436
  63.7 19.4 %collective-permute-start.11 = (f32[4,8,24,128]{3,2,1,0:T(8,128)S(1)}, f32[4,8,24,128]{3,2,1,0:T(8,128)S(1)}, u32[]{:S(2)}, u32[]{:S(2)}) collective-permute-start(f32[4,8,24,128]{3,2,1,0:T(8,128)S(1)} %get-tuple-element.56), channel_id=1, source_target_pairs={{0,24},{8,0},{16,8},{24,16},{1,25},{9,1},{17,9},{25,17},{2,26},{10... | collective-permute-start | bytes 1179656 | tf_op jit(solution)/shard_map/ppermute | solution.py:436
  (4 other events, 29.1 us)

commit v4 on v3

--- a/solution.py
+++ b/solution.py
@@ -88,8 +88,8 @@
     return parts[0]
 
 
-def split_kernel(nt, q_ref, amp_ref, *refs):
-    ins, outs = refs[:nt], refs[nt:]
+def split_kernel(nt, q_ref, yc_ref, me_ref, amp_ref, diff_ref, par_ref, *refs):
+    ins, outs, diff_out, par_out = refs[:nt], refs[nt : 2 * nt], refs[2 * nt], refs[2 * nt + 1]
     steps = amp_ref.shape[0]
     rows = outs[0].shape[0] - steps
     cq = outs[0].shape[1]
@@ -97,6 +97,8 @@
         outs[d][0:rows, :] = ins[d][...].reshape(rows, cq)
         for k in range(steps):
             outs[d][rows + k : rows + k + 1, :] = jnp.full((1, cq), amp_ref[k], F32)
+    diff_out[...] = jnp.full(diff_out.shape, diff_ref[0], F32)
+    par_out[...] = jnp.full(par_out.shape, par_ref[0], F32)
 
 
 def forward_block(x, c_ref, kxh_ref, kxl_ref):
@@ -108,43 +110,17 @@
     return const_times(kxh_ref[...], kxl_ref[...], z).reshape(nx, SUB, cq)
 
 
-def forward_first_kernel(
-    q_ref, yc_ref, me_ref, sy_ref, diff_ref, par_ref, x_hbm, c_hbm, kxh_hbm, kxl_hbm,
-    out_ref, diff_out, par_out, x_s, c_s, kxh_s, kxl_s, sem,
-):
-    tiles, nx, _, _ = x_s.shape
-    hy = tiles * SUB
+def forward_kernel(with_sy, q_ref, sy_ref, x_ref, c_ref, kxh_ref, kxl_ref, out_ref):
+    nx, hy, _ = x_ref.shape
     cq = out_ref.shape[2]
-    copies = [
-        pltpu.make_async_copy(c_hbm.at[q_ref[0]], c_s, sem.at[0]),
-        pltpu.make_async_copy(x_hbm.at[:, 0:SUB, :], x_s.at[0], sem.at[3]),
-        pltpu.make_async_copy(kxh_hbm, kxh_s, sem.at[1]),
-        pltpu.make_async_copy(kxl_hbm, kxl_s, sem.at[2]),
-    ]
-    copies += [
-        pltpu.make_async_copy(x_hbm.at[:, t * SUB : (t + 1) * SUB, :], x_s.at[t], sem.at[3 + t])
-        for t in range(1, tiles)
-    ]
-    for copy in copies:
-        copy.start()
-    for r in range(hy):
-        b = tiles * (r % SUB) + r // SUB
-        out_ref[nx, r : r + 1, :] = jnp.full((1, cq), sy_ref[b], F32)
-    diff_out[...] = jnp.full(diff_out.shape, diff_ref[0], F32)
-    par_out[...] = jnp.full(par_out.shape, par_ref[0], F32)
-    for copy in copies[:4]:
-        copy.wait()
-    for t in range(tiles):
-        if t > 0:
-            copies[3 + t].wait()
-        out_ref[0:nx, t * SUB : (t + 1) * SUB, :] = forward_block(x_s[t], c_s, kxh_s, kxl_s)
-
-
-def forward_kernel(q_ref, x_ref, c_ref, kxh_ref, kxl_ref, out_ref):
-    tiles = x_ref.shape[1] // SUB
+    tiles = hy // SUB
+    if with_sy:
+        for r in range(hy):
+            b = tiles * (r % SUB) + r // SUB
+            out_ref[nx, r : r + 1, :] = jnp.full((1, cq), sy_ref[b], F32)
     for t in range(tiles):
         at = slice(t * SUB, (t + 1) * SUB)
-        out_ref[:, at, :] = forward_block(x_ref[:, at, :], c_ref.at[q_ref[0]], kxh_ref, kxl_ref)
+        out_ref[0:nx, at, :] = forward_block(x_ref[:, at, :], c_ref.at[q_ref[0]], kxh_ref, kxl_ref)
 
 
 def factor_into(f_ref, sx_ref, diff_ref, sy, sz):
@@ -163,10 +139,8 @@
         w = jnp.bitwise_xor(q_ref[0], d)
         u_ref[w] = ins[d][0:rows, :].reshape(u_ref.shape[1:])
         amp_ref[w] = ins[d][rows:, :]
-    w = 0
-    for out in outs:
-        out[...] = u_ref[w : w + out.shape[0]]
-        w += out.shape[0]
+    for i, out in enumerate(outs):
+        out[...] = u_ref[jnp.where(i < q_ref[0], i, i + 1)]
     for face in range(2):
         i = lax.rem(me_ref[0] + space - 1, space) if face == 0 else me_ref[0]
         for g in range(hy // tiles):
@@ -279,11 +253,44 @@
         lax.fori_loop(0, steps, combine, 0)
 
 
-def other_kernel(dims, first, count, prior, q_ref, yc_ref, m_ref, s_ref, f_ref, u_s, amp_ref, clos_ref, ki_ref, kxh_ref, kxl_ref, *refs):
+def window_of(nt, q, slot):
+    if nt == 4 and slot >= 2:
+        return jnp.bitwise_xor(q, jnp.where(q == 1, 5 - slot, slot))
+    return jnp.bitwise_xor(q, slot)
+
+
+def late_slots(nt):
+    return [0, 1, 3] if nt == 4 else list(range(nt))
+
+
+def other_kernel(
+    dims, late, q_ref, yc_ref, m_ref, s_ref, f_ref, amp_ref, clos_ref, ki_ref, kxh_ref, kxl_ref, own_ref, *refs
+):
     nt, steps, nx, hy, cq = dims
-    refs = refs[prior:]
-    outs = refs[:nt]
-    st_ref, cl, t_s, x_s = refs[nt:]
+    slots = late_slots(nt) if late else range(nt)
+    chunks, refs = (refs[:1], refs[1 + len(slots) :]) if late else (refs[: nt - 2], refs[nt - 2 :])
+    outs = refs[: len(slots)]
+    st_ref, cl, t_s, x_s, u_s = refs[len(slots) :]
+    q = q_ref[0]
+    edge = jnp.where(q == nt - 1, nt - 2, nt - 1)
+    lo, hi, base = (edge, nt, nt - 2) if late else (0, edge, 0)
+
+    def put(when, w, ref):
+        @pl.when(when)
+        def _():
+            u_s[w - base] = ref[...]
+
+    if late:
+        put(q == nt - 1, nt - 1, own_ref)
+        put(q < nt - 1, nt - 1, chunks[0])
+        put(q == nt - 1, nt - 2, chunks[0])
+    else:
+        for w in range(nt - 1):
+            put(q == w, w, own_ref)
+            if w < nt - 2:
+                put(q > w, w, chunks[w])
+            if w > 0:
+                put(q < w, w, chunks[w - 1])
     tiles = hy // SUB
     ha = nx // 2
     for j in range(tiles):
@@ -296,50 +303,58 @@
             def window(w, cur, j=j, par=par, rows=rows, modes=modes, s=s, f=f):
                 cur = list(cur)
                 for k in range(steps):
-                    r0 = u_s[w, 0, k, pl.ds(j, SUB, stride=tiles), :]
-                    r1 = u_s[w, 1, k, pl.ds(j, SUB, stride=tiles), :]
+                    r0 = u_s[w - base, 0, k, pl.ds(j, SUB, stride=tiles), :]
+                    r1 = u_s[w - base, 1, k, pl.ds(j, SUB, stride=tiles), :]
                     u = r0 + r1 if par == 0 else r0 - r1
-                    amp = amp_ref[w + first, k : k + 1, :]
+                    amp = amp_ref[w, k : k + 1, :]
                     cur = [(x + (amp * y + u)) * z for x, y, z in zip(cur, s, f)]
                 for a, x in zip(modes, cur):
-                    cl[w, a, rows, :] = x
+                    cl[w - base, a, rows, :] = x
                 return tuple(cur)
 
-            end = lax.fori_loop(0, count, window, tuple(m_ref[a, rows, :] for a in modes))
+            end = lax.fori_loop(lo, hi, window, tuple(m_ref[a, rows, :] for a in modes))
             for a, x in zip(modes, end):
                 st_ref[a, rows, :] = x
     pack = ki_ref.shape[2] // hy
     half = pack * hy
-    width = count * cq
     yc = yc_ref[0]
 
-    def yback(ag, _):
-        at = pl.ds(ag * pack, pack)
-        cols = [
-            jnp.concatenate([clos_ref[first + w, at].reshape(half, cq), cl[w, at].reshape(half, cq)], axis=0)
-            for w in range(count)
-        ]
-        res = const_times(ki_ref[yc, 0], ki_ref[yc, 1], jnp.concatenate(cols, axis=1))
-        t_s[at] = res.reshape(pack, hy, width)
+    def back(w, _):
+        def yback(ag, _):
+            at = pl.ds(ag * pack, pack)
+            col = [clos_ref[w, at].reshape(half, cq), cl[w - base, at].reshape(half, cq)]
+            res = const_times(ki_ref[yc, 0], ki_ref[yc, 1], jnp.concatenate(col, axis=0))
+            t_s[at] = res.reshape(pack, hy, cq)
+            return 0
+
+        lax.fori_loop(0, nx // pack, yback, 0, unroll=2)
+        for yb in range(tiles):
+            at = slice(yb * SUB, (yb + 1) * SUB)
+            res = const_times(kxh_ref[...], kxl_ref[...], t_s[:, at, :].reshape(nx * SUB, cq))
+            x_s[:, at, :] = res.reshape(nx, SUB, cq)
+        for slot, out in zip(slots, outs):
+
+            @pl.when(window_of(nt, q, slot) == w)
+            def _(out=out):
+                out[...] = x_s[...]
+
         return 0
 
-    lax.fori_loop(0, nx // pack, yback, 0)
-    for yb in range(tiles):
-        at = slice(yb * SUB, (yb + 1) * SUB)
-        res = const_times(kxh_ref[...], kxl_ref[...], t_s[:, at, :].reshape(nx * SUB, width))
-        res = res.reshape(nx, SUB, width)
-        for w in range(count):
-            x_s[w, :, at, :] = res[:, :, w * cq : (w + 1) * cq]
-    for w in range(count):
-        for d in range(nt):
-
-            @pl.when(jnp.bitwise_xor(q_ref[0], d) == first + w)
-            def _(w=w, d=d):
-                outs[d][...] = x_s[w]
+    lax.fori_loop(lo, hi, back, 0)
+
+
+def relay_kernel(nt, q_ref, early_ref, late_ref, out_ref):
+    @pl.when(q_ref[0] == nt - 1)
+    def _():
+        out_ref[...] = early_ref[...]
+
+    @pl.when(q_ref[0] != nt - 1)
+    def _():
+        out_ref[...] = late_ref[...]
 
 
 def final_kernel(nt, q_ref, *refs):
-    ws, ins, (out_ref, wh, wl) = refs[:nt], refs[nt : 2 * nt], refs[2 * nt :]
+    ws, ins, (out_ref, wh, wl) = refs[:nt], refs[nt:-3], refs[-3:]
     xb, hy, nz = out_ref.shape[1:]
     cq = nz // nt
 
@@ -349,7 +364,12 @@
             wh[d * cq : (d + 1) * cq, :] = ws[d][0]
             wl[d * cq : (d + 1) * cq, :] = ws[d][1]
 
-    xh, xl = cut(jnp.concatenate([x[...].reshape(xb * hy, cq) for x in ins], axis=1))
+    parts = [x[...].reshape(xb * hy, cq) for x in ins]
+    if nt == 4:
+        relayed = parts.pop()
+        parts[2] = jnp.where(q_ref[0] == 3, relayed, parts[2])
+        parts[3] = jnp.where(q_ref[0] == 2, relayed, parts[3])
+    xh, xl = cut(jnp.concatenate(parts, axis=1))
     res = mm(xh, wh[...]) + mm(xh, wl[...]) + mm(xl, wh[...])
     out_ref[0] = res.reshape(xb, hy, nz)
 
@@ -440,71 +460,59 @@
     kxh, kxl = (jnp.asarray(w) for w in np_bar(nx, False))
     kxih, kxil = (jnp.asarray(w) for w in np_bar(nx, True))
     ky, ki = (jnp.asarray(w) for w in np_second(hy))
-    HB = pl.BlockSpec(memory_space=pltpu.HBM)
-    n0, diff_rows, robin_param = pl.pallas_call(
-        forward_first_kernel,
-        out_shape=[sds(nx + 1, hy, cq), sds(SUB, cq), sds(SUB, cq)],
-        in_specs=[SM] * 6 + [HB] * 4,
-        out_specs=[VM] * 3,
-        scratch_shapes=[
-            pltpu.VMEM((tiles, nx, SUB, nz), F32),
-            pltpu.VMEM((2, cq, nz), BF16),
-            pltpu.VMEM((nx * SUB, nx * SUB), BF16),
-            pltpu.VMEM((nx * SUB, nx * SUB), BF16),
-            pltpu.SemaphoreType.DMA((3 + tiles,)),
-        ],
-        compiler_params=grant(60),
-        cost_estimate=cost(1e9, 3e6),
-        name="forward0",
-    )(qv, ycv, mev, spectrum_y, diffusivity, robin_param, initial_state, base, kxh, kxl)
-    n1 = swap(n0)
 
     rows = 2 * steps * hy
     block = (None, 2, steps, hy, cq)
     cutting = pl.pallas_call(
         functools.partial(split_kernel, nt),
-        out_shape=[sds(rows + steps, cq)] * nt,
+        out_shape=[sds(rows + steps, cq)] * nt + [sds(SUB, cq)] * 2,
         grid_spec=pltpu.PrefetchScalarGridSpec(
-            num_scalar_prefetch=1,
+            num_scalar_prefetch=3,
             grid=(1,),
-            in_specs=[SM]
+            in_specs=[SM] * 3
             + [
-                pl.BlockSpec(block, lambda i, q, d=d: (0, 0, 0, 0, jnp.bitwise_xor(q[0], d)))
+                pl.BlockSpec(block, lambda i, q, y, z, d=d: (0, 0, 0, 0, jnp.bitwise_xor(q[0], d)))
                 for d in range(nt)
             ],
-            out_specs=[pl.BlockSpec((rows + steps, cq), lambda i, q: (0, 0))] * nt,
+            out_specs=[pl.BlockSpec((rows + steps, cq), lambda i, q, y, z: (0, 0))] * nt
+            + [pl.BlockSpec((SUB, cq), lambda i, q, y, z: (0, 0))] * 2,
         ),
         compiler_params=grant(18),
         cost_estimate=cost(0, 8 * nt * rows * cq),
         name="split",
     )
-    dealt = list(cutting(qv, source_amplitude, *([robin_in] * nt)))
+    *dealt, diff_rows, robin_param = cutting(
+        qv, ycv, mev, source_amplitude, diffusivity, robin_param, *([robin_in] * nt)
+    )
+    piece = swap(dealt[0])
+
+    def forward(values, planes):
+        return pl.pallas_call(
+            functools.partial(forward_kernel, planes > 0),
+            out_shape=sds(nx + planes, hy, cq),
+            in_specs=[SM] * 2 + [VM] * 4,
+            out_specs=VM,
+            compiler_params=grant(18),
+            cost_estimate=cost(1e9, 3e6),
+        )(qv, spectrum_y, values, base, kxh, kxl)
+
+    n0 = forward(initial_state, 1)
+    n1 = swap(n0)
     for d in range(1, nt):
         dealt[d] = xor_permute(dealt[d], d)
-
-    s0 = pl.pallas_call(
-        forward_kernel,
-        out_shape=sds(nx, hy, cq),
-        in_specs=[SM] + [VM] * 4,
-        out_specs=VM,
-        compiler_params=grant(18),
-        cost_estimate=cost(1e9, 3e6),
-        name="forward1",
-    )(qv, heat_source, base, kxh, kxl)
+    s0 = forward(heat_source, 0)
     s1 = swap(s0)
     right_param = along(robin_param, -1)
     left_param = along(robin_param, 1)
 
-    counts = [nt - 2] + [1, 1]
-    counts = [c for c in counts if c > 0]
     table = jax.ShapeDtypeStruct((2 * hy + 2 * (tiles - 1) * SUB, cq), jnp.int32)
-    u_own, amps, tab, f_own, f_there, *windows = pl.pallas_call(
+    u_own, amps, tab, f_own, f_there, *chunks = pl.pallas_call(
         functools.partial(order_kernel, nt, space),
         out_shape=[sds(nt, 2, steps, hy, cq), sds(nt, steps, cq), table]
         + [sds(nx, hy, cq)] * 2
-        + [sds(c, 2, steps, hy, cq) for c in counts],
+        + [sds(2, steps, hy, cq)] * (nt - 1),
         in_specs=[SM] * 6 + [VM] * (3 + nt),
-        out_specs=[VM] * (5 + len(counts)),
+        out_specs=[VM] * (4 + nt),
         compiler_params=grant(18),
         cost_estimate=cost(0, 3e6),
         name="order",
@@ -512,9 +520,8 @@
         qv, mev, spectrum_x, spectrum_y, open_flag, owner_side, diff_rows,
         spectrum_z.reshape(nt, cq), n1, *dealt,
     )
-    there = []
-    for u in windows:
-        there.append(swap(u))
+    for i in range(nt - 1):
+        chunks[i] = swap(chunks[i])
 
     short = sds(2, steps, (tiles - 1) * SUB, cq)
     *hands, clos, m_there, s_there = pl.pallas_call(
@@ -531,25 +538,44 @@
     for d in range(1, nt):
         hands[d] = xor_permute(hands[d], d)
 
-    state, ends, first = m_there, [], 0
-    for i, count in enumerate(counts):
-        *ends, state = pl.pallas_call(
-            functools.partial(other_kernel, dims, first, count, len(ends)),
-            out_shape=[sds(nx, hy, cq)] * (nt + 1),
-            in_specs=[SM] * 2 + [VM] * (9 + len(ends)),
-            out_specs=[VM] * (nt + 1),
+    state, ends = m_there, [None] * nt
+    piece = piece[:rows].reshape(2, steps, hy, cq)
+    for late, got in ((False, chunks[:-1]), (True, chunks[-1:])):
+        span = 2 if late else nt - 1
+        slots = late_slots(nt) if late else list(range(nt))
+        prior = [ends[d] for d in slots] if late else []
+        *outs, state = pl.pallas_call(
+            functools.partial(other_kernel, dims, late),
+            out_shape=[sds(nx, hy, cq)] * (len(slots) + 1),
+            in_specs=[SM] * 2 + [VM] * (9 + len(got) + len(prior)),
+            out_specs=[VM] * (len(slots) + 1),
             scratch_shapes=[
-                pltpu.VMEM((count, nx, hy, cq), F32),
-                pltpu.VMEM((nx, hy, count * cq), F32),
-                pltpu.VMEM((count, nx, hy, cq), F32),
+                pltpu.VMEM((span, nx, hy, cq), F32),
+                pltpu.VMEM((nx, hy, cq), F32),
+                pltpu.VMEM((nx, hy, cq), F32),
+                pltpu.VMEM((span, 2, steps, hy, cq), F32),
             ],
-            input_output_aliases={11 + d: d for d in range(len(ends))},
+            input_output_aliases={11 + len(got) + d: d for d in range(len(prior))},
             compiler_params=grant(18),
-            cost_estimate=cost(1.5e9 * count, 2e6 * count),
-        )(qv, ycv, state, s_there, f_there, there[i], amps, clos, ki, kxih, kxil, *ends)
-        first += count
-    for d in range(1, nt):
-        ends[d] = xor_permute(ends[d], d)
+            cost_estimate=cost(4e9, 4e6),
+            name="other1" if late else "other0",
+        )(qv, ycv, state, s_there, f_there, amps, clos, ki, kxih, kxil, piece, *got, *prior)
+        for d, out in zip(slots, outs):
+            ends[d] = out
+        for d in range(1, nt):
+            if late and d in slots or not late and d not in late_slots(nt):
+                ends[d] = xor_permute(ends[d], d)
+    if nt == 4:
+        passing = pl.pallas_call(
+            functools.partial(relay_kernel, nt),
+            out_shape=sds(nx, hy, cq),
+            in_specs=[SM] + [VM] * 2,
+            out_specs=VM,
+            compiler_params=grant(18),
+            cost_estimate=cost(0, 1e6),
+            name="relay",
+        )(qv, ends[2], ends[3])
+        ends.append(xor_permute(passing, 1))
     left, right = pl.pallas_call(
         functools.partial(merge_kernel, nt),
         out_shape=[sds(nt, steps, (tiles - 1) * SUB, cq)] * 2,
@@ -572,7 +598,7 @@
                 pl.BlockSpec((None, 2, cq, nz), lambda i, q, d=d: (jnp.bitwise_xor(q[0], d), 0, 0, 0))
                 for d in range(nt)
             ]
-            + [pl.BlockSpec((xb, hy, cq), lambda i, q: (i, 0, 0))] * nt,
+            + [pl.BlockSpec((xb, hy, cq), lambda i, q: (i, 0, 0))] * len(ends),
             out_specs=pl.BlockSpec((1, xb, hy, nz), lambda i, q: (0, i, 0, 0)),
             scratch_shapes=[pltpu.VMEM((nz, nz), BF16)] * 2,
         ),

time: 88.6 us -> 128 us (1.44)
  waiting for transfers between devices: 36.3 us -> 71.5 us
  starting transfers between devices: 19.2 us -> 23.9 us
  Pallas kernels: 30.3 us -> 27.6 us
  local copies, waits for them, and re-layouts: 0.11 us -> 2.66 us
    ppermute x9 -> x10, waiting for transfers between devices: 12.7 us -> 36.1 us  [xor_permute(): return lax.ppermute(x, 'tm', [(i, i ^ d) for i in range(nt)])]
    ppermute x5 -> x6, waiting for transfers between devices: 5.09 us -> 19.6 us  [swap(): return lax.ppermute(x, 'cores', [(0, 1), (1, 0)])]
    pallas_call x6, Pallas kernels: 17 us -> 14.2 us  [the longest x2 9.28 us: local(): pl.pallas_call(functools.partial(other_kernel, dims, late), out_shape=[sd...]
    ppermute x4, waiting for transfers between devices: 18.5 us -> 15.8 us  [along(): lax.ppermute(x, 'space', [(i, (i + by) % space) for i in range(space)])]
    ppermute x5 -> x6, starting transfers between devices: 5.73 us -> 8.27 us  [swap(): return lax.ppermute(x, 'cores', [(0, 1), (1, 0)])]
    unnamed x36 -> x32, local copies, waits for them, and re-layouts: 0.11 us -> 2.64 us
    ppermute x4, starting transfers between devices: 7.76 us -> 9.57 us  [along(): lax.ppermute(x, 'space', [(i, (i + by) % space) for i in range(space)])]
    ppermute x9 -> x10, starting transfers between devices: 5.66 us -> 6.11 us  [xor_permute(): return lax.ppermute(x, 'tm', [(i, i ^ d) for i in range(nt)])]
  transfers between devices with their start and end apart: 18 -> 20, of which waited for: 9 -> 9; matrix products, arithmetic and copies ran while one was open for 0% -> 0% of each run, Pallas kernels for 25% -> 16%
where the time goes in v4:
time: 128 us
  waiting for transfers between devices  71.5 us (56%)
  Pallas kernels  27.6 us (22%)
  starting transfers between devices  23.9 us (19%)
  local copies, waits for them, and re-layouts  2.66 us (2%)
  between operations  2.18 us (2%)
    ppermute x10, waiting for transfers between devices, xor_permute(): return lax.ppermute(x, 'tm', [(i, i ^ d) for i in range(nt)])  36.1 us
    ppermute x6, waiting for transfers between devices, swap(): return lax.ppermute(x, 'cores', [(0, 1), (1, 0)])  19.6 us
    ppermute x4, waiting for transfers between devices, along(): lax.ppermute(x, 'space', [(i, (i + by) % space) for i in range(space)])  15.8 us
    ppermute x4, starting transfers between devices, along(): lax.ppermute(x, 'space', [(i, (i + by) % space) for i in range(space)])  9.57 us
    pallas_call x2, Pallas kernels, local(): pl.pallas_call(functools.partial(other_kernel, dims, late), out_shape=[sd...  9.28 us
    ppermute x6, starting transfers between devices, swap(): return lax.ppermute(x, 'cores', [(0, 1), (1, 0)])  8.27 us
    pallas_call x1, Pallas kernels, local(): pl.pallas_call(functools.partial(own_kernel, dims), out_shape=[short] * n...  7.35 us
    ppermute x10, starting transfers between devices, xor_permute(): return lax.ppermute(x, 'tm', [(i, i ^ d) for i in range(nt)])  6.11 us
  transfers between devices with their start and end apart: 20, of which 9 were waited for; matrix products, arithmetic and copies ran while one was open for 0% of the time, Pallas kernels for 16%

profile of v4, /device:TPU:0, one launch (start us, length us, event | category | flops | bytes accessed | tf_op | source)
XLA Modules:
  0.0 127.9 jit_solution(848518913064571727)
XLA Ops:
  1.9 1.2 copy-done.1
  3.2 0.7 copy-done.11
  3.8 0.6 split.1
  4.5 0.6 collective-permute-start.1
  5.0 0.7 copy-done.2
  5.7 2.1 %shard_map.185.refs_3_ = f32[33,32,128]{2,1,0:T(8,128)S(1)} custom-call(s32[1]{0:T(128)} %bitcast.q_ref, f32[32]{0:T(128)S(1)} %copy-done.6, f32[32,32,512]{2,1,0:T(8,128)S(1)} %copy-done.2, bf16[4,2,128,512]{3,2,1,0:T(8,128)(2,1)S(1)} %copy-done, bf16[256,256]{1,0:T(8,128)(2,1)S(1)} %copy-done.4, bf16[256,256]{1,0:T(8,128)(2,1)S(1)} %copy-done.5), custom_call_target="tpu_custom_call" | custom-call | flops 1000000000 | bytes 3000000 | tf_op jit(solution)/shard_map/pallas_call | solution.py:490
  7.9 3.1 %collective-permute-start = (f32[33,32,128]{2,1,0:T(8,128)S(1)}, f32[33,32,128]{2,1,0:T(8,128)S(1)}, u32[]{:S(2)}, u32[]{:S(2)}) collective-permute-start(f32[33,32,128]{2,1,0:T(8,128)S(1)} %shard_map.185.refs_3_), channel_id=1, source_target_pairs={{0,1},{1,0},{2,3},{3,2},{4,5},{5,4},{6,7},{7,6},{8,9},{9,8},{10,11... | collective-permute-start | bytes 1622024 | tf_op jit(solution)/shard_map/ppermute | solution.py:453
  11.0 2.1 %shard_map.186.refs_4_ = f32[32,32,128]{2,1,0:T(8,128)S(1)} custom-call(s32[1]{0:T(128)} %bitcast.q_ref, f32[32]{0:T(128)S(1)} %copy-done.6, f32[32,32,512]{2,1,0:T(8,128)S(1)} %copy-done.3, bf16[4,2,128,512]{3,2,1,0:T(8,128)(2,1)S(1)} %copy-done, bf16[256,256]{1,0:T(8,128)(2,1)S(1)} %copy-done.4, bf16[256,256]{1,0:T(8,128)(2,1)S(1)} %copy-done.5), custom_call_target="tpu_custom_call" | custom-call | flops 1000000000 | bytes 3000000 | tf_op jit(solution)/shard_map/pallas_call | solution.py:490
  13.2 2.0 %collective-permute-start.2 = (f32[520,128]{1,0:T(8,128)S(1)}, f32[520,128]{1,0:T(8,128)S(1)}, u32[]{:S(2)}, u32[]{:S(2)}) collective-permute-start(f32[520,128]{1,0:T(8,128)S(1)} %get-tuple-element.36), channel_id=1, source_target_pairs={{0,4},{2,6},{4,0},{6,2},{1,5},{3,7},{5,1},{7,3},{8,12},{10,14},{12... | collective-permute-start | bytes 798728 | tf_op jit(solution)/shard_map/ppermute | solution.py:450
  15.2 1.5 %collective-permute-start.12 = (f32[520,128]{1,0:T(8,128)S(1)}, f32[520,128]{1,0:T(8,128)S(1)}, u32[]{:S(2)}, u32[]{:S(2)}) collective-permute-start(f32[520,128]{1,0:T(8,128)S(1)} %get-tuple-element.34.refs_0_), channel_id=1, source_target_pairs={{0,1},{1,0},{2,3},{3,2},{4,5},{5,4},{6,7},{7,6},{8,9},{9,8},{10,11... | collective-permute-start | bytes 798728 | tf_op jit(solution)/shard_map/ppermute | solution.py:453
  16.7 5.8 %collective-permute-done.2.refs_2_ = f32[520,128]{1,0:T(8,128)S(1)} collective-permute-done((f32[520,128]{1,0:T(8,128)S(1)}, f32[520,128]{1,0:T(8,128)S(1)}, u32[]{:S(2)}, u32[]{:S(2)}) %collective-permute-start.2) | collective-permute-done | bytes 266272 | tf_op jit(solution)/shard_map/ppermute | solution.py:450
  22.6 1.9 %collective-permute-start.4 = (f32[8,128]{1,0:T(8,128)S(1)}, f32[8,128]{1,0:T(8,128)S(1)}, u32[]{:S(2)}, u32[]{:S(2)}) collective-permute-start(f32[8,128]{1,0:T(8,128)S(1)} %get-tuple-element.39.refs_1_), channel_id=1, source_target_pairs={{0,8},{8,16},{16,24},{24,0},{1,9},{9,17},{17,25},{25,1},{2,10},{10... | collective-permute-start | bytes 12296 | tf_op jit(solution)/shard_map/ppermute | solution.py:456
  24.4 15.8 %collective-permute-done.12 = f32[520,128]{1,0:T(8,128)S(1)} collective-permute-done((f32[520,128]{1,0:T(8,128)S(1)}, f32[520,128]{1,0:T(8,128)S(1)}, u32[]{:S(2)}, u32[]{:S(2)}) %collective-permute-start.12) | collective-permute-done | bytes 266272 | tf_op jit(solution)/shard_map/ppermute | solution.py:453
  40.2 3.8 %collective-permute-start.5 = (f32[8,128]{1,0:T(8,128)S(1)}, f32[8,128]{1,0:T(8,128)S(1)}, u32[]{:S(2)}, u32[]{:S(2)}) collective-permute-start(f32[8,128]{1,0:T(8,128)S(1)} %get-tuple-element.39.refs_1_), channel_id=1, source_target_pairs={{0,24},{8,0},{16,8},{24,16},{1,25},{9,1},{17,9},{25,17},{2,26},{10... | collective-permute-start | bytes 12296 | tf_op jit(solution)/shard_map/ppermute | solution.py:456
  44.1 1.0 order.1
  45.1 1.6 %collective-permute-start.13 = (f32[2,8,32,128]{3,2,1,0:T(8,128)S(1)}, f32[2,8,32,128]{3,2,1,0:T(8,128)S(1)}, u32[]{:S(2)}, u32[]{:S(2)}) collective-permute-start(f32[2,8,32,128]{3,2,1,0:T(8,128)S(1)} %get-tuple-element.53), channel_id=1, source_target_pairs={{0,1},{1,0},{2,3},{3,2},{4,5},{5,4},{6,7},{7,6},{8,9},{9,8},{10,11... | collective-permute-start | bytes 786440 | tf_op jit(solution)/shard_map/ppermute | solution.py:453
  47.2 1.5 %collective-permute-start.15 = (f32[2,8,32,128]{3,2,1,0:T(8,128)S(1)}, f32[2,8,32,128]{3,2,1,0:T(8,128)S(1)}, u32[]{:S(2)}, u32[]{:S(2)}) collective-permute-start(f32[2,8,32,128]{3,2,1,0:T(8,128)S(1)} %get-tuple-element.56), channel_id=1, source_target_pairs={{0,1},{1,0},{2,3},{3,2},{4,5},{5,4},{6,7},{7,6},{8,9},{9,8},{10,11... | collective-permute-start | bytes 786440 | tf_op jit(solution)/shard_map/ppermute | solution.py:453
  48.8 7.3 %own.1 = (f32[2,8,24,128]{3,2,1,0:T(8,128)S(1)}, f32[2,8,24,128]{3,2,1,0:T(8,128)S(1)}, f32[2,8,24,128]{3,2,1,0:T(8,128)S(1)}, f32[2,8,24,128]{3,2,1,0:T(8,128)S...) custom-call(s32[1]{0:T(128)} %bitcast.q_ref, s32[1]{0:T(128)} %bitcast.2.yc_ref, ...), custom_call_target="tpu_custom_call" | custom-call | flops 4000000000 | bytes 8000000 | tf_op jit(solution)/shard_map/own/pallas_call | solution.py:527
  56.2 3.8 %collective-permute-done.14.refs_1_ = f32[2,8,32,128]{3,2,1,0:T(8,128)S(1)} collective-permute-done((f32[2,8,32,128]{3,2,1,0:T(8,128)S(1)}, f32[2,8,32,128]{3,2,1,0:T(8,128)S(1)}, u32[]{:S(2)}, u32[]{:S(2)}) %collective-permute-start.14) | collective-permute-done | bytes 262176 | tf_op jit(solution)/shard_map/ppermute | solution.py:453
  60.0 6.3 %other0.1 = (f32[32,32,128]{2,1,0:T(8,128)S(1)}, f32[32,32,128]{2,1,0:T(8,128)S(1)}, f32[32,32,128]{2,1,0:T(8,128)S(1)}, f32[32,32,128]{2,1,0:T(8,128)S(1)}, f32[32,32,128]{2,1,0:T(8,128)S(1)}) custom-call(s32[1]{0:T(128)} %bitcast.q_ref, s32[1]{0:T(128)} %bitcast.2.yc_ref, f32[32,32,128]{2,1,0:T(8,128)S(1)} %get-tuple-element.49.m_ref, ...), custom_call_target="tpu_custom_call" | custom-call | flops 4000000000 | bytes 4000000 | tf_op jit(solution)/shard_map/other0/pallas_call | solution.py:547
  66.4 2.9 %other1.1 = (f32[32,32,128]{2,1,0:T(8,128)S(1)}, f32[32,32,128]{2,1,0:T(8,128)S(1)}, f32[32,32,128]{2,1,0:T(8,128)S(1)}, f32[32,32,128]{2,1,0:T(8,128)}) custom-call(s32[1]{0:T(128)} %bitcast.q_ref, s32[1]{0:T(128)} %bitcast.2.yc_ref, f32[32,32,128]{2,1,0:T(8,128)S(1)} %get-tuple-element.55.m_ref, ...), custom_call_target="tpu_custom_call", output_to_operand_aliasing={{0}: (12, {}), {1}: (13, {}), {2}: (14, {})} | custom-call | flops 4000000000 | bytes 4000000 | tf_op jit(solution)/shard_map/other1/pallas_call | solution.py:547
  69.3 1.5 %collective-permute-start.17 = (f32[32,32,128]{2,1,0:T(8,128)S(1)}, f32[32,32,128]{2,1,0:T(8,128)S(1)}, u32[]{:S(2)}, u32[]{:S(2)}) collective-permute-start(f32[32,32,128]{2,1,0:T(8,128)S(1)} %get-tuple-element.62), channel_id=1, source_target_pairs={{0,4},{2,6},{4,0},{6,2},{1,5},{3,7},{5,1},{7,3},{8,12},{10,14},{12... | collective-permute-start | bytes 1572872 | tf_op jit(solution)/shard_map/ppermute | solution.py:450
  71.2 1.5 %collective-permute-start.8 = (f32[2,8,24,128]{3,2,1,0:T(8,128)S(1)}, f32[2,8,24,128]{3,2,1,0:T(8,128)S(1)}, u32[]{:S(2)}, u32[]{:S(2)}) collective-permute-start(f32[2,8,24,128]{3,2,1,0:T(8,128)S(1)} %get-tuple-element.45), channel_id=1, source_target_pairs={{0,4},{2,6},{4,0},{6,2},{1,5},{3,7},{5,1},{7,3},{8,12},{10,14},{12... | collective-permute-start | bytes 589832 | tf_op jit(solution)/shard_map/ppermute | solution.py:450
  72.7 10.8 %collective-permute-done.18.late_ref.refs_7_ = f32[32,32,128]{2,1,0:T(8,128)S(1)} collective-permute-done((f32[32,32,128]{2,1,0:T(8,128)S(1)}, f32[32,32,128]{2,1,0:T(8,128)S(1)}, u32[]{:S(2)}, u32[]{:S(2)}) %collective-permute-start.18) | collective-permute-done | bytes 524320 | tf_op jit(solution)/shard_map/ppermute | solution.py:450
  83.6 11.2 %collective-permute-done.17.early_ref.refs_6_ = f32[32,32,128]{2,1,0:T(8,128)S(1)} collective-permute-done((f32[32,32,128]{2,1,0:T(8,128)S(1)}, f32[32,32,128]{2,1,0:T(8,128)S(1)}, u32[]{:S(2)}, u32[]{:S(2)}) %collective-permute-start.17) | collective-permute-done | bytes 524320 | tf_op jit(solution)/shard_map/ppermute | solution.py:450
  94.9 4.1 %collective-permute-done.8.refs_2_ = f32[2,8,24,128]{3,2,1,0:T(8,128)S(1)} collective-permute-done((f32[2,8,24,128]{3,2,1,0:T(8,128)S(1)}, f32[2,8,24,128]{3,2,1,0:T(8,128)S(1)}, u32[]{:S(2)}, u32[]{:S(2)}) %collective-permute-start.8) | collective-permute-done | bytes 196640 | tf_op jit(solution)/shard_map/ppermute | solution.py:450
  99.0 4.1 %collective-permute-done.9.refs_3_ = f32[2,8,24,128]{3,2,1,0:T(8,128)S(1)} collective-permute-done((f32[2,8,24,128]{3,2,1,0:T(8,128)S(1)}, f32[2,8,24,128]{3,2,1,0:T(8,128)S(1)}, u32[]{:S(2)}, u32[]{:S(2)}) %collective-permute-start.9) | collective-permute-done | bytes 196640 | tf_op jit(solution)/shard_map/ppermute | solution.py:450
  103.3 3.8 %collective-permute-start.11 = (f32[4,8,24,128]{3,2,1,0:T(8,128)S(1)}, f32[4,8,24,128]{3,2,1,0:T(8,128)S(1)}, u32[]{:S(2)}, u32[]{:S(2)}) collective-permute-start(f32[4,8,24,128]{3,2,1,0:T(8,128)S(1)} %get-tuple-element.48), channel_id=1, source_target_pairs={{0,24},{8,0},{16,8},{24,16},{1,25},{9,1},{17,9},{25,17},{2,26},{10... | collective-permute-start | bytes 1179656 | tf_op jit(solution)/shard_map/ppermute | solution.py:456
  107.1 10.0 %collective-permute-done.10.left_ref = f32[4,8,24,128]{3,2,1,0:T(8,128)S(1)} collective-permute-done((f32[4,8,24,128]{3,2,1,0:T(8,128)S(1)}, f32[4,8,24,128]{3,2,1,0:T(8,128)S(1)}, u32[]{:S(2)}, u32[]{:S(2)}) %collective-permute-start.10) | collective-permute-done | bytes 393248 | tf_op jit(solution)/shard_map/ppermute | solution.py:456
  117.1 5.8 %collective-permute-done.11.right_ref = f32[4,8,24,128]{3,2,1,0:T(8,128)S(1)} collective-permute-done((f32[4,8,24,128]{3,2,1,0:T(8,128)S(1)}, f32[4,8,24,128]{3,2,1,0:T(8,128)S(1)}, u32[]{:S(2)}, u32[]{:S(2)}) %collective-permute-start.11) | collective-permute-done | bytes 393248 | tf_op jit(solution)/shard_map/ppermute | solution.py:456
  122.9 1.5 %spread.1 = f32[1,2,8,32,512]{4,3,2,1,0:T(8,128)} custom-call(s32[112,128]{1,0:T(8,128)S(1)} %get-tuple-element.38.refs_9_.tab_ref, f32[4,8,24,128]{3,2,1,0:T(8,128)S(1)} %collective-permute-done.10.left_ref, f32[4,8,24,128]{3,2,1,0:T(8,128)S(1)} %collective-permute-done.11.right_ref), custom_call_target="tpu_custom_call" | custom-call | bytes 2000000 | tf_op jit(solution)/shard_map/spread/pallas_call | solution.py:610
  124.4 3.5 %final.1 = f32[1,32,32,512]{3,2,1,0:T(8,128)} custom-call(s32[1]{0:T(128)} %bitcast.q_ref, bf16[4,2,128,512]{3,2,1,0:T(8,128)(2,1)S(1)} %copy-done, bf16[4,2,128,512]{3,2,1,0:T(8,128)(2,1)S(1)} %copy-done, bf16[4,2,128,512]{3,2,1,0:T(8,128)(2,1)S(1)} %copy-done, bf16[4,2,128,512]{3,2,1,0:T(8,128)(2,1)S(1)} %copy-done, ...), custom_call_target="tpu_custom_call" | custom-call | flops 2000000000 | bytes 6000000 | tf_op jit(solution)/shard_map/final/pallas_call | solution.py:591
  (52 shorter events, 1.4 us)
Async XLA Ops:
  3.8 1.9 %copy-start.2 = (f32[32,32,512]{2,1,0:T(8,128)S(1)}, f32[32,32,512]{2,1,0:T(8,128)}, u32[]{:S(2)}) copy-start(f32[32,32,512]{2,1,0:T(8,128)} %x_ref.2) | copy-start | bytes 6291460
  3.8 1.9 %copy-start.4 = (bf16[256,256]{1,0:T(8,128)(2,1)S(1)}, bf16[256,256]{1,0:T(8,128)(2,1)}, u32[]{:S(2)}) copy-start(bf16[256,256]{1,0:T(8,128)(2,1)} %constant.26.clone.kxh_ref) | copy-start | bytes 393220
  3.8 1.9 %copy-start.5 = (bf16[256,256]{1,0:T(8,128)(2,1)S(1)}, bf16[256,256]{1,0:T(8,128)(2,1)}, u32[]{:S(2)}) copy-start(bf16[256,256]{1,0:T(8,128)(2,1)} %constant.27.clone.kxl_ref) | copy-start | bytes 393220
  4.5 6.6 %copy-start.3 = (f32[32,32,512]{2,1,0:T(8,128)S(1)}, f32[32,32,512]{2,1,0:T(8,128)}, u32[]{:S(2)}) copy-start(f32[32,32,512]{2,1,0:T(8,128)} %x_ref.3) | copy-start | bytes 6291460
  4.5 12.3 %collective-permute-start.1 = (f32[520,128]{1,0:T(8,128)S(1)}, f32[520,128]{1,0:T(8,128)S(1)}, u32[]{:S(2)}, u32[]{:S(2)}) collective-permute-start(f32[520,128]{1,0:T(8,128)S(1)} %get-tuple-element.35), channel_id=1, source_target_pairs={{0,2},{2,0},{4,6},{6,4},{1,3},{3,1},{5,7},{7,5},{8,10},{10,8},{12,... | collective-permute-start | bytes 798728 | tf_op jit(solution)/shard_map/ppermute | solution.py:450
  7.9 36.2 %copy-start.7 = (s32[4,32]{1,0:T(4,128)S(1)}, s32[4,32]{1,0:T(4,128)}, u32[]{:S(2)}) copy-start(s32[4,32]{1,0:T(4,128)} %open_ref.1) | copy-start | bytes 1540
  7.9 36.2 %copy-start.8 = (s32[4,32]{1,0:T(4,128)S(1)}, s32[4,32]{1,0:T(4,128)}, u32[]{:S(2)}) copy-start(s32[4,32]{1,0:T(4,128)} %owner_ref.1) | copy-start | bytes 1540
  7.9 36.2 %copy-start.9 = (f32[512]{0:T(512)S(1)}, f32[512]{0:T(512)}, u32[]{:S(2)}) copy-start(f32[512]{0:T(512)} %param.25) | copy-start | bytes 6148
  7.9 36.2 %copy-start.10 = (f32[32]{0:T(128)S(1)}, f32[32]{0:T(128)}, u32[]{:S(2)}) copy-start(f32[32]{0:T(128)} %sx_ref.1) | copy-start | bytes 388
  7.9 40.8 %copy-start.12 = (bf16[2,2,256,256]{3,2,1,0:T(8,128)(2,1)S(1)}, bf16[2,2,256,256]{3,2,1,0:T(8,128)(2,1)}, u32[]{:S(2)}) copy-start(bf16[2,2,256,256]{3,2,1,0:T(8,128)(2,1)} %constant.30.clone.refs_11_) | copy-start | bytes 1572868
  7.9 36.1 %collective-permute-start = (f32[33,32,128]{2,1,0:T(8,128)S(1)}, f32[33,32,128]{2,1,0:T(8,128)S(1)}, u32[]{:S(2)}, u32[]{:S(2)}) collective-permute-start(f32[33,32,128]{2,1,0:T(8,128)S(1)} %shard_map.185.refs_3_), channel_id=1, source_target_pairs={{0,1},{1,0},{2,3},{3,2},{4,5},{5,4},{6,7},{7,6},{8,9},{9,8},{10,11... | collective-permute-start | bytes 1622024 | tf_op jit(solution)/shard_map/ppermute | solution.py:453
  13.2 35.6 %collective-permute-start.6 = (f32[32,32,128]{2,1,0:T(8,128)S(1)}, f32[32,32,128]{2,1,0:T(8,128)S(1)}, u32[]{:S(2)}, u32[]{:S(2)}) collective-permute-start(f32[32,32,128]{2,1,0:T(8,128)S(1)} %shard_map.186.refs_4_), channel_id=1, source_target_pairs={{0,1},{1,0},{2,3},{3,2},{4,5},{5,4},{6,7},{7,6},{8,9},{9,8},{10,11... | collective-permute-start | bytes 1572872 | tf_op jit(solution)/shard_map/ppermute | solution.py:453
  13.2 9.3 %collective-permute-start.2 = (f32[520,128]{1,0:T(8,128)S(1)}, f32[520,128]{1,0:T(8,128)S(1)}, u32[]{:S(2)}, u32[]{:S(2)}) collective-permute-start(f32[520,128]{1,0:T(8,128)S(1)} %get-tuple-element.36), channel_id=1, source_target_pairs={{0,4},{2,6},{4,0},{6,2},{1,5},{3,7},{5,1},{7,3},{8,12},{10,14},{12... | collective-permute-start | bytes 798728 | tf_op jit(solution)/shard_map/ppermute | solution.py:450
  15.2 25.0 %collective-permute-start.12 = (f32[520,128]{1,0:T(8,128)S(1)}, f32[520,128]{1,0:T(8,128)S(1)}, u32[]{:S(2)}, u32[]{:S(2)}) collective-permute-start(f32[520,128]{1,0:T(8,128)S(1)} %get-tuple-element.34.refs_0_), channel_id=1, source_target_pairs={{0,1},{1,0},{2,3},{3,2},{4,5},{5,4},{6,7},{7,6},{8,9},{9,8},{10,11... | collective-permute-start | bytes 798728 | tf_op jit(solution)/shard_map/ppermute | solution.py:453
  16.7 27.3 %collective-permute-start.3 = (f32[520,128]{1,0:T(8,128)S(1)}, f32[520,128]{1,0:T(8,128)S(1)}, u32[]{:S(2)}, u32[]{:S(2)}) collective-permute-start(f32[520,128]{1,0:T(8,128)S(1)} %get-tuple-element.37), channel_id=1, source_target_pairs={{0,6},{2,4},{4,2},{6,0},{1,7},{3,5},{5,3},{7,1},{8,14},{10,12},{12... | collective-permute-start | bytes 798728 | tf_op jit(solution)/shard_map/ppermute | solution.py:450
  22.6 24.7 %collective-permute-start.4 = (f32[8,128]{1,0:T(8,128)S(1)}, f32[8,128]{1,0:T(8,128)S(1)}, u32[]{:S(2)}, u32[]{:S(2)}) collective-permute-start(f32[8,128]{1,0:T(8,128)S(1)} %get-tuple-element.39.refs_1_), channel_id=1, source_target_pairs={{0,8},{8,16},{16,24},{24,0},{1,9},{9,17},{17,25},{25,1},{2,10},{10... | collective-permute-start | bytes 12296 | tf_op jit(solution)/shard_map/ppermute | solution.py:456
  40.2 8.5 %collective-permute-start.5 = (f32[8,128]{1,0:T(8,128)S(1)}, f32[8,128]{1,0:T(8,128)S(1)}, u32[]{:S(2)}, u32[]{:S(2)}) collective-permute-start(f32[8,128]{1,0:T(8,128)S(1)} %get-tuple-element.39.refs_1_), channel_id=1, source_target_pairs={{0,24},{8,0},{16,8},{24,16},{1,25},{9,1},{17,9},{25,17},{2,26},{10... | collective-permute-start | bytes 12296 | tf_op jit(solution)/shard_map/ppermute | solution.py:456
  45.1 11.0 %collective-permute-start.13 = (f32[2,8,32,128]{3,2,1,0:T(8,128)S(1)}, f32[2,8,32,128]{3,2,1,0:T(8,128)S(1)}, u32[]{:S(2)}, u32[]{:S(2)}) collective-permute-start(f32[2,8,32,128]{3,2,1,0:T(8,128)S(1)} %get-tuple-element.53), channel_id=1, source_target_pairs={{0,1},{1,0},{2,3},{3,2},{4,5},{5,4},{6,7},{7,6},{8,9},{9,8},{10,11... | collective-permute-start | bytes 786440 | tf_op jit(solution)/shard_map/ppermute | solution.py:453
  46.7 13.3 %collective-permute-start.14 = (f32[2,8,32,128]{3,2,1,0:T(8,128)S(1)}, f32[2,8,32,128]{3,2,1,0:T(8,128)S(1)}, u32[]{:S(2)}, u32[]{:S(2)}) collective-permute-start(f32[2,8,32,128]{3,2,1,0:T(8,128)S(1)} %get-tuple-element.54), channel_id=1, source_target_pairs={{0,1},{1,0},{2,3},{3,2},{4,5},{5,4},{6,7},{7,6},{8,9},{9,8},{10,11... | collective-permute-start | bytes 786440 | tf_op jit(solution)/shard_map/ppermute | solution.py:453
  47.2 19.1 %collective-permute-start.15 = (f32[2,8,32,128]{3,2,1,0:T(8,128)S(1)}, f32[2,8,32,128]{3,2,1,0:T(8,128)S(1)}, u32[]{:S(2)}, u32[]{:S(2)}) collective-permute-start(f32[2,8,32,128]{3,2,1,0:T(8,128)S(1)} %get-tuple-element.56), channel_id=1, source_target_pairs={{0,1},{1,0},{2,3},{3,2},{4,5},{5,4},{6,7},{7,6},{8,9},{9,8},{10,11... | collective-permute-start | bytes 786440 | tf_op jit(solution)/shard_map/ppermute | solution.py:453
  48.8 11.2 %copy-start.13 = (bf16[2,2,128,256]{3,2,1,0:T(8,128)(2,1)S(1)}, bf16[2,2,128,256]{3,2,1,0:T(8,128)(2,1)}, u32[]{:S(2)}) copy-start(bf16[2,2,128,256]{3,2,1,0:T(8,128)(2,1)} %constant.31.clone.ki_ref) | copy-start | bytes 786436
  48.8 11.2 %copy-start.14 = (bf16[256,256]{1,0:T(8,128)(2,1)S(1)}, bf16[256,256]{1,0:T(8,128)(2,1)}, u32[]{:S(2)}) copy-start(bf16[256,256]{1,0:T(8,128)(2,1)} %constant.28.clone.kxh_ref) | copy-start | bytes 393220
  48.8 11.2 %copy-start.15 = (bf16[256,256]{1,0:T(8,128)(2,1)S(1)}, bf16[256,256]{1,0:T(8,128)(2,1)}, u32[]{:S(2)}) copy-start(bf16[256,256]{1,0:T(8,128)(2,1)} %constant.29.clone.kxl_ref) | copy-start | bytes 393220
  69.3 14.2 %collective-permute-start.18 = (f32[32,32,128]{2,1,0:T(8,128)S(1)}, f32[32,32,128]{2,1,0:T(8,128)S(1)}, u32[]{:S(2)}, u32[]{:S(2)}) collective-permute-start(f32[32,32,128]{2,1,0:T(8,128)S(1)} %get-tuple-element.63), channel_id=1, source_target_pairs={{0,6},{2,4},{4,2},{6,0},{1,7},{3,5},{5,3},{7,1},{8,14},{10,12},{12... | collective-permute-start | bytes 1572872 | tf_op jit(solution)/shard_map/ppermute | solution.py:450
  69.3 25.5 %collective-permute-start.17 = (f32[32,32,128]{2,1,0:T(8,128)S(1)}, f32[32,32,128]{2,1,0:T(8,128)S(1)}, u32[]{:S(2)}, u32[]{:S(2)}) collective-permute-start(f32[32,32,128]{2,1,0:T(8,128)S(1)} %get-tuple-element.62), channel_id=1, source_target_pairs={{0,4},{2,6},{4,0},{6,2},{1,5},{3,7},{5,1},{7,3},{8,12},{10,14},{12... | collective-permute-start | bytes 1572872 | tf_op jit(solution)/shard_map/ppermute | solution.py:450
  70.8 24.1 %collective-permute-start.7 = (f32[2,8,24,128]{3,2,1,0:T(8,128)S(1)}, f32[2,8,24,128]{3,2,1,0:T(8,128)S(1)}, u32[]{:S(2)}, u32[]{:S(2)}) collective-permute-start(f32[2,8,24,128]{3,2,1,0:T(8,128)S(1)} %get-tuple-element.44), channel_id=1, source_target_pairs={{0,2},{2,0},{4,6},{6,4},{1,3},{3,1},{5,7},{7,5},{8,10},{10,8},{12,... | collective-permute-start | bytes 589832 | tf_op jit(solution)/shard_map/ppermute | solution.py:450
  71.2 27.9 %collective-permute-start.8 = (f32[2,8,24,128]{3,2,1,0:T(8,128)S(1)}, f32[2,8,24,128]{3,2,1,0:T(8,128)S(1)}, u32[]{:S(2)}, u32[]{:S(2)}) collective-permute-start(f32[2,8,24,128]{3,2,1,0:T(8,128)S(1)} %get-tuple-element.45), channel_id=1, source_target_pairs={{0,4},{2,6},{4,0},{6,2},{1,5},{3,7},{5,1},{7,3},{8,12},{10,14},{12... | collective-permute-start | bytes 589832 | tf_op jit(solution)/shard_map/ppermute | solution.py:450
  72.7 30.5 %collective-permute-start.9 = (f32[2,8,24,128]{3,2,1,0:T(8,128)S(1)}, f32[2,8,24,128]{3,2,1,0:T(8,128)S(1)}, u32[]{:S(2)}, u32[]{:S(2)}) collective-permute-start(f32[2,8,24,128]{3,2,1,0:T(8,128)S(1)} %get-tuple-element.46), channel_id=1, source_target_pairs={{0,6},{2,4},{4,2},{6,0},{1,7},{3,5},{5,3},{7,1},{8,14},{10,12},{12... | collective-permute-start | bytes 589832 | tf_op jit(solution)/shard_map/ppermute | solution.py:450
  83.5 40.9 %collective-permute-start.16 = (f32[32,32,128]{2,1,0:T(8,128)S(1)}, f32[32,32,128]{2,1,0:T(8,128)S(1)}, u32[]{:S(2)}, u32[]{:S(2)}) collective-permute-start(f32[32,32,128]{2,1,0:T(8,128)S(1)} %get-tuple-element.61), channel_id=1, source_target_pairs={{0,2},{2,0},{4,6},{6,4},{1,3},{3,1},{5,7},{7,5},{8,10},{10,8},{12,... | collective-permute-start | bytes 1572872 | tf_op jit(solution)/shard_map/ppermute | solution.py:450
  94.8 29.5 %collective-permute-start.19 = (f32[32,32,128]{2,1,0:T(8,128)S(1)}, f32[32,32,128]{2,1,0:T(8,128)S(1)}, u32[]{:S(2)}, u32[]{:S(2)}) collective-permute-start(f32[32,32,128]{2,1,0:T(8,128)S(1)} %relay.1), channel_id=1, source_target_pairs={{0,2},{2,0},{4,6},{6,4},{1,3},{3,1},{5,7},{7,5},{8,10},{10,8},{12,... | collective-permute-start | bytes 1572872 | tf_op jit(solution)/shard_map/ppermute | solution.py:450
  103.2 13.9 %collective-permute-start.10 = (f32[4,8,24,128]{3,2,1,0:T(8,128)S(1)}, f32[4,8,24,128]{3,2,1,0:T(8,128)S(1)}, u32[]{:S(2)}, u32[]{:S(2)}) collective-permute-start(f32[4,8,24,128]{3,2,1,0:T(8,128)S(1)} %get-tuple-element.47), channel_id=1, source_target_pairs={{0,8},{8,16},{16,24},{24,0},{1,9},{9,17},{17,25},{25,1},{2,10},{10... | collective-permute-start | bytes 1179656 | tf_op jit(solution)/shard_map/ppermute | solution.py:456
  103.3 19.6 %collective-permute-start.11 = (f32[4,8,24,128]{3,2,1,0:T(8,128)S(1)}, f32[4,8,24,128]{3,2,1,0:T(8,128)S(1)}, u32[]{:S(2)}, u32[]{:S(2)}) collective-permute-start(f32[4,8,24,128]{3,2,1,0:T(8,128)S(1)} %get-tuple-element.48), channel_id=1, source_target_pairs={{0,24},{8,0},{16,8},{24,16},{1,25},{9,1},{17,9},{25,17},{2,26},{10... | collective-permute-start | bytes 1179656 | tf_op jit(solution)/shard_map/ppermute | solution.py:456
  (4 other events, 5.0 us)

commit v5 on v4

--- a/solution.py
+++ b/solution.py
@@ -129,7 +129,7 @@
         f_ref[i] = 1.0 / (1.0 + diff_ref[0:1, :] * rate)
 
 
-def order_kernel(nt, space, q_ref, me_ref, sx_ref, sy_ref, open_ref, owner_ref, diff_ref, sz_ref, n1_ref, *refs):
+def order_kernel(nt, space, q_ref, me_ref, sx_ref, sy_ref, open_ref, owner_ref, diff_ref, sz_ref, there_ref, *refs):
     ins, (u_ref, amp_ref, tab_ref, fo_ref, ft_ref), outs = refs[:nt], refs[nt : nt + 5], refs[nt + 5 :]
     steps = amp_ref.shape[1]
     rows = ins[0].shape[0] - steps
@@ -158,7 +158,7 @@
         b = tiles * (r % SUB) + r // SUB
         fo_ref[0, r : r + 1, :] = jnp.full((1, cq), sy_ref[b], F32)
     factor_into(fo_ref, sx_ref, diff_ref, fo_ref[0], sz)
-    factor_into(ft_ref, sx_ref, diff_ref, n1_ref[nx], sz)
+    factor_into(ft_ref, sx_ref, diff_ref, there_ref[nx], sz)
 
 
 def closed_rows(tab_ref, face, tiles, hy):
@@ -166,35 +166,39 @@
     return [tab_ref[base + i * SUB : base + (i + 1) * SUB, :] > 0 for i in range(tiles - 1)]
 
 
-def own_kernel(dims, q_ref, yc_ref, *refs):
-    nt, steps, nx, hy, cq = dims
-    params, (n0, s0, n1, s1, u_s, amp_s, tab_ref, f_s, ky_ref) = refs[:3], refs[3:12]
-    hands, (clos_ref, mo_ref, so_ref) = refs[12 : 12 + nt], refs[12 + nt : 15 + nt]
-    m_s, s_s, vd = refs[15 + nt :]
-    tiles = hy // SUB
+def transform_second(ky_ref, yc, here, there, own, oth):
+    nx, hy, cq = own.shape
     pack = ky_ref.shape[2] // (2 * hy)
     half = pack * hy
-    yc = yc_ref[0]
-
-    def ytrans(ag, _):
-        at = pl.ds(ag * pack, pack)
+
+    def step(ag, _):
+        ats = [pl.ds((2 * ag + i) * pack, pack) for i in range(2)]
         cols = [
-            jnp.concatenate([here[at].reshape(half, cq), there[at].reshape(half, cq)], axis=0)
-            for here, there in ((n0, n1), (s0, s1))
+            jnp.concatenate([here[at].reshape(half, cq), there[at].reshape(half, cq)], axis=0) for at in ats
         ]
         res = const_times(ky_ref[yc, 0], ky_ref[yc, 1], jnp.concatenate(cols, axis=1))
-        for f, own, oth in ((0, m_s, mo_ref), (1, s_s, so_ref)):
-            part = res[:, f * cq : (f + 1) * cq]
+        for i, at in enumerate(ats):
+            part = res[:, i * cq : (i + 1) * cq]
             own[at] = part[:half].reshape(pack, hy, cq)
             oth[at] = part[half:].reshape(pack, hy, cq)
         return 0
 
-    lax.fori_loop(0, nx // pack, ytrans, 0)
+    lax.fori_loop(0, nx // (2 * pack), step, 0)
+
+
+def np_edges(nx):
+    order = np_modes(nx)
+    edge = np_cosine(nx, order, np.zeros(nx)).astype(np.float64)
+    return edge, np_cosine(nx, order, np.ones(nx)).astype(np.float64) - edge
+
+
+def driven_kernel(dims, yc_ref, s0, s1, u_s, amp_s, f_s, ky_ref, vd, clos_ref, so_ref, s_s):
+    nt, steps, nx, hy, cq = dims
+    tiles = hy // SUB
+    transform_second(ky_ref, yc_ref[0], s0, s1, s_s, so_ref)
     ha = nx // 2
     chunk = min(SUB, ha)
-    order = np_modes(nx)
-    edge = np_cosine(nx, order, np.zeros(nx)).astype(np.float64)
-    slope = np_cosine(nx, order, np.ones(nx)).astype(np.float64) - edge
+    edge, slope = np_edges(nx)
     for j in range(tiles):
         rows = slice(j * SUB, (j + 1) * SUB)
         for par in range(2):
@@ -225,7 +229,38 @@
                         clos_ref[w, a, rows, :] = x
                     return tuple(cur)
 
-                lax.fori_loop(0, nt, window, tuple(m_s[a, rows, :] for a in modes))
+                lax.fori_loop(0, nt, window, (jnp.zeros((SUB, cq), F32),) * chunk)
+
+
+def own_kernel(dims, q_ref, yc_ref, *refs):
+    nt, steps, nx, hy, _ = dims
+    params, (n0, n1, driven, clos_in, tab_ref, f_s, ky_ref) = refs[:3], refs[3:10]
+    hands, (clos_ref, mo_ref) = refs[10 : 10 + nt], refs[10 + nt : 12 + nt]
+    m_s, vd = refs[12 + nt :]
+    tiles = hy // SUB
+    transform_second(ky_ref, yc_ref[0], n0, n1, m_s, mo_ref)
+    ha = nx // 2
+    edge, slope = np_edges(nx)
+    for j in range(tiles):
+        rows = slice(j * SUB, (j + 1) * SUB)
+        for par in range(2):
+            modes = [par * ha + i for i in range(ha)]
+            f = [f_s[a, rows, :] for a in modes]
+            ratio = [float(np.float32(slope[a] / edge[a])) for a in modes]
+
+            def window(w, cur, j=j, par=par, rows=rows, modes=modes, f=f, ratio=ratio):
+                cur = list(cur)
+                for k in range(steps):
+                    cur = [x * z for x, z in zip(cur, f)]
+                    m = w * steps + k
+                    vd[par, 0, m, j] = tree(cur)
+                    vd[par, 1, m, j] = tree([x * y for x, y in zip(cur, ratio)])
+                for a, x in zip(modes, cur):
+                    clos_ref[w, a, rows, :] = clos_in[w, a, rows, :] + x * float(np.float32(edge[a] ** -2))
+                return tuple(cur)
+
+            start = tuple(m_s[a, rows, :] * float(np.float32(edge[a] ** 2)) for a in modes)
+            lax.fori_loop(0, nt, window, start)
 
     params = [ref[...] for ref in params]
     for slot in range(nt):
@@ -235,8 +270,9 @@
             m = w * steps + k
             left, right = [], []
             for j in range(tiles):
-                ve, vo = vd[0, 0, m, j], vd[1, 0, m, j]
-                de, do = vd[0, 1, m, j], vd[1, 1, m, j]
+                ve, vo, de, do = (
+                    driven[par, kind, m, j] + vd[par, kind, m, j] for kind in range(2) for par in range(2)
+                )
                 p = [
                     jnp.where(
                         tab_ref[i * hy + j * SUB : i * hy + (j + 1) * SUB, :] == 0, params[i], params[i + 1]
@@ -264,33 +300,39 @@
 
 
 def other_kernel(
-    dims, late, q_ref, yc_ref, m_ref, s_ref, f_ref, amp_ref, clos_ref, ki_ref, kxh_ref, kxl_ref, own_ref, *refs
+    dims, stage, q_ref, yc_ref, m_ref, s_ref, f_ref, amp_ref, clos_ref, ki_ref, kxh_ref, kxl_ref, own_ref, *refs
 ):
     nt, steps, nx, hy, cq = dims
-    slots = late_slots(nt) if late else range(nt)
-    chunks, refs = (refs[:1], refs[1 + len(slots) :]) if late else (refs[: nt - 2], refs[nt - 2 :])
+    slots = late_slots(nt) if stage == 2 else range(nt)
+    given = nt - 3 if stage == 0 else 1
+    prior = 0 if stage == 0 else len(slots)
+    chunks, refs = refs[:given], refs[given + prior :]
     outs = refs[: len(slots)]
     st_ref, cl, t_s, x_s, u_s = refs[len(slots) :]
     q = q_ref[0]
-    edge = jnp.where(q == nt - 1, nt - 2, nt - 1)
-    lo, hi, base = (edge, nt, nt - 2) if late else (0, edge, 0)
-
-    def put(when, w, ref):
+    edge = jnp.where(q < nt - 2, nt - 2, nt - 3)
+    lo, hi = ((0, edge), (edge, edge + 1), (edge + 1, nt))[stage]
+
+    def put(when, at, ref):
         @pl.when(when)
         def _():
-            u_s[w - base] = ref[...]
-
-    if late:
-        put(q == nt - 1, nt - 1, own_ref)
-        put(q < nt - 1, nt - 1, chunks[0])
-        put(q == nt - 1, nt - 2, chunks[0])
-    else:
-        for w in range(nt - 1):
+            u_s[at] = ref[...]
+
+    if stage == 0:
+        for w in range(nt - 2):
             put(q == w, w, own_ref)
-            if w < nt - 2:
+            if w < nt - 3:
                 put(q > w, w, chunks[w])
             if w > 0:
                 put(q < w, w, chunks[w - 1])
+    elif stage == 1:
+        u_s[0] = chunks[0][...]
+    else:
+        put(q != nt - 2, 0, chunks[0])
+        put(q == nt - 2, 0, own_ref)
+        put(q == nt - 2, 1, chunks[0])
+        put(q == nt - 1, 1, own_ref)
+    base = lo
     tiles = hy // SUB
     ha = nx // 2
     for j in range(tiles):
@@ -353,25 +395,35 @@
         out_ref[...] = late_ref[...]
 
 
-def final_kernel(nt, q_ref, *refs):
-    ws, ins, (out_ref, wh, wl) = refs[:nt], refs[nt:-3], refs[-3:]
+def half_kernel(nt, q_ref, c_ref, *refs):
+    ins, (acc_ref, wh_ref, wl_ref) = refs[:2], refs[2:]
+    nx, hy, nz = acc_ref.shape
+    cq = nz // nt
+    q = q_ref[0]
+    for d in range(2, nt):
+        at = slice((d - 2) * cq, (d - 1) * cq)
+        wh_ref[at, :] = c_ref[jnp.bitwise_xor(q, d), 0]
+        wl_ref[at, :] = c_ref[jnp.bitwise_xor(q, d), 1]
+    wh, wl = (jnp.concatenate([c_ref[jnp.bitwise_xor(q, d), i] for d in range(2)], axis=0) for i in range(2))
+    for x in range(0, nx, SUB):
+        part = [ref[x : x + SUB].reshape(SUB * hy, cq) for ref in ins]
+        xh, xl = cut(jnp.concatenate(part, axis=1))
+        res = mm(xh, wh) + mm(xh, wl) + mm(xl, wh)
+        acc_ref[x : x + SUB] = res.reshape(SUB, hy, nz)
+
+
+def final_kernel(nt, q_ref, acc_ref, wh_ref, wl_ref, *refs):
+    ins, out_ref = refs[:-1], refs[-1]
     xb, hy, nz = out_ref.shape[1:]
     cq = nz // nt
-
-    @pl.when(pl.program_id(0) == 0)
-    def _():
-        for d in range(nt):
-            wh[d * cq : (d + 1) * cq, :] = ws[d][0]
-            wl[d * cq : (d + 1) * cq, :] = ws[d][1]
-
     parts = [x[...].reshape(xb * hy, cq) for x in ins]
     if nt == 4:
         relayed = parts.pop()
-        parts[2] = jnp.where(q_ref[0] == 3, relayed, parts[2])
-        parts[3] = jnp.where(q_ref[0] == 2, relayed, parts[3])
+        parts[0] = jnp.where(q_ref[0] == 3, relayed, parts[0])
+        parts[1] = jnp.where(q_ref[0] == 2, relayed, parts[1])
     xh, xl = cut(jnp.concatenate(parts, axis=1))
-    res = mm(xh, wh[...]) + mm(xh, wl[...]) + mm(xl, wh[...])
-    out_ref[0] = res.reshape(xb, hy, nz)
+    res = mm(xh, wh_ref[...]) + mm(xh, wl_ref[...]) + mm(xl, wh_ref[...])
+    out_ref[0] = acc_ref[...] + res.reshape(xb, hy, nz)
 
 
 def merge_kernel(nt, q_ref, *refs):
@@ -434,7 +486,7 @@
     nx, hy, nz = initial_state.shape
     nt = lax.axis_size("tm")
     ncores = lax.axis_size("cores")
-    assert ncores == 2 and nt & (nt - 1) == 0 and nt >= 2
+    assert ncores == 2 and nt & (nt - 1) == 0 and nt >= 4
     cq = nz // nt
     steps = source_amplitude.shape[0]
     tiles = hy // SUB
@@ -496,12 +548,12 @@
             cost_estimate=cost(1e9, 3e6),
         )(qv, spectrum_y, values, base, kxh, kxl)
 
-    n0 = forward(initial_state, 1)
-    n1 = swap(n0)
+    s0 = forward(heat_source, 1)
+    s1 = swap(s0)
     for d in range(1, nt):
         dealt[d] = xor_permute(dealt[d], d)
-    s0 = forward(heat_source, 0)
-    s1 = swap(s0)
+    n0 = forward(initial_state, 0)
+    n1 = swap(n0)
     right_param = along(robin_param, -1)
     left_param = along(robin_param, 1)
 
@@ -518,34 +570,44 @@
         name="order",
     )(
         qv, mev, spectrum_x, spectrum_y, open_flag, owner_side, diff_rows,
-        spectrum_z.reshape(nt, cq), n1, *dealt,
+        spectrum_z.reshape(nt, cq), s1, *dealt,
     )
     for i in range(nt - 1):
         chunks[i] = swap(chunks[i])
 
+    ends_shape, traces = sds(nt, nx, hy, cq), sds(2, 2, nt * steps, tiles, SUB, cq)
+    driven, clos, s_there = pl.pallas_call(
+        functools.partial(driven_kernel, dims),
+        out_shape=[traces, ends_shape, sds(nx, hy, cq)],
+        in_specs=[SM] + [VM] * 6,
+        out_specs=[VM] * 3,
+        scratch_shapes=[pltpu.VMEM((nx, hy, cq), F32)],
+        compiler_params=grant(18),
+        cost_estimate=cost(3e9, 6e6),
+        name="driven",
+    )(ycv, s0, s1, u_own, amps, f_own, ky)
     short = sds(2, steps, (tiles - 1) * SUB, cq)
-    *hands, clos, m_there, s_there = pl.pallas_call(
+    *hands, clos, m_there = pl.pallas_call(
         functools.partial(own_kernel, dims),
-        out_shape=[short] * nt + [sds(nt, nx, hy, cq), sds(nx, hy, cq), sds(nx, hy, cq)],
-        in_specs=[SM] * 2 + [VM] * 12,
-        out_specs=[VM] * (nt + 3),
-        scratch_shapes=[pltpu.VMEM((nx, hy, cq), F32)] * 2
-        + [pltpu.VMEM((2, 2, nt * steps, tiles, SUB, cq), F32)],
+        out_shape=[short] * nt + [ends_shape, sds(nx, hy, cq)],
+        in_specs=[SM] * 2 + [VM] * 10,
+        out_specs=[VM] * (nt + 2),
+        scratch_shapes=[pltpu.VMEM((nx, hy, cq), F32), pltpu.VMEM(traces.shape, F32)],
         compiler_params=grant(18),
-        cost_estimate=cost(4e9, 8e6),
+        cost_estimate=cost(3e9, 8e6),
         name="own",
-    )(qv, ycv, left_param, robin_param, right_param, n0, s0, n1, s1, u_own, amps, tab, f_own, ky)
+    )(qv, ycv, left_param, robin_param, right_param, n0, n1, driven, clos, tab, f_own, ky)
     for d in range(1, nt):
         hands[d] = xor_permute(hands[d], d)
 
     state, ends = m_there, [None] * nt
     piece = piece[:rows].reshape(2, steps, hy, cq)
-    for late, got in ((False, chunks[:-1]), (True, chunks[-1:])):
-        span = 2 if late else nt - 1
-        slots = late_slots(nt) if late else list(range(nt))
-        prior = [ends[d] for d in slots] if late else []
+    for stage, got in enumerate((chunks[:-2], chunks[-2:-1], chunks[-1:])):
+        span = (nt - 2, 1, 2)[stage]
+        slots = late_slots(nt) if stage == 2 else list(range(nt))
+        prior = [ends[d] for d in slots] if stage else []
         *outs, state = pl.pallas_call(
-            functools.partial(other_kernel, dims, late),
+            functools.partial(other_kernel, dims, stage),
             out_shape=[sds(nx, hy, cq)] * (len(slots) + 1),
             in_specs=[SM] * 2 + [VM] * (9 + len(got) + len(prior)),
             out_specs=[VM] * (len(slots) + 1),
@@ -557,13 +619,12 @@
             ],
             input_output_aliases={11 + len(got) + d: d for d in range(len(prior))},
             compiler_params=grant(18),
-            cost_estimate=cost(4e9, 4e6),
-            name="other1" if late else "other0",
+            cost_estimate=cost(2e9 * span, 2e6 * span),
         )(qv, ycv, state, s_there, f_there, amps, clos, ki, kxih, kxil, piece, *got, *prior)
         for d, out in zip(slots, outs):
             ends[d] = out
         for d in range(1, nt):
-            if late and d in slots or not late and d not in late_slots(nt):
+            if stage == 2 and d in slots or stage == 1 and d not in late_slots(nt):
                 ends[d] = xor_permute(ends[d], d)
     if nt == 4:
         passing = pl.pallas_call(
@@ -587,6 +648,15 @@
     )(qv, *hands)
     from_right = along(left, -1)
     from_left = along(right, 1)
+    acc, wh, wl = pl.pallas_call(
+        functools.partial(half_kernel, nt),
+        out_shape=[sds(nx, hy, nz)] + [jax.ShapeDtypeStruct(((nt - 2) * cq, nz), BF16)] * 2,
+        in_specs=[SM] + [VM] * 3,
+        out_specs=[VM] * 3,
+        compiler_params=grant(18),
+        cost_estimate=cost(1e9, 4e6),
+        name="half",
+    )(qv, base, ends[0], ends[1])
     xb = SUB
     window_end = pl.pallas_call(
         functools.partial(final_kernel, nt),
@@ -594,18 +664,15 @@
         grid_spec=pltpu.PrefetchScalarGridSpec(
             num_scalar_prefetch=1,
             grid=(nx // xb,),
-            in_specs=[
-                pl.BlockSpec((None, 2, cq, nz), lambda i, q, d=d: (jnp.bitwise_xor(q[0], d), 0, 0, 0))
-                for d in range(nt)
-            ]
-            + [pl.BlockSpec((xb, hy, cq), lambda i, q: (i, 0, 0))] * len(ends),
+            in_specs=[pl.BlockSpec((xb, hy, nz), lambda i, q: (i, 0, 0))]
+            + [pl.BlockSpec(wh.shape, lambda i, q: (0, 0))] * 2
+            + [pl.BlockSpec((xb, hy, cq), lambda i, q: (i, 0, 0))] * (len(ends) - 2),
             out_specs=pl.BlockSpec((1, xb, hy, nz), lambda i, q: (0, i, 0, 0)),
-            scratch_shapes=[pltpu.VMEM((nz, nz), BF16)] * 2,
         ),
         compiler_params=grant(18),
-        cost_estimate=cost(2e9, 6e6),
+        cost_estimate=cost(1e9, 6e6),
         name="final",
-    )(qv, *([base] * nt), *ends)
+    )(qv, acc, wh, wl, *ends[2:])
 
     robin_out = pl.pallas_call(
         functools.partial(spread_kernel, nt, steps),

time: 128 us -> 121 us (0.945)
  waiting for transfers between devices: 71.5 us -> 55.9 us
  Pallas kernels: 27.6 us -> 30.8 us
  local copies, waits for them, and re-layouts: 2.66 us -> 5.46 us
  starting transfers between devices: 23.9 us -> 26.5 us
    ppermute x10, waiting for transfers between devices: 36.1 us -> 22.6 us  [xor_permute(): return lax.ppermute(x, 'tm', [(i, i ^ d) for i in range(nt)])]
    pallas_call x2 -> x5, Pallas kernels: 9.28 us -> 16.5 us  [the longest x3 9.63 us: local(): pl.pallas_call(functools.partial(other_kernel, dims, stage), out_shape=[s...]
    ppermute x10, starting transfers between devices: 6.11 us -> 11.4 us  [xor_permute(): return lax.ppermute(x, 'tm', [(i, i ^ d) for i in range(nt)])]
    ppermute x6, waiting for transfers between devices: 19.6 us -> 15.8 us  [swap(): return lax.ppermute(x, 'cores', [(0, 1), (1, 0)])]
    pallas_call x1, Pallas kernels: 7.35 us -> 4.06 us  [local(): pl.pallas_call(functools.partial(own_kernel, dims), out_shape=[short] * n...]
    unnamed x32 -> x40, local copies, waits for them, and re-layouts: 2.64 us -> 5.44 us
    ppermute x4, starting transfers between devices: 9.57 us -> 7.52 us  [along(): lax.ppermute(x, 'space', [(i, (i + by) % space) for i in range(space)])]
    ppermute x4, waiting for transfers between devices: 15.8 us -> 17.5 us  [along(): lax.ppermute(x, 'space', [(i, (i + by) % space) for i in range(space)])]
  transfers between devices with their start and end apart: 20 -> 20, of which waited for: 9 -> 10; matrix products, arithmetic and copies ran while one was open for 0% -> 0% of each run, Pallas kernels for 16% -> 19%
where the time goes in v5:
time: 121 us
  waiting for transfers between devices  55.9 us (46%)
  Pallas kernels  30.8 us (25%)
  starting transfers between devices  26.5 us (22%)
  local copies, waits for them, and re-layouts  5.46 us (5%)
  between operations  2.25 us (2%)
    ppermute x10, waiting for transfers between devices, xor_permute(): return lax.ppermute(x, 'tm', [(i, i ^ d) for i in range(nt)])  22.6 us
    ppermute x4, waiting for transfers between devices, along(): lax.ppermute(x, 'space', [(i, (i + by) % space) for i in range(space)])  17.5 us
    ppermute x6, waiting for transfers between devices, swap(): return lax.ppermute(x, 'cores', [(0, 1), (1, 0)])  15.8 us
    ppermute x10, starting transfers between devices, xor_permute(): return lax.ppermute(x, 'tm', [(i, i ^ d) for i in range(nt)])  11.4 us
    pallas_call x3, Pallas kernels, local(): pl.pallas_call(functools.partial(other_kernel, dims, stage), out_shape=[s...  9.63 us
    ppermute x6, starting transfers between devices, swap(): return lax.ppermute(x, 'cores', [(0, 1), (1, 0)])  7.56 us
    ppermute x4, starting transfers between devices, along(): lax.ppermute(x, 'space', [(i, (i + by) % space) for i in range(space)])  7.52 us
    pallas_call x1, Pallas kernels, local(): pl.pallas_call(functools.partial(driven_kernel, dims), out_shape=[traces,...  5.84 us
  transfers between devices with their start and end apart: 20, of which 10 were waited for; matrix products, arithmetic and copies ran while one was open for 0% of the time, Pallas kernels for 19%

profile of v5, /device:TPU:0, one launch (start us, length us, event | category | flops | bytes accessed | tf_op | source)
XLA Modules:
  0.0 120.9 jit_solution(14090655213531036769)
XLA Ops:
  0.7 1.3 %copy-done.1 = bf16[4,2,128,512]{3,2,1,0:T(8,128)(2,1)S(1)} copy-done((bf16[4,2,128,512]{3,2,1,0:T(8,128)(2,1)S(1)}, bf16[4,2,128,512]{3,2,1,0:T(8,128)(2,1)}, u32[]{:S(2)}) %copy-start.1) | copy-done | bytes 1048600
  2.0 1.6 %copy-done.3 = f32[32,32,512]{2,1,0:T(8,128)S(1)} copy-done((f32[32,32,512]{2,1,0:T(8,128)S(1)}, f32[32,32,512]{2,1,0:T(8,128)}, u32[]{:S(2)}) %copy-start.3) | copy-done | bytes 2097176
  6.0 2.1 %shard_map.185.s0 = f32[33,32,128]{2,1,0:T(8,128)S(1)} custom-call(s32[1]{0:T(128)} %bitcast.q_ref, f32[32]{0:T(128)S(1)} %copy-done.9, f32[32,32,512]{2,1,0:T(8,128)S(1)} %copy-done.3, bf16[4,2,128,512]{3,2,1,0:T(8,128)(2,1)S(1)} %copy-done.1, bf16[256,256]{1,0:T(8,128)(2,1)S(1)} %copy-done.7, bf16[256,256]{1,0:T(8,128)(2,1)S(1)} %copy-done.5), custom_call_target="tpu_custom_call" | custom-call | flops 1000000000 | bytes 3000000 | tf_op jit(solution)/shard_map/pallas_call | solution.py:542
  8.2 3.1 %collective-permute-start = (f32[33,32,128]{2,1,0:T(8,128)S(1)}, f32[33,32,128]{2,1,0:T(8,128)S(1)}, u32[]{:S(2)}, u32[]{:S(2)}) collective-permute-start(f32[33,32,128]{2,1,0:T(8,128)S(1)} %shard_map.185.s0), channel_id=1, source_target_pairs={{0,1},{1,0},{2,3},{3,2},{4,5},{5,4},{6,7},{7,6},{8,9},{9,8},{10,11... | collective-permute-start | bytes 1622024 | tf_op jit(solution)/shard_map/ppermute | solution.py:505
  13.4 1.9 %collective-permute-start.2 = (f32[520,128]{1,0:T(8,128)S(1)}, f32[520,128]{1,0:T(8,128)S(1)}, u32[]{:S(2)}, u32[]{:S(2)}) collective-permute-start(f32[520,128]{1,0:T(8,128)S(1)} %get-tuple-element.46), channel_id=1, source_target_pairs={{0,4},{2,6},{4,0},{6,2},{1,5},{3,7},{5,1},{7,3},{8,12},{10,14},{12... | collective-permute-start | bytes 798728 | tf_op jit(solution)/shard_map/ppermute | solution.py:502
  15.5 2.1 %shard_map.186.refs_3_ = f32[32,32,128]{2,1,0:T(8,128)S(1)} custom-call(s32[1]{0:T(128)} %bitcast.q_ref, f32[32]{0:T(128)S(1)} %copy-done.10, f32[32,32,512]{2,1,0:T(8,128)S(1)} %copy-done.4, bf16[4,2,128,512]{3,2,1,0:T(8,128)(2,1)S(1)} %copy-done.2, bf16[256,256]{1,0:T(8,128)(2,1)S(1)} %copy-done.8, bf16[256,256]{1,0:T(8,128)(2,1)S(1)} %copy-done.6), custom_call_target="tpu_custom_call" | custom-call | flops 1000000000 | bytes 3000000 | tf_op jit(solution)/shard_map/pallas_call | solution.py:542
  17.7 11.5 %collective-permute-done.12 = f32[520,128]{1,0:T(8,128)S(1)} collective-permute-done((f32[520,128]{1,0:T(8,128)S(1)}, f32[520,128]{1,0:T(8,128)S(1)}, u32[]{:S(2)}, u32[]{:S(2)}) %collective-permute-start.12) | collective-permute-done | bytes 266272 | tf_op jit(solution)/shard_map/ppermute | solution.py:505
  29.2 1.7 %collective-permute-start.6 = (f32[32,32,128]{2,1,0:T(8,128)S(1)}, f32[32,32,128]{2,1,0:T(8,128)S(1)}, u32[]{:S(2)}, u32[]{:S(2)}) collective-permute-start(f32[32,32,128]{2,1,0:T(8,128)S(1)} %shard_map.186.refs_3_), channel_id=1, source_target_pairs={{0,1},{1,0},{2,3},{3,2},{4,5},{5,4},{6,7},{7,6},{8,9},{9,8},{10,11... | collective-permute-start | bytes 1572872 | tf_op jit(solution)/shard_map/ppermute | solution.py:505
  31.0 3.6 %collective-permute-start.5 = (f32[8,128]{1,0:T(8,128)S(1)}, f32[8,128]{1,0:T(8,128)S(1)}, u32[]{:S(2)}, u32[]{:S(2)}) collective-permute-start(f32[8,128]{1,0:T(8,128)S(1)} %get-tuple-element.49.refs_1_), channel_id=1, source_target_pairs={{0,24},{8,0},{16,8},{24,16},{1,25},{9,1},{17,9},{25,17},{2,26},{10... | collective-permute-start | bytes 12296 | tf_op jit(solution)/shard_map/ppermute | solution.py:508
  36.3 1.5 %collective-permute-start.14 = (f32[2,8,32,128]{3,2,1,0:T(8,128)S(1)}, f32[2,8,32,128]{3,2,1,0:T(8,128)S(1)}, u32[]{:S(2)}, u32[]{:S(2)}) collective-permute-start(f32[2,8,32,128]{3,2,1,0:T(8,128)S(1)} %get-tuple-element.67), channel_id=1, source_target_pairs={{0,1},{1,0},{2,3},{3,2},{4,5},{5,4},{6,7},{7,6},{8,9},{9,8},{10,11... | collective-permute-start | bytes 786440 | tf_op jit(solution)/shard_map/ppermute | solution.py:505
  37.8 5.8 %driven.1 = (f32[2,2,32,4,8,128]{5,4,3,2,1,0:T(8,128)S(1)}, f32[4,32,32,128]{3,2,1,0:T(8,128)S(1)}, f32[32,32,128]{2,1,0:T(8,128)S(1)}) custom-call(s32[1]{0:T(128)} %bitcast.2.yc_ref, f32[33,32,128]{2,1,0:T(8,128)S(1)} %shard_map.185.s0, f32[33,32,128]{2,1,0:T(8,128)S(1)} %collective-permute-done.there_ref.s1, ...), custom_call_target="tpu_custom_call" | custom-call | flops 3000000000 | bytes 6000000 | tf_op jit(solution)/shard_map/driven/pallas_call | solution.py:579
  44.3 4.1 %own.1 = (f32[2,8,24,128]{3,2,1,0:T(8,128)S(1)}, f32[2,8,24,128]{3,2,1,0:T(8,128)S(1)}, f32[2,8,24,128]{3,2,1,0:T(8,128)S(1)}, f32[2,8,24,128]{3,2,1,0:T(8,128)S...) custom-call(s32[1]{0:T(128)} %bitcast.q_ref, s32[1]{0:T(128)} %bitcast.2.yc_ref, ...), custom_call_target="tpu_custom_call" | custom-call | flops 3000000000 | bytes 8000000 | tf_op jit(solution)/shard_map/own/pallas_call | solution.py:590
  48.3 1.3 %collective-permute-done.13.refs_0_ = f32[2,8,32,128]{3,2,1,0:T(8,128)S(1)} collective-permute-done((f32[2,8,32,128]{3,2,1,0:T(8,128)S(1)}, f32[2,8,32,128]{3,2,1,0:T(8,128)S(1)}, u32[]{:S(2)}, u32[]{:S(2)}) %collective-permute-start.13) | collective-permute-done | bytes 262176 | tf_op jit(solution)/shard_map/ppermute | solution.py:505
  49.6 4.2 %shard_map.187 = (f32[32,32,128]{2,1,0:T(8,128)S(1)}, f32[32,32,128]{2,1,0:T(8,128)S(1)}, f32[32,32,128]{2,1,0:T(8,128)S(1)}, f32[32,32,128]{2,1,0:T(8,128)S(1)}, f32[32,32,128]{2,1,0:T(8,128)S(1)}) custom-call(s32[1]{0:T(128)} %bitcast.q_ref, s32[1]{0:T(128)} %bitcast.2.yc_ref, f32[32,32,128]{2,1,0:T(8,128)S(1)} %get-tuple-element.61.m_ref, ...), custom_call_target="tpu_custom_call" | custom-call | flops 4000000000 | bytes 4000000 | tf_op jit(solution)/shard_map/pallas_call | solution.py:609
  53.9 1.4 %collective-permute-done.14.refs_0_ = f32[2,8,32,128]{3,2,1,0:T(8,128)S(1)} collective-permute-done((f32[2,8,32,128]{3,2,1,0:T(8,128)S(1)}, f32[2,8,32,128]{3,2,1,0:T(8,128)S(1)}, u32[]{:S(2)}, u32[]{:S(2)}) %collective-permute-start.14) | collective-permute-done | bytes 262176 | tf_op jit(solution)/shard_map/ppermute | solution.py:505
  55.2 2.3 %shard_map.188 = (f32[32,32,128]{2,1,0:T(8,128)S(1)}, f32[32,32,128]{2,1,0:T(8,128)S(1)}, f32[32,32,128]{2,1,0:T(8,128)S(1)}, f32[32,32,128]{2,1,0:T(8,128)S(1)}, f32[32,32,128]{2,1,0:T(8,128)S(1)}) custom-call(s32[1]{0:T(128)} %bitcast.q_ref, s32[1]{0:T(128)} %bitcast.2.yc_ref, ...), custom_call_target="tpu_custom_call", output_to_operand_aliasing={{0}: (12, {}), {1}: (13, {}), {2}: (14, {}), {3}: (15, {})} | custom-call | flops 2000000000 | bytes 2000000 | tf_op jit(solution)/shard_map/pallas_call | solution.py:609
  57.6 1.6 %collective-permute-done.15.refs_0_ = f32[2,8,32,128]{3,2,1,0:T(8,128)S(1)} collective-permute-done((f32[2,8,32,128]{3,2,1,0:T(8,128)S(1)}, f32[2,8,32,128]{3,2,1,0:T(8,128)S(1)}, u32[]{:S(2)}, u32[]{:S(2)}) %collective-permute-start.15) | collective-permute-done | bytes 262176 | tf_op jit(solution)/shard_map/ppermute | solution.py:505
  59.2 3.1 %shard_map.189 = (f32[32,32,128]{2,1,0:T(8,128)S(1)}, f32[32,32,128]{2,1,0:T(8,128)S(1)}, f32[32,32,128]{2,1,0:T(8,128)S(1)}, f32[32,32,128]{2,1,0:T(8,128)}) custom-call(s32[1]{0:T(128)} %bitcast.q_ref, s32[1]{0:T(128)} %bitcast.2.yc_ref, f32[32,32,128]{2,1,0:T(8,128)S(1)} %get-tuple-element.72.m_ref, ...), custom_call_target="tpu_custom_call", output_to_operand_aliasing={{0}: (12, {}), {1}: (13, {}), {2}: (14, {})} | custom-call | flops 4000000000 | bytes 4000000 | tf_op jit(solution)/shard_map/pallas_call | solution.py:609
  62.3 1.2 collective-permute-start.18
  63.4 2.3 %collective-permute-start.17 = (f32[32,32,128]{2,1,0:T(8,128)S(1)}, f32[32,32,128]{2,1,0:T(8,128)S(1)}, u32[]{:S(2)}, u32[]{:S(2)}) collective-permute-start(f32[32,32,128]{2,1,0:T(8,128)S(1)} %get-tuple-element.82), channel_id=1, source_target_pairs={{0,4},{2,6},{4,0},{6,2},{1,5},{3,7},{5,1},{7,3},{8,12},{10,14},{12... | collective-permute-start | bytes 1572872 | tf_op jit(solution)/shard_map/ppermute | solution.py:502
  65.8 1.7 %collective-permute-start.8 = (f32[2,8,24,128]{3,2,1,0:T(8,128)S(1)}, f32[2,8,24,128]{3,2,1,0:T(8,128)S(1)}, u32[]{:S(2)}, u32[]{:S(2)}) collective-permute-start(f32[2,8,24,128]{3,2,1,0:T(8,128)S(1)} %get-tuple-element.57), channel_id=1, source_target_pairs={{0,4},{2,6},{4,0},{6,2},{1,5},{3,7},{5,1},{7,3},{8,12},{10,14},{12... | collective-permute-start | bytes 589832 | tf_op jit(solution)/shard_map/ppermute | solution.py:502
  67.6 6.9 %collective-permute-done.18.late_ref.refs_1_ = f32[32,32,128]{2,1,0:T(8,128)S(1)} collective-permute-done((f32[32,32,128]{2,1,0:T(8,128)S(1)}, f32[32,32,128]{2,1,0:T(8,128)S(1)}, u32[]{:S(2)}, u32[]{:S(2)}) %collective-permute-start.18) | collective-permute-done | bytes 524320 | tf_op jit(solution)/shard_map/ppermute | solution.py:502
  74.5 3.8 %collective-permute-start.16 = (f32[32,32,128]{2,1,0:T(8,128)S(1)}, f32[32,32,128]{2,1,0:T(8,128)S(1)}, u32[]{:S(2)}, u32[]{:S(2)}) collective-permute-start(f32[32,32,128]{2,1,0:T(8,128)S(1)} %get-tuple-element.78), channel_id=1, source_target_pairs={{0,2},{2,0},{4,6},{6,4},{1,3},{3,1},{5,7},{7,5},{8,10},{10,8},{12,... | collective-permute-start | bytes 1572872 | tf_op jit(solution)/shard_map/ppermute | solution.py:502
  78.3 11.4 %collective-permute-done.17.early_ref.refs_0_ = f32[32,32,128]{2,1,0:T(8,128)S(1)} collective-permute-done((f32[32,32,128]{2,1,0:T(8,128)S(1)}, f32[32,32,128]{2,1,0:T(8,128)S(1)}, u32[]{:S(2)}, u32[]{:S(2)}) %collective-permute-start.17) | collective-permute-done | bytes 524320 | tf_op jit(solution)/shard_map/ppermute | solution.py:502
  89.9 4.1 %collective-permute-done.8.refs_2_ = f32[2,8,24,128]{3,2,1,0:T(8,128)S(1)} collective-permute-done((f32[2,8,24,128]{3,2,1,0:T(8,128)S(1)}, f32[2,8,24,128]{3,2,1,0:T(8,128)S(1)}, u32[]{:S(2)}, u32[]{:S(2)}) %collective-permute-start.8) | collective-permute-done | bytes 196640 | tf_op jit(solution)/shard_map/ppermute | solution.py:502
  94.2 1.5 %collective-permute-start.10 = (f32[4,8,24,128]{3,2,1,0:T(8,128)S(1)}, f32[4,8,24,128]{3,2,1,0:T(8,128)S(1)}, u32[]{:S(2)}, u32[]{:S(2)}) collective-permute-start(f32[4,8,24,128]{3,2,1,0:T(8,128)S(1)} %get-tuple-element.59), channel_id=1, source_target_pairs={{0,8},{8,16},{16,24},{24,0},{1,9},{9,17},{17,25},{25,1},{2,10},{10... | collective-permute-start | bytes 1179656 | tf_op jit(solution)/shard_map/ppermute | solution.py:508
  95.7 2.4 %collective-permute-start.11 = (f32[4,8,24,128]{3,2,1,0:T(8,128)S(1)}, f32[4,8,24,128]{3,2,1,0:T(8,128)S(1)}, u32[]{:S(2)}, u32[]{:S(2)}) collective-permute-start(f32[4,8,24,128]{3,2,1,0:T(8,128)S(1)} %get-tuple-element.60), channel_id=1, source_target_pairs={{0,24},{8,0},{16,8},{24,16},{1,25},{9,1},{17,9},{25,17},{2,26},{10... | collective-permute-start | bytes 1179656 | tf_op jit(solution)/shard_map/ppermute | solution.py:508
  98.1 9.2 %collective-permute-done.10.left_ref = f32[4,8,24,128]{3,2,1,0:T(8,128)S(1)} collective-permute-done((f32[4,8,24,128]{3,2,1,0:T(8,128)S(1)}, f32[4,8,24,128]{3,2,1,0:T(8,128)S(1)}, u32[]{:S(2)}, u32[]{:S(2)}) %collective-permute-start.10) | collective-permute-done | bytes 393248 | tf_op jit(solution)/shard_map/ppermute | solution.py:508
  107.3 8.3 %collective-permute-done.11.right_ref = f32[4,8,24,128]{3,2,1,0:T(8,128)S(1)} collective-permute-done((f32[4,8,24,128]{3,2,1,0:T(8,128)S(1)}, f32[4,8,24,128]{3,2,1,0:T(8,128)S(1)}, u32[]{:S(2)}, u32[]{:S(2)}) %collective-permute-start.11) | collective-permute-done | bytes 393248 | tf_op jit(solution)/shard_map/ppermute | solution.py:508
  115.6 1.5 %spread.1 = f32[1,2,8,32,512]{4,3,2,1,0:T(8,128)} custom-call(s32[112,128]{1,0:T(8,128)S(1)} %get-tuple-element.48.refs_7_.tab_ref, f32[4,8,24,128]{3,2,1,0:T(8,128)S(1)} %collective-permute-done.10.left_ref, f32[4,8,24,128]{3,2,1,0:T(8,128)S(1)} %collective-permute-done.11.right_ref), custom_call_target="tpu_custom_call" | custom-call | bytes 2000000 | tf_op jit(solution)/shard_map/spread/pallas_call | solution.py:677
  117.1 1.0 half.1
  118.1 2.7 %final.1 = f32[1,32,32,512]{3,2,1,0:T(8,128)} custom-call(s32[1]{0:T(128)} %bitcast.q_ref, f32[32,32,512]{2,1,0:T(8,128)S(1)} %get-tuple-element.79.acc_ref, bf16[256,512]{1,0:T(8,128)(2,1)S(1)} %get-tuple-element.80.wh_ref, bf16[256,512]{1,0:T(8,128)(2,1)S(1)} %get-tuple-element.81.wl_ref, f32[32,32,128]{2,1,0:T(8,128)S(1)} %collective-permute-done.17.early_ref.refs_0_, ...), custom_call_target="tpu_custom_call" | custom-call | flops 1000000000 | bytes 6000000 | tf_op jit(solution)/shard_map/final/pallas_call | solution.py:661
  (63 shorter events, 6.2 us)
Async XLA Ops:
  0.6 11.9 %copy-start = (f32[1,2,8,32,512]{4,3,2,1,0:T(8,128)S(1)}, f32[1,2,8,32,512]{4,3,2,1,0:T(8,128)}, u32[]{:S(2)}) copy-start(f32[1,2,8,32,512]{4,3,2,1,0:T(8,128)} %refs_3_.1) | copy-start | bytes 3145732
  6.0 6.5 %copy-start.15 = (f32[8]{0:T(128)S(1)}, f32[8]{0:T(128)}, u32[]{:S(2)}) copy-start(f32[8]{0:T(128)} %amp_ref.1) | copy-start | bytes 100
  8.2 26.5 %collective-permute-start = (f32[33,32,128]{2,1,0:T(8,128)S(1)}, f32[33,32,128]{2,1,0:T(8,128)S(1)}, u32[]{:S(2)}, u32[]{:S(2)}) collective-permute-start(f32[33,32,128]{2,1,0:T(8,128)S(1)} %shard_map.185.s0), channel_id=1, source_target_pairs={{0,1},{1,0},{2,3},{3,2},{4,5},{5,4},{6,7},{7,6},{8,9},{9,8},{10,11... | collective-permute-start | bytes 1622024 | tf_op jit(solution)/shard_map/ppermute | solution.py:505
  12.5 3.0 %copy-start.2 = (bf16[4,2,128,512]{3,2,1,0:T(8,128)(2,1)S(1)}, bf16[4,2,128,512]{3,2,1,0:T(8,128)(2,1)}, u32[]{:S(2)}) copy-start(bf16[4,2,128,512]{3,2,1,0:T(8,128)(2,1)} %constant.25.clone.c_ref) | copy-start | bytes 3145732
  12.6 3.0 %copy-start.4 = (f32[32,32,512]{2,1,0:T(8,128)S(1)}, f32[32,32,512]{2,1,0:T(8,128)}, u32[]{:S(2)}) copy-start(f32[32,32,512]{2,1,0:T(8,128)} %x_ref.3) | copy-start | bytes 6291460
  13.2 16.0 %collective-permute-start.12 = (f32[520,128]{1,0:T(8,128)S(1)}, f32[520,128]{1,0:T(8,128)S(1)}, u32[]{:S(2)}, u32[]{:S(2)}) collective-permute-start(f32[520,128]{1,0:T(8,128)S(1)} %get-tuple-element.44.refs_0_), channel_id=1, source_target_pairs={{0,1},{1,0},{2,3},{3,2},{4,5},{5,4},{6,7},{7,6},{8,9},{9,8},{10,11... | collective-permute-start | bytes 798728 | tf_op jit(solution)/shard_map/ppermute | solution.py:505
  13.3 17.7 %collective-permute-start.1 = (f32[520,128]{1,0:T(8,128)S(1)}, f32[520,128]{1,0:T(8,128)S(1)}, u32[]{:S(2)}, u32[]{:S(2)}) collective-permute-start(f32[520,128]{1,0:T(8,128)S(1)} %get-tuple-element.45), channel_id=1, source_target_pairs={{0,2},{2,0},{4,6},{6,4},{1,3},{3,1},{5,7},{7,5},{8,10},{10,8},{12,... | collective-permute-start | bytes 798728 | tf_op jit(solution)/shard_map/ppermute | solution.py:502
  13.4 21.2 %collective-permute-start.2 = (f32[520,128]{1,0:T(8,128)S(1)}, f32[520,128]{1,0:T(8,128)S(1)}, u32[]{:S(2)}, u32[]{:S(2)}) collective-permute-start(f32[520,128]{1,0:T(8,128)S(1)} %get-tuple-element.46), channel_id=1, source_target_pairs={{0,4},{2,6},{4,0},{6,2},{1,5},{3,7},{5,1},{7,3},{8,12},{10,14},{12... | collective-permute-start | bytes 798728 | tf_op jit(solution)/shard_map/ppermute | solution.py:502
  15.3 19.3 %copy-start.11 = (s32[4,32]{1,0:T(4,128)S(1)}, s32[4,32]{1,0:T(4,128)}, u32[]{:S(2)}) copy-start(s32[4,32]{1,0:T(4,128)} %open_ref.1) | copy-start | bytes 1540
  15.3 19.4 %copy-start.12 = (s32[4,32]{1,0:T(4,128)S(1)}, s32[4,32]{1,0:T(4,128)}, u32[]{:S(2)}) copy-start(s32[4,32]{1,0:T(4,128)} %owner_ref.1) | copy-start | bytes 1540
  15.3 19.4 %copy-start.13 = (f32[512]{0:T(512)S(1)}, f32[512]{0:T(512)}, u32[]{:S(2)}) copy-start(f32[512]{0:T(512)} %param.25) | copy-start | bytes 6148
  15.3 19.4 %copy-start.14 = (f32[32]{0:T(128)S(1)}, f32[32]{0:T(128)}, u32[]{:S(2)}) copy-start(f32[32]{0:T(128)} %sx_ref.1) | copy-start | bytes 388
  15.3 22.5 %copy-start.16 = (bf16[2,2,256,256]{3,2,1,0:T(8,128)(2,1)S(1)}, bf16[2,2,256,256]{3,2,1,0:T(8,128)(2,1)}, u32[]{:S(2)}) copy-start(bf16[2,2,256,256]{3,2,1,0:T(8,128)(2,1)} %constant.30.clone.ky_ref.refs_9_) | copy-start | bytes 1572868
  15.3 19.3 %collective-permute-start.3 = (f32[520,128]{1,0:T(8,128)S(1)}, f32[520,128]{1,0:T(8,128)S(1)}, u32[]{:S(2)}, u32[]{:S(2)}) collective-permute-start(f32[520,128]{1,0:T(8,128)S(1)} %get-tuple-element.47), channel_id=1, source_target_pairs={{0,6},{2,4},{4,2},{6,0},{1,7},{3,5},{5,3},{7,1},{8,14},{10,12},{12... | collective-permute-start | bytes 798728 | tf_op jit(solution)/shard_map/ppermute | solution.py:502
  29.2 15.0 %collective-permute-start.6 = (f32[32,32,128]{2,1,0:T(8,128)S(1)}, f32[32,32,128]{2,1,0:T(8,128)S(1)}, u32[]{:S(2)}, u32[]{:S(2)}) collective-permute-start(f32[32,32,128]{2,1,0:T(8,128)S(1)} %shard_map.186.refs_3_), channel_id=1, source_target_pairs={{0,1},{1,0},{2,3},{3,2},{4,5},{5,4},{6,7},{7,6},{8,9},{9,8},{10,11... | collective-permute-start | bytes 1572872 | tf_op jit(solution)/shard_map/ppermute | solution.py:505
  31.0 12.6 %collective-permute-start.5 = (f32[8,128]{1,0:T(8,128)S(1)}, f32[8,128]{1,0:T(8,128)S(1)}, u32[]{:S(2)}, u32[]{:S(2)}) collective-permute-start(f32[8,128]{1,0:T(8,128)S(1)} %get-tuple-element.49.refs_1_), channel_id=1, source_target_pairs={{0,24},{8,0},{16,8},{24,16},{1,25},{9,1},{17,9},{25,17},{2,26},{10... | collective-permute-start | bytes 12296 | tf_op jit(solution)/shard_map/ppermute | solution.py:508
  34.6 9.6 %collective-permute-start.4 = (f32[8,128]{1,0:T(8,128)S(1)}, f32[8,128]{1,0:T(8,128)S(1)}, u32[]{:S(2)}, u32[]{:S(2)}) collective-permute-start(f32[8,128]{1,0:T(8,128)S(1)} %get-tuple-element.49.refs_1_), channel_id=1, source_target_pairs={{0,8},{8,16},{16,24},{24,0},{1,9},{9,17},{17,25},{25,1},{2,10},{10... | collective-permute-start | bytes 12296 | tf_op jit(solution)/shard_map/ppermute | solution.py:508
  35.7 13.9 %collective-permute-start.13 = (f32[2,8,32,128]{3,2,1,0:T(8,128)S(1)}, f32[2,8,32,128]{3,2,1,0:T(8,128)S(1)}, u32[]{:S(2)}, u32[]{:S(2)}) collective-permute-start(f32[2,8,32,128]{3,2,1,0:T(8,128)S(1)} %get-tuple-element.65), channel_id=1, source_target_pairs={{0,1},{1,0},{2,3},{3,2},{4,5},{5,4},{6,7},{7,6},{8,9},{9,8},{10,11... | collective-permute-start | bytes 786440 | tf_op jit(solution)/shard_map/ppermute | solution.py:505
  36.3 19.0 %collective-permute-start.14 = (f32[2,8,32,128]{3,2,1,0:T(8,128)S(1)}, f32[2,8,32,128]{3,2,1,0:T(8,128)S(1)}, u32[]{:S(2)}, u32[]{:S(2)}) collective-permute-start(f32[2,8,32,128]{3,2,1,0:T(8,128)S(1)} %get-tuple-element.67), channel_id=1, source_target_pairs={{0,1},{1,0},{2,3},{3,2},{4,5},{5,4},{6,7},{7,6},{8,9},{9,8},{10,11... | collective-permute-start | bytes 786440 | tf_op jit(solution)/shard_map/ppermute | solution.py:505
  43.6 15.5 %collective-permute-start.15 = (f32[2,8,32,128]{3,2,1,0:T(8,128)S(1)}, f32[2,8,32,128]{3,2,1,0:T(8,128)S(1)}, u32[]{:S(2)}, u32[]{:S(2)}) collective-permute-start(f32[2,8,32,128]{3,2,1,0:T(8,128)S(1)} %get-tuple-element.73), channel_id=1, source_target_pairs={{0,1},{1,0},{2,3},{3,2},{4,5},{5,4},{6,7},{7,6},{8,9},{9,8},{10,11... | collective-permute-start | bytes 786440 | tf_op jit(solution)/shard_map/ppermute | solution.py:505
  44.2 5.4 %copy-start.17 = (bf16[2,2,128,256]{3,2,1,0:T(8,128)(2,1)S(1)}, bf16[2,2,128,256]{3,2,1,0:T(8,128)(2,1)}, u32[]{:S(2)}) copy-start(bf16[2,2,128,256]{3,2,1,0:T(8,128)(2,1)} %constant.31.clone.ki_ref) | copy-start | bytes 786436
  44.2 5.4 %copy-start.18 = (bf16[256,256]{1,0:T(8,128)(2,1)S(1)}, bf16[256,256]{1,0:T(8,128)(2,1)}, u32[]{:S(2)}) copy-start(bf16[256,256]{1,0:T(8,128)(2,1)} %constant.29.clone.kxl_ref) | copy-start | bytes 393220
  44.2 5.4 %copy-start.19 = (bf16[256,256]{1,0:T(8,128)(2,1)S(1)}, bf16[256,256]{1,0:T(8,128)(2,1)}, u32[]{:S(2)}) copy-start(bf16[256,256]{1,0:T(8,128)(2,1)} %constant.28.clone.kxh_ref) | copy-start | bytes 393220
  62.3 12.2 %collective-permute-start.18 = (f32[32,32,128]{2,1,0:T(8,128)S(1)}, f32[32,32,128]{2,1,0:T(8,128)S(1)}, u32[]{:S(2)}, u32[]{:S(2)}) collective-permute-start(f32[32,32,128]{2,1,0:T(8,128)S(1)} %get-tuple-element.83), channel_id=1, source_target_pairs={{0,6},{2,4},{4,2},{6,0},{1,7},{3,5},{5,3},{7,1},{8,14},{10,12},{12... | collective-permute-start | bytes 1572872 | tf_op jit(solution)/shard_map/ppermute | solution.py:502
  63.4 26.3 %collective-permute-start.17 = (f32[32,32,128]{2,1,0:T(8,128)S(1)}, f32[32,32,128]{2,1,0:T(8,128)S(1)}, u32[]{:S(2)}, u32[]{:S(2)}) collective-permute-start(f32[32,32,128]{2,1,0:T(8,128)S(1)} %get-tuple-element.82), channel_id=1, source_target_pairs={{0,4},{2,6},{4,0},{6,2},{1,5},{3,7},{5,1},{7,3},{8,12},{10,14},{12... | collective-permute-start | bytes 1572872 | tf_op jit(solution)/shard_map/ppermute | solution.py:502
  65.7 24.1 %collective-permute-start.7 = (f32[2,8,24,128]{3,2,1,0:T(8,128)S(1)}, f32[2,8,24,128]{3,2,1,0:T(8,128)S(1)}, u32[]{:S(2)}, u32[]{:S(2)}) collective-permute-start(f32[2,8,24,128]{3,2,1,0:T(8,128)S(1)} %get-tuple-element.56), channel_id=1, source_target_pairs={{0,2},{2,0},{4,6},{6,4},{1,3},{3,1},{5,7},{7,5},{8,10},{10,8},{12,... | collective-permute-start | bytes 589832 | tf_op jit(solution)/shard_map/ppermute | solution.py:502
  65.8 28.1 %collective-permute-start.8 = (f32[2,8,24,128]{3,2,1,0:T(8,128)S(1)}, f32[2,8,24,128]{3,2,1,0:T(8,128)S(1)}, u32[]{:S(2)}, u32[]{:S(2)}) collective-permute-start(f32[2,8,24,128]{3,2,1,0:T(8,128)S(1)} %get-tuple-element.57), channel_id=1, source_target_pairs={{0,4},{2,6},{4,0},{6,2},{1,5},{3,7},{5,1},{7,3},{8,12},{10,14},{12... | collective-permute-start | bytes 589832 | tf_op jit(solution)/shard_map/ppermute | solution.py:502
  67.6 26.5 %collective-permute-start.9 = (f32[2,8,24,128]{3,2,1,0:T(8,128)S(1)}, f32[2,8,24,128]{3,2,1,0:T(8,128)S(1)}, u32[]{:S(2)}, u32[]{:S(2)}) collective-permute-start(f32[2,8,24,128]{3,2,1,0:T(8,128)S(1)} %get-tuple-element.58), channel_id=1, source_target_pairs={{0,6},{2,4},{4,2},{6,0},{1,7},{3,5},{5,3},{7,1},{8,14},{10,12},{12... | collective-permute-start | bytes 589832 | tf_op jit(solution)/shard_map/ppermute | solution.py:502
  74.5 42.6 %collective-permute-start.16 = (f32[32,32,128]{2,1,0:T(8,128)S(1)}, f32[32,32,128]{2,1,0:T(8,128)S(1)}, u32[]{:S(2)}, u32[]{:S(2)}) collective-permute-start(f32[32,32,128]{2,1,0:T(8,128)S(1)} %get-tuple-element.78), channel_id=1, source_target_pairs={{0,2},{2,0},{4,6},{6,4},{1,3},{3,1},{5,7},{7,5},{8,10},{10,8},{12,... | collective-permute-start | bytes 1572872 | tf_op jit(solution)/shard_map/ppermute | solution.py:502
  89.8 28.4 %collective-permute-start.19 = (f32[32,32,128]{2,1,0:T(8,128)S(1)}, f32[32,32,128]{2,1,0:T(8,128)S(1)}, u32[]{:S(2)}, u32[]{:S(2)}) collective-permute-start(f32[32,32,128]{2,1,0:T(8,128)S(1)} %relay.1), channel_id=1, source_target_pairs={{0,2},{2,0},{4,6},{6,4},{1,3},{3,1},{5,7},{7,5},{8,10},{10,8},{12,... | collective-permute-start | bytes 1572872 | tf_op jit(solution)/shard_map/ppermute | solution.py:502
  94.2 13.1 %collective-permute-start.10 = (f32[4,8,24,128]{3,2,1,0:T(8,128)S(1)}, f32[4,8,24,128]{3,2,1,0:T(8,128)S(1)}, u32[]{:S(2)}, u32[]{:S(2)}) collective-permute-start(f32[4,8,24,128]{3,2,1,0:T(8,128)S(1)} %get-tuple-element.59), channel_id=1, source_target_pairs={{0,8},{8,16},{16,24},{24,0},{1,9},{9,17},{17,25},{25,1},{2,10},{10... | collective-permute-start | bytes 1179656 | tf_op jit(solution)/shard_map/ppermute | solution.py:508
  95.7 19.9 %collective-permute-start.11 = (f32[4,8,24,128]{3,2,1,0:T(8,128)S(1)}, f32[4,8,24,128]{3,2,1,0:T(8,128)S(1)}, u32[]{:S(2)}, u32[]{:S(2)}) collective-permute-start(f32[4,8,24,128]{3,2,1,0:T(8,128)S(1)} %get-tuple-element.60), channel_id=1, source_target_pairs={{0,24},{8,0},{16,8},{24,16},{1,25},{9,1},{17,9},{25,17},{2,26},{10... | collective-permute-start | bytes 1179656 | tf_op jit(solution)/shard_map/ppermute | solution.py:508
  (8 other events, 14.2 us)

commit v6 on v5

--- a/solution.py
+++ b/solution.py
@@ -88,8 +88,24 @@
     return parts[0]
 
 
-def split_kernel(nt, q_ref, yc_ref, me_ref, amp_ref, diff_ref, par_ref, *refs):
-    ins, outs, diff_out, par_out = refs[:nt], refs[nt : 2 * nt], refs[2 * nt], refs[2 * nt + 1]
+def piece_kernel(q_ref, yc_ref, me_ref, robin_ref, out_ref, sem):
+    cq = out_ref.shape[3]
+    at = pl.ds(pl.multiple_of(q_ref[0] * cq, cq), cq)
+    copies = [
+        pltpu.make_async_copy(robin_ref.at[0, face, :, :, at], out_ref.at[face], sem.at[face]) for face in range(2)
+    ]
+    for copy in copies:
+        copy.start()
+    for copy in copies:
+        copy.wait()
+
+
+def split_kernel(nt, q_ref, amp_ref, *refs):
+    ins, (diff_ref, par_ref), refs = refs[:nt], refs[nt : nt + 2], refs[nt + 2 :]
+    outs, (diff_out, par_out, diff_s, par_s, sem) = refs[:nt], refs[nt:]
+    copies = [pltpu.make_async_copy(diff_ref, diff_s, sem.at[0]), pltpu.make_async_copy(par_ref, par_s, sem.at[1])]
+    for copy in copies:
+        copy.start()
     steps = amp_ref.shape[0]
     rows = outs[0].shape[0] - steps
     cq = outs[0].shape[1]
@@ -97,8 +113,10 @@
         outs[d][0:rows, :] = ins[d][...].reshape(rows, cq)
         for k in range(steps):
             outs[d][rows + k : rows + k + 1, :] = jnp.full((1, cq), amp_ref[k], F32)
-    diff_out[...] = jnp.full(diff_out.shape, diff_ref[0], F32)
-    par_out[...] = jnp.full(par_out.shape, par_ref[0], F32)
+    for copy in copies:
+        copy.wait()
+    diff_out[...] = jnp.full(diff_out.shape, diff_s[0], F32)
+    par_out[...] = jnp.full(par_out.shape, par_s[0], F32)
 
 
 def forward_block(x, c_ref, kxh_ref, kxl_ref):
@@ -299,16 +317,24 @@
     return [0, 1, 3] if nt == 4 else list(range(nt))
 
 
+def slot_parts(slots, nt, nx):
+    parts = []
+    for slot in slots:
+        cuts = (0, nx // 2, nx) if slot == nt - 1 else (0, nx)
+        parts += [(slot, lo, hi) for lo, hi in zip(cuts[:-1], cuts[1:])]
+    return parts
+
+
 def other_kernel(
     dims, stage, q_ref, yc_ref, m_ref, s_ref, f_ref, amp_ref, clos_ref, ki_ref, kxh_ref, kxl_ref, own_ref, *refs
 ):
     nt, steps, nx, hy, cq = dims
-    slots = late_slots(nt) if stage == 2 else range(nt)
+    parts = slot_parts(late_slots(nt) if stage == 2 else range(nt), nt, nx)
     given = nt - 3 if stage == 0 else 1
-    prior = 0 if stage == 0 else len(slots)
+    prior = 0 if stage == 0 else len(parts)
     chunks, refs = refs[:given], refs[given + prior :]
-    outs = refs[: len(slots)]
-    st_ref, cl, t_s, x_s, u_s = refs[len(slots) :]
+    outs = refs[: len(parts)]
+    st_ref, cl, t_s, x_s, u_s = refs[len(parts) :]
     q = q_ref[0]
     edge = jnp.where(q < nt - 2, nt - 2, nt - 3)
     lo, hi = ((0, edge), (edge, edge + 1), (edge + 1, nt))[stage]
@@ -374,21 +400,21 @@
             at = slice(yb * SUB, (yb + 1) * SUB)
             res = const_times(kxh_ref[...], kxl_ref[...], t_s[:, at, :].reshape(nx * SUB, cq))
             x_s[:, at, :] = res.reshape(nx, SUB, cq)
-        for slot, out in zip(slots, outs):
+        for (slot, r0, r1), out in zip(parts, outs):
 
             @pl.when(window_of(nt, q, slot) == w)
-            def _(out=out):
-                out[...] = x_s[...]
+            def _(out=out, r0=r0, r1=r1):
+                out[...] = x_s[r0:r1]
 
         return 0
 
     lax.fori_loop(lo, hi, back, 0)
 
 
-def relay_kernel(nt, q_ref, early_ref, late_ref, out_ref):
+def relay_kernel(nt, at, q_ref, early_ref, late_ref, out_ref):
     @pl.when(q_ref[0] == nt - 1)
     def _():
-        out_ref[...] = early_ref[...]
+        out_ref[...] = early_ref[at : at + out_ref.shape[0]]
 
     @pl.when(q_ref[0] != nt - 1)
     def _():
@@ -412,18 +438,27 @@
         acc_ref[x : x + SUB] = res.reshape(SUB, hy, nz)
 
 
-def final_kernel(nt, q_ref, acc_ref, wh_ref, wl_ref, *refs):
-    ins, out_ref = refs[:-1], refs[-1]
-    xb, hy, nz = out_ref.shape[1:]
+def final_kernel(nt, at, q_ref, acc_ref, wh_ref, wl_ref, *refs):
+    count = nt - 2 + (nt == 4)
+    ins, (out_ref, blocks, sem) = refs[:count], refs[-3:]
+    n, xb, hy, nz = blocks.shape
     cq = nz // nt
-    parts = [x[...].reshape(xb * hy, cq) for x in ins]
-    if nt == 4:
-        relayed = parts.pop()
-        parts[0] = jnp.where(q_ref[0] == 3, relayed, parts[0])
-        parts[1] = jnp.where(q_ref[0] == 2, relayed, parts[1])
-    xh, xl = cut(jnp.concatenate(parts, axis=1))
-    res = mm(xh, wh_ref[...]) + mm(xh, wl_ref[...]) + mm(xl, wh_ref[...])
-    out_ref[0] = acc_ref[...] + res.reshape(xb, hy, nz)
+    copies = []
+    for i in range(n):
+        rows = slice(i * xb, (i + 1) * xb)
+        whole = slice(at + i * xb, at + (i + 1) * xb)
+        parts = [x[whole if d < nt - 3 else rows].reshape(xb * hy, cq) for d, x in enumerate(ins)]
+        if nt == 4:
+            relayed = parts.pop()
+            parts[0] = jnp.where(q_ref[0] == 3, relayed, parts[0])
+            parts[1] = jnp.where(q_ref[0] == 2, relayed, parts[1])
+        xh, xl = cut(jnp.concatenate(parts, axis=1))
+        res = mm(xh, wh_ref[...]) + mm(xh, wl_ref[...]) + mm(xl, wh_ref[...])
+        blocks[i] = acc_ref[whole] + res.reshape(xb, hy, nz)
+        copies.append(pltpu.make_async_copy(blocks.at[i], out_ref.at[0, whole], sem.at[i]))
+        copies[-1].start()
+    for copy in copies:
+        copy.wait()
 
 
 def merge_kernel(nt, q_ref, *refs):
@@ -433,9 +468,10 @@
             outs[face][jnp.bitwise_xor(q_ref[0], d)] = ins[d][face]
 
 
-def spread_kernel(nt, steps, tab_ref, left_ref, right_ref, out_ref, line):
+def spread_kernel(nt, steps, tab_ref, left_ref, right_ref, out_ref, line, lanes, sem):
     hy = out_ref.shape[3]
     cq = out_ref.shape[4] // nt
+    copies = []
     tiles = hy // SUB
     zero = jnp.zeros((SUB, cq), F32)
     for face, ref in enumerate((left_ref, right_ref)):
@@ -452,10 +488,17 @@
                     else:
                         v = jnp.where(le[j - 1], r[j - 1], zero)
                     line[face, k, pl.ds(j, SUB, stride=tiles), :] = v
-                out_ref[0, face, k, :, c * cq : (c + 1) * cq] = line[face, k]
+                lanes[face, k, :, c * cq : (c + 1) * cq] = line[face, k]
                 return 0
 
             lax.fori_loop(0, steps, step, 0)
+        for part in range(2):
+            ks = slice(part * steps // 2, (part + 1) * steps // 2)
+            copy = pltpu.make_async_copy(lanes.at[face, ks], out_ref.at[0, face, ks], sem.at[2 * face + part])
+            copy.start()
+            copies.append(copy)
+    for copy in copies:
+        copy.wait()
 
 
 def sds(*shape):
@@ -515,28 +558,41 @@
 
     rows = 2 * steps * hy
     block = (None, 2, steps, hy, cq)
+    AN = pl.BlockSpec(memory_space=pl.ANY)
+    piece = pl.pallas_call(
+        piece_kernel,
+        out_shape=sds(2, steps, hy, cq),
+        in_specs=[SM] * 3 + [AN],
+        out_specs=VM,
+        scratch_shapes=[pltpu.SemaphoreType.DMA((2,))],
+        compiler_params=grant(60),
+        cost_estimate=cost(0, 5e5),
+        name="piece",
+    )(qv, ycv, mev, robin_in)
+    piece = swap(piece)
     cutting = pl.pallas_call(
         functools.partial(split_kernel, nt),
         out_shape=[sds(rows + steps, cq)] * nt + [sds(SUB, cq)] * 2,
         grid_spec=pltpu.PrefetchScalarGridSpec(
-            num_scalar_prefetch=3,
+            num_scalar_prefetch=1,
             grid=(1,),
-            in_specs=[SM] * 3
+            in_specs=[SM]
             + [
-                pl.BlockSpec(block, lambda i, q, y, z, d=d: (0, 0, 0, 0, jnp.bitwise_xor(q[0], d)))
+                pl.BlockSpec(block, lambda i, q, d=d: (0, 0, 0, 0, jnp.bitwise_xor(q[0], d)))
                 for d in range(nt)
-            ],
-            out_specs=[pl.BlockSpec((rows + steps, cq), lambda i, q, y, z: (0, 0))] * nt
-            + [pl.BlockSpec((SUB, cq), lambda i, q, y, z: (0, 0))] * 2,
+            ]
+            + [AN] * 2,
+            out_specs=[pl.BlockSpec((rows + steps, cq), lambda i, q: (0, 0))] * nt
+            + [pl.BlockSpec((SUB, cq), lambda i, q: (0, 0))] * 2,
+            scratch_shapes=[pltpu.SMEM((1,), F32)] * 2 + [pltpu.SemaphoreType.DMA((2,))],
         ),
         compiler_params=grant(18),
         cost_estimate=cost(0, 8 * nt * rows * cq),
         name="split",
     )
     *dealt, diff_rows, robin_param = cutting(
-        qv, ycv, mev, source_amplitude, diffusivity, robin_param, *([robin_in] * nt)
+        qv, source_amplitude, *([robin_in] * nt), diffusivity, robin_param
     )
-    piece = swap(dealt[0])
 
     def forward(values, planes):
         return pl.pallas_call(
@@ -600,17 +656,16 @@
     for d in range(1, nt):
         hands[d] = xor_permute(hands[d], d)
 
-    state, ends = m_there, [None] * nt
-    piece = piece[:rows].reshape(2, steps, hy, cq)
+    state, ends = m_there, {}
     for stage, got in enumerate((chunks[:-2], chunks[-2:-1], chunks[-1:])):
         span = (nt - 2, 1, 2)[stage]
-        slots = late_slots(nt) if stage == 2 else list(range(nt))
-        prior = [ends[d] for d in slots] if stage else []
+        parts = slot_parts(late_slots(nt) if stage == 2 else range(nt), nt, nx)
+        prior = [ends[part] for part in parts] if stage else []
         *outs, state = pl.pallas_call(
             functools.partial(other_kernel, dims, stage),
-            out_shape=[sds(nx, hy, cq)] * (len(slots) + 1),
+            out_shape=[sds(r1 - r0, hy, cq) for _, r0, r1 in parts] + [sds(nx, hy, cq)],
             in_specs=[SM] * 2 + [VM] * (9 + len(got) + len(prior)),
-            out_specs=[VM] * (len(slots) + 1),
+            out_specs=[VM] * (len(parts) + 1),
             scratch_shapes=[
                 pltpu.VMEM((span, nx, hy, cq), F32),
                 pltpu.VMEM((nx, hy, cq), F32),
@@ -621,22 +676,25 @@
             compiler_params=grant(18),
             cost_estimate=cost(2e9 * span, 2e6 * span),
         )(qv, ycv, state, s_there, f_there, amps, clos, ki, kxih, kxil, piece, *got, *prior)
-        for d, out in zip(slots, outs):
-            ends[d] = out
-        for d in range(1, nt):
-            if stage == 2 and d in slots or stage == 1 and d not in late_slots(nt):
-                ends[d] = xor_permute(ends[d], d)
-    if nt == 4:
+        for part, out in zip(parts, outs):
+            ends[part] = out
+        early = slot_parts([d for d in range(1, nt) if d not in late_slots(nt)], nt, nx)
+        for d, r0, r1 in (early, parts)[stage - 1] if stage else ():
+            if d:
+                ends[d, r0, r1] = xor_permute(ends[d, r0, r1], d)
+    middle = [ends[d, 0, nx] for d in range(nt - 1)]
+    lasts = [ends[nt - 1, r0, r1] for r0, r1 in ((0, nx // 2), (nx // 2, nx))]
+    passed = []
+    for h, last in enumerate(lasts if nt == 4 else []):
         passing = pl.pallas_call(
-            functools.partial(relay_kernel, nt),
-            out_shape=sds(nx, hy, cq),
+            functools.partial(relay_kernel, nt, h * nx // 2),
+            out_shape=sds(nx // 2, hy, cq),
             in_specs=[SM] + [VM] * 2,
             out_specs=VM,
             compiler_params=grant(18),
             cost_estimate=cost(0, 1e6),
-            name="relay",
-        )(qv, ends[2], ends[3])
-        ends.append(xor_permute(passing, 1))
+        )(qv, middle[2], last)
+        passed.append(xor_permute(passing, 1))
     left, right = pl.pallas_call(
         functools.partial(merge_kernel, nt),
         out_shape=[sds(nt, steps, (tiles - 1) * SUB, cq)] * 2,
@@ -656,35 +714,42 @@
         compiler_params=grant(18),
         cost_estimate=cost(1e9, 4e6),
         name="half",
-    )(qv, base, ends[0], ends[1])
-    xb = SUB
-    window_end = pl.pallas_call(
-        functools.partial(final_kernel, nt),
-        out_shape=sds(1, nx, hy, nz),
-        grid_spec=pltpu.PrefetchScalarGridSpec(
-            num_scalar_prefetch=1,
-            grid=(nx // xb,),
-            in_specs=[pl.BlockSpec((xb, hy, nz), lambda i, q: (i, 0, 0))]
-            + [pl.BlockSpec(wh.shape, lambda i, q: (0, 0))] * 2
-            + [pl.BlockSpec((xb, hy, cq), lambda i, q: (i, 0, 0))] * (len(ends) - 2),
-            out_specs=pl.BlockSpec((1, xb, hy, nz), lambda i, q: (0, i, 0, 0)),
-        ),
-        compiler_params=grant(18),
-        cost_estimate=cost(1e9, 6e6),
-        name="final",
-    )(qv, acc, wh, wl, *ends[2:])
+    )(qv, base, *middle[:2])
+    xb = 4
+    window_end = []
+    for h, last in enumerate(lasts):
+        operands = (qv, acc, wh, wl, *middle[2:], last, *passed[h : h + 1])
+        window_end = [
+            pl.pallas_call(
+                functools.partial(final_kernel, nt, h * nx // 2),
+                out_shape=sds(1, nx, hy, nz),
+                in_specs=[SM] + [VM] * (len(operands) - 1) + [AN] * len(window_end),
+                out_specs=AN,
+                scratch_shapes=[
+                    pltpu.VMEM((nx // 2 // xb, xb, hy, nz), F32),
+                    pltpu.SemaphoreType.DMA((nx // 2 // xb,)),
+                ],
+                input_output_aliases={len(operands): 0} if window_end else {},
+                compiler_params=grant(18),
+                cost_estimate=cost(1e9, 3e6),
+            )(*operands, *window_end)
+        ]
 
     robin_out = pl.pallas_call(
         functools.partial(spread_kernel, nt, steps),
         out_shape=sds(1, 2, steps, hy, nz),
         in_specs=[VM] * 3,
-        out_specs=VM,
-        scratch_shapes=[pltpu.VMEM((2, steps, hy, cq), F32)],
+        out_specs=AN,
+        scratch_shapes=[
+            pltpu.VMEM((2, steps, hy, cq), F32),
+            pltpu.VMEM((2, steps, hy, nz), F32),
+            pltpu.SemaphoreType.DMA((4,)),
+        ],
         compiler_params=grant(18),
         cost_estimate=cost(0, 2e6),
         name="spread",
     )(tab, from_left, from_right)
-    return robin_out, window_end
+    return robin_out, window_end[0]
 
 
 def solution(mesh):

time: 121 us -> 107 us (0.88)
  waiting for transfers between devices: 55.9 us -> 35.5 us
  Pallas kernels: 30.8 us -> 35.3 us
  starting transfers between devices: 26.5 us -> 28.5 us
    ppermute x6, waiting for transfers between devices: 15.8 us -> 2.89 us  [swap(): return lax.ppermute(x, 'cores', [(0, 1), (1, 0)])]
    ppermute x4, waiting for transfers between devices: 17.5 us -> 8.9 us  [along(): lax.ppermute(x, 'space', [(i, (i + by) % space) for i in range(space)])]
    pallas_call x3 -> x6, Pallas kernels: 3.4 us -> 6.49 us  [the longest x2 2.7 us: local(): pl.pallas_call(functools.partial(final_kernel, nt, h * nx // 2), out_shap...]
    ppermute x4, starting transfers between devices: 7.52 us -> 9.35 us  [along(): lax.ppermute(x, 'space', [(i, (i + by) % space) for i in range(space)])]
    ppermute x10 -> x12, waiting for transfers between devices: 22.6 us -> 23.7 us  [xor_permute(): return lax.ppermute(x, 'tm', [(i, i ^ d) for i in range(nt)])]
    ppermute x10 -> x12, starting transfers between devices: 11.4 us -> 11.6 us  [xor_permute(): return lax.ppermute(x, 'tm', [(i, i ^ d) for i in range(nt)])]
    unnamed x40 -> x38, local copies, waits for them, and re-layouts: 5.44 us -> 5.42 us
  transfers between devices with their start and end apart: 20 -> 22, of which waited for: 10 -> 10; matrix products, arithmetic and copies ran while one was open for 0% -> 0% of each run, Pallas kernels for 19% -> 30%
where the time goes in v6:
time: 107 us
  waiting for transfers between devices  35.5 us (33%)
  Pallas kernels  35.3 us (33%)
  starting transfers between devices  28.5 us (27%)
  local copies, waits for them, and re-layouts  5.42 us (5%)
  between operations  2.4 us (2%)
    ppermute x12, waiting for transfers between devices, xor_permute(): return lax.ppermute(x, 'tm', [(i, i ^ d) for i in range(nt)])  23.7 us
    ppermute x12, starting transfers between devices, xor_permute(): return lax.ppermute(x, 'tm', [(i, i ^ d) for i in range(nt)])  11.6 us
    pallas_call x3, Pallas kernels, local(): pl.pallas_call(functools.partial(other_kernel, dims, stage), out_shape=[s...  9.64 us
    ppermute x4, starting transfers between devices, along(): lax.ppermute(x, 'space', [(i, (i + by) % space) for i in range(space)])  9.35 us
    ppermute x4, waiting for transfers between devices, along(): lax.ppermute(x, 'space', [(i, (i + by) % space) for i in range(space)])  8.9 us
    ppermute x6, starting transfers between devices, swap(): return lax.ppermute(x, 'cores', [(0, 1), (1, 0)])  7.58 us
    pallas_call x1, Pallas kernels, local(): pl.pallas_call(functools.partial(driven_kernel, dims), out_shape=[traces,...  5.84 us
    unnamed x38, local copies, waits for them, and re-layouts  5.42 us
  transfers between devices with their start and end apart: 22, of which 10 were waited for; matrix products, arithmetic and copies ran while one was open for 0% of the time, Pallas kernels for 30%

profile of v6, /device:TPU:0, one launch (start us, length us, event | category | flops | bytes accessed | tf_op | source)
XLA Modules:
  0.0 107.0 jit_solution(17797670285573873527)
XLA Ops:
  2.0 1.6 %copy-done.3 = f32[32,32,512]{2,1,0:T(8,128)S(1)} copy-done((f32[32,32,512]{2,1,0:T(8,128)S(1)}, f32[32,32,512]{2,1,0:T(8,128)}, u32[]{:S(2)}) %copy-start.3) | copy-done | bytes 2097176
  6.0 2.2 %shard_map.185.s0 = f32[33,32,128]{2,1,0:T(8,128)S(1)} custom-call(s32[1]{0:T(128)} %bitcast.q_ref, f32[32]{0:T(128)S(1)} %copy-done.8, f32[32,32,512]{2,1,0:T(8,128)S(1)} %copy-done.3, bf16[4,2,128,512]{3,2,1,0:T(8,128)(2,1)S(1)} %copy-done.1, bf16[256,256]{1,0:T(8,128)(2,1)S(1)} %copy-done.5, bf16[256,256]{1,0:T(8,128)(2,1)S(1)} %copy-done.6), custom_call_target="tpu_custom_call" | custom-call | flops 1000000000 | bytes 3000000 | tf_op jit(solution)/shard_map/pallas_call | solution.py:598
  8.2 3.1 %collective-permute-start = (f32[33,32,128]{2,1,0:T(8,128)S(1)}, f32[33,32,128]{2,1,0:T(8,128)S(1)}, u32[]{:S(2)}, u32[]{:S(2)}) collective-permute-start(f32[33,32,128]{2,1,0:T(8,128)S(1)} %shard_map.185.s0), channel_id=1, source_target_pairs={{0,1},{1,0},{2,3},{3,2},{4,5},{5,4},{6,7},{7,6},{8,9},{9,8},{10,11... | collective-permute-start | bytes 1622024 | tf_op jit(solution)/shard_map/ppermute | solution.py:548
  12.6 2.0 %split.1 = (f32[520,128]{1,0:T(8,128)S(1)}, f32[520,128]{1,0:T(8,128)}, f32[520,128]{1,0:T(8,128)}, f32[520,128]{1,0:T(8,128)}, f32[8,128]{1,0:T(8,128)S(1)}, /*index=5*/f32[8,128]{1,0:T(8,128)S(1)}) custom-call(s32[1]{0:T(128)} %bitcast.q_ref, f32[8]{0:T(128)S(1)} %copy-done.14, f32[1,2,8,32,512]{4,3,2,1,0:T(8,128)S(1)} %copy-done, ...), custom_call_target="tpu_custom_call" | custom-call | bytes 2097152 | tf_op jit(solution)/shard_map/split/pallas_call | solution.py:593
  14.7 1.5 %collective-permute-start.2 = (f32[520,128]{1,0:T(8,128)}, f32[520,128]{1,0:T(8,128)}, u32[]{:S(2)}, u32[]{:S(2)}) collective-permute-start(f32[520,128]{1,0:T(8,128)} %get-tuple-element.49), channel_id=1, source_target_pairs={{0,4},{2,6},{4,0},{6,2},{1,5},{3,7},{5,1},{7,3},{8,12},{10,14},{12... | collective-permute-start | bytes 798728 | tf_op jit(solution)/shard_map/ppermute | solution.py:545
  16.6 2.1 %shard_map.186.refs_3_ = f32[32,32,128]{2,1,0:T(8,128)S(1)} custom-call(s32[1]{0:T(128)} %bitcast.q_ref, f32[32]{0:T(128)S(1)} %copy-done.9, f32[32,32,512]{2,1,0:T(8,128)S(1)} %copy-done.4, bf16[4,2,128,512]{3,2,1,0:T(8,128)(2,1)S(1)} %copy-done.2, bf16[256,256]{1,0:T(8,128)(2,1)S(1)} %copy-done.5, bf16[256,256]{1,0:T(8,128)(2,1)S(1)} %copy-done.7), custom_call_target="tpu_custom_call" | custom-call | flops 1000000000 | bytes 3000000 | tf_op jit(solution)/shard_map/pallas_call | solution.py:598
  19.1 1.8 %piece.1 = f32[2,8,32,128]{3,2,1,0:T(8,128)} custom-call(s32[1]{0:T(128)} %bitcast.q_ref, s32[1]{0:T(128)} %bitcast.3.yc_ref, s32[1]{0:T(128)} %bitcast.1.me_ref, f32[1,2,8,32,512]{4,3,2,1,0:T(8,128)} %robin_ref.1), custom_call_target="tpu_custom_call" | custom-call | bytes 500000 | tf_op jit(solution)/shard_map/piece/pallas_call | solution.py:562
  20.9 1.9 %collective-permute-start.4 = (f32[8,128]{1,0:T(8,128)S(1)}, f32[8,128]{1,0:T(8,128)S(1)}, u32[]{:S(2)}, u32[]{:S(2)}) collective-permute-start(f32[8,128]{1,0:T(8,128)S(1)} %get-tuple-element.52.refs_1_), channel_id=1, source_target_pairs={{0,8},{8,16},{16,24},{24,0},{1,9},{9,17},{17,25},{25,1},{2,10},{10... | collective-permute-start | bytes 12296 | tf_op jit(solution)/shard_map/ppermute | solution.py:551
  22.7 1.6 %collective-permute-done.2.refs_2_ = f32[520,128]{1,0:T(8,128)} collective-permute-done((f32[520,128]{1,0:T(8,128)}, f32[520,128]{1,0:T(8,128)}, u32[]{:S(2)}, u32[]{:S(2)}) %collective-permute-start.2) | collective-permute-done | bytes 266272 | tf_op jit(solution)/shard_map/ppermute | solution.py:545
  24.4 3.6 %collective-permute-start.5 = (f32[8,128]{1,0:T(8,128)S(1)}, f32[8,128]{1,0:T(8,128)S(1)}, u32[]{:S(2)}, u32[]{:S(2)}) collective-permute-start(f32[8,128]{1,0:T(8,128)S(1)} %get-tuple-element.52.refs_1_), channel_id=1, source_target_pairs={{0,24},{8,0},{16,8},{24,16},{1,25},{9,1},{17,9},{25,17},{2,26},{10... | collective-permute-start | bytes 12296 | tf_op jit(solution)/shard_map/ppermute | solution.py:551
  29.5 1.4 %order.1 = (f32[4,2,8,32,128]{4,3,2,1,0:T(8,128)S(1)}, f32[4,8,128]{2,1,0:T(8,128)S(1)}, s32[112,128]{1,0:T(8,128)S(1)}, f32[32,32,128]{2,1,0:T(8,128)S(1)}, f32...) custom-call(s32[1]{0:T(128)} %bitcast.q_ref, ...), custom_call_target="tpu_custom_call" | custom-call | bytes 3000000 | tf_op jit(solution)/shard_map/order/pallas_call | solution.py:617
  30.9 1.6 %collective-permute-start.13 = (f32[2,8,32,128]{3,2,1,0:T(8,128)S(1)}, f32[2,8,32,128]{3,2,1,0:T(8,128)S(1)}, u32[]{:S(2)}, u32[]{:S(2)}) collective-permute-start(f32[2,8,32,128]{3,2,1,0:T(8,128)S(1)} %get-tuple-element.68), channel_id=1, source_target_pairs={{0,1},{1,0},{2,3},{3,2},{4,5},{5,4},{6,7},{7,6},{8,9},{9,8},{10,11... | collective-permute-start | bytes 786440 | tf_op jit(solution)/shard_map/ppermute | solution.py:548
  32.5 5.8 %driven.1 = (f32[2,2,32,4,8,128]{5,4,3,2,1,0:T(8,128)S(1)}, f32[4,32,32,128]{3,2,1,0:T(8,128)S(1)}, f32[32,32,128]{2,1,0:T(8,128)S(1)}) custom-call(s32[1]{0:T(128)} %bitcast.3.yc_ref, f32[33,32,128]{2,1,0:T(8,128)S(1)} %shard_map.185.s0, f32[33,32,128]{2,1,0:T(8,128)S(1)} %collective-permute-done.there_ref.s1, ...), custom_call_target="tpu_custom_call" | custom-call | flops 3000000000 | bytes 6000000 | tf_op jit(solution)/shard_map/driven/pallas_call | solution.py:635
  39.0 1.5 %collective-permute-start.15 = (f32[2,8,32,128]{3,2,1,0:T(8,128)S(1)}, f32[2,8,32,128]{3,2,1,0:T(8,128)S(1)}, u32[]{:S(2)}, u32[]{:S(2)}) collective-permute-start(f32[2,8,32,128]{3,2,1,0:T(8,128)S(1)} %get-tuple-element.77), channel_id=1, source_target_pairs={{0,1},{1,0},{2,3},{3,2},{4,5},{5,4},{6,7},{7,6},{8,9},{9,8},{10,11... | collective-permute-start | bytes 786440 | tf_op jit(solution)/shard_map/ppermute | solution.py:548
  40.5 5.1 %own.1 = (f32[2,8,24,128]{3,2,1,0:T(8,128)S(1)}, f32[2,8,24,128]{3,2,1,0:T(8,128)S(1)}, f32[2,8,24,128]{3,2,1,0:T(8,128)S(1)}, f32[2,8,24,128]{3,2,1,0:T(8,128)S...) custom-call(s32[1]{0:T(128)} %bitcast.q_ref, s32[1]{0:T(128)} %bitcast.3.yc_ref, ...), custom_call_target="tpu_custom_call" | custom-call | flops 3000000000 | bytes 8000000 | tf_op jit(solution)/shard_map/own/pallas_call | solution.py:646
  46.9 4.2 %shard_map.187 = (f32[32,32,128]{2,1,0:T(8,128)S(1)}, f32[32,32,128]{2,1,0:T(8,128)S(1)}, f32[32,32,128]{2,1,0:T(8,128)S(1)}, f32[16,32,128]{2,1,0:T(8,128)S(1)}...) custom-call(s32[1]{0:T(128)} %bitcast.q_ref, s32[1]{0:T(128)} %bitcast.3.yc_ref, ...), custom_call_target="tpu_custom_call" | custom-call | flops 4000000000 | bytes 4000000 | tf_op jit(solution)/shard_map/pallas_call | solution.py:664
  51.1 1.4 %collective-permute-done.14.refs_0_ = f32[2,8,32,128]{3,2,1,0:T(8,128)S(1)} collective-permute-done((f32[2,8,32,128]{3,2,1,0:T(8,128)S(1)}, f32[2,8,32,128]{3,2,1,0:T(8,128)S(1)}, u32[]{:S(2)}, u32[]{:S(2)}) %collective-permute-start.14) | collective-permute-done | bytes 262176 | tf_op jit(solution)/shard_map/ppermute | solution.py:548
  52.5 2.3 %shard_map.188 = (f32[32,32,128]{2,1,0:T(8,128)S(1)}, f32[32,32,128]{2,1,0:T(8,128)S(1)}, f32[32,32,128]{2,1,0:T(8,128)S(1)}, f32[16,32,128]{2,1,0:T(8,128)S(1)}...) custom-call(s32[1]{0:T(128)} %bitcast.q_ref, ...), custom_call_target="tpu_custom_call", output_to_operand_aliasing={{0}: (12, {}), {1}: (13, {}), {2}: (14, {}), {3}: (15, {}),... | custom-call | flops 2000000000 | bytes 2000000 | tf_op jit(solution)/shard_map/pallas_call | solution.py:664
  54.8 2.1 %collective-permute-start.17 = (f32[32,32,128]{2,1,0:T(8,128)S(1)}, f32[32,32,128]{2,1,0:T(8,128)S(1)}, u32[]{:S(2)}, u32[]{:S(2)}) collective-permute-start(f32[32,32,128]{2,1,0:T(8,128)S(1)} %get-tuple-element.87), channel_id=1, source_target_pairs={{0,4},{2,6},{4,0},{6,2},{1,5},{3,7},{5,1},{7,3},{8,12},{10,14},{12... | collective-permute-start | bytes 1572872 | tf_op jit(solution)/shard_map/ppermute | solution.py:545
  57.2 3.1 %shard_map.189 = (f32[32,32,128]{2,1,0:T(8,128)S(1)}, f32[32,32,128]{2,1,0:T(8,128)S(1)}, f32[16,32,128]{2,1,0:T(8,128)S(1)}, f32[16,32,128]{2,1,0:T(8,128)S(1)}, f32[32,32,128]{2,1,0:T(8,128)}) custom-call(s32[1]{0:T(128)} %bitcast.q_ref, s32[1]{0:T(128)} %bitcast.3.yc_ref, ...), custom_call_target="tpu_custom_call", output_to_operand_aliasing={{0}: (12, {}), {1}: (13, {}), {2}: (14, {}), {3}: (15, {})} | custom-call | flops 4000000000 | bytes 4000000 | tf_op jit(solution)/shard_map/pallas_call | solution.py:664
  60.3 2.3 %collective-permute-start.20 = (f32[16,32,128]{2,1,0:T(8,128)S(1)}, f32[16,32,128]{2,1,0:T(8,128)S(1)}, u32[]{:S(2)}, u32[]{:S(2)}) collective-permute-start(f32[16,32,128]{2,1,0:T(8,128)S(1)} %get-tuple-element.89), channel_id=1, source_target_pairs={{0,6},{2,4},{4,2},{6,0},{1,7},{3,5},{5,3},{7,1},{8,14},{10,12},{12... | collective-permute-start | bytes 786440 | tf_op jit(solution)/shard_map/ppermute | solution.py:545
  62.7 1.4 %collective-permute-start.8 = (f32[2,8,24,128]{3,2,1,0:T(8,128)S(1)}, f32[2,8,24,128]{3,2,1,0:T(8,128)S(1)}, u32[]{:S(2)}, u32[]{:S(2)}) collective-permute-start(f32[2,8,24,128]{3,2,1,0:T(8,128)S(1)} %get-tuple-element.60), channel_id=1, source_target_pairs={{0,4},{2,6},{4,0},{6,2},{1,5},{3,7},{5,1},{7,3},{8,12},{10,14},{12... | collective-permute-start | bytes 589832 | tf_op jit(solution)/shard_map/ppermute | solution.py:545
  64.1 1.5 %collective-permute-start.9 = (f32[2,8,24,128]{3,2,1,0:T(8,128)S(1)}, f32[2,8,24,128]{3,2,1,0:T(8,128)S(1)}, u32[]{:S(2)}, u32[]{:S(2)}) collective-permute-start(f32[2,8,24,128]{3,2,1,0:T(8,128)S(1)} %get-tuple-element.61), channel_id=1, source_target_pairs={{0,6},{2,4},{4,2},{6,0},{1,7},{3,5},{5,3},{7,1},{8,14},{10,12},{12... | collective-permute-start | bytes 589832 | tf_op jit(solution)/shard_map/ppermute | solution.py:545
  65.5 13.5 %collective-permute-done.8.refs_2_ = f32[2,8,24,128]{3,2,1,0:T(8,128)S(1)} collective-permute-done((f32[2,8,24,128]{3,2,1,0:T(8,128)S(1)}, f32[2,8,24,128]{3,2,1,0:T(8,128)S(1)}, u32[]{:S(2)}, u32[]{:S(2)}) %collective-permute-start.8) | collective-permute-done | bytes 196640 | tf_op jit(solution)/shard_map/ppermute | solution.py:545
  80.1 1.6 %collective-permute-start.10 = (f32[4,8,24,128]{3,2,1,0:T(8,128)S(1)}, f32[4,8,24,128]{3,2,1,0:T(8,128)S(1)}, u32[]{:S(2)}, u32[]{:S(2)}) collective-permute-start(f32[4,8,24,128]{3,2,1,0:T(8,128)S(1)} %get-tuple-element.62), channel_id=1, source_target_pairs={{0,8},{8,16},{16,24},{24,0},{1,9},{9,17},{17,25},{25,1},{2,10},{10... | collective-permute-start | bytes 1179656 | tf_op jit(solution)/shard_map/ppermute | solution.py:551
  81.8 2.3 %collective-permute-start.11 = (f32[4,8,24,128]{3,2,1,0:T(8,128)S(1)}, f32[4,8,24,128]{3,2,1,0:T(8,128)S(1)}, u32[]{:S(2)}, u32[]{:S(2)}) collective-permute-start(f32[4,8,24,128]{3,2,1,0:T(8,128)S(1)} %get-tuple-element.63), channel_id=1, source_target_pairs={{0,24},{8,0},{16,8},{24,16},{1,25},{9,1},{17,9},{25,17},{2,26},{10... | collective-permute-start | bytes 1179656 | tf_op jit(solution)/shard_map/ppermute | solution.py:551
  84.0 1.4 %collective-permute-start.18 = (f32[16,32,128]{2,1,0:T(8,128)S(1)}, f32[16,32,128]{2,1,0:T(8,128)S(1)}, u32[]{:S(2)}, u32[]{:S(2)}) collective-permute-start(f32[16,32,128]{2,1,0:T(8,128)S(1)} %get-tuple-element.88), channel_id=1, source_target_pairs={{0,6},{2,4},{4,2},{6,0},{1,7},{3,5},{5,3},{7,1},{8,14},{10,12},{12... | collective-permute-start | bytes 786440 | tf_op jit(solution)/shard_map/ppermute | solution.py:545
  85.6 6.5 %collective-permute-done.18.late_ref.refs_1_ = f32[16,32,128]{2,1,0:T(8,128)S(1)} collective-permute-done((f32[16,32,128]{2,1,0:T(8,128)S(1)}, f32[16,32,128]{2,1,0:T(8,128)S(1)}, u32[]{:S(2)}, u32[]{:S(2)}) %collective-permute-start.18) | collective-permute-done | bytes 262176 | tf_op jit(solution)/shard_map/ppermute | solution.py:545
  94.0 7.7 %collective-permute-done.11.right_ref = f32[4,8,24,128]{3,2,1,0:T(8,128)S(1)} collective-permute-done((f32[4,8,24,128]{3,2,1,0:T(8,128)S(1)}, f32[4,8,24,128]{3,2,1,0:T(8,128)S(1)}, u32[]{:S(2)}, u32[]{:S(2)}) %collective-permute-start.11) | collective-permute-done | bytes 393248 | tf_op jit(solution)/shard_map/ppermute | solution.py:551
  101.7 1.4 %spread.1 = f32[1,2,8,32,512]{4,3,2,1,0:T(8,128)} custom-call(s32[112,128]{1,0:T(8,128)S(1)} %get-tuple-element.51.refs_7_.tab_ref, f32[4,8,24,128]{3,2,1,0:T(8,128)S(1)} %collective-permute-done.10.left_ref, f32[4,8,24,128]{3,2,1,0:T(8,128)S(1)} %collective-permute-done.11.right_ref), custom_call_target="tpu_custom_call" | custom-call | bytes 2000000 | tf_op jit(solution)/shard_map/spread/pallas_call | solution.py:738
  104.2 1.3 %shard_map.192.refs_3_ = f32[1,32,32,512]{3,2,1,0:T(8,128)} custom-call(s32[1]{0:T(128)} %bitcast.q_ref, f32[32,32,512]{2,1,0:T(8,128)S(1)} %get-tuple-element.84.acc_ref, bf16[256,512]{1,0:T(8,128)(2,1)S(1)} %get-tuple-element.85.wh_ref, bf16[256,512]{1,0:T(8,128)(2,1)S(1)} %get-tuple-element.86.wl_ref, ...), custom_call_target="tpu_custom_call" | custom-call | flops 1000000000 | bytes 3000000 | tf_op jit(solution)/shard_map/pallas_call | solution.py:723
  105.5 1.4 %shard_map.193 = f32[1,32,32,512]{3,2,1,0:T(8,128)} custom-call(s32[1]{0:T(128)} %bitcast.q_ref, f32[32,32,512]{2,1,0:T(8,128)S(1)} %get-tuple-element.84.acc_ref, bf16[256,512]{1,0:T(8,128)(2,1)S(1)} %get-tuple-element.85.wh_ref, bf16[256,512]{1,0:T(8,128)(2,1)S(1)} %get-tuple-element.86.wl_ref, ...), custom_call_target="tpu_custom_call", output_to_operand_aliasing={{}: (7, {})} | custom-call | flops 1000000000 | bytes 3000000 | tf_op jit(solution)/shard_map/pallas_call | solution.py:723
  (67 shorter events, 12.5 us)
Async XLA Ops:
  0.6 11.9 %copy-start = (f32[1,2,8,32,512]{4,3,2,1,0:T(8,128)S(1)}, f32[1,2,8,32,512]{4,3,2,1,0:T(8,128)}, u32[]{:S(2)}) copy-start(f32[1,2,8,32,512]{4,3,2,1,0:T(8,128)} %robin_ref.1) | copy-start | bytes 3145732
  6.0 6.5 %copy-start.14 = (f32[8]{0:T(128)S(1)}, f32[8]{0:T(128)}, u32[]{:S(2)}) copy-start(f32[8]{0:T(128)} %amp_ref.1) | copy-start | bytes 100
  8.2 21.3 %collective-permute-start = (f32[33,32,128]{2,1,0:T(8,128)S(1)}, f32[33,32,128]{2,1,0:T(8,128)S(1)}, u32[]{:S(2)}, u32[]{:S(2)}) collective-permute-start(f32[33,32,128]{2,1,0:T(8,128)S(1)} %shard_map.185.s0), channel_id=1, source_target_pairs={{0,1},{1,0},{2,3},{3,2},{4,5},{5,4},{6,7},{7,6},{8,9},{9,8},{10,11... | collective-permute-start | bytes 1622024 | tf_op jit(solution)/shard_map/ppermute | solution.py:548
  14.6 6.2 %collective-permute-start.1 = (f32[520,128]{1,0:T(8,128)}, f32[520,128]{1,0:T(8,128)S(1)}, u32[]{:S(2)}, u32[]{:S(2)}) collective-permute-start(f32[520,128]{1,0:T(8,128)} %get-tuple-element.48), channel_id=1, source_target_pairs={{0,2},{2,0},{4,6},{6,4},{1,3},{3,1},{5,7},{7,5},{8,10},{10,8},{12,... | collective-permute-start | bytes 798728 | tf_op jit(solution)/shard_map/ppermute | solution.py:545
  14.7 9.6 %collective-permute-start.2 = (f32[520,128]{1,0:T(8,128)}, f32[520,128]{1,0:T(8,128)}, u32[]{:S(2)}, u32[]{:S(2)}) collective-permute-start(f32[520,128]{1,0:T(8,128)} %get-tuple-element.49), channel_id=1, source_target_pairs={{0,4},{2,6},{4,0},{6,2},{1,5},{3,7},{5,1},{7,3},{8,12},{10,14},{12... | collective-permute-start | bytes 798728 | tf_op jit(solution)/shard_map/ppermute | solution.py:545
  16.2 13.2 %copy-start.10 = (s32[4,32]{1,0:T(4,128)S(1)}, s32[4,32]{1,0:T(4,128)}, u32[]{:S(2)}) copy-start(s32[4,32]{1,0:T(4,128)} %open_ref.1) | copy-start | bytes 1540
  16.3 13.2 %copy-start.11 = (s32[4,32]{1,0:T(4,128)S(1)}, s32[4,32]{1,0:T(4,128)}, u32[]{:S(2)}) copy-start(s32[4,32]{1,0:T(4,128)} %owner_ref.1) | copy-start | bytes 1540
  16.3 13.2 %copy-start.12 = (f32[512]{0:T(512)S(1)}, f32[512]{0:T(512)}, u32[]{:S(2)}) copy-start(f32[512]{0:T(512)} %param.25) | copy-start | bytes 6148
  16.3 13.2 %copy-start.13 = (f32[32]{0:T(128)S(1)}, f32[32]{0:T(128)}, u32[]{:S(2)}) copy-start(f32[32]{0:T(128)} %sx_ref.1) | copy-start | bytes 388
  16.3 12.7 %collective-permute-start.3 = (f32[520,128]{1,0:T(8,128)}, f32[520,128]{1,0:T(8,128)}, u32[]{:S(2)}, u32[]{:S(2)}) collective-permute-start(f32[520,128]{1,0:T(8,128)} %get-tuple-element.50), channel_id=1, source_target_pairs={{0,6},{2,4},{4,2},{6,0},{1,7},{3,5},{5,3},{7,1},{8,14},{10,12},{12... | collective-permute-start | bytes 798728 | tf_op jit(solution)/shard_map/ppermute | solution.py:545
  18.8 21.7 %collective-permute-start.6 = (f32[32,32,128]{2,1,0:T(8,128)S(1)}, f32[32,32,128]{2,1,0:T(8,128)}, u32[]{:S(2)}, u32[]{:S(2)}) collective-permute-start(f32[32,32,128]{2,1,0:T(8,128)S(1)} %shard_map.186.refs_3_), channel_id=1, source_target_pairs={{0,1},{1,0},{2,3},{3,2},{4,5},{5,4},{6,7},{7,6},{8,9},{9,8},{10,11... | collective-permute-start | bytes 1572872 | tf_op jit(solution)/shard_map/ppermute | solution.py:548
  19.1 13.4 %copy-start.15 = (bf16[2,2,256,256]{3,2,1,0:T(8,128)(2,1)S(1)}, bf16[2,2,256,256]{3,2,1,0:T(8,128)(2,1)}, u32[]{:S(2)}) copy-start(bf16[2,2,256,256]{3,2,1,0:T(8,128)(2,1)} %constant.30.clone.ky_ref.refs_9_) | copy-start | bytes 1572868
  20.9 17.5 %collective-permute-start.4 = (f32[8,128]{1,0:T(8,128)S(1)}, f32[8,128]{1,0:T(8,128)S(1)}, u32[]{:S(2)}, u32[]{:S(2)}) collective-permute-start(f32[8,128]{1,0:T(8,128)S(1)} %get-tuple-element.52.refs_1_), channel_id=1, source_target_pairs={{0,8},{8,16},{16,24},{24,0},{1,9},{9,17},{17,25},{25,1},{2,10},{10... | collective-permute-start | bytes 12296 | tf_op jit(solution)/shard_map/ppermute | solution.py:551
  24.4 14.6 %collective-permute-start.5 = (f32[8,128]{1,0:T(8,128)S(1)}, f32[8,128]{1,0:T(8,128)S(1)}, u32[]{:S(2)}, u32[]{:S(2)}) collective-permute-start(f32[8,128]{1,0:T(8,128)S(1)} %get-tuple-element.52.refs_1_), channel_id=1, source_target_pairs={{0,24},{8,0},{16,8},{24,16},{1,25},{9,1},{17,9},{25,17},{2,26},{10... | collective-permute-start | bytes 12296 | tf_op jit(solution)/shard_map/ppermute | solution.py:551
  29.0 16.7 %collective-permute-start.12 = (f32[2,8,32,128]{3,2,1,0:T(8,128)}, f32[2,8,32,128]{3,2,1,0:T(8,128)S(1)}, u32[]{:S(2)}, u32[]{:S(2)}) collective-permute-start(f32[2,8,32,128]{3,2,1,0:T(8,128)} %piece.1), channel_id=1, source_target_pairs={{0,1},{1,0},{2,3},{3,2},{4,5},{5,4},{6,7},{7,6},{8,9},{9,8},{10,11... | collective-permute-start | bytes 786440 | tf_op jit(solution)/shard_map/ppermute | solution.py:548
  30.9 15.9 %collective-permute-start.13 = (f32[2,8,32,128]{3,2,1,0:T(8,128)S(1)}, f32[2,8,32,128]{3,2,1,0:T(8,128)S(1)}, u32[]{:S(2)}, u32[]{:S(2)}) collective-permute-start(f32[2,8,32,128]{3,2,1,0:T(8,128)S(1)} %get-tuple-element.68), channel_id=1, source_target_pairs={{0,1},{1,0},{2,3},{3,2},{4,5},{5,4},{6,7},{7,6},{8,9},{9,8},{10,11... | collective-permute-start | bytes 786440 | tf_op jit(solution)/shard_map/ppermute | solution.py:548
  38.4 14.1 %collective-permute-start.14 = (f32[2,8,32,128]{3,2,1,0:T(8,128)S(1)}, f32[2,8,32,128]{3,2,1,0:T(8,128)S(1)}, u32[]{:S(2)}, u32[]{:S(2)}) collective-permute-start(f32[2,8,32,128]{3,2,1,0:T(8,128)S(1)} %get-tuple-element.70), channel_id=1, source_target_pairs={{0,1},{1,0},{2,3},{3,2},{4,5},{5,4},{6,7},{7,6},{8,9},{9,8},{10,11... | collective-permute-start | bytes 786440 | tf_op jit(solution)/shard_map/ppermute | solution.py:548
  39.0 18.3 %collective-permute-start.15 = (f32[2,8,32,128]{3,2,1,0:T(8,128)S(1)}, f32[2,8,32,128]{3,2,1,0:T(8,128)S(1)}, u32[]{:S(2)}, u32[]{:S(2)}) collective-permute-start(f32[2,8,32,128]{3,2,1,0:T(8,128)S(1)} %get-tuple-element.77), channel_id=1, source_target_pairs={{0,1},{1,0},{2,3},{3,2},{4,5},{5,4},{6,7},{7,6},{8,9},{9,8},{10,11... | collective-permute-start | bytes 786440 | tf_op jit(solution)/shard_map/ppermute | solution.py:548
  40.5 6.4 %copy-start.16 = (bf16[2,2,128,256]{3,2,1,0:T(8,128)(2,1)S(1)}, bf16[2,2,128,256]{3,2,1,0:T(8,128)(2,1)}, u32[]{:S(2)}) copy-start(bf16[2,2,128,256]{3,2,1,0:T(8,128)(2,1)} %constant.31.clone.ki_ref) | copy-start | bytes 786436
  40.5 6.4 %copy-start.17 = (bf16[256,256]{1,0:T(8,128)(2,1)S(1)}, bf16[256,256]{1,0:T(8,128)(2,1)}, u32[]{:S(2)}) copy-start(bf16[256,256]{1,0:T(8,128)(2,1)} %constant.28.clone.kxh_ref) | copy-start | bytes 393220
  40.5 6.4 %copy-start.18 = (bf16[256,256]{1,0:T(8,128)(2,1)S(1)}, bf16[256,256]{1,0:T(8,128)(2,1)}, u32[]{:S(2)}) copy-start(bf16[256,256]{1,0:T(8,128)(2,1)} %constant.29.clone.kxl_ref) | copy-start | bytes 393220
  45.6 19.9 %collective-permute-start.7 = (f32[2,8,24,128]{3,2,1,0:T(8,128)S(1)}, f32[2,8,24,128]{3,2,1,0:T(8,128)S(1)}, u32[]{:S(2)}, u32[]{:S(2)}) collective-permute-start(f32[2,8,24,128]{3,2,1,0:T(8,128)S(1)} %get-tuple-element.59), channel_id=1, source_target_pairs={{0,2},{2,0},{4,6},{6,4},{1,3},{3,1},{5,7},{7,5},{8,10},{10,8},{12,... | collective-permute-start | bytes 589832 | tf_op jit(solution)/shard_map/ppermute | solution.py:545
  54.8 30.7 %collective-permute-start.17 = (f32[32,32,128]{2,1,0:T(8,128)S(1)}, f32[32,32,128]{2,1,0:T(8,128)S(1)}, u32[]{:S(2)}, u32[]{:S(2)}) collective-permute-start(f32[32,32,128]{2,1,0:T(8,128)S(1)} %get-tuple-element.87), channel_id=1, source_target_pairs={{0,4},{2,6},{4,0},{6,2},{1,5},{3,7},{5,1},{7,3},{8,12},{10,14},{12... | collective-permute-start | bytes 1572872 | tf_op jit(solution)/shard_map/ppermute | solution.py:545
  60.3 23.7 %collective-permute-start.20 = (f32[16,32,128]{2,1,0:T(8,128)S(1)}, f32[16,32,128]{2,1,0:T(8,128)S(1)}, u32[]{:S(2)}, u32[]{:S(2)}) collective-permute-start(f32[16,32,128]{2,1,0:T(8,128)S(1)} %get-tuple-element.89), channel_id=1, source_target_pairs={{0,6},{2,4},{4,2},{6,0},{1,7},{3,5},{5,3},{7,1},{8,14},{10,12},{12... | collective-permute-start | bytes 786440 | tf_op jit(solution)/shard_map/ppermute | solution.py:545
  62.7 16.4 %collective-permute-start.8 = (f32[2,8,24,128]{3,2,1,0:T(8,128)S(1)}, f32[2,8,24,128]{3,2,1,0:T(8,128)S(1)}, u32[]{:S(2)}, u32[]{:S(2)}) collective-permute-start(f32[2,8,24,128]{3,2,1,0:T(8,128)S(1)} %get-tuple-element.60), channel_id=1, source_target_pairs={{0,4},{2,6},{4,0},{6,2},{1,5},{3,7},{5,1},{7,3},{8,12},{10,14},{12... | collective-permute-start | bytes 589832 | tf_op jit(solution)/shard_map/ppermute | solution.py:545
  64.1 16.0 %collective-permute-start.9 = (f32[2,8,24,128]{3,2,1,0:T(8,128)S(1)}, f32[2,8,24,128]{3,2,1,0:T(8,128)S(1)}, u32[]{:S(2)}, u32[]{:S(2)}) collective-permute-start(f32[2,8,24,128]{3,2,1,0:T(8,128)S(1)} %get-tuple-element.61), channel_id=1, source_target_pairs={{0,6},{2,4},{4,2},{6,0},{1,7},{3,5},{5,3},{7,1},{8,14},{10,12},{12... | collective-permute-start | bytes 589832 | tf_op jit(solution)/shard_map/ppermute | solution.py:545
  65.5 37.6 %collective-permute-start.16 = (f32[32,32,128]{2,1,0:T(8,128)S(1)}, f32[32,32,128]{2,1,0:T(8,128)S(1)}, u32[]{:S(2)}, u32[]{:S(2)}) collective-permute-start(f32[32,32,128]{2,1,0:T(8,128)S(1)} %get-tuple-element.83), channel_id=1, source_target_pairs={{0,2},{2,0},{4,6},{6,4},{1,3},{3,1},{5,7},{7,5},{8,10},{10,8},{12,... | collective-permute-start | bytes 1572872 | tf_op jit(solution)/shard_map/ppermute | solution.py:545
  80.1 13.9 %collective-permute-start.10 = (f32[4,8,24,128]{3,2,1,0:T(8,128)S(1)}, f32[4,8,24,128]{3,2,1,0:T(8,128)S(1)}, u32[]{:S(2)}, u32[]{:S(2)}) collective-permute-start(f32[4,8,24,128]{3,2,1,0:T(8,128)S(1)} %get-tuple-element.62), channel_id=1, source_target_pairs={{0,8},{8,16},{16,24},{24,0},{1,9},{9,17},{17,25},{25,1},{2,10},{10... | collective-permute-start | bytes 1179656 | tf_op jit(solution)/shard_map/ppermute | solution.py:551
  81.8 20.0 %collective-permute-start.11 = (f32[4,8,24,128]{3,2,1,0:T(8,128)S(1)}, f32[4,8,24,128]{3,2,1,0:T(8,128)S(1)}, u32[]{:S(2)}, u32[]{:S(2)}) collective-permute-start(f32[4,8,24,128]{3,2,1,0:T(8,128)S(1)} %get-tuple-element.63), channel_id=1, source_target_pairs={{0,24},{8,0},{16,8},{24,16},{1,25},{9,1},{17,9},{25,17},{2,26},{10... | collective-permute-start | bytes 1179656 | tf_op jit(solution)/shard_map/ppermute | solution.py:551
  84.0 8.1 %collective-permute-start.18 = (f32[16,32,128]{2,1,0:T(8,128)S(1)}, f32[16,32,128]{2,1,0:T(8,128)S(1)}, u32[]{:S(2)}, u32[]{:S(2)}) collective-permute-start(f32[16,32,128]{2,1,0:T(8,128)S(1)} %get-tuple-element.88), channel_id=1, source_target_pairs={{0,6},{2,4},{4,2},{6,0},{1,7},{3,5},{5,3},{7,1},{8,14},{10,12},{12... | collective-permute-start | bytes 786440 | tf_op jit(solution)/shard_map/ppermute | solution.py:545
  85.5 18.7 %collective-permute-start.21 = (f32[16,32,128]{2,1,0:T(8,128)S(1)}, f32[16,32,128]{2,1,0:T(8,128)S(1)}, u32[]{:S(2)}, u32[]{:S(2)}) collective-permute-start(f32[16,32,128]{2,1,0:T(8,128)S(1)} %shard_map.191), channel_id=1, source_target_pairs={{0,2},{2,0},{4,6},{6,4},{1,3},{3,1},{5,7},{7,5},{8,10},{10,8},{12,... | collective-permute-start | bytes 786440 | tf_op jit(solution)/shard_map/ppermute | solution.py:545
  92.1 13.4 %collective-permute-start.19 = (f32[16,32,128]{2,1,0:T(8,128)S(1)}, f32[16,32,128]{2,1,0:T(8,128)S(1)}, u32[]{:S(2)}, u32[]{:S(2)}) collective-permute-start(f32[16,32,128]{2,1,0:T(8,128)S(1)} %shard_map.190), channel_id=1, source_target_pairs={{0,2},{2,0},{4,6},{6,4},{1,3},{3,1},{5,7},{7,5},{8,10},{10,8},{12,... | collective-permute-start | bytes 786440 | tf_op jit(solution)/shard_map/ppermute | solution.py:545
  (9 other events, 21.6 us)

commit v7 on v6

--- a/solution.py
+++ b/solution.py
@@ -88,35 +88,16 @@
     return parts[0]
 
 
-def piece_kernel(q_ref, yc_ref, me_ref, robin_ref, out_ref, sem):
-    cq = out_ref.shape[3]
-    at = pl.ds(pl.multiple_of(q_ref[0] * cq, cq), cq)
-    copies = [
-        pltpu.make_async_copy(robin_ref.at[0, face, :, :, at], out_ref.at[face], sem.at[face]) for face in range(2)
-    ]
-    for copy in copies:
-        copy.start()
-    for copy in copies:
-        copy.wait()
-
-
-def split_kernel(nt, q_ref, amp_ref, *refs):
-    ins, (diff_ref, par_ref), refs = refs[:nt], refs[nt : nt + 2], refs[nt + 2 :]
-    outs, (diff_out, par_out, diff_s, par_s, sem) = refs[:nt], refs[nt:]
-    copies = [pltpu.make_async_copy(diff_ref, diff_s, sem.at[0]), pltpu.make_async_copy(par_ref, par_s, sem.at[1])]
-    for copy in copies:
-        copy.start()
+def split_kernel(nt, q_ref, yc_ref, me_ref, amp_ref, *refs):
+    ins, outs, piece_ref = refs[:nt], refs[nt : 2 * nt], refs[2 * nt]
     steps = amp_ref.shape[0]
     rows = outs[0].shape[0] - steps
     cq = outs[0].shape[1]
+    piece_ref[...] = ins[0][...]
     for d in range(nt):
         outs[d][0:rows, :] = ins[d][...].reshape(rows, cq)
         for k in range(steps):
             outs[d][rows + k : rows + k + 1, :] = jnp.full((1, cq), amp_ref[k], F32)
-    for copy in copies:
-        copy.wait()
-    diff_out[...] = jnp.full(diff_out.shape, diff_s[0], F32)
-    par_out[...] = jnp.full(par_out.shape, par_s[0], F32)
 
 
 def forward_block(x, c_ref, kxh_ref, kxl_ref):
@@ -139,6 +120,12 @@
     for t in range(tiles):
         at = slice(t * SUB, (t + 1) * SUB)
         out_ref[0:nx, at, :] = forward_block(x_ref[:, at, :], c_ref.at[q_ref[0]], kxh_ref, kxl_ref)
+
+
+def forward_second_kernel(q_ref, diff_ref, par_ref, x_ref, c_ref, kxh_ref, kxl_ref, out_ref, diff_out, par_out):
+    diff_out[...] = jnp.full(diff_out.shape, diff_ref[0], F32)
+    par_out[...] = jnp.full(par_out.shape, par_ref[0], F32)
+    forward_kernel(False, q_ref, None, x_ref, c_ref, kxh_ref, kxl_ref, out_ref)
 
 
 def factor_into(f_ref, sx_ref, diff_ref, sy, sz):
@@ -559,56 +546,48 @@
     rows = 2 * steps * hy
     block = (None, 2, steps, hy, cq)
     AN = pl.BlockSpec(memory_space=pl.ANY)
-    piece = pl.pallas_call(
-        piece_kernel,
-        out_shape=sds(2, steps, hy, cq),
-        in_specs=[SM] * 3 + [AN],
-        out_specs=VM,
-        scratch_shapes=[pltpu.SemaphoreType.DMA((2,))],
-        compiler_params=grant(60),
-        cost_estimate=cost(0, 5e5),
-        name="piece",
-    )(qv, ycv, mev, robin_in)
-    piece = swap(piece)
     cutting = pl.pallas_call(
         functools.partial(split_kernel, nt),
-        out_shape=[sds(rows + steps, cq)] * nt + [sds(SUB, cq)] * 2,
+        out_shape=[sds(rows + steps, cq)] * nt + [sds(2, steps, hy, cq)],
         grid_spec=pltpu.PrefetchScalarGridSpec(
-            num_scalar_prefetch=1,
+            num_scalar_prefetch=3,
             grid=(1,),
             in_specs=[SM]
             + [
-                pl.BlockSpec(block, lambda i, q, d=d: (0, 0, 0, 0, jnp.bitwise_xor(q[0], d)))
+                pl.BlockSpec(block, lambda i, q, y, z, d=d: (0, 0, 0, 0, jnp.bitwise_xor(q[0], d)))
                 for d in range(nt)
-            ]
-            + [AN] * 2,
-            out_specs=[pl.BlockSpec((rows + steps, cq), lambda i, q: (0, 0))] * nt
-            + [pl.BlockSpec((SUB, cq), lambda i, q: (0, 0))] * 2,
-            scratch_shapes=[pltpu.SMEM((1,), F32)] * 2 + [pltpu.SemaphoreType.DMA((2,))],
+            ],
+            out_specs=[pl.BlockSpec((rows + steps, cq), lambda i, q, y, z: (0, 0))] * nt
+            + [pl.BlockSpec((2, steps, hy, cq), lambda i, q, y, z: (0, 0, 0, 0))],
         ),
         compiler_params=grant(18),
         cost_estimate=cost(0, 8 * nt * rows * cq),
         name="split",
     )
-    *dealt, diff_rows, robin_param = cutting(
-        qv, source_amplitude, *([robin_in] * nt), diffusivity, robin_param
-    )
-
-    def forward(values, planes):
-        return pl.pallas_call(
-            functools.partial(forward_kernel, planes > 0),
-            out_shape=sds(nx + planes, hy, cq),
-            in_specs=[SM] * 2 + [VM] * 4,
-            out_specs=VM,
-            compiler_params=grant(18),
-            cost_estimate=cost(1e9, 3e6),
-        )(qv, spectrum_y, values, base, kxh, kxl)
-
-    s0 = forward(heat_source, 1)
-    s1 = swap(s0)
+    *dealt, piece = cutting(qv, ycv, mev, source_amplitude, *([robin_in] * nt))
+    piece = swap(piece)
     for d in range(1, nt):
         dealt[d] = xor_permute(dealt[d], d)
-    n0 = forward(initial_state, 0)
+
+    s0 = pl.pallas_call(
+        functools.partial(forward_kernel, True),
+        out_shape=sds(nx + 1, hy, cq),
+        in_specs=[SM] * 2 + [VM] * 4,
+        out_specs=VM,
+        compiler_params=grant(18),
+        cost_estimate=cost(1e9, 3e6),
+        name="forward0",
+    )(qv, spectrum_y, heat_source, base, kxh, kxl)
+    s1 = swap(s0)
+    n0, diff_rows, robin_param = pl.pallas_call(
+        forward_second_kernel,
+        out_shape=[sds(nx, hy, cq), sds(SUB, cq), sds(SUB, cq)],
+        in_specs=[SM] * 3 + [VM] * 4,
+        out_specs=[VM] * 3,
+        compiler_params=grant(18),
+        cost_estimate=cost(1e9, 3e6),
+        name="forward1",
+    )(qv, diffusivity, robin_param, initial_state, base, kxh, kxl)
     n1 = swap(n0)
     right_param = along(robin_param, -1)
     left_param = along(robin_param, 1)

time: 107 us -> 107 us (level)
  waiting for transfers between devices: 35.5 us -> 40.7 us
  Pallas kernels: 35.3 us -> 30.1 us
    ppermute x6, waiting for transfers between devices: 2.89 us -> 7.33 us  [swap(): return lax.ppermute(x, 'cores', [(0, 1), (1, 0)])]
    pallas_call x4 -> x3, Pallas kernels: 8.03 us -> 4.38 us  [the longest x1 2.14 us: local(): pl.pallas_call(functools.partial(forward_kernel, True), out_shape=sds(nx...]
    pallas_call x1, Pallas kernels: 5.13 us -> 4.05 us  [local(): pl.pallas_call(functools.partial(own_kernel, dims), out_shape=[short] * n...]
    unnamed x38 -> x40, local copies, waits for them, and re-layouts: 5.42 us -> 5.43 us
  transfers between devices with their start and end apart: 22 -> 22, of which waited for: 10 -> 10; matrix products, arithmetic and copies ran while one was open for 0% -> 0% of each run, Pallas kernels for 30% -> 25%
where the time goes in v7:
time: 107 us
  waiting for transfers between devices  40.7 us (38%)
  Pallas kernels  30.1 us (28%)
  starting transfers between devices  28.4 us (27%)
  local copies, waits for them, and re-layouts  5.43 us (5%)
  between operations  2.43 us (2%)
    ppermute x12, waiting for transfers between devices, xor_permute(): return lax.ppermute(x, 'tm', [(i, i ^ d) for i in range(nt)])  24.4 us
    ppermute x12, starting transfers between devices, xor_permute(): return lax.ppermute(x, 'tm', [(i, i ^ d) for i in range(nt)])  11.5 us
    pallas_call x3, Pallas kernels, local(): pl.pallas_call(functools.partial(other_kernel, dims, stage), out_shape=[s...  9.64 us
    ppermute x4, starting transfers between devices, along(): lax.ppermute(x, 'space', [(i, (i + by) % space) for i in range(space)])  9.31 us
    ppermute x4, waiting for transfers between devices, along(): lax.ppermute(x, 'space', [(i, (i + by) % space) for i in range(space)])  8.91 us
    ppermute x6, starting transfers between devices, swap(): return lax.ppermute(x, 'cores', [(0, 1), (1, 0)])  7.56 us
    ppermute x6, waiting for transfers between devices, swap(): return lax.ppermute(x, 'cores', [(0, 1), (1, 0)])  7.33 us
    pallas_call x1, Pallas kernels, local(): pl.pallas_call(functools.partial(driven_kernel, dims), out_shape=[traces,...  5.85 us
  transfers between devices with their start and end apart: 22, of which 10 were waited for; matrix products, arithmetic and copies ran while one was open for 0% of the time, Pallas kernels for 25%

profile of v7, /device:TPU:0, one launch (start us, length us, event | category | flops | bytes accessed | tf_op | source)
XLA Modules:
  0.0 107.0 jit_solution(5501727305611129157)
XLA Ops:
  0.7 1.7 %copy-done.1 = f32[32,32,512]{2,1,0:T(8,128)S(1)} copy-done((f32[32,32,512]{2,1,0:T(8,128)S(1)}, f32[32,32,512]{2,1,0:T(8,128)}, u32[]{:S(2)}) %copy-start.1) | copy-done | bytes 2097176
  2.3 1.2 %copy-done.2 = bf16[4,2,128,512]{3,2,1,0:T(8,128)(2,1)S(1)} copy-done((bf16[4,2,128,512]{3,2,1,0:T(8,128)(2,1)S(1)}, bf16[4,2,128,512]{3,2,1,0:T(8,128)(2,1)}, u32[]{:S(2)}) %copy-start.2) | copy-done | bytes 1048600
  6.0 2.1 %forward0.1.s0 = f32[33,32,128]{2,1,0:T(8,128)S(1)} custom-call(s32[1]{0:T(128)} %bitcast.q_ref, f32[32]{0:T(128)S(1)} %copy-done.8, f32[32,32,512]{2,1,0:T(8,128)S(1)} %copy-done.1, bf16[4,2,128,512]{3,2,1,0:T(8,128)(2,1)S(1)} %copy-done.2, bf16[256,256]{1,0:T(8,128)(2,1)S(1)} %copy-done.6, bf16[256,256]{1,0:T(8,128)(2,1)S(1)} %copy-done.4), custom_call_target="tpu_custom_call" | custom-call | flops 1000000000 | bytes 3000000 | tf_op jit(solution)/shard_map/forward0/pallas_call | solution.py:572
  8.2 3.1 %collective-permute-start = (f32[33,32,128]{2,1,0:T(8,128)S(1)}, f32[33,32,128]{2,1,0:T(8,128)S(1)}, u32[]{:S(2)}, u32[]{:S(2)}) collective-permute-start(f32[33,32,128]{2,1,0:T(8,128)S(1)} %forward0.1.s0), channel_id=1, source_target_pairs={{0,1},{1,0},{2,3},{3,2},{4,5},{5,4},{6,7},{7,6},{8,9},{9,8},{10,11... | collective-permute-start | bytes 1622024 | tf_op jit(solution)/shard_map/ppermute | solution.py:535
  12.1 1.6 %collective-permute-start.2 = (f32[520,128]{1,0:T(8,128)S(1)}, f32[520,128]{1,0:T(8,128)S(1)}, u32[]{:S(2)}, u32[]{:S(2)}) collective-permute-start(f32[520,128]{1,0:T(8,128)S(1)} %get-tuple-element.51), channel_id=1, source_target_pairs={{0,4},{2,6},{4,0},{6,2},{1,5},{3,7},{5,1},{7,3},{8,12},{10,14},{12... | collective-permute-start | bytes 798728 | tf_op jit(solution)/shard_map/ppermute | solution.py:532
  15.3 1.6 %forward1.1 = (f32[32,32,128]{2,1,0:T(8,128)S(1)}, f32[8,128]{1,0:T(8,128)S(1)}, f32[8,128]{1,0:T(8,128)S(1)}) custom-call(s32[1]{0:T(128)} %bitcast.q_ref, f32[1]{0:T(128)S(6)} %copy.40.diff_ref, f32[1]{0:T(128)S(6)} %copy.41.par_ref, f32[32,32,512]{2,1,0:T(8,128)S(1)} %copy-done.15, bf16[4,2,128,512]{3,2,1,0:T(8,128)(2,1)S(1)} %copy-done.3, ...), custom_call_target="tpu_custom_call" | custom-call | flops 1000000000 | bytes 3000000 | tf_op jit(solution)/shard_map/forward1/pallas_call | solution.py:582
  17.2 3.9 %collective-permute-start.5 = (f32[8,128]{1,0:T(8,128)S(1)}, f32[8,128]{1,0:T(8,128)S(1)}, u32[]{:S(2)}, u32[]{:S(2)}) collective-permute-start(f32[8,128]{1,0:T(8,128)S(1)} %get-tuple-element.54.refs_1_), channel_id=1, source_target_pairs={{0,24},{8,0},{16,8},{24,16},{1,25},{9,1},{17,9},{25,17},{2,26},{10... | collective-permute-start | bytes 12296 | tf_op jit(solution)/shard_map/ppermute | solution.py:538
  21.4 1.6 %collective-permute-start.4 = (f32[8,128]{1,0:T(8,128)S(1)}, f32[8,128]{1,0:T(8,128)S(1)}, u32[]{:S(2)}, u32[]{:S(2)}) collective-permute-start(f32[8,128]{1,0:T(8,128)S(1)} %get-tuple-element.54.refs_1_), channel_id=1, source_target_pairs={{0,8},{8,16},{16,24},{24,0},{1,9},{9,17},{17,25},{25,1},{2,10},{10... | collective-permute-start | bytes 12296 | tf_op jit(solution)/shard_map/ppermute | solution.py:538
  23.0 3.0 %collective-permute-done.3.refs_3_ = f32[520,128]{1,0:T(8,128)S(1)} collective-permute-done((f32[520,128]{1,0:T(8,128)S(1)}, f32[520,128]{1,0:T(8,128)S(1)}, u32[]{:S(2)}, u32[]{:S(2)}) %collective-permute-start.3) | collective-permute-done | bytes 266272 | tf_op jit(solution)/shard_map/ppermute | solution.py:532
  27.5 1.6 %collective-permute-start.13 = (f32[2,8,32,128]{3,2,1,0:T(8,128)S(1)}, f32[2,8,32,128]{3,2,1,0:T(8,128)S(1)}, u32[]{:S(2)}, u32[]{:S(2)}) collective-permute-start(f32[2,8,32,128]{3,2,1,0:T(8,128)S(1)} %get-tuple-element.72), channel_id=1, source_target_pairs={{0,1},{1,0},{2,3},{3,2},{4,5},{5,4},{6,7},{7,6},{8,9},{9,8},{10,11... | collective-permute-start | bytes 786440 | tf_op jit(solution)/shard_map/ppermute | solution.py:535
  29.1 5.8 %driven.1 = (f32[2,2,32,4,8,128]{5,4,3,2,1,0:T(8,128)S(1)}, f32[4,32,32,128]{3,2,1,0:T(8,128)S(1)}, f32[32,32,128]{2,1,0:T(8,128)S(1)}) custom-call(s32[1]{0:T(128)} %bitcast.3.yc_ref, f32[33,32,128]{2,1,0:T(8,128)S(1)} %forward0.1.s0, f32[33,32,128]{2,1,0:T(8,128)S(1)} %collective-permute-done.there_ref.s1, ...), custom_call_target="tpu_custom_call" | custom-call | flops 3000000000 | bytes 6000000 | tf_op jit(solution)/shard_map/driven/pallas_call | solution.py:614
  35.5 1.6 %collective-permute-start.15 = (f32[2,8,32,128]{3,2,1,0:T(8,128)S(1)}, f32[2,8,32,128]{3,2,1,0:T(8,128)S(1)}, u32[]{:S(2)}, u32[]{:S(2)}) collective-permute-start(f32[2,8,32,128]{3,2,1,0:T(8,128)S(1)} %get-tuple-element.81), channel_id=1, source_target_pairs={{0,1},{1,0},{2,3},{3,2},{4,5},{5,4},{6,7},{7,6},{8,9},{9,8},{10,11... | collective-permute-start | bytes 786440 | tf_op jit(solution)/shard_map/ppermute | solution.py:535
  37.1 4.1 %own.1 = (f32[2,8,24,128]{3,2,1,0:T(8,128)S(1)}, f32[2,8,24,128]{3,2,1,0:T(8,128)S(1)}, f32[2,8,24,128]{3,2,1,0:T(8,128)S(1)}, f32[2,8,24,128]{3,2,1,0:T(8,128)S...) custom-call(s32[1]{0:T(128)} %bitcast.q_ref, s32[1]{0:T(128)} %bitcast.3.yc_ref, ...), custom_call_target="tpu_custom_call" | custom-call | flops 3000000000 | bytes 8000000 | tf_op jit(solution)/shard_map/own/pallas_call | solution.py:625
  41.3 5.6 %collective-permute-done.13.refs_0_ = f32[2,8,32,128]{3,2,1,0:T(8,128)S(1)} collective-permute-done((f32[2,8,32,128]{3,2,1,0:T(8,128)S(1)}, f32[2,8,32,128]{3,2,1,0:T(8,128)S(1)}, u32[]{:S(2)}, u32[]{:S(2)}) %collective-permute-start.13) | collective-permute-done | bytes 262176 | tf_op jit(solution)/shard_map/ppermute | solution.py:535
  46.8 4.2 %shard_map.185 = (f32[32,32,128]{2,1,0:T(8,128)S(1)}, f32[32,32,128]{2,1,0:T(8,128)S(1)}, f32[32,32,128]{2,1,0:T(8,128)S(1)}, f32[16,32,128]{2,1,0:T(8,128)S(1)}...) custom-call(s32[1]{0:T(128)} %bitcast.q_ref, s32[1]{0:T(128)} %bitcast.3.yc_ref, ...), custom_call_target="tpu_custom_call" | custom-call | flops 4000000000 | bytes 4000000 | tf_op jit(solution)/shard_map/pallas_call | solution.py:643
  51.1 1.4 %collective-permute-done.14.refs_0_ = f32[2,8,32,128]{3,2,1,0:T(8,128)S(1)} collective-permute-done((f32[2,8,32,128]{3,2,1,0:T(8,128)S(1)}, f32[2,8,32,128]{3,2,1,0:T(8,128)S(1)}, u32[]{:S(2)}, u32[]{:S(2)}) %collective-permute-start.14) | collective-permute-done | bytes 262176 | tf_op jit(solution)/shard_map/ppermute | solution.py:535
  52.4 2.3 %shard_map.186 = (f32[32,32,128]{2,1,0:T(8,128)S(1)}, f32[32,32,128]{2,1,0:T(8,128)S(1)}, f32[32,32,128]{2,1,0:T(8,128)S(1)}, f32[16,32,128]{2,1,0:T(8,128)S(1)}...) custom-call(s32[1]{0:T(128)} %bitcast.q_ref, ...), custom_call_target="tpu_custom_call", output_to_operand_aliasing={{0}: (12, {}), {1}: (13, {}), {2}: (14, {}), {3}: (15, {}),... | custom-call | flops 2000000000 | bytes 2000000 | tf_op jit(solution)/shard_map/pallas_call | solution.py:643
  54.8 2.0 %collective-permute-start.17 = (f32[32,32,128]{2,1,0:T(8,128)S(1)}, f32[32,32,128]{2,1,0:T(8,128)S(1)}, u32[]{:S(2)}, u32[]{:S(2)}) collective-permute-start(f32[32,32,128]{2,1,0:T(8,128)S(1)} %get-tuple-element.91), channel_id=1, source_target_pairs={{0,4},{2,6},{4,0},{6,2},{1,5},{3,7},{5,1},{7,3},{8,12},{10,14},{12... | collective-permute-start | bytes 1572872 | tf_op jit(solution)/shard_map/ppermute | solution.py:532
  57.2 3.1 %shard_map.187 = (f32[32,32,128]{2,1,0:T(8,128)S(1)}, f32[32,32,128]{2,1,0:T(8,128)S(1)}, f32[16,32,128]{2,1,0:T(8,128)S(1)}, f32[16,32,128]{2,1,0:T(8,128)S(1)}, f32[32,32,128]{2,1,0:T(8,128)}) custom-call(s32[1]{0:T(128)} %bitcast.q_ref, s32[1]{0:T(128)} %bitcast.3.yc_ref, ...), custom_call_target="tpu_custom_call", output_to_operand_aliasing={{0}: (12, {}), {1}: (13, {}), {2}: (14, {}), {3}: (15, {})} | custom-call | flops 4000000000 | bytes 4000000 | tf_op jit(solution)/shard_map/pallas_call | solution.py:643
  60.3 2.3 %collective-permute-start.20 = (f32[16,32,128]{2,1,0:T(8,128)S(1)}, f32[16,32,128]{2,1,0:T(8,128)S(1)}, u32[]{:S(2)}, u32[]{:S(2)}) collective-permute-start(f32[16,32,128]{2,1,0:T(8,128)S(1)} %get-tuple-element.93), channel_id=1, source_target_pairs={{0,6},{2,4},{4,2},{6,0},{1,7},{3,5},{5,3},{7,1},{8,14},{10,12},{12... | collective-permute-start | bytes 786440 | tf_op jit(solution)/shard_map/ppermute | solution.py:532
  62.7 1.4 %collective-permute-start.8 = (f32[2,8,24,128]{3,2,1,0:T(8,128)S(1)}, f32[2,8,24,128]{3,2,1,0:T(8,128)S(1)}, u32[]{:S(2)}, u32[]{:S(2)}) collective-permute-start(f32[2,8,24,128]{3,2,1,0:T(8,128)S(1)} %get-tuple-element.63), channel_id=1, source_target_pairs={{0,4},{2,6},{4,0},{6,2},{1,5},{3,7},{5,1},{7,3},{8,12},{10,14},{12... | collective-permute-start | bytes 589832 | tf_op jit(solution)/shard_map/ppermute | solution.py:532
  64.1 1.5 %collective-permute-start.9 = (f32[2,8,24,128]{3,2,1,0:T(8,128)S(1)}, f32[2,8,24,128]{3,2,1,0:T(8,128)S(1)}, u32[]{:S(2)}, u32[]{:S(2)}) collective-permute-start(f32[2,8,24,128]{3,2,1,0:T(8,128)S(1)} %get-tuple-element.64), channel_id=1, source_target_pairs={{0,6},{2,4},{4,2},{6,0},{1,7},{3,5},{5,3},{7,1},{8,14},{10,12},{12... | collective-permute-start | bytes 589832 | tf_op jit(solution)/shard_map/ppermute | solution.py:532
  65.5 13.5 %collective-permute-done.8.refs_2_ = f32[2,8,24,128]{3,2,1,0:T(8,128)S(1)} collective-permute-done((f32[2,8,24,128]{3,2,1,0:T(8,128)S(1)}, f32[2,8,24,128]{3,2,1,0:T(8,128)S(1)}, u32[]{:S(2)}, u32[]{:S(2)}) %collective-permute-start.8) | collective-permute-done | bytes 196640 | tf_op jit(solution)/shard_map/ppermute | solution.py:532
  80.1 1.6 %collective-permute-start.10 = (f32[4,8,24,128]{3,2,1,0:T(8,128)S(1)}, f32[4,8,24,128]{3,2,1,0:T(8,128)S(1)}, u32[]{:S(2)}, u32[]{:S(2)}) collective-permute-start(f32[4,8,24,128]{3,2,1,0:T(8,128)S(1)} %get-tuple-element.65), channel_id=1, source_target_pairs={{0,8},{8,16},{16,24},{24,0},{1,9},{9,17},{17,25},{25,1},{2,10},{10... | collective-permute-start | bytes 1179656 | tf_op jit(solution)/shard_map/ppermute | solution.py:538
  81.7 2.2 %collective-permute-start.11 = (f32[4,8,24,128]{3,2,1,0:T(8,128)S(1)}, f32[4,8,24,128]{3,2,1,0:T(8,128)S(1)}, u32[]{:S(2)}, u32[]{:S(2)}) collective-permute-start(f32[4,8,24,128]{3,2,1,0:T(8,128)S(1)} %get-tuple-element.66), channel_id=1, source_target_pairs={{0,24},{8,0},{16,8},{24,16},{1,25},{9,1},{17,9},{25,17},{2,26},{10... | collective-permute-start | bytes 1179656 | tf_op jit(solution)/shard_map/ppermute | solution.py:538
  84.0 1.5 %collective-permute-start.18 = (f32[16,32,128]{2,1,0:T(8,128)S(1)}, f32[16,32,128]{2,1,0:T(8,128)S(1)}, u32[]{:S(2)}, u32[]{:S(2)}) collective-permute-start(f32[16,32,128]{2,1,0:T(8,128)S(1)} %get-tuple-element.92), channel_id=1, source_target_pairs={{0,6},{2,4},{4,2},{6,0},{1,7},{3,5},{5,3},{7,1},{8,14},{10,12},{12... | collective-permute-start | bytes 786440 | tf_op jit(solution)/shard_map/ppermute | solution.py:532
  85.6 6.5 %collective-permute-done.18.late_ref.refs_1_ = f32[16,32,128]{2,1,0:T(8,128)S(1)} collective-permute-done((f32[16,32,128]{2,1,0:T(8,128)S(1)}, f32[16,32,128]{2,1,0:T(8,128)S(1)}, u32[]{:S(2)}, u32[]{:S(2)}) %collective-permute-start.18) | collective-permute-done | bytes 262176 | tf_op jit(solution)/shard_map/ppermute | solution.py:532
  92.8 1.2 %collective-permute-done.10.left_ref = f32[4,8,24,128]{3,2,1,0:T(8,128)S(1)} collective-permute-done((f32[4,8,24,128]{3,2,1,0:T(8,128)S(1)}, f32[4,8,24,128]{3,2,1,0:T(8,128)S(1)}, u32[]{:S(2)}, u32[]{:S(2)}) %collective-permute-start.10) | collective-permute-done | bytes 393248 | tf_op jit(solution)/shard_map/ppermute | solution.py:538
  94.0 7.7 %collective-permute-done.11.right_ref = f32[4,8,24,128]{3,2,1,0:T(8,128)S(1)} collective-permute-done((f32[4,8,24,128]{3,2,1,0:T(8,128)S(1)}, f32[4,8,24,128]{3,2,1,0:T(8,128)S(1)}, u32[]{:S(2)}, u32[]{:S(2)}) %collective-permute-start.11) | collective-permute-done | bytes 393248 | tf_op jit(solution)/shard_map/ppermute | solution.py:538
  101.7 1.4 %spread.1 = f32[1,2,8,32,512]{4,3,2,1,0:T(8,128)} custom-call(s32[112,128]{1,0:T(8,128)S(1)} %get-tuple-element.53.refs_7_.tab_ref, f32[4,8,24,128]{3,2,1,0:T(8,128)S(1)} %collective-permute-done.10.left_ref, f32[4,8,24,128]{3,2,1,0:T(8,128)S(1)} %collective-permute-done.11.right_ref), custom_call_target="tpu_custom_call" | custom-call | bytes 2000000 | tf_op jit(solution)/shard_map/spread/pallas_call | solution.py:717
  104.2 1.3 %shard_map.190.refs_3_ = f32[1,32,32,512]{3,2,1,0:T(8,128)} custom-call(s32[1]{0:T(128)} %bitcast.q_ref, f32[32,32,512]{2,1,0:T(8,128)S(1)} %get-tuple-element.88.acc_ref, bf16[256,512]{1,0:T(8,128)(2,1)S(1)} %get-tuple-element.89.wh_ref, bf16[256,512]{1,0:T(8,128)(2,1)S(1)} %get-tuple-element.90.wl_ref, ...), custom_call_target="tpu_custom_call" | custom-call | flops 1000000000 | bytes 3000000 | tf_op jit(solution)/shard_map/pallas_call | solution.py:702
  105.5 1.4 %shard_map.191 = f32[1,32,32,512]{3,2,1,0:T(8,128)} custom-call(s32[1]{0:T(128)} %bitcast.q_ref, f32[32,32,512]{2,1,0:T(8,128)S(1)} %get-tuple-element.88.acc_ref, bf16[256,512]{1,0:T(8,128)(2,1)S(1)} %get-tuple-element.89.wh_ref, bf16[256,512]{1,0:T(8,128)(2,1)S(1)} %get-tuple-element.90.wl_ref, ...), custom_call_target="tpu_custom_call", output_to_operand_aliasing={{}: (7, {})} | custom-call | flops 1000000000 | bytes 3000000 | tf_op jit(solution)/shard_map/pallas_call | solution.py:702
  (68 shorter events, 9.7 us)
Async XLA Ops:
  0.6 10.6 %copy-start = (f32[1,2,8,32,512]{4,3,2,1,0:T(8,128)S(1)}, f32[1,2,8,32,512]{4,3,2,1,0:T(8,128)}, u32[]{:S(2)}) copy-start(f32[1,2,8,32,512]{4,3,2,1,0:T(8,128)} %refs_3_.1) | copy-start | bytes 3145732
  8.2 18.3 %collective-permute-start = (f32[33,32,128]{2,1,0:T(8,128)S(1)}, f32[33,32,128]{2,1,0:T(8,128)S(1)}, u32[]{:S(2)}, u32[]{:S(2)}) collective-permute-start(f32[33,32,128]{2,1,0:T(8,128)S(1)} %forward0.1.s0), channel_id=1, source_target_pairs={{0,1},{1,0},{2,3},{3,2},{4,5},{5,4},{6,7},{7,6},{8,9},{9,8},{10,11... | collective-permute-start | bytes 1622024 | tf_op jit(solution)/shard_map/ppermute | solution.py:535
  11.9 14.6 %copy-start.9 = (f32[32]{0:T(128)S(1)}, f32[32]{0:T(128)}, u32[]{:S(2)}) copy-start(f32[32]{0:T(128)} %sy_ref.3) | copy-start | bytes 388
  11.9 14.6 %copy-start.10 = (s32[4,32]{1,0:T(4,128)S(1)}, s32[4,32]{1,0:T(4,128)}, u32[]{:S(2)}) copy-start(s32[4,32]{1,0:T(4,128)} %open_ref.1) | copy-start | bytes 1540
  11.9 14.5 %copy-start.11 = (s32[4,32]{1,0:T(4,128)S(1)}, s32[4,32]{1,0:T(4,128)}, u32[]{:S(2)}) copy-start(s32[4,32]{1,0:T(4,128)} %owner_ref.1) | copy-start | bytes 1540
  12.0 14.5 %copy-start.12 = (f32[512]{0:T(512)S(1)}, f32[512]{0:T(512)}, u32[]{:S(2)}) copy-start(f32[512]{0:T(512)} %param.25) | copy-start | bytes 6148
  12.0 14.5 %copy-start.13 = (f32[32]{0:T(128)S(1)}, f32[32]{0:T(128)}, u32[]{:S(2)}) copy-start(f32[32]{0:T(128)} %sx_ref.1) | copy-start | bytes 388
  12.0 5.2 %collective-permute-start.1 = (f32[520,128]{1,0:T(8,128)S(1)}, f32[520,128]{1,0:T(8,128)S(1)}, u32[]{:S(2)}, u32[]{:S(2)}) collective-permute-start(f32[520,128]{1,0:T(8,128)S(1)} %get-tuple-element.50), channel_id=1, source_target_pairs={{0,2},{2,0},{4,6},{6,4},{1,3},{3,1},{5,7},{7,5},{8,10},{10,8},{12,... | collective-permute-start | bytes 798728 | tf_op jit(solution)/shard_map/ppermute | solution.py:532
  12.1 9.3 %collective-permute-start.2 = (f32[520,128]{1,0:T(8,128)S(1)}, f32[520,128]{1,0:T(8,128)S(1)}, u32[]{:S(2)}, u32[]{:S(2)}) collective-permute-start(f32[520,128]{1,0:T(8,128)S(1)} %get-tuple-element.51), channel_id=1, source_target_pairs={{0,4},{2,6},{4,0},{6,2},{1,5},{3,7},{5,1},{7,3},{8,12},{10,14},{12... | collective-permute-start | bytes 798728 | tf_op jit(solution)/shard_map/ppermute | solution.py:532
  13.6 12.4 %collective-permute-start.3 = (f32[520,128]{1,0:T(8,128)S(1)}, f32[520,128]{1,0:T(8,128)S(1)}, u32[]{:S(2)}, u32[]{:S(2)}) collective-permute-start(f32[520,128]{1,0:T(8,128)S(1)} %get-tuple-element.52), channel_id=1, source_target_pairs={{0,6},{2,4},{4,2},{6,0},{1,7},{3,5},{5,3},{7,1},{8,14},{10,12},{12... | collective-permute-start | bytes 798728 | tf_op jit(solution)/shard_map/ppermute | solution.py:532
  15.2 13.9 %copy-start.16 = (bf16[2,2,256,256]{3,2,1,0:T(8,128)(2,1)S(1)}, bf16[2,2,256,256]{3,2,1,0:T(8,128)(2,1)}, u32[]{:S(2)}) copy-start(bf16[2,2,256,256]{3,2,1,0:T(8,128)(2,1)} %constant.30.clone.ky_ref.refs_9_) | copy-start | bytes 1572868
  16.9 20.2 %collective-permute-start.6 = (f32[32,32,128]{2,1,0:T(8,128)S(1)}, f32[32,32,128]{2,1,0:T(8,128)S(1)}, u32[]{:S(2)}, u32[]{:S(2)}) collective-permute-start(f32[32,32,128]{2,1,0:T(8,128)S(1)} %get-tuple-element.55.refs_3_), channel_id=1, source_target_pairs={{0,1},{1,0},{2,3},{3,2},{4,5},{5,4},{6,7},{7,6},{8,9},{9,8},{10,11... | collective-permute-start | bytes 1572872 | tf_op jit(solution)/shard_map/ppermute | solution.py:535
  17.2 17.8 %collective-permute-start.5 = (f32[8,128]{1,0:T(8,128)S(1)}, f32[8,128]{1,0:T(8,128)S(1)}, u32[]{:S(2)}, u32[]{:S(2)}) collective-permute-start(f32[8,128]{1,0:T(8,128)S(1)} %get-tuple-element.54.refs_1_), channel_id=1, source_target_pairs={{0,24},{8,0},{16,8},{24,16},{1,25},{9,1},{17,9},{25,17},{2,26},{10... | collective-permute-start | bytes 12296 | tf_op jit(solution)/shard_map/ppermute | solution.py:538
  21.4 14.1 %collective-permute-start.4 = (f32[8,128]{1,0:T(8,128)S(1)}, f32[8,128]{1,0:T(8,128)S(1)}, u32[]{:S(2)}, u32[]{:S(2)}) collective-permute-start(f32[8,128]{1,0:T(8,128)S(1)} %get-tuple-element.54.refs_1_), channel_id=1, source_target_pairs={{0,8},{8,16},{16,24},{24,0},{1,9},{9,17},{17,25},{25,1},{2,10},{10... | collective-permute-start | bytes 12296 | tf_op jit(solution)/shard_map/ppermute | solution.py:538
  26.0 15.3 %collective-permute-start.12 = (f32[2,8,32,128]{3,2,1,0:T(8,128)S(1)}, f32[2,8,32,128]{3,2,1,0:T(8,128)S(1)}, u32[]{:S(2)}, u32[]{:S(2)}) collective-permute-start(f32[2,8,32,128]{3,2,1,0:T(8,128)S(1)} %get-tuple-element.71), channel_id=1, source_target_pairs={{0,1},{1,0},{2,3},{3,2},{4,5},{5,4},{6,7},{7,6},{8,9},{9,8},{10,11... | collective-permute-start | bytes 786440 | tf_op jit(solution)/shard_map/ppermute | solution.py:535
  27.5 19.3 %collective-permute-start.13 = (f32[2,8,32,128]{3,2,1,0:T(8,128)S(1)}, f32[2,8,32,128]{3,2,1,0:T(8,128)S(1)}, u32[]{:S(2)}, u32[]{:S(2)}) collective-permute-start(f32[2,8,32,128]{3,2,1,0:T(8,128)S(1)} %get-tuple-element.72), channel_id=1, source_target_pairs={{0,1},{1,0},{2,3},{3,2},{4,5},{5,4},{6,7},{7,6},{8,9},{9,8},{10,11... | collective-permute-start | bytes 786440 | tf_op jit(solution)/shard_map/ppermute | solution.py:535
  35.0 17.4 %collective-permute-start.14 = (f32[2,8,32,128]{3,2,1,0:T(8,128)S(1)}, f32[2,8,32,128]{3,2,1,0:T(8,128)S(1)}, u32[]{:S(2)}, u32[]{:S(2)}) collective-permute-start(f32[2,8,32,128]{3,2,1,0:T(8,128)S(1)} %get-tuple-element.74), channel_id=1, source_target_pairs={{0,1},{1,0},{2,3},{3,2},{4,5},{5,4},{6,7},{7,6},{8,9},{9,8},{10,11... | collective-permute-start | bytes 786440 | tf_op jit(solution)/shard_map/ppermute | solution.py:535
  35.5 21.7 %collective-permute-start.15 = (f32[2,8,32,128]{3,2,1,0:T(8,128)S(1)}, f32[2,8,32,128]{3,2,1,0:T(8,128)S(1)}, u32[]{:S(2)}, u32[]{:S(2)}) collective-permute-start(f32[2,8,32,128]{3,2,1,0:T(8,128)S(1)} %get-tuple-element.81), channel_id=1, source_target_pairs={{0,1},{1,0},{2,3},{3,2},{4,5},{5,4},{6,7},{7,6},{8,9},{9,8},{10,11... | collective-permute-start | bytes 786440 | tf_op jit(solution)/shard_map/ppermute | solution.py:535
  37.1 9.7 %copy-start.17 = (bf16[2,2,128,256]{3,2,1,0:T(8,128)(2,1)S(1)}, bf16[2,2,128,256]{3,2,1,0:T(8,128)(2,1)}, u32[]{:S(2)}) copy-start(bf16[2,2,128,256]{3,2,1,0:T(8,128)(2,1)} %constant.31.clone.ki_ref) | copy-start | bytes 786436
  37.1 9.7 %copy-start.18 = (bf16[256,256]{1,0:T(8,128)(2,1)S(1)}, bf16[256,256]{1,0:T(8,128)(2,1)}, u32[]{:S(2)}) copy-start(bf16[256,256]{1,0:T(8,128)(2,1)} %constant.29.clone.kxl_ref) | copy-start | bytes 393220
  37.1 9.7 %copy-start.19 = (bf16[256,256]{1,0:T(8,128)(2,1)S(1)}, bf16[256,256]{1,0:T(8,128)(2,1)}, u32[]{:S(2)}) copy-start(bf16[256,256]{1,0:T(8,128)(2,1)} %constant.28.clone.kxh_ref) | copy-start | bytes 393220
  41.2 24.4 %collective-permute-start.7 = (f32[2,8,24,128]{3,2,1,0:T(8,128)S(1)}, f32[2,8,24,128]{3,2,1,0:T(8,128)S(1)}, u32[]{:S(2)}, u32[]{:S(2)}) collective-permute-start(f32[2,8,24,128]{3,2,1,0:T(8,128)S(1)} %get-tuple-element.62), channel_id=1, source_target_pairs={{0,2},{2,0},{4,6},{6,4},{1,3},{3,1},{5,7},{7,5},{8,10},{10,8},{12,... | collective-permute-start | bytes 589832 | tf_op jit(solution)/shard_map/ppermute | solution.py:532
  54.8 30.7 %collective-permute-start.17 = (f32[32,32,128]{2,1,0:T(8,128)S(1)}, f32[32,32,128]{2,1,0:T(8,128)S(1)}, u32[]{:S(2)}, u32[]{:S(2)}) collective-permute-start(f32[32,32,128]{2,1,0:T(8,128)S(1)} %get-tuple-element.91), channel_id=1, source_target_pairs={{0,4},{2,6},{4,0},{6,2},{1,5},{3,7},{5,1},{7,3},{8,12},{10,14},{12... | collective-permute-start | bytes 1572872 | tf_op jit(solution)/shard_map/ppermute | solution.py:532
  60.3 23.7 %collective-permute-start.20 = (f32[16,32,128]{2,1,0:T(8,128)S(1)}, f32[16,32,128]{2,1,0:T(8,128)S(1)}, u32[]{:S(2)}, u32[]{:S(2)}) collective-permute-start(f32[16,32,128]{2,1,0:T(8,128)S(1)} %get-tuple-element.93), channel_id=1, source_target_pairs={{0,6},{2,4},{4,2},{6,0},{1,7},{3,5},{5,3},{7,1},{8,14},{10,12},{12... | collective-permute-start | bytes 786440 | tf_op jit(solution)/shard_map/ppermute | solution.py:532
  62.7 16.4 %collective-permute-start.8 = (f32[2,8,24,128]{3,2,1,0:T(8,128)S(1)}, f32[2,8,24,128]{3,2,1,0:T(8,128)S(1)}, u32[]{:S(2)}, u32[]{:S(2)}) collective-permute-start(f32[2,8,24,128]{3,2,1,0:T(8,128)S(1)} %get-tuple-element.63), channel_id=1, source_target_pairs={{0,4},{2,6},{4,0},{6,2},{1,5},{3,7},{5,1},{7,3},{8,12},{10,14},{12... | collective-permute-start | bytes 589832 | tf_op jit(solution)/shard_map/ppermute | solution.py:532
  64.1 16.0 %collective-permute-start.9 = (f32[2,8,24,128]{3,2,1,0:T(8,128)S(1)}, f32[2,8,24,128]{3,2,1,0:T(8,128)S(1)}, u32[]{:S(2)}, u32[]{:S(2)}) collective-permute-start(f32[2,8,24,128]{3,2,1,0:T(8,128)S(1)} %get-tuple-element.64), channel_id=1, source_target_pairs={{0,6},{2,4},{4,2},{6,0},{1,7},{3,5},{5,3},{7,1},{8,14},{10,12},{12... | collective-permute-start | bytes 589832 | tf_op jit(solution)/shard_map/ppermute | solution.py:532
  65.5 37.5 %collective-permute-start.16 = (f32[32,32,128]{2,1,0:T(8,128)S(1)}, f32[32,32,128]{2,1,0:T(8,128)S(1)}, u32[]{:S(2)}, u32[]{:S(2)}) collective-permute-start(f32[32,32,128]{2,1,0:T(8,128)S(1)} %get-tuple-element.87), channel_id=1, source_target_pairs={{0,2},{2,0},{4,6},{6,4},{1,3},{3,1},{5,7},{7,5},{8,10},{10,8},{12,... | collective-permute-start | bytes 1572872 | tf_op jit(solution)/shard_map/ppermute | solution.py:532
  80.1 13.9 %collective-permute-start.10 = (f32[4,8,24,128]{3,2,1,0:T(8,128)S(1)}, f32[4,8,24,128]{3,2,1,0:T(8,128)S(1)}, u32[]{:S(2)}, u32[]{:S(2)}) collective-permute-start(f32[4,8,24,128]{3,2,1,0:T(8,128)S(1)} %get-tuple-element.65), channel_id=1, source_target_pairs={{0,8},{8,16},{16,24},{24,0},{1,9},{9,17},{17,25},{25,1},{2,10},{10... | collective-permute-start | bytes 1179656 | tf_op jit(solution)/shard_map/ppermute | solution.py:538
  81.7 20.0 %collective-permute-start.11 = (f32[4,8,24,128]{3,2,1,0:T(8,128)S(1)}, f32[4,8,24,128]{3,2,1,0:T(8,128)S(1)}, u32[]{:S(2)}, u32[]{:S(2)}) collective-permute-start(f32[4,8,24,128]{3,2,1,0:T(8,128)S(1)} %get-tuple-element.66), channel_id=1, source_target_pairs={{0,24},{8,0},{16,8},{24,16},{1,25},{9,1},{17,9},{25,17},{2,26},{10... | collective-permute-start | bytes 1179656 | tf_op jit(solution)/shard_map/ppermute | solution.py:538
  84.0 8.1 %collective-permute-start.18 = (f32[16,32,128]{2,1,0:T(8,128)S(1)}, f32[16,32,128]{2,1,0:T(8,128)S(1)}, u32[]{:S(2)}, u32[]{:S(2)}) collective-permute-start(f32[16,32,128]{2,1,0:T(8,128)S(1)} %get-tuple-element.92), channel_id=1, source_target_pairs={{0,6},{2,4},{4,2},{6,0},{1,7},{3,5},{5,3},{7,1},{8,14},{10,12},{12... | collective-permute-start | bytes 786440 | tf_op jit(solution)/shard_map/ppermute | solution.py:532
  85.5 18.7 %collective-permute-start.21 = (f32[16,32,128]{2,1,0:T(8,128)S(1)}, f32[16,32,128]{2,1,0:T(8,128)S(1)}, u32[]{:S(2)}, u32[]{:S(2)}) collective-permute-start(f32[16,32,128]{2,1,0:T(8,128)S(1)} %shard_map.189), channel_id=1, source_target_pairs={{0,2},{2,0},{4,6},{6,4},{1,3},{3,1},{5,7},{7,5},{8,10},{10,8},{12,... | collective-permute-start | bytes 786440 | tf_op jit(solution)/shard_map/ppermute | solution.py:532
  92.1 13.4 %collective-permute-start.19 = (f32[16,32,128]{2,1,0:T(8,128)S(1)}, f32[16,32,128]{2,1,0:T(8,128)S(1)}, u32[]{:S(2)}, u32[]{:S(2)}) collective-permute-start(f32[16,32,128]{2,1,0:T(8,128)S(1)} %shard_map.188), channel_id=1, source_target_pairs={{0,2},{2,0},{4,6},{6,4},{1,3},{3,1},{5,7},{7,5},{8,10},{10,8},{12,... | collective-permute-start | bytes 786440 | tf_op jit(solution)/shard_map/ppermute | solution.py:532
  (10 other events, 26.5 us)

commit v8 on v7

--- a/solution.py
+++ b/solution.py
@@ -88,16 +88,9 @@
     return parts[0]
 
 
-def split_kernel(nt, q_ref, yc_ref, me_ref, amp_ref, *refs):
-    ins, outs, piece_ref = refs[:nt], refs[nt : 2 * nt], refs[2 * nt]
-    steps = amp_ref.shape[0]
-    rows = outs[0].shape[0] - steps
-    cq = outs[0].shape[1]
-    piece_ref[...] = ins[0][...]
-    for d in range(nt):
-        outs[d][0:rows, :] = ins[d][...].reshape(rows, cq)
-        for k in range(steps):
-            outs[d][rows + k : rows + k + 1, :] = jnp.full((1, cq), amp_ref[k], F32)
+def split_kernel(nt, q_ref, yc_ref, me_ref, *refs):
+    for share, out in zip(refs[:nt], refs[nt:]):
+        out[...] = share[...]
 
 
 def forward_block(x, c_ref, kxh_ref, kxl_ref):
@@ -109,23 +102,17 @@
     return const_times(kxh_ref[...], kxl_ref[...], z).reshape(nx, SUB, cq)
 
 
-def forward_kernel(with_sy, q_ref, sy_ref, x_ref, c_ref, kxh_ref, kxl_ref, out_ref):
-    nx, hy, _ = x_ref.shape
-    cq = out_ref.shape[2]
-    tiles = hy // SUB
-    if with_sy:
-        for r in range(hy):
-            b = tiles * (r % SUB) + r // SUB
-            out_ref[nx, r : r + 1, :] = jnp.full((1, cq), sy_ref[b], F32)
+def forward_kernel(q_ref, x_ref, c_ref, kxh_ref, kxl_ref, out_ref):
+    tiles = x_ref.shape[1] // SUB
     for t in range(tiles):
         at = slice(t * SUB, (t + 1) * SUB)
-        out_ref[0:nx, at, :] = forward_block(x_ref[:, at, :], c_ref.at[q_ref[0]], kxh_ref, kxl_ref)
+        out_ref[:, at, :] = forward_block(x_ref[:, at, :], c_ref.at[q_ref[0]], kxh_ref, kxl_ref)
 
 
 def forward_second_kernel(q_ref, diff_ref, par_ref, x_ref, c_ref, kxh_ref, kxl_ref, out_ref, diff_out, par_out):
     diff_out[...] = jnp.full(diff_out.shape, diff_ref[0], F32)
     par_out[...] = jnp.full(par_out.shape, par_ref[0], F32)
-    forward_kernel(False, q_ref, None, x_ref, c_ref, kxh_ref, kxl_ref, out_ref)
+    forward_kernel(q_ref, x_ref, c_ref, kxh_ref, kxl_ref, out_ref)
 
 
 def factor_into(f_ref, sx_ref, diff_ref, sy, sz):
@@ -134,16 +121,17 @@
         f_ref[i] = 1.0 / (1.0 + diff_ref[0:1, :] * rate)
 
 
-def order_kernel(nt, space, q_ref, me_ref, sx_ref, sy_ref, open_ref, owner_ref, diff_ref, sz_ref, there_ref, *refs):
+def order_kernel(nt, space, q_ref, me_ref, sx_ref, sy_ref, syt_ref, open_ref, owner_ref, *refs):
+    amps, (diff_ref, sz_ref), refs = refs[:nt], refs[nt : nt + 2], refs[nt + 2 :]
     ins, (u_ref, amp_ref, tab_ref, fo_ref, ft_ref), outs = refs[:nt], refs[nt : nt + 5], refs[nt + 5 :]
     steps = amp_ref.shape[1]
-    rows = ins[0].shape[0] - steps
-    nx, hy, cq = fo_ref.shape
+    _, hy, cq = fo_ref.shape
     tiles = hy // SUB
     for d in range(nt):
         w = jnp.bitwise_xor(q_ref[0], d)
-        u_ref[w] = ins[d][0:rows, :].reshape(u_ref.shape[1:])
-        amp_ref[w] = ins[d][rows:, :]
+        u_ref[w] = ins[d][...]
+        for k in range(steps):
+            amp_ref[w, k : k + 1, :] = jnp.full((1, cq), amps[d][k], F32)
     for i, out in enumerate(outs):
         out[...] = u_ref[jnp.where(i < q_ref[0], i, i + 1)]
     for face in range(2):
@@ -162,8 +150,9 @@
     for r in range(hy):
         b = tiles * (r % SUB) + r // SUB
         fo_ref[0, r : r + 1, :] = jnp.full((1, cq), sy_ref[b], F32)
+        ft_ref[0, r : r + 1, :] = jnp.full((1, cq), syt_ref[b], F32)
     factor_into(fo_ref, sx_ref, diff_ref, fo_ref[0], sz)
-    factor_into(ft_ref, sx_ref, diff_ref, there_ref[nx], sz)
+    factor_into(ft_ref, sx_ref, diff_ref, ft_ref[0], sz)
 
 
 def closed_rows(tab_ref, face, tiles, hy):
@@ -304,10 +293,14 @@
     return [0, 1, 3] if nt == 4 else list(range(nt))
 
 
+def late_cut(nx):
+    return max(nx * 5 // 8 // 4 * 4, 4)
+
+
 def slot_parts(slots, nt, nx):
     parts = []
     for slot in slots:
-        cuts = (0, nx // 2, nx) if slot == nt - 1 else (0, nx)
+        cuts = (0, late_cut(nx), nx) if slot == nt - 1 else (0, nx)
         parts += [(slot, lo, hi) for lo, hi in zip(cuts[:-1], cuts[1:])]
     return parts
 
@@ -548,36 +541,34 @@
     AN = pl.BlockSpec(memory_space=pl.ANY)
     cutting = pl.pallas_call(
         functools.partial(split_kernel, nt),
-        out_shape=[sds(rows + steps, cq)] * nt + [sds(2, steps, hy, cq)],
+        out_shape=[sds(2, steps, hy, cq)] * nt,
         grid_spec=pltpu.PrefetchScalarGridSpec(
             num_scalar_prefetch=3,
             grid=(1,),
-            in_specs=[SM]
-            + [
+            in_specs=[
                 pl.BlockSpec(block, lambda i, q, y, z, d=d: (0, 0, 0, 0, jnp.bitwise_xor(q[0], d)))
                 for d in range(nt)
             ],
-            out_specs=[pl.BlockSpec((rows + steps, cq), lambda i, q, y, z: (0, 0))] * nt
-            + [pl.BlockSpec((2, steps, hy, cq), lambda i, q, y, z: (0, 0, 0, 0))],
+            out_specs=[pl.BlockSpec((2, steps, hy, cq), lambda i, q, y, z: (0, 0, 0, 0))] * nt,
         ),
         compiler_params=grant(18),
         cost_estimate=cost(0, 8 * nt * rows * cq),
         name="split",
     )
-    *dealt, piece = cutting(qv, ycv, mev, source_amplitude, *([robin_in] * nt))
-    piece = swap(piece)
+    dealt = list(cutting(qv, ycv, mev, *([robin_in] * nt)))
+    piece = swap(dealt[0])
     for d in range(1, nt):
         dealt[d] = xor_permute(dealt[d], d)
 
     s0 = pl.pallas_call(
-        functools.partial(forward_kernel, True),
-        out_shape=sds(nx + 1, hy, cq),
-        in_specs=[SM] * 2 + [VM] * 4,
+        forward_kernel,
+        out_shape=sds(nx, hy, cq),
+        in_specs=[SM] + [VM] * 4,
         out_specs=VM,
         compiler_params=grant(18),
         cost_estimate=cost(1e9, 3e6),
         name="forward0",
-    )(qv, spectrum_y, heat_source, base, kxh, kxl)
+    )(qv, heat_source, base, kxh, kxl)
     s1 = swap(s0)
     n0, diff_rows, robin_param = pl.pallas_call(
         forward_second_kernel,
@@ -589,6 +580,10 @@
         name="forward1",
     )(qv, diffusivity, robin_param, initial_state, base, kxh, kxl)
     n1 = swap(n0)
+    amplitudes = [source_amplitude]
+    for d in range(1, nt):
+        amplitudes.append(xor_permute(source_amplitude, d))
+    sy_there = swap(spectrum_y)
     right_param = along(robin_param, -1)
     left_param = along(robin_param, 1)
 
@@ -598,14 +593,14 @@
         out_shape=[sds(nt, 2, steps, hy, cq), sds(nt, steps, cq), table]
         + [sds(nx, hy, cq)] * 2
         + [sds(2, steps, hy, cq)] * (nt - 1),
-        in_specs=[SM] * 6 + [VM] * (3 + nt),
+        in_specs=[SM] * (7 + nt) + [VM] * (2 + nt),
         out_specs=[VM] * (4 + nt),
         compiler_params=grant(18),
         cost_estimate=cost(0, 3e6),
         name="order",
     )(
-        qv, mev, spectrum_x, spectrum_y, open_flag, owner_side, diff_rows,
-        spectrum_z.reshape(nt, cq), s1, *dealt,
+        qv, mev, spectrum_x, spectrum_y, sy_there, open_flag, owner_side, *amplitudes, diff_rows,
+        spectrum_z.reshape(nt, cq), *dealt,
     )
     for i in range(nt - 1):
         chunks[i] = swap(chunks[i])
@@ -662,12 +657,13 @@
             if d:
                 ends[d, r0, r1] = xor_permute(ends[d, r0, r1], d)
     middle = [ends[d, 0, nx] for d in range(nt - 1)]
-    lasts = [ends[nt - 1, r0, r1] for r0, r1 in ((0, nx // 2), (nx // 2, nx))]
+    spans = [(0, late_cut(nx)), (late_cut(nx), nx)]
+    lasts = [ends[nt - 1, r0, r1] for r0, r1 in spans]
     passed = []
     for h, last in enumerate(lasts if nt == 4 else []):
         passing = pl.pallas_call(
-            functools.partial(relay_kernel, nt, h * nx // 2),
-            out_shape=sds(nx // 2, hy, cq),
+            functools.partial(relay_kernel, nt, spans[h][0]),
+            out_shape=sds(*last.shape),
             in_specs=[SM] + [VM] * 2,
             out_specs=VM,
             compiler_params=grant(18),
@@ -700,13 +696,13 @@
         operands = (qv, acc, wh, wl, *middle[2:], last, *passed[h : h + 1])
         window_end = [
             pl.pallas_call(
-                functools.partial(final_kernel, nt, h * nx // 2),
+                functools.partial(final_kernel, nt, spans[h][0]),
                 out_shape=sds(1, nx, hy, nz),
                 in_specs=[SM] + [VM] * (len(operands) - 1) + [AN] * len(window_end),
                 out_specs=AN,
                 scratch_shapes=[
-                    pltpu.VMEM((nx // 2 // xb, xb, hy, nz), F32),
-                    pltpu.SemaphoreType.DMA((nx // 2 // xb,)),
+                    pltpu.VMEM((last.shape[0] // xb, xb, hy, nz), F32),
+                    pltpu.SemaphoreType.DMA((last.shape[0] // xb,)),
                 ],
                 input_output_aliases={len(operands): 0} if window_end else {},
                 compiler_params=grant(18),

time: 107 us -> 107 us (level)
  starting transfers between devices: 28.4 us -> 29.9 us
    ppermute x12 -> x15, waiting for transfers between devices: 24.4 us -> 21.1 us  [xor_permute(): return lax.ppermute(x, 'tm', [(i, i ^ d) for i in range(nt)])]
    ppermute x6 -> x7, waiting for transfers between devices: 7.33 us -> 10.5 us  [swap(): return lax.ppermute(x, 'cores', [(0, 1), (1, 0)])]
    ppermute x12 -> x15, starting transfers between devices: 11.5 us -> 13.4 us  [xor_permute(): return lax.ppermute(x, 'tm', [(i, i ^ d) for i in range(nt)])]
    ppermute x4, starting transfers between devices: 9.31 us -> 7.48 us  [along(): lax.ppermute(x, 'space', [(i, (i + by) % space) for i in range(space)])]
    ppermute x6 -> x7, starting transfers between devices: 7.56 us -> 9.07 us  [swap(): return lax.ppermute(x, 'cores', [(0, 1), (1, 0)])]
    pallas_call x6, Pallas kernels: 5.52 us -> 4.44 us  [the longest x2 2.68 us: local(): pl.pallas_call(functools.partial(final_kernel, nt, spans[h][0]), out_shap...]
    unnamed x40 -> x38, local copies, waits for them, and re-layouts: 5.43 us -> 4.78 us
  transfers between devices with their start and end apart: 22 -> 26, of which waited for: 10 -> 9; matrix products, arithmetic and copies ran while one was open for 0% -> 0% of each run, Pallas kernels for 25% -> 25%
where the time goes in v8:
time: 107 us; the launch traced here: 106 us
  waiting for transfers between devices  40.2 us (38%)
  starting transfers between devices  29.9 us (28%)
  Pallas kernels  29.1 us (27%)
  local copies, waits for them, and re-layouts  4.78 us (4%)
  between operations  2.4 us (2%)
    ppermute x15, waiting for transfers between devices, xor_permute(): return lax.ppermute(x, 'tm', [(i, i ^ d) for i in range(nt)])  21.1 us
    ppermute x15, starting transfers between devices, xor_permute(): return lax.ppermute(x, 'tm', [(i, i ^ d) for i in range(nt)])  13.4 us
    ppermute x7, waiting for transfers between devices, swap(): return lax.ppermute(x, 'cores', [(0, 1), (1, 0)])  10.5 us
    pallas_call x3, Pallas kernels, local(): pl.pallas_call(functools.partial(other_kernel, dims, stage), out_shape=[s...  9.64 us
    ppermute x7, starting transfers between devices, swap(): return lax.ppermute(x, 'cores', [(0, 1), (1, 0)])  9.07 us
    ppermute x4, waiting for transfers between devices, along(): lax.ppermute(x, 'space', [(i, (i + by) % space) for i in range(space)])  8.55 us
    ppermute x4, starting transfers between devices, along(): lax.ppermute(x, 'space', [(i, (i + by) % space) for i in range(space)])  7.48 us
    pallas_call x1, Pallas kernels, local(): pl.pallas_call(functools.partial(driven_kernel, dims), out_shape=[traces,...  5.84 us
  transfers between devices with their start and end apart: 26, of which 9 were waited for; matrix products, arithmetic and copies ran while one was open for 0% of the time, Pallas kernels for 25%

profile of v8, /device:TPU:0, one launch (start us, length us, event | category | flops | bytes accessed | tf_op | source)
XLA Modules:
  0.0 106.4 jit_solution(10157713103807644586)
XLA Ops:
  0.7 1.7 %copy-done.1 = f32[32,32,512]{2,1,0:T(8,128)S(1)} copy-done((f32[32,32,512]{2,1,0:T(8,128)S(1)}, f32[32,32,512]{2,1,0:T(8,128)}, u32[]{:S(2)}) %copy-start.1) | copy-done | bytes 2097176
  2.3 1.2 %copy-done.2 = bf16[4,2,128,512]{3,2,1,0:T(8,128)(2,1)S(1)} copy-done((bf16[4,2,128,512]{3,2,1,0:T(8,128)(2,1)S(1)}, bf16[4,2,128,512]{3,2,1,0:T(8,128)(2,1)}, u32[]{:S(2)}) %copy-start.2) | copy-done | bytes 1048600
  5.4 1.6 %forward0.1.s0 = f32[32,32,128]{2,1,0:T(8,128)S(1)} custom-call(s32[1]{0:T(128)} %bitcast.q_ref, f32[32,32,512]{2,1,0:T(8,128)S(1)} %copy-done.1, bf16[4,2,128,512]{3,2,1,0:T(8,128)(2,1)S(1)} %copy-done.2, bf16[256,256]{1,0:T(8,128)(2,1)S(1)} %copy-done.6, bf16[256,256]{1,0:T(8,128)(2,1)S(1)} %copy-done.4), custom_call_target="tpu_custom_call" | custom-call | flops 1000000000 | bytes 3000000 | tf_op jit(solution)/shard_map/forward0/pallas_call | solution.py:563
  6.9 3.1 %collective-permute-start.10 = (f32[32,32,128]{2,1,0:T(8,128)S(1)}, f32[32,32,128]{2,1,0:T(8,128)S(1)}, u32[]{:S(2)}, u32[]{:S(2)}) collective-permute-start(f32[32,32,128]{2,1,0:T(8,128)S(1)} %forward0.1.s0), channel_id=1, source_target_pairs={{0,1},{1,0},{2,3},{3,2},{4,5},{5,4},{6,7},{7,6},{8,9},{9,8},{10,11... | collective-permute-start | bytes 1572872 | tf_op jit(solution)/shard_map/ppermute | solution.py:528
  10.0 1.5 %collective-permute-start.2 = (f32[8]{0:T(128)S(1)}, f32[8]{0:T(128)S(1)}, u32[]{:S(2)}, u32[]{:S(2)}) collective-permute-start(f32[8]{0:T(128)S(1)} %copy-done.13), channel_id=1, source_target_pairs={{0,4},{2,6},{4,0},{6,2},{1,5},{3,7},{5,1},{7,3},{8,12},{10,14},{12... | collective-permute-start | bytes 104 | tf_op jit(solution)/shard_map/ppermute | solution.py:525
  13.9 2.0 %collective-permute-start.5 = (f32[2,8,32,128]{3,2,1,0:T(8,128)S(1)}, f32[2,8,32,128]{3,2,1,0:T(8,128)S(1)}, u32[]{:S(2)}, u32[]{:S(2)}) collective-permute-start(f32[2,8,32,128]{3,2,1,0:T(8,128)S(1)} %get-tuple-element.50), channel_id=1, source_target_pairs={{0,4},{2,6},{4,0},{6,2},{1,5},{3,7},{5,1},{7,3},{8,12},{10,14},{12... | collective-permute-start | bytes 786440 | tf_op jit(solution)/shard_map/ppermute | solution.py:525
  16.0 1.6 %forward1.1 = (f32[32,32,128]{2,1,0:T(8,128)S(1)}, f32[8,128]{1,0:T(8,128)S(1)}, f32[8,128]{1,0:T(8,128)S(1)}) custom-call(s32[1]{0:T(128)} %bitcast.q_ref, f32[1]{0:T(128)S(6)} %copy.40.diff_ref, f32[1]{0:T(128)S(6)} %copy.41.par_ref, f32[32,32,512]{2,1,0:T(8,128)S(1)} %copy-done.14, bf16[4,2,128,512]{3,2,1,0:T(8,128)(2,1)S(1)} %copy-done.3, ...), custom_call_target="tpu_custom_call" | custom-call | flops 1000000000 | bytes 3000000 | tf_op jit(solution)/shard_map/forward1/pallas_call | solution.py:573
  17.6 4.4 %collective-permute-done.syt_ref = f32[32]{0:T(128)S(1)} collective-permute-done((f32[32]{0:T(128)S(1)}, f32[32]{0:T(128)S(1)}, u32[]{:S(2)}, u32[]{:S(2)}) %collective-permute-start) | collective-permute-done | bytes 160 | tf_op jit(solution)/shard_map/ppermute | solution.py:528
  22.0 1.7 %collective-permute-start.9 = (f32[32,32,128]{2,1,0:T(8,128)S(1)}, f32[32,32,128]{2,1,0:T(8,128)S(1)}, u32[]{:S(2)}, u32[]{:S(2)}) collective-permute-start(f32[32,32,128]{2,1,0:T(8,128)S(1)} %get-tuple-element.54.refs_3_), channel_id=1, source_target_pairs={{0,1},{1,0},{2,3},{3,2},{4,5},{5,4},{6,7},{7,6},{8,9},{9,8},{10,11... | collective-permute-start | bytes 1572872 | tf_op jit(solution)/shard_map/ppermute | solution.py:528
  23.8 3.6 %collective-permute-start.8 = (f32[8,128]{1,0:T(8,128)S(1)}, f32[8,128]{1,0:T(8,128)S(1)}, u32[]{:S(2)}, u32[]{:S(2)}) collective-permute-start(f32[8,128]{1,0:T(8,128)S(1)} %get-tuple-element.53.refs_1_), channel_id=1, source_target_pairs={{0,24},{8,0},{16,8},{24,16},{1,25},{9,1},{17,9},{25,17},{2,26},{10... | collective-permute-start | bytes 12296 | tf_op jit(solution)/shard_map/ppermute | solution.py:531
  28.0 1.6 %collective-permute-start.16 = (f32[2,8,32,128]{3,2,1,0:T(8,128)S(1)}, f32[2,8,32,128]{3,2,1,0:T(8,128)S(1)}, u32[]{:S(2)}, u32[]{:S(2)}) collective-permute-start(f32[2,8,32,128]{3,2,1,0:T(8,128)S(1)} %get-tuple-element.48.refs_6_), channel_id=1, source_target_pairs={{0,1},{1,0},{2,3},{3,2},{4,5},{5,4},{6,7},{7,6},{8,9},{9,8},{10,11... | collective-permute-start | bytes 786440 | tf_op jit(solution)/shard_map/ppermute | solution.py:528
  29.6 1.1 order.1
  31.2 5.8 %driven.1 = (f32[2,2,32,4,8,128]{5,4,3,2,1,0:T(8,128)S(1)}, f32[4,32,32,128]{3,2,1,0:T(8,128)S(1)}, f32[32,32,128]{2,1,0:T(8,128)S(1)}) custom-call(s32[1]{0:T(128)} %bitcast.3.yc_ref, f32[32,32,128]{2,1,0:T(8,128)S(1)} %forward0.1.s0, f32[32,32,128]{2,1,0:T(8,128)S(1)} %collective-permute-done.10.s1, f32[4,2,8,32,128]{4,3,2,1,0:T(8,128)S(1)} %get-tuple-element.55.u_s, ...), custom_call_target="tpu_custom_call" | custom-call | flops 3000000000 | bytes 6000000 | tf_op jit(solution)/shard_map/driven/pallas_call | solution.py:609
  37.1 1.7 %collective-permute-start.18 = (f32[2,8,32,128]{3,2,1,0:T(8,128)S(1)}, f32[2,8,32,128]{3,2,1,0:T(8,128)S(1)}, u32[]{:S(2)}, u32[]{:S(2)}) collective-permute-start(f32[2,8,32,128]{3,2,1,0:T(8,128)S(1)} %get-tuple-element.72), channel_id=1, source_target_pairs={{0,1},{1,0},{2,3},{3,2},{4,5},{5,4},{6,7},{7,6},{8,9},{9,8},{10,11... | collective-permute-start | bytes 786440 | tf_op jit(solution)/shard_map/ppermute | solution.py:528
  39.2 4.1 %own.1 = (f32[2,8,24,128]{3,2,1,0:T(8,128)S(1)}, f32[2,8,24,128]{3,2,1,0:T(8,128)S(1)}, f32[2,8,24,128]{3,2,1,0:T(8,128)S(1)}, f32[2,8,24,128]{3,2,1,0:T(8,128)S...) custom-call(s32[1]{0:T(128)} %bitcast.q_ref, s32[1]{0:T(128)} %bitcast.3.yc_ref, ...), custom_call_target="tpu_custom_call" | custom-call | flops 3000000000 | bytes 8000000 | tf_op jit(solution)/shard_map/own/pallas_call | solution.py:620
  43.3 4.8 %collective-permute-done.17.refs_0_ = f32[2,8,32,128]{3,2,1,0:T(8,128)S(1)} collective-permute-done((f32[2,8,32,128]{3,2,1,0:T(8,128)S(1)}, f32[2,8,32,128]{3,2,1,0:T(8,128)S(1)}, u32[]{:S(2)}, u32[]{:S(2)}) %collective-permute-start.17) | collective-permute-done | bytes 262176 | tf_op jit(solution)/shard_map/ppermute | solution.py:528
  48.1 4.2 %shard_map.185 = (f32[32,32,128]{2,1,0:T(8,128)S(1)}, f32[32,32,128]{2,1,0:T(8,128)S(1)}, f32[32,32,128]{2,1,0:T(8,128)S(1)}, f32[20,32,128]{2,1,0:T(8,128)S(1)}...) custom-call(s32[1]{0:T(128)} %bitcast.q_ref, s32[1]{0:T(128)} %bitcast.3.yc_ref, ...), custom_call_target="tpu_custom_call" | custom-call | flops 4000000000 | bytes 4000000 | tf_op jit(solution)/shard_map/pallas_call | solution.py:638
  52.3 1.4 %collective-permute-done.18.refs_0_ = f32[2,8,32,128]{3,2,1,0:T(8,128)S(1)} collective-permute-done((f32[2,8,32,128]{3,2,1,0:T(8,128)S(1)}, f32[2,8,32,128]{3,2,1,0:T(8,128)S(1)}, u32[]{:S(2)}, u32[]{:S(2)}) %collective-permute-start.18) | collective-permute-done | bytes 262176 | tf_op jit(solution)/shard_map/ppermute | solution.py:528
  53.7 2.3 %shard_map.186 = (f32[32,32,128]{2,1,0:T(8,128)S(1)}, f32[32,32,128]{2,1,0:T(8,128)S(1)}, f32[32,32,128]{2,1,0:T(8,128)S(1)}, f32[20,32,128]{2,1,0:T(8,128)S(1)}...) custom-call(s32[1]{0:T(128)} %bitcast.q_ref, ...), custom_call_target="tpu_custom_call", output_to_operand_aliasing={{0}: (12, {}), {1}: (13, {}), {2}: (14, {}), {3}: (15, {}),... | custom-call | flops 2000000000 | bytes 2000000 | tf_op jit(solution)/shard_map/pallas_call | solution.py:638
  56.0 1.8 %collective-permute-start.21 = (f32[32,32,128]{2,1,0:T(8,128)S(1)}, f32[32,32,128]{2,1,0:T(8,128)S(1)}, u32[]{:S(2)}, u32[]{:S(2)}) collective-permute-start(f32[32,32,128]{2,1,0:T(8,128)S(1)} %get-tuple-element.89), channel_id=1, source_target_pairs={{0,4},{2,6},{4,0},{6,2},{1,5},{3,7},{5,1},{7,3},{8,12},{10,14},{12... | collective-permute-start | bytes 1572872 | tf_op jit(solution)/shard_map/ppermute | solution.py:525
  57.8 3.1 %shard_map.187 = (f32[32,32,128]{2,1,0:T(8,128)S(1)}, f32[32,32,128]{2,1,0:T(8,128)S(1)}, f32[20,32,128]{2,1,0:T(8,128)S(1)}, f32[12,32,128]{2,1,0:T(8,128)S(1)}, f32[32,32,128]{2,1,0:T(8,128)}) custom-call(s32[1]{0:T(128)} %bitcast.q_ref, s32[1]{0:T(128)} %bitcast.3.yc_ref, ...), custom_call_target="tpu_custom_call", output_to_operand_aliasing={{0}: (12, {}), {1}: (13, {}), {2}: (14, {}), {3}: (15, {})} | custom-call | flops 4000000000 | bytes 4000000 | tf_op jit(solution)/shard_map/pallas_call | solution.py:638
  61.7 2.5 %collective-permute-start.20 = (f32[32,32,128]{2,1,0:T(8,128)S(1)}, f32[32,32,128]{2,1,0:T(8,128)S(1)}, u32[]{:S(2)}, u32[]{:S(2)}) collective-permute-start(f32[32,32,128]{2,1,0:T(8,128)S(1)} %get-tuple-element.85), channel_id=1, source_target_pairs={{0,2},{2,0},{4,6},{6,4},{1,3},{3,1},{5,7},{7,5},{8,10},{10,8},{12,... | collective-permute-start | bytes 1572872 | tf_op jit(solution)/shard_map/ppermute | solution.py:525
  64.2 1.4 %collective-permute-start.13 = (f32[2,8,24,128]{3,2,1,0:T(8,128)S(1)}, f32[2,8,24,128]{3,2,1,0:T(8,128)S(1)}, u32[]{:S(2)}, u32[]{:S(2)}) collective-permute-start(f32[2,8,24,128]{3,2,1,0:T(8,128)S(1)} %get-tuple-element.63), channel_id=1, source_target_pairs={{0,6},{2,4},{4,2},{6,0},{1,7},{3,5},{5,3},{7,1},{8,14},{10,12},{12... | collective-permute-start | bytes 589832 | tf_op jit(solution)/shard_map/ppermute | solution.py:525
  65.5 14.2 %collective-permute-done.12.refs_2_ = f32[2,8,24,128]{3,2,1,0:T(8,128)S(1)} collective-permute-done((f32[2,8,24,128]{3,2,1,0:T(8,128)S(1)}, f32[2,8,24,128]{3,2,1,0:T(8,128)S(1)}, u32[]{:S(2)}, u32[]{:S(2)}) %collective-permute-start.12) | collective-permute-done | bytes 196640 | tf_op jit(solution)/shard_map/ppermute | solution.py:525
  80.6 1.6 %collective-permute-start.14 = (f32[4,8,24,128]{3,2,1,0:T(8,128)S(1)}, f32[4,8,24,128]{3,2,1,0:T(8,128)S(1)}, u32[]{:S(2)}, u32[]{:S(2)}) collective-permute-start(f32[4,8,24,128]{3,2,1,0:T(8,128)S(1)} %get-tuple-element.64), channel_id=1, source_target_pairs={{0,8},{8,16},{16,24},{24,0},{1,9},{9,17},{17,25},{25,1},{2,10},{10... | collective-permute-start | bytes 1179656 | tf_op jit(solution)/shard_map/ppermute | solution.py:531
  82.2 2.2 %collective-permute-start.15 = (f32[4,8,24,128]{3,2,1,0:T(8,128)S(1)}, f32[4,8,24,128]{3,2,1,0:T(8,128)S(1)}, u32[]{:S(2)}, u32[]{:S(2)}) collective-permute-start(f32[4,8,24,128]{3,2,1,0:T(8,128)S(1)} %get-tuple-element.65), channel_id=1, source_target_pairs={{0,24},{8,0},{16,8},{24,16},{1,25},{9,1},{17,9},{25,17},{2,26},{10... | collective-permute-start | bytes 1179656 | tf_op jit(solution)/shard_map/ppermute | solution.py:531
  85.2 1.5 %collective-permute-start.22 = (f32[12,32,128]{2,1,0:T(8,128)S(1)}, f32[12,32,128]{2,1,0:T(8,128)S(1)}, u32[]{:S(2)}, u32[]{:S(2)}) collective-permute-start(f32[12,32,128]{2,1,0:T(8,128)S(1)} %get-tuple-element.90), channel_id=1, source_target_pairs={{0,6},{2,4},{4,2},{6,0},{1,7},{3,5},{5,3},{7,1},{8,14},{10,12},{12... | collective-permute-start | bytes 589832 | tf_op jit(solution)/shard_map/ppermute | solution.py:525
  86.7 5.5 %collective-permute-done.22.late_ref.refs_1_ = f32[12,32,128]{2,1,0:T(8,128)S(1)} collective-permute-done((f32[12,32,128]{2,1,0:T(8,128)S(1)}, f32[12,32,128]{2,1,0:T(8,128)S(1)}, u32[]{:S(2)}, u32[]{:S(2)}) %collective-permute-start.22) | collective-permute-done | bytes 196640 | tf_op jit(solution)/shard_map/ppermute | solution.py:525
  94.3 7.8 %collective-permute-done.15.right_ref = f32[4,8,24,128]{3,2,1,0:T(8,128)S(1)} collective-permute-done((f32[4,8,24,128]{3,2,1,0:T(8,128)S(1)}, f32[4,8,24,128]{3,2,1,0:T(8,128)S(1)}, u32[]{:S(2)}, u32[]{:S(2)}) %collective-permute-start.15) | collective-permute-done | bytes 393248 | tf_op jit(solution)/shard_map/ppermute | solution.py:531
  102.2 1.4 %spread.1 = f32[1,2,8,32,512]{4,3,2,1,0:T(8,128)} custom-call(s32[112,128]{1,0:T(8,128)S(1)} %get-tuple-element.52.refs_7_.tab_ref, f32[4,8,24,128]{3,2,1,0:T(8,128)S(1)} %collective-permute-done.14.left_ref, f32[4,8,24,128]{3,2,1,0:T(8,128)S(1)} %collective-permute-done.15.right_ref), custom_call_target="tpu_custom_call" | custom-call | bytes 2000000 | tf_op jit(solution)/shard_map/spread/pallas_call | solution.py:713
  103.6 1.5 %shard_map.190.refs_3_ = f32[1,32,32,512]{3,2,1,0:T(8,128)} custom-call(s32[1]{0:T(128)} %bitcast.q_ref, f32[32,32,512]{2,1,0:T(8,128)S(1)} %get-tuple-element.86.acc_ref, bf16[256,512]{1,0:T(8,128)(2,1)S(1)} %get-tuple-element.87.wh_ref, bf16[256,512]{1,0:T(8,128)(2,1)S(1)} %get-tuple-element.88.wl_ref, ...), custom_call_target="tpu_custom_call" | custom-call | flops 1000000000 | bytes 3000000 | tf_op jit(solution)/shard_map/pallas_call | solution.py:698
  105.0 1.2 %shard_map.191 = f32[1,32,32,512]{3,2,1,0:T(8,128)} custom-call(s32[1]{0:T(128)} %bitcast.q_ref, f32[32,32,512]{2,1,0:T(8,128)S(1)} %get-tuple-element.86.acc_ref, bf16[256,512]{1,0:T(8,128)(2,1)S(1)} %get-tuple-element.87.wh_ref, bf16[256,512]{1,0:T(8,128)(2,1)S(1)} %get-tuple-element.88.wl_ref, ...), custom_call_target="tpu_custom_call", output_to_operand_aliasing={{}: (7, {})} | custom-call | flops 1000000000 | bytes 3000000 | tf_op jit(solution)/shard_map/pallas_call | solution.py:698
  (74 shorter events, 9.2 us)
Async XLA Ops:
  0.6 12.9 %copy-start = (f32[1,2,8,32,512]{4,3,2,1,0:T(8,128)S(1)}, f32[1,2,8,32,512]{4,3,2,1,0:T(8,128)}, u32[]{:S(2)}) copy-start(f32[1,2,8,32,512]{4,3,2,1,0:T(8,128)} %refs_3_.1) | copy-start | bytes 3145732
  6.9 23.8 %collective-permute-start.10 = (f32[32,32,128]{2,1,0:T(8,128)S(1)}, f32[32,32,128]{2,1,0:T(8,128)S(1)}, u32[]{:S(2)}, u32[]{:S(2)}) collective-permute-start(f32[32,32,128]{2,1,0:T(8,128)S(1)} %forward0.1.s0), channel_id=1, source_target_pairs={{0,1},{1,0},{2,3},{3,2},{4,5},{5,4},{6,7},{7,6},{8,9},{9,8},{10,11... | collective-permute-start | bytes 1572872 | tf_op jit(solution)/shard_map/ppermute | solution.py:528
  10.0 3.8 %collective-permute-start.2 = (f32[8]{0:T(128)S(1)}, f32[8]{0:T(128)S(1)}, u32[]{:S(2)}, u32[]{:S(2)}) collective-permute-start(f32[8]{0:T(128)S(1)} %copy-done.13), channel_id=1, source_target_pairs={{0,4},{2,6},{4,0},{6,2},{1,5},{3,7},{5,1},{7,3},{8,12},{10,14},{12... | collective-permute-start | bytes 104 | tf_op jit(solution)/shard_map/ppermute | solution.py:525
  11.5 2.4 %collective-permute-start.1 = (f32[8]{0:T(128)S(1)}, f32[8]{0:T(128)S(1)}, u32[]{:S(2)}, u32[]{:S(2)}) collective-permute-start(f32[8]{0:T(128)S(1)} %copy-done.13), channel_id=1, source_target_pairs={{0,2},{2,0},{4,6},{6,4},{1,3},{3,1},{5,7},{7,5},{8,10},{10,8},{12,... | collective-permute-start | bytes 104 | tf_op jit(solution)/shard_map/ppermute | solution.py:525
  11.5 4.4 %collective-permute-start.3 = (f32[8]{0:T(128)S(1)}, f32[8]{0:T(128)S(1)}, u32[]{:S(2)}, u32[]{:S(2)}) collective-permute-start(f32[8]{0:T(128)S(1)} %copy-done.13), channel_id=1, source_target_pairs={{0,6},{2,4},{4,2},{6,0},{1,7},{3,5},{5,3},{7,1},{8,14},{10,12},{12... | collective-permute-start | bytes 104 | tf_op jit(solution)/shard_map/ppermute | solution.py:525
  12.2 9.9 %collective-permute-start = (f32[32]{0:T(128)S(1)}, f32[32]{0:T(128)S(1)}, u32[]{:S(2)}, u32[]{:S(2)}) collective-permute-start(f32[32]{0:T(128)S(1)} %copy-done.12), channel_id=1, source_target_pairs={{0,1},{1,0},{2,3},{3,2},{4,5},{5,4},{6,7},{7,6},{8,9},{9,8},{10,11... | collective-permute-start | bytes 392 | tf_op jit(solution)/shard_map/ppermute | solution.py:528
  13.8 15.9 %copy-start.8 = (s32[4,32]{1,0:T(4,128)S(1)}, s32[4,32]{1,0:T(4,128)}, u32[]{:S(2)}) copy-start(s32[4,32]{1,0:T(4,128)} %open_ref.1) | copy-start | bytes 1540
  13.8 15.9 %copy-start.9 = (s32[4,32]{1,0:T(4,128)S(1)}, s32[4,32]{1,0:T(4,128)}, u32[]{:S(2)}) copy-start(s32[4,32]{1,0:T(4,128)} %owner_ref.1) | copy-start | bytes 1540
  13.8 15.8 %copy-start.10 = (f32[512]{0:T(512)S(1)}, f32[512]{0:T(512)}, u32[]{:S(2)}) copy-start(f32[512]{0:T(512)} %param.25) | copy-start | bytes 6148
  13.8 15.8 %copy-start.11 = (f32[32]{0:T(128)S(1)}, f32[32]{0:T(128)}, u32[]{:S(2)}) copy-start(f32[32]{0:T(128)} %sx_ref.1) | copy-start | bytes 388
  13.8 10.0 %collective-permute-start.4 = (f32[2,8,32,128]{3,2,1,0:T(8,128)S(1)}, f32[2,8,32,128]{3,2,1,0:T(8,128)S(1)}, u32[]{:S(2)}, u32[]{:S(2)}) collective-permute-start(f32[2,8,32,128]{3,2,1,0:T(8,128)S(1)} %get-tuple-element.49), channel_id=1, source_target_pairs={{0,2},{2,0},{4,6},{6,4},{1,3},{3,1},{5,7},{7,5},{8,10},{10,8},{12,... | collective-permute-start | bytes 786440 | tf_op jit(solution)/shard_map/ppermute | solution.py:525
  13.9 13.5 %collective-permute-start.5 = (f32[2,8,32,128]{3,2,1,0:T(8,128)S(1)}, f32[2,8,32,128]{3,2,1,0:T(8,128)S(1)}, u32[]{:S(2)}, u32[]{:S(2)}) collective-permute-start(f32[2,8,32,128]{3,2,1,0:T(8,128)S(1)} %get-tuple-element.50), channel_id=1, source_target_pairs={{0,4},{2,6},{4,0},{6,2},{1,5},{3,7},{5,1},{7,3},{8,12},{10,14},{12... | collective-permute-start | bytes 786440 | tf_op jit(solution)/shard_map/ppermute | solution.py:525
  15.9 15.3 %copy-start.15 = (bf16[2,2,256,256]{3,2,1,0:T(8,128)(2,1)S(1)}, bf16[2,2,256,256]{3,2,1,0:T(8,128)(2,1)}, u32[]{:S(2)}) copy-start(bf16[2,2,256,256]{3,2,1,0:T(8,128)(2,1)} %constant.30.clone.ky_ref.refs_9_) | copy-start | bytes 1572868
  15.9 12.1 %collective-permute-start.6 = (f32[2,8,32,128]{3,2,1,0:T(8,128)S(1)}, f32[2,8,32,128]{3,2,1,0:T(8,128)S(1)}, u32[]{:S(2)}, u32[]{:S(2)}) collective-permute-start(f32[2,8,32,128]{3,2,1,0:T(8,128)S(1)} %get-tuple-element.51), channel_id=1, source_target_pairs={{0,6},{2,4},{4,2},{6,0},{1,7},{3,5},{5,3},{7,1},{8,14},{10,12},{12... | collective-permute-start | bytes 786440 | tf_op jit(solution)/shard_map/ppermute | solution.py:525
  22.0 17.1 %collective-permute-start.9 = (f32[32,32,128]{2,1,0:T(8,128)S(1)}, f32[32,32,128]{2,1,0:T(8,128)S(1)}, u32[]{:S(2)}, u32[]{:S(2)}) collective-permute-start(f32[32,32,128]{2,1,0:T(8,128)S(1)} %get-tuple-element.54.refs_3_), channel_id=1, source_target_pairs={{0,1},{1,0},{2,3},{3,2},{4,5},{5,4},{6,7},{7,6},{8,9},{9,8},{10,11... | collective-permute-start | bytes 1572872 | tf_op jit(solution)/shard_map/ppermute | solution.py:528
  23.8 13.3 %collective-permute-start.8 = (f32[8,128]{1,0:T(8,128)S(1)}, f32[8,128]{1,0:T(8,128)S(1)}, u32[]{:S(2)}, u32[]{:S(2)}) collective-permute-start(f32[8,128]{1,0:T(8,128)S(1)} %get-tuple-element.53.refs_1_), channel_id=1, source_target_pairs={{0,24},{8,0},{16,8},{24,16},{1,25},{9,1},{17,9},{25,17},{2,26},{10... | collective-permute-start | bytes 12296 | tf_op jit(solution)/shard_map/ppermute | solution.py:531
  27.4 11.3 %collective-permute-start.7 = (f32[8,128]{1,0:T(8,128)S(1)}, f32[8,128]{1,0:T(8,128)S(1)}, u32[]{:S(2)}, u32[]{:S(2)}) collective-permute-start(f32[8,128]{1,0:T(8,128)S(1)} %get-tuple-element.53.refs_1_), channel_id=1, source_target_pairs={{0,8},{8,16},{16,24},{24,0},{1,9},{9,17},{17,25},{25,1},{2,10},{10... | collective-permute-start | bytes 12296 | tf_op jit(solution)/shard_map/ppermute | solution.py:531
  28.0 15.3 %collective-permute-start.16 = (f32[2,8,32,128]{3,2,1,0:T(8,128)S(1)}, f32[2,8,32,128]{3,2,1,0:T(8,128)S(1)}, u32[]{:S(2)}, u32[]{:S(2)}) collective-permute-start(f32[2,8,32,128]{3,2,1,0:T(8,128)S(1)} %get-tuple-element.48.refs_6_), channel_id=1, source_target_pairs={{0,1},{1,0},{2,3},{3,2},{4,5},{5,4},{6,7},{7,6},{8,9},{9,8},{10,11... | collective-permute-start | bytes 786440 | tf_op jit(solution)/shard_map/ppermute | solution.py:528
  30.7 17.4 %collective-permute-start.17 = (f32[2,8,32,128]{3,2,1,0:T(8,128)S(1)}, f32[2,8,32,128]{3,2,1,0:T(8,128)S(1)}, u32[]{:S(2)}, u32[]{:S(2)}) collective-permute-start(f32[2,8,32,128]{3,2,1,0:T(8,128)S(1)} %get-tuple-element.70), channel_id=1, source_target_pairs={{0,1},{1,0},{2,3},{3,2},{4,5},{5,4},{6,7},{7,6},{8,9},{9,8},{10,11... | collective-permute-start | bytes 786440 | tf_op jit(solution)/shard_map/ppermute | solution.py:528
  37.1 16.6 %collective-permute-start.18 = (f32[2,8,32,128]{3,2,1,0:T(8,128)S(1)}, f32[2,8,32,128]{3,2,1,0:T(8,128)S(1)}, u32[]{:S(2)}, u32[]{:S(2)}) collective-permute-start(f32[2,8,32,128]{3,2,1,0:T(8,128)S(1)} %get-tuple-element.72), channel_id=1, source_target_pairs={{0,1},{1,0},{2,3},{3,2},{4,5},{5,4},{6,7},{7,6},{8,9},{9,8},{10,11... | collective-permute-start | bytes 786440 | tf_op jit(solution)/shard_map/ppermute | solution.py:528
  38.7 19.1 %collective-permute-start.19 = (f32[2,8,32,128]{3,2,1,0:T(8,128)S(1)}, f32[2,8,32,128]{3,2,1,0:T(8,128)S(1)}, u32[]{:S(2)}, u32[]{:S(2)}) collective-permute-start(f32[2,8,32,128]{3,2,1,0:T(8,128)S(1)} %get-tuple-element.79), channel_id=1, source_target_pairs={{0,1},{1,0},{2,3},{3,2},{4,5},{5,4},{6,7},{7,6},{8,9},{9,8},{10,11... | collective-permute-start | bytes 786440 | tf_op jit(solution)/shard_map/ppermute | solution.py:528
  43.2 21.0 %collective-permute-start.11 = (f32[2,8,24,128]{3,2,1,0:T(8,128)S(1)}, f32[2,8,24,128]{3,2,1,0:T(8,128)S(1)}, u32[]{:S(2)}, u32[]{:S(2)}) collective-permute-start(f32[2,8,24,128]{3,2,1,0:T(8,128)S(1)} %get-tuple-element.61), channel_id=1, source_target_pairs={{0,2},{2,0},{4,6},{6,4},{1,3},{3,1},{5,7},{7,5},{8,10},{10,8},{12,... | collective-permute-start | bytes 589832 | tf_op jit(solution)/shard_map/ppermute | solution.py:525
  56.0 28.5 %collective-permute-start.21 = (f32[32,32,128]{2,1,0:T(8,128)S(1)}, f32[32,32,128]{2,1,0:T(8,128)S(1)}, u32[]{:S(2)}, u32[]{:S(2)}) collective-permute-start(f32[32,32,128]{2,1,0:T(8,128)S(1)} %get-tuple-element.89), channel_id=1, source_target_pairs={{0,4},{2,6},{4,0},{6,2},{1,5},{3,7},{5,1},{7,3},{8,12},{10,14},{12... | collective-permute-start | bytes 1572872 | tf_op jit(solution)/shard_map/ppermute | solution.py:525
  60.9 23.6 %collective-permute-start.24 = (f32[20,32,128]{2,1,0:T(8,128)S(1)}, f32[20,32,128]{2,1,0:T(8,128)S(1)}, u32[]{:S(2)}, u32[]{:S(2)}) collective-permute-start(f32[20,32,128]{2,1,0:T(8,128)S(1)} %get-tuple-element.91), channel_id=1, source_target_pairs={{0,6},{2,4},{4,2},{6,0},{1,7},{3,5},{5,3},{7,1},{8,14},{10,12},{12... | collective-permute-start | bytes 983048 | tf_op jit(solution)/shard_map/ppermute | solution.py:525
  61.7 30.9 %collective-permute-start.20 = (f32[32,32,128]{2,1,0:T(8,128)S(1)}, f32[32,32,128]{2,1,0:T(8,128)S(1)}, u32[]{:S(2)}, u32[]{:S(2)}) collective-permute-start(f32[32,32,128]{2,1,0:T(8,128)S(1)} %get-tuple-element.85), channel_id=1, source_target_pairs={{0,2},{2,0},{4,6},{6,4},{1,3},{3,1},{5,7},{7,5},{8,10},{10,8},{12,... | collective-permute-start | bytes 1572872 | tf_op jit(solution)/shard_map/ppermute | solution.py:525
  64.2 15.6 %collective-permute-start.12 = (f32[2,8,24,128]{3,2,1,0:T(8,128)S(1)}, f32[2,8,24,128]{3,2,1,0:T(8,128)S(1)}, u32[]{:S(2)}, u32[]{:S(2)}) collective-permute-start(f32[2,8,24,128]{3,2,1,0:T(8,128)S(1)} %get-tuple-element.62), channel_id=1, source_target_pairs={{0,4},{2,6},{4,0},{6,2},{1,5},{3,7},{5,1},{7,3},{8,12},{10,14},{12... | collective-permute-start | bytes 589832 | tf_op jit(solution)/shard_map/ppermute | solution.py:525
  64.2 16.3 %collective-permute-start.13 = (f32[2,8,24,128]{3,2,1,0:T(8,128)S(1)}, f32[2,8,24,128]{3,2,1,0:T(8,128)S(1)}, u32[]{:S(2)}, u32[]{:S(2)}) collective-permute-start(f32[2,8,24,128]{3,2,1,0:T(8,128)S(1)} %get-tuple-element.63), channel_id=1, source_target_pairs={{0,6},{2,4},{4,2},{6,0},{1,7},{3,5},{5,3},{7,1},{8,14},{10,12},{12... | collective-permute-start | bytes 589832 | tf_op jit(solution)/shard_map/ppermute | solution.py:525
  80.6 13.7 %collective-permute-start.14 = (f32[4,8,24,128]{3,2,1,0:T(8,128)S(1)}, f32[4,8,24,128]{3,2,1,0:T(8,128)S(1)}, u32[]{:S(2)}, u32[]{:S(2)}) collective-permute-start(f32[4,8,24,128]{3,2,1,0:T(8,128)S(1)} %get-tuple-element.64), channel_id=1, source_target_pairs={{0,8},{8,16},{16,24},{24,0},{1,9},{9,17},{17,25},{25,1},{2,10},{10... | collective-permute-start | bytes 1179656 | tf_op jit(solution)/shard_map/ppermute | solution.py:531
  82.2 20.0 %collective-permute-start.15 = (f32[4,8,24,128]{3,2,1,0:T(8,128)S(1)}, f32[4,8,24,128]{3,2,1,0:T(8,128)S(1)}, u32[]{:S(2)}, u32[]{:S(2)}) collective-permute-start(f32[4,8,24,128]{3,2,1,0:T(8,128)S(1)} %get-tuple-element.65), channel_id=1, source_target_pairs={{0,24},{8,0},{16,8},{24,16},{1,25},{9,1},{17,9},{25,17},{2,26},{10... | collective-permute-start | bytes 1179656 | tf_op jit(solution)/shard_map/ppermute | solution.py:531
  84.5 19.0 %collective-permute-start.25 = (f32[20,32,128]{2,1,0:T(8,128)S(1)}, f32[20,32,128]{2,1,0:T(8,128)S(1)}, u32[]{:S(2)}, u32[]{:S(2)}) collective-permute-start(f32[20,32,128]{2,1,0:T(8,128)S(1)} %shard_map.189), channel_id=1, source_target_pairs={{0,2},{2,0},{4,6},{6,4},{1,3},{3,1},{5,7},{7,5},{8,10},{10,8},{12,... | collective-permute-start | bytes 983048 | tf_op jit(solution)/shard_map/ppermute | solution.py:525
  85.2 6.9 %collective-permute-start.22 = (f32[12,32,128]{2,1,0:T(8,128)S(1)}, f32[12,32,128]{2,1,0:T(8,128)S(1)}, u32[]{:S(2)}, u32[]{:S(2)}) collective-permute-start(f32[12,32,128]{2,1,0:T(8,128)S(1)} %get-tuple-element.90), channel_id=1, source_target_pairs={{0,6},{2,4},{4,2},{6,0},{1,7},{3,5},{5,3},{7,1},{8,14},{10,12},{12... | collective-permute-start | bytes 589832 | tf_op jit(solution)/shard_map/ppermute | solution.py:525
  92.1 12.9 %collective-permute-start.23 = (f32[12,32,128]{2,1,0:T(8,128)S(1)}, f32[12,32,128]{2,1,0:T(8,128)S(1)}, u32[]{:S(2)}, u32[]{:S(2)}) collective-permute-start(f32[12,32,128]{2,1,0:T(8,128)S(1)} %shard_map.188), channel_id=1, source_target_pairs={{0,2},{2,0},{4,6},{6,4},{1,3},{3,1},{5,7},{7,5},{8,10},{10,8},{12,... | collective-permute-start | bytes 589832 | tf_op jit(solution)/shard_map/ppermute | solution.py:525
  (13 other events, 52.6 us)
